TPU v7x, 32 devices: a whole 2x2x4 slice. The times are simulated.
32 devices in a mesh: gx: 8 (over z, y), gy: 4 (over x, core).
Axes of the slice: x: 2, y: 2, z: 4, core: 2. Of those that a mesh axis runs over, the one named last changes fastest.
Arguments:
- state_in: float32 [5, 16, 32, 32, 128], P(None, None, 'gx', 'gy'), may hold values from -6 to 6
- sponge: float32 [32, 32, 128], P('gx', 'gy'), may hold values from 0.05 to 0.5
- mean_velocity: float32 [3], replicated, may hold values from -0.6 to 0.6
- wall_vector: float32 [5], replicated, may hold values from -3 to 3
- mode_shapes: float32 [16, 8192], P(None, ('gx', 'gy')), may hold values from -6 to 6
- wall_nodes: int32 [4, 32, 128], P(None, 'gx'), may hold values from 0 to 8191
- wall_weights: float32 [4, 32, 128], P(None, 'gx'), may hold values from 0.1 to 1
- wall_count: int32 [32], P('gx'), may hold values from 32 to 128
Outputs:
- state_out: float32 [5, 16, 32, 32, 128], P(None, None, 'gx', 'gy')
- r_factor: float32 [32, 32], replicated
All inputs are finite; a program needn't handle non-finite values.
Results may differ from a plain program's by a relative error of at most 0.00013.
Values sent between devices are 32-bit elements; how exact they have to be, the bound alone decides.
No kernel may reach another device: no remote copies, remote signals or barrier semaphores. Data moves between devices by JAX's collectives and lax.ppermute only.
A program may use at most 192 MiB of HBM per device.

v0:
```python
import math

import jax
import jax.numpy as jnp
import numpy as np
from jax import lax
from jax.sharding import PartitionSpec as P

STEPS = 2


C_SOUND = 1.0
NU_DAMP = 0.25
DT_STEP = 0.4
PULSE_MID = 0.8
PULSE_WIDTH = 0.5


def padded_2(x, sides, width):
    for axis, dim in sides:
        size, length = (lax.axis_size(axis), x.shape[dim])
        up = [(i, (i + 1) % size) for i in range(size - 1)]
        down = [(j, i) for i, j in up]
        last = lax.slice_in_dim(x, length - width, length, axis=dim)
        initial = lax.slice_in_dim(x, 0, width, axis=dim)
        before = lax.ppermute(last, axis, up)
        after = lax.ppermute(initial, axis, down)
        x = jnp.concatenate([before, x, after], axis=dim)
    return x


def pulse(time_now):
    return math.exp(-(((time_now - PULSE_MID) / PULSE_WIDTH) ** 2))


def jacobians(velocity):
    identity = jnp.eye(5, dtype=velocity.dtype)
    matrices = []
    for dimension in range(3):
        coupling = np.zeros((5, 5))
        coupling[0, 1 + dimension] = 1.0
        coupling[1 + dimension, 4] = 1.0
        coupling[4, 1 + dimension] = C_SOUND * C_SOUND
        matrices.append(velocity[dimension] * identity + jnp.asarray(coupling, velocity.dtype))
    return jnp.stack(matrices)


def rates(padded, jacobian, sponge_here, wall_rows, wall_line):
    highest = lax.Precision.HIGHEST
    center = padded[:, :, 1:-1, 1:-1, :]
    east_side = padded[:, :, 2:, 1:-1, :]
    west_side = padded[:, :, :-2, 1:-1, :]
    north_side = padded[:, :, 1:-1, 2:, :]
    south_side = padded[:, :, 1:-1, :-2, :]
    zero_plane = jnp.zeros_like(center[..., :1])
    upper_side = jnp.concatenate([center[..., 1:], zero_plane], axis=4)
    lower_side = jnp.concatenate([zero_plane, center[..., :-1]], axis=4)
    flux_sum = (
        jnp.einsum("fg,gmxyz->fmxyz", jacobian[0], east_side - west_side, precision=highest)
        + jnp.einsum("fg,gmxyz->fmxyz", jacobian[1], north_side - south_side, precision=highest)
        + jnp.einsum("fg,gmxyz->fmxyz", jacobian[2], upper_side - lower_side, precision=highest)
    )
    source = wall_rows[:, :, :, None, :] * wall_line[None, None, None, :, None]
    neighbours = east_side + west_side + north_side + south_side + upper_side + lower_side
    return (
        -0.5 * flux_sum
        + NU_DAMP * (neighbours - 6.0 * center)
        - sponge_here[None, None] * center
        + source
    )


def gather_terms(node_piece, local_pos, weights):
    piece_size = node_piece.shape[1]
    inside = (local_pos >= 0) & (local_pos < piece_size)
    values_taken = jnp.take(node_piece, jnp.clip(local_pos, 0, piece_size - 1), axis=1)
    return jnp.sum(jnp.where(inside, weights, 0.0)[None] * values_taken, axis=1)


def face_rate(field_state, jacobian, sponge, wall_rows, wall_line):
    padded = padded_2(field_state, (("gx", 2), ("gy", 3)), 1)
    return rates(padded, jacobian, sponge, wall_rows, wall_line)


def runge_step(state, rate_fn, time_now):
    rate_one = rate_fn(state, time_now)
    rate_two = rate_fn(state + 0.5 * DT_STEP * rate_one, time_now + 0.5 * DT_STEP)
    rate_three = rate_fn(state + 0.5 * DT_STEP * rate_two, time_now + 0.5 * DT_STEP)
    rate_four = rate_fn(state + DT_STEP * rate_three, time_now + DT_STEP)
    return state + DT_STEP / 6.0 * (rate_one + 2.0 * rate_two + 2.0 * rate_three + rate_four)


def local(
    state_in, sponge, mean_velocity, wall_vector, mode_shapes, wall_nodes, wall_weights, wall_count
):
    modes_here = state_in.shape[1]
    cells_x = state_in.shape[2]
    cells_y = state_in.shape[3]
    cells_z = state_in.shape[4]
    gx_size = lax.axis_size("gx")
    gy_size = lax.axis_size("gy")
    gy_here = lax.axis_index("gy")
    jacobian = jacobians(mean_velocity)
    forcing = gather_terms(
        lax.all_gather(mode_shapes, ("gx", "gy"), axis=1, tiled=True), wall_nodes, wall_weights
    )
    wall_mask = (jnp.arange(cells_z)[None, :] < wall_count[:, None]).astype(jnp.float32)
    forcing = forcing * wall_mask[None]
    wall_rows = wall_vector[:, None, None, None] * forcing[None]
    state = state_in
    wall_base = (jnp.arange(cells_y) + gy_here * cells_y == 0).astype(jnp.float32)

    def advance(state_now, time_now):

        def rate_fn(field_state, time_at):
            return face_rate(field_state, jacobian, sponge, wall_rows, wall_base * pulse(time_at))

        return runge_step(state_now, rate_fn, time_now)

    stacked = []
    for step in range(STEPS):
        state = advance(state, step * DT_STEP)
        stacked.append(state)
    rows_total = 5.0 * cells_x * gx_size * cells_y * gy_size * cells_z
    snap_count = STEPS * modes_here
    snapshots = jnp.stack(stacked)
    local_gram = jnp.einsum(
        "sfmxyz,tfnxyz->smtn", snapshots, snapshots, precision=lax.Precision.HIGHEST
    ).reshape(snap_count, snap_count)
    gram_matrix = lax.psum(local_gram, ("gx", "gy")) / rows_total
    r_factor = jnp.linalg.cholesky(gram_matrix).T
    return (stacked[-1], r_factor)


def solution(mesh):
    placed = (
        P(None, None, "gx", "gy", None),
        P("gx", "gy", None),
        P(),
        P(),
        P(None, ("gx", "gy")),
        P(None, "gx", None),
        P(None, "gx", None),
        P("gx"),
    )
    return jax.shard_map(
        local,
        mesh=mesh,
        in_specs=placed,
        out_specs=(P(None, None, "gx", "gy", None), P()),
        check_vma=False,
    )
```

profile of v0, /device:TPU:0, one launch (start us, length us, event | category | flops | bytes accessed | tf_op | source)
XLA Modules:
  0.0 501.6 jit_solution(947815659723375712)
XLA Ops:
  5.2 6.3 %collective-permute-start.1 = (f32[5,16,1,8,128]{4,0,3,2,1:T(8,128)}, f32[5,16,1,8,128]{4,0,3,2,1:T(8,128)}, u32[]{:S(2)}, u32[]{:S(2)}) collective-permute-start(f32[5,16,1,8,128]{4,0,3,2,1:T(8,128)} %get-tuple-element.53), channel_id=1, source_target_pairs={{0,4},{4,8},{8,12},{12,16},{16,20},{20,24},{24,28},{1,5},{5,9},{9,... | collective-permute-start | bytes 983048 | tf_op jit(solution)/shard_map/ppermute | solution.py:26
  15.2 62.8 %all_gather.3 = f32[16,8192]{0,1:T(8,128)} all-gather(f32[16,256]{0,1:T(8,128)S(1)} %copy.42), channel_id=1, replica_groups=mesh['gx'=8,'gy'=4] {'gx','gy'}, dimensions={1}, use_global_device_ids=true | all-gather | bytes 540672 | tf_op jit(solution)/shard_map/all_gather | solution.py:105
  78.1 7.7 %gather_fusion = f32[2048,16]{1,0:T(8,128)S(1)} fusion(f32[16,8192]{0,1:T(8,128)} %all_gather.3, s32[2048]{0:T(1024)S(1)} %broadcast_clamp_fusion), kind=kCustom, calls=%fused_computation | custom fusion | bytes 270336 | tf_op jit(solution)/shard_map/jit(_take)/gather | solution.py:76
  87.3 6.4 %fusion.63 = f32[5,16,4,8,128]{4,0,3,2,1:T(8,128)} fusion(f32[5,16,4,8,127]{4,0,3,2,1:T(8,128)} %get-tuple-element.55, f32[5,16,4,8,127]{4,0,3,2,1:T(8,128)} %get-tuple-element.54, f32[5,5]{1,0:T(8,128)S(1)} %copy-done.5, f32[]{:T(128)} %bitcast.6), kind=kOutput, calls=%fused_computation.127 | convolution fusion | flops 19988556 | bytes 3911784 | tf_op jit(solution)/shard_map/fg,gmxyz->fmxyz/dot_general | solution.py:61
  112.0 8.1 %multiply_add_fusion.13 = (f32[5,16,4,8,128]{4,0,3,2,1:T(8,128)S(1)}, f32[5,16,4,8,128]{4,0,3,2,1:T(8,128)S(1)}) fusion(f32[5,16,4,8,128]{4,3,2,1,0:T(8,128)S(1)} %copy-done.3, f32[8]{0:T(128)S(1)} %broadcast_select_fusion.3, f32[5,16,4,128]{3,0,2,1:T(8,128)S(1)} %broadcast_multiply_fusion, f32[4,8,128]{2,1,0:T(8,128)S(1)} %copy-done.7, ...), kind=kOutput, calls=%fused_computation.124 | convolution fusion | flops 27852876 | bytes 13758600 | tf_op jit(solution)/shard_map/fg,gmxyz->fmxyz/dot_general | solution.py:59
  131.3 8.5 %collective-permute-done.4 = f32[5,16,1,8,128]{4,0,3,2,1:T(8,128)S(1)} collective-permute-done((f32[5,16,1,8,128]{4,0,3,2,1:T(8,128)S(1)}, f32[5,16,1,8,128]{4,0,3,2,1:T(8,128)S(1)}, u32[]{:S(2)}, u32[]{:S(2)}) %collective-permute-start.4) | collective-permute-done | bytes 327712 | tf_op jit(solution)/shard_map/ppermute | solution.py:27
  139.9 9.8 %collective-permute-start.7 = (f32[5,16,6,1,128]{4,0,3,2,1:T(8,128)S(1)}, f32[5,16,6,1,128]{4,0,3,2,1:T(8,128)S(1)}, u32[]{:S(2)}, u32[]{:S(2)}) collective-permute-start(f32[5,16,6,1,128]{4,0,3,2,1:T(8,128)S(1)} %get-tuple-element.20), channel_id=1, source_target_pairs={{0,1},{1,2},{2,3},{4,5},{5,6},{6,7},{8,9},{9,10},{10,11},{12,13},{... | collective-permute-start | bytes 737288 | tf_op jit(solution)/shard_map/ppermute | solution.py:26
  156.3 7.6 %multiply_add_fusion.12 = (f32[5,16,4,8,128]{4,0,3,2,1:T(8,128)S(1)}, f32[5,16,4,8,128]{4,0,3,2,1:T(8,128)}) fusion(f32[5,16,4,8,128]{4,3,2,1,0:T(8,128)S(1)} %copy-done.3, f32[8]{0:T(128)S(1)} %broadcast_select_fusion.2, f32[5,16,4,128]{3,0,2,1:T(8,128)S(1)} %broadcast_multiply_fusion, f32[5,16,4,8,128]{4,0,3,2,1:T(8,128)S(1)} %get-tuple-element.59, ...), kind=kOutput, calls=%fused_computation.117 | convolution fusion | flops 29163596 | bytes 11792520 | tf_op jit(solution)/shard_map/fg,gmxyz->fmxyz/dot_general | solution.py:59
  170.2 5.6 %collective-permute-done.9 = f32[5,16,1,8,128]{4,0,3,2,1:T(8,128)S(1)} collective-permute-done((f32[5,16,1,8,128]{4,0,3,2,1:T(8,128)S(1)}, f32[5,16,1,8,128]{4,0,3,2,1:T(8,128)S(1)}, u32[]{:S(2)}, u32[]{:S(2)}) %collective-permute-start.9) | collective-permute-done | bytes 327712 | tf_op jit(solution)/shard_map/ppermute | solution.py:26
  175.8 9.8 %collective-permute-done.8 = f32[5,16,1,8,128]{4,0,3,2,1:T(8,128)S(1)} collective-permute-done((f32[5,16,1,8,128]{4,0,3,2,1:T(8,128)S(1)}, f32[5,16,1,8,128]{4,0,3,2,1:T(8,128)S(1)}, u32[]{:S(2)}, u32[]{:S(2)}) %collective-permute-start.8) | collective-permute-done | bytes 327712 | tf_op jit(solution)/shard_map/ppermute | solution.py:27
  185.7 8.0 %collective-permute-start.11 = (f32[5,16,6,1,128]{4,0,3,2,1:T(8,128)S(1)}, f32[5,16,6,1,128]{4,0,3,2,1:T(8,128)S(1)}, u32[]{:S(2)}, u32[]{:S(2)}) collective-permute-start(f32[5,16,6,1,128]{4,0,3,2,1:T(8,128)S(1)} %get-tuple-element.18), channel_id=1, source_target_pairs={{0,1},{1,2},{2,3},{4,5},{5,6},{6,7},{8,9},{9,10},{10,11},{12,13},{... | collective-permute-start | bytes 737288 | tf_op jit(solution)/shard_map/ppermute | solution.py:26
  200.6 7.5 %multiply_add_fusion.11 = (f32[5,16,4,8,128]{4,0,3,2,1:T(8,128)S(1)}, f32[5,16,4,8,128]{4,0,3,2,1:T(8,128)}) fusion(f32[5,16,4,8,128]{4,3,2,1,0:T(8,128)S(1)} %copy-done.3, f32[8]{0:T(128)S(1)} %broadcast_select_fusion.2, f32[5,16,4,128]{3,0,2,1:T(8,128)S(1)} %broadcast_multiply_fusion, f32[5,16,4,8,128]{4,0,3,2,1:T(8,128)S(1)} %get-tuple-element.61, ...), kind=kOutput, calls=%fused_computation.110 | convolution fusion | flops 29163596 | bytes 11792520 | tf_op jit(solution)/shard_map/fg,gmxyz->fmxyz/dot_general | solution.py:59
  214.4 5.4 %collective-permute-done.13 = f32[5,16,1,8,128]{4,0,3,2,1:T(8,128)S(1)} collective-permute-done((f32[5,16,1,8,128]{4,0,3,2,1:T(8,128)S(1)}, f32[5,16,1,8,128]{4,0,3,2,1:T(8,128)S(1)}, u32[]{:S(2)}, u32[]{:S(2)}) %collective-permute-start.13) | collective-permute-done | bytes 327712 | tf_op jit(solution)/shard_map/ppermute | solution.py:26
  219.9 11.1 %collective-permute-done.12 = f32[5,16,1,8,128]{4,0,3,2,1:T(8,128)S(1)} collective-permute-done((f32[5,16,1,8,128]{4,0,3,2,1:T(8,128)S(1)}, f32[5,16,1,8,128]{4,0,3,2,1:T(8,128)S(1)}, u32[]{:S(2)}, u32[]{:S(2)}) %collective-permute-start.12) | collective-permute-done | bytes 327712 | tf_op jit(solution)/shard_map/ppermute | solution.py:27
  231.0 6.1 %collective-permute-start.15 = (f32[5,16,6,1,128]{4,0,3,2,1:T(8,128)S(1)}, f32[5,16,6,1,128]{4,0,3,2,1:T(8,128)S(1)}, u32[]{:S(2)}, u32[]{:S(2)}) collective-permute-start(f32[5,16,6,1,128]{4,0,3,2,1:T(8,128)S(1)} %get-tuple-element.16), channel_id=1, source_target_pairs={{0,1},{1,2},{2,3},{4,5},{5,6},{6,7},{8,9},{9,10},{10,11},{12,13},{... | collective-permute-start | bytes 737288 | tf_op jit(solution)/shard_map/ppermute | solution.py:26
  244.4 8.5 %fusion.6 = f32[5,16,4,8,128]{4,0,3,2,1:T(8,128)S(1)} fusion(f32[5,16,4,8,128]{4,0,3,2,1:T(8,128)S(1)} %get-tuple-element.63, f32[5,16,4,8,128]{4,0,3,2,1:T(8,128)S(1)} %fusion.39, f32[5,16,4,8,128]{4,0,3,2,1:T(8,128)S(1)} %fusion.41, f32[5,16,1,8,128]{4,0,3,2,1:T(8,128)S(1)} %collective-permute-done.12, ...), kind=kOutput, calls=%fused_computation.14 | convolution fusion | flops 32112716 | bytes 14413992 | tf_op jit(solution)/shard_map/fg,gmxyz->fmxyz/dot_general | solution.py:59
  264.8 12.4 %collective-permute-done.16 = f32[5,16,1,8,128]{4,0,3,2,1:T(8,128)S(1)} collective-permute-done((f32[5,16,1,8,128]{4,0,3,2,1:T(8,128)S(1)}, f32[5,16,1,8,128]{4,0,3,2,1:T(8,128)S(1)}, u32[]{:S(2)}, u32[]{:S(2)}) %collective-permute-start.16) | collective-permute-done | bytes 327712 | tf_op jit(solution)/shard_map/ppermute | solution.py:27
  277.2 6.2 %collective-permute-start.19 = (f32[5,16,6,1,128]{4,0,3,2,1:T(8,128)S(1)}, f32[5,16,6,1,128]{4,0,3,2,1:T(8,128)S(1)}, u32[]{:S(2)}, u32[]{:S(2)}) collective-permute-start(f32[5,16,6,1,128]{4,0,3,2,1:T(8,128)S(1)} %get-tuple-element.14), channel_id=1, source_target_pairs={{0,1},{1,2},{2,3},{4,5},{5,6},{6,7},{8,9},{9,10},{10,11},{12,13},{... | collective-permute-start | bytes 737288 | tf_op jit(solution)/shard_map/ppermute | solution.py:26
  290.6 6.1 %multiply_add_fusion.9 = (f32[5,16,4,8,128]{4,0,3,2,1:T(8,128)S(1)}, f32[5,16,4,8,128]{4,0,3,2,1:T(8,128)}) fusion(f32[5,16,4,8,128]{4,0,3,2,1:T(8,128)S(1)} %fusion.6, f32[8]{0:T(128)S(1)} %broadcast_select_fusion.1, f32[5,16,4,128]{3,0,2,1:T(8,128)S(1)} %broadcast_multiply_fusion, f32[4,8,128]{2,1,0:T(8,128)S(1)} %copy-done.7, ...), kind=kOutput, calls=%fused_computation.96 | convolution fusion | flops 29163596 | bytes 10481800 | tf_op jit(solution)/shard_map/fg,gmxyz->fmxyz/dot_general | solution.py:59
  303.7 6.0 %collective-permute-done.21 = f32[5,16,1,8,128]{4,0,3,2,1:T(8,128)S(1)} collective-permute-done((f32[5,16,1,8,128]{4,0,3,2,1:T(8,128)S(1)}, f32[5,16,1,8,128]{4,0,3,2,1:T(8,128)S(1)}, u32[]{:S(2)}, u32[]{:S(2)}) %collective-permute-start.21) | collective-permute-done | bytes 327712 | tf_op jit(solution)/shard_map/ppermute | solution.py:26
  309.6 11.8 %collective-permute-done.20 = f32[5,16,1,8,128]{4,0,3,2,1:T(8,128)S(1)} collective-permute-done((f32[5,16,1,8,128]{4,0,3,2,1:T(8,128)S(1)}, f32[5,16,1,8,128]{4,0,3,2,1:T(8,128)S(1)}, u32[]{:S(2)}, u32[]{:S(2)}) %collective-permute-start.20) | collective-permute-done | bytes 327712 | tf_op jit(solution)/shard_map/ppermute | solution.py:27
  321.5 6.1 %collective-permute-start.23 = (f32[5,16,6,1,128]{4,0,3,2,1:T(8,128)S(1)}, f32[5,16,6,1,128]{4,0,3,2,1:T(8,128)S(1)}, u32[]{:S(2)}, u32[]{:S(2)}) collective-permute-start(f32[5,16,6,1,128]{4,0,3,2,1:T(8,128)S(1)} %get-tuple-element.12), channel_id=1, source_target_pairs={{0,1},{1,2},{2,3},{4,5},{5,6},{6,7},{8,9},{9,10},{10,11},{12,13},{... | collective-permute-start | bytes 737288 | tf_op jit(solution)/shard_map/ppermute | solution.py:26
  346.0 5.5 %collective-permute-done.25 = f32[5,16,1,8,128]{4,0,3,2,1:T(8,128)S(1)} collective-permute-done((f32[5,16,1,8,128]{4,0,3,2,1:T(8,128)S(1)}, f32[5,16,1,8,128]{4,0,3,2,1:T(8,128)S(1)}, u32[]{:S(2)}, u32[]{:S(2)}) %collective-permute-start.25) | collective-permute-done | bytes 327712 | tf_op jit(solution)/shard_map/ppermute | solution.py:26
  351.4 11.8 %collective-permute-done.24 = f32[5,16,1,8,128]{4,0,3,2,1:T(8,128)S(1)} collective-permute-done((f32[5,16,1,8,128]{4,0,3,2,1:T(8,128)S(1)}, f32[5,16,1,8,128]{4,0,3,2,1:T(8,128)S(1)}, u32[]{:S(2)}, u32[]{:S(2)}) %collective-permute-start.24) | collective-permute-done | bytes 327712 | tf_op jit(solution)/shard_map/ppermute | solution.py:27
  363.3 6.6 %collective-permute-start.27 = (f32[5,16,6,1,128]{4,0,3,2,1:T(8,128)S(1)}, f32[5,16,6,1,128]{4,0,3,2,1:T(8,128)S(1)}, u32[]{:S(2)}, u32[]{:S(2)}) collective-permute-start(f32[5,16,6,1,128]{4,0,3,2,1:T(8,128)S(1)} %get-tuple-element.10), channel_id=1, source_target_pairs={{0,1},{1,2},{2,3},{4,5},{5,6},{6,7},{8,9},{9,10},{10,11},{12,13},{... | collective-permute-start | bytes 737288 | tf_op jit(solution)/shard_map/ppermute | solution.py:26
  376.8 6.1 %multiply_add_fusion.7 = (f32[5,16,4,8,128]{4,0,3,2,1:T(8,128)S(1)}, f32[5,16,4,8,128]{4,0,3,2,1:T(8,128)}) fusion(f32[5,16,4,8,128]{4,0,3,2,1:T(8,128)S(1)} %fusion.6, f32[8]{0:T(128)S(1)} %broadcast_select_fusion, f32[5,16,4,128]{3,0,2,1:T(8,128)S(1)} %broadcast_multiply_fusion, f32[5,16,4,8,128]{4,0,3,2,1:T(8,128)S(1)} %get-tuple-element.67, ...), kind=kOutput, calls=%fused_computation.82 | convolution fusion | flops 29163596 | bytes 11792520 | tf_op jit(solution)/shard_map/fg,gmxyz->fmxyz/dot_general | solution.py:59
  390.1 5.3 %collective-permute-done.29 = f32[5,16,1,8,128]{4,0,3,2,1:T(8,128)S(1)} collective-permute-done((f32[5,16,1,8,128]{4,0,3,2,1:T(8,128)S(1)}, f32[5,16,1,8,128]{4,0,3,2,1:T(8,128)S(1)}, u32[]{:S(2)}, u32[]{:S(2)}) %collective-permute-start.29) | collective-permute-done | bytes 327712 | tf_op jit(solution)/shard_map/ppermute | solution.py:26
  395.4 11.8 %collective-permute-done.28 = f32[5,16,1,8,128]{4,0,3,2,1:T(8,128)S(1)} collective-permute-done((f32[5,16,1,8,128]{4,0,3,2,1:T(8,128)S(1)}, f32[5,16,1,8,128]{4,0,3,2,1:T(8,128)S(1)}, u32[]{:S(2)}, u32[]{:S(2)}) %collective-permute-start.28) | collective-permute-done | bytes 327712 | tf_op jit(solution)/shard_map/ppermute | solution.py:27
  407.3 6.6 %collective-permute-start.31 = (f32[5,16,6,1,128]{4,0,3,2,1:T(8,128)S(1)}, f32[5,16,6,1,128]{4,0,3,2,1:T(8,128)S(1)}, u32[]{:S(2)}, u32[]{:S(2)}) collective-permute-start(f32[5,16,6,1,128]{4,0,3,2,1:T(8,128)S(1)} %get-tuple-element.8), channel_id=1, source_target_pairs={{0,1},{1,2},{2,3},{4,5},{5,6},{6,7},{8,9},{9,10},{10,11},{12,13},{... | collective-permute-start | bytes 737288 | tf_op jit(solution)/shard_map/ppermute | solution.py:26
  422.4 7.6 %multiply_add_fusion.6 = f32[5,16,4,8,128]{4,0,3,2,1:T(8,128)S(1)} fusion(f32[5,16,4,8,128]{4,0,3,2,1:T(8,128)S(1)} %fusion.6, f32[5,16,4,8,128]{4,0,3,2,1:T(8,128)S(1)} %get-tuple-element.69, f32[5,16,4,8,128]{4,0,3,2,1:T(8,128)S(1)} %fusion.7, f32[5,16,4,8,128]{4,0,3,2,1:T(8,128)} %fusion.9, f32[5,16,1,8,128]{4,0,3,2,1:T(8,128)S(1)} %collective-permute-done.28, ...), kind=kOutput, calls=%fused_computation.75 | convolution fusion | flops 32112716 | bytes 14413992 | tf_op jit(solution)/shard_map/fg,gmxyz->fmxyz/dot_general | solution.py:59
  432.3 11.1 %fusion.87 = f32[2,16,2,16]{3,1,2,0:T(8,128)S(1)} fusion(f32[2,5,16,4,8,128]{5,1,4,3,2,0:T(8,128)S(1)} %get-tuple-element.7, f32[2,5,16,4,8,128,1]{5,1,4,3,2,0,6:T(8,128)S(1)} %get-tuple-element.6), kind=kOutput, calls=%fused_computation.150 | convolution fusion | flops 251658240 | bytes 5246976 | tf_op jit(solution)/shard_map/sfmxyz,tfnxyz->smtn/dot_general | solution.py:127
  443.6 52.5 %psum.7 = f32[32,32]{0,1:T(8,128)S(1)} all-reduce(f32[32,32]{0,1:T(8,128)S(1)} %reshape.62), channel_id=1, replica_groups=mesh['gx'=8,'gy'=4] {'gx','gy'}, use_global_device_ids=true, to_apply=%region_1.2 | all-reduce | flops 1024 | bytes 8192 | tf_op jit(solution)/shard_map/psum | solution.py:130
  (146 shorter events, 147.0 us)
Async XLA Ops:
  3.9 91.8 %collective-permute-start = (f32[5,16,1,8,128]{4,0,3,2,1:T(8,128)}, f32[5,16,1,8,128]{4,0,3,2,1:T(8,128)}, u32[]{:S(2)}, u32[]{:S(2)}) collective-permute-start(f32[5,16,1,8,128]{4,0,3,2,1:T(8,128)} %get-tuple-element.52), channel_id=1, source_target_pairs={{4,0},{8,4},{12,8},{16,12},{20,16},{24,20},{28,24},{5,1},{9,5},{13... | collective-permute-start | bytes 983048 | tf_op jit(solution)/shard_map/ppermute | solution.py:27
  5.2 88.5 %collective-permute-start.1 = (f32[5,16,1,8,128]{4,0,3,2,1:T(8,128)}, f32[5,16,1,8,128]{4,0,3,2,1:T(8,128)}, u32[]{:S(2)}, u32[]{:S(2)}) collective-permute-start(f32[5,16,1,8,128]{4,0,3,2,1:T(8,128)} %get-tuple-element.53), channel_id=1, source_target_pairs={{0,4},{4,8},{8,12},{12,16},{16,20},{20,24},{24,28},{1,5},{5,9},{9,... | collective-permute-start | bytes 983048 | tf_op jit(solution)/shard_map/ppermute | solution.py:26
  99.5 5.5 %collective-permute-start.3 = (f32[5,16,6,1,128]{4,0,3,2,1:T(8,128)}, f32[5,16,6,1,128]{4,0,3,2,1:T(8,128)}, u32[]{:S(2)}, u32[]{:S(2)}) collective-permute-start(f32[5,16,6,1,128]{4,0,3,2,1:T(8,128)} %get-tuple-element.22), channel_id=1, source_target_pairs={{0,1},{1,2},{2,3},{4,5},{5,6},{6,7},{8,9},{9,10},{10,11},{12,13},{... | collective-permute-start | bytes 737288 | tf_op jit(solution)/shard_map/ppermute | solution.py:26
  102.5 4.2 collective-permute-start.2
  120.2 11.0 %collective-permute-start.5 = (f32[5,16,1,8,128]{4,0,3,2,1:T(8,128)S(1)}, f32[5,16,1,8,128]{4,0,3,2,1:T(8,128)S(1)}, u32[]{:S(2)}, u32[]{:S(2)}) collective-permute-start(f32[5,16,1,8,128]{4,0,3,2,1:T(8,128)S(1)} %get-tuple-element.48), channel_id=1, source_target_pairs={{0,4},{4,8},{8,12},{12,16},{16,20},{20,24},{24,28},{1,5},{5,9},{9,... | collective-permute-start | bytes 983048 | tf_op jit(solution)/shard_map/ppermute | solution.py:26
  124.1 15.7 %collective-permute-start.4 = (f32[5,16,1,8,128]{4,0,3,2,1:T(8,128)S(1)}, f32[5,16,1,8,128]{4,0,3,2,1:T(8,128)S(1)}, u32[]{:S(2)}, u32[]{:S(2)}) collective-permute-start(f32[5,16,1,8,128]{4,0,3,2,1:T(8,128)S(1)} %get-tuple-element.49), channel_id=1, source_target_pairs={{4,0},{8,4},{12,8},{16,12},{20,16},{24,20},{28,24},{5,1},{9,5},{13... | collective-permute-start | bytes 983048 | tf_op jit(solution)/shard_map/ppermute | solution.py:27
  139.9 14.0 %collective-permute-start.7 = (f32[5,16,6,1,128]{4,0,3,2,1:T(8,128)S(1)}, f32[5,16,6,1,128]{4,0,3,2,1:T(8,128)S(1)}, u32[]{:S(2)}, u32[]{:S(2)}) collective-permute-start(f32[5,16,6,1,128]{4,0,3,2,1:T(8,128)S(1)} %get-tuple-element.20), channel_id=1, source_target_pairs={{0,1},{1,2},{2,3},{4,5},{5,6},{6,7},{8,9},{9,10},{10,11},{12,13},{... | collective-permute-start | bytes 737288 | tf_op jit(solution)/shard_map/ppermute | solution.py:26
  149.7 4.2 collective-permute-start.6
  164.0 11.8 %collective-permute-start.9 = (f32[5,16,1,8,128]{4,0,3,2,1:T(8,128)S(1)}, f32[5,16,1,8,128]{4,0,3,2,1:T(8,128)S(1)}, u32[]{:S(2)}, u32[]{:S(2)}) collective-permute-start(f32[5,16,1,8,128]{4,0,3,2,1:T(8,128)S(1)} %get-tuple-element.44), channel_id=1, source_target_pairs={{0,4},{4,8},{8,12},{12,16},{16,20},{20,24},{24,28},{1,5},{5,9},{9,... | collective-permute-start | bytes 983048 | tf_op jit(solution)/shard_map/ppermute | solution.py:26
  168.1 17.5 %collective-permute-start.8 = (f32[5,16,1,8,128]{4,0,3,2,1:T(8,128)S(1)}, f32[5,16,1,8,128]{4,0,3,2,1:T(8,128)S(1)}, u32[]{:S(2)}, u32[]{:S(2)}) collective-permute-start(f32[5,16,1,8,128]{4,0,3,2,1:T(8,128)S(1)} %get-tuple-element.45), channel_id=1, source_target_pairs={{4,0},{8,4},{12,8},{16,12},{20,16},{24,20},{28,24},{5,1},{9,5},{13... | collective-permute-start | bytes 983048 | tf_op jit(solution)/shard_map/ppermute | solution.py:27
  185.7 12.4 %collective-permute-start.11 = (f32[5,16,6,1,128]{4,0,3,2,1:T(8,128)S(1)}, f32[5,16,6,1,128]{4,0,3,2,1:T(8,128)S(1)}, u32[]{:S(2)}, u32[]{:S(2)}) collective-permute-start(f32[5,16,6,1,128]{4,0,3,2,1:T(8,128)S(1)} %get-tuple-element.18), channel_id=1, source_target_pairs={{0,1},{1,2},{2,3},{4,5},{5,6},{6,7},{8,9},{9,10},{10,11},{12,13},{... | collective-permute-start | bytes 737288 | tf_op jit(solution)/shard_map/ppermute | solution.py:26
  193.7 4.4 collective-permute-start.10
  208.2 11.7 %collective-permute-start.13 = (f32[5,16,1,8,128]{4,0,3,2,1:T(8,128)S(1)}, f32[5,16,1,8,128]{4,0,3,2,1:T(8,128)S(1)}, u32[]{:S(2)}, u32[]{:S(2)}) collective-permute-start(f32[5,16,1,8,128]{4,0,3,2,1:T(8,128)S(1)} %get-tuple-element.40), channel_id=1, source_target_pairs={{0,4},{4,8},{8,12},{12,16},{16,20},{20,24},{24,28},{1,5},{5,9},{9,... | collective-permute-start | bytes 983048 | tf_op jit(solution)/shard_map/ppermute | solution.py:26
  212.3 18.7 %collective-permute-start.12 = (f32[5,16,1,8,128]{4,0,3,2,1:T(8,128)S(1)}, f32[5,16,1,8,128]{4,0,3,2,1:T(8,128)S(1)}, u32[]{:S(2)}, u32[]{:S(2)}) collective-permute-start(f32[5,16,1,8,128]{4,0,3,2,1:T(8,128)S(1)} %get-tuple-element.41), channel_id=1, source_target_pairs={{4,0},{8,4},{12,8},{16,12},{20,16},{24,20},{28,24},{5,1},{9,5},{13... | collective-permute-start | bytes 983048 | tf_op jit(solution)/shard_map/ppermute | solution.py:27
  231.0 10.5 %collective-permute-start.15 = (f32[5,16,6,1,128]{4,0,3,2,1:T(8,128)S(1)}, f32[5,16,6,1,128]{4,0,3,2,1:T(8,128)S(1)}, u32[]{:S(2)}, u32[]{:S(2)}) collective-permute-start(f32[5,16,6,1,128]{4,0,3,2,1:T(8,128)S(1)} %get-tuple-element.16), channel_id=1, source_target_pairs={{0,1},{1,2},{2,3},{4,5},{5,6},{6,7},{8,9},{9,10},{10,11},{12,13},{... | collective-permute-start | bytes 737288 | tf_op jit(solution)/shard_map/ppermute | solution.py:26
  237.1 4.9 collective-permute-start.14
  253.0 11.8 %collective-permute-start.17 = (f32[5,16,1,8,128]{4,0,3,2,1:T(8,128)S(1)}, f32[5,16,1,8,128]{4,0,3,2,1:T(8,128)S(1)}, u32[]{:S(2)}, u32[]{:S(2)}) collective-permute-start(f32[5,16,1,8,128]{4,0,3,2,1:T(8,128)S(1)} %get-tuple-element.36), channel_id=1, source_target_pairs={{0,4},{4,8},{8,12},{12,16},{16,20},{20,24},{24,28},{1,5},{5,9},{9,... | collective-permute-start | bytes 983048 | tf_op jit(solution)/shard_map/ppermute | solution.py:26
  257.5 19.6 %collective-permute-start.16 = (f32[5,16,1,8,128]{4,0,3,2,1:T(8,128)S(1)}, f32[5,16,1,8,128]{4,0,3,2,1:T(8,128)S(1)}, u32[]{:S(2)}, u32[]{:S(2)}) collective-permute-start(f32[5,16,1,8,128]{4,0,3,2,1:T(8,128)S(1)} %get-tuple-element.37), channel_id=1, source_target_pairs={{4,0},{8,4},{12,8},{16,12},{20,16},{24,20},{28,24},{5,1},{9,5},{13... | collective-permute-start | bytes 983048 | tf_op jit(solution)/shard_map/ppermute | solution.py:27
  277.2 10.9 %collective-permute-start.19 = (f32[5,16,6,1,128]{4,0,3,2,1:T(8,128)S(1)}, f32[5,16,6,1,128]{4,0,3,2,1:T(8,128)S(1)}, u32[]{:S(2)}, u32[]{:S(2)}) collective-permute-start(f32[5,16,6,1,128]{4,0,3,2,1:T(8,128)S(1)} %get-tuple-element.14), channel_id=1, source_target_pairs={{0,1},{1,2},{2,3},{4,5},{5,6},{6,7},{8,9},{9,10},{10,11},{12,13},{... | collective-permute-start | bytes 737288 | tf_op jit(solution)/shard_map/ppermute | solution.py:26
  283.4 4.7 collective-permute-start.18
  296.8 12.9 %collective-permute-start.21 = (f32[5,16,1,8,128]{4,0,3,2,1:T(8,128)S(1)}, f32[5,16,1,8,128]{4,0,3,2,1:T(8,128)S(1)}, u32[]{:S(2)}, u32[]{:S(2)}) collective-permute-start(f32[5,16,1,8,128]{4,0,3,2,1:T(8,128)S(1)} %get-tuple-element.32), channel_id=1, source_target_pairs={{0,4},{4,8},{8,12},{12,16},{16,20},{20,24},{24,28},{1,5},{5,9},{9,... | collective-permute-start | bytes 983048 | tf_op jit(solution)/shard_map/ppermute | solution.py:26
  301.6 19.8 %collective-permute-start.20 = (f32[5,16,1,8,128]{4,0,3,2,1:T(8,128)S(1)}, f32[5,16,1,8,128]{4,0,3,2,1:T(8,128)S(1)}, u32[]{:S(2)}, u32[]{:S(2)}) collective-permute-start(f32[5,16,1,8,128]{4,0,3,2,1:T(8,128)S(1)} %get-tuple-element.33), channel_id=1, source_target_pairs={{4,0},{8,4},{12,8},{16,12},{20,16},{24,20},{28,24},{5,1},{9,5},{13... | collective-permute-start | bytes 983048 | tf_op jit(solution)/shard_map/ppermute | solution.py:27
  321.5 10.4 %collective-permute-start.23 = (f32[5,16,6,1,128]{4,0,3,2,1:T(8,128)S(1)}, f32[5,16,6,1,128]{4,0,3,2,1:T(8,128)S(1)}, u32[]{:S(2)}, u32[]{:S(2)}) collective-permute-start(f32[5,16,6,1,128]{4,0,3,2,1:T(8,128)S(1)} %get-tuple-element.12), channel_id=1, source_target_pairs={{0,1},{1,2},{2,3},{4,5},{5,6},{6,7},{8,9},{9,10},{10,11},{12,13},{... | collective-permute-start | bytes 737288 | tf_op jit(solution)/shard_map/ppermute | solution.py:26
  327.6 4.3 collective-permute-start.22
  339.0 12.4 %collective-permute-start.25 = (f32[5,16,1,8,128]{4,0,3,2,1:T(8,128)S(1)}, f32[5,16,1,8,128]{4,0,3,2,1:T(8,128)S(1)}, u32[]{:S(2)}, u32[]{:S(2)}) collective-permute-start(f32[5,16,1,8,128]{4,0,3,2,1:T(8,128)S(1)} %get-tuple-element.28), channel_id=1, source_target_pairs={{0,4},{4,8},{8,12},{12,16},{16,20},{20,24},{24,28},{1,5},{5,9},{9,... | collective-permute-start | bytes 983048 | tf_op jit(solution)/shard_map/ppermute | solution.py:26
  343.9 19.3 %collective-permute-start.24 = (f32[5,16,1,8,128]{4,0,3,2,1:T(8,128)S(1)}, f32[5,16,1,8,128]{4,0,3,2,1:T(8,128)S(1)}, u32[]{:S(2)}, u32[]{:S(2)}) collective-permute-start(f32[5,16,1,8,128]{4,0,3,2,1:T(8,128)S(1)} %get-tuple-element.29), channel_id=1, source_target_pairs={{4,0},{8,4},{12,8},{16,12},{20,16},{24,20},{28,24},{5,1},{9,5},{13... | collective-permute-start | bytes 983048 | tf_op jit(solution)/shard_map/ppermute | solution.py:27
  363.3 11.0 %collective-permute-start.27 = (f32[5,16,6,1,128]{4,0,3,2,1:T(8,128)S(1)}, f32[5,16,6,1,128]{4,0,3,2,1:T(8,128)S(1)}, u32[]{:S(2)}, u32[]{:S(2)}) collective-permute-start(f32[5,16,6,1,128]{4,0,3,2,1:T(8,128)S(1)} %get-tuple-element.10), channel_id=1, source_target_pairs={{0,1},{1,2},{2,3},{4,5},{5,6},{6,7},{8,9},{9,10},{10,11},{12,13},{... | collective-permute-start | bytes 737288 | tf_op jit(solution)/shard_map/ppermute | solution.py:26
  369.9 4.4 collective-permute-start.26
  383.1 12.3 %collective-permute-start.29 = (f32[5,16,1,8,128]{4,0,3,2,1:T(8,128)S(1)}, f32[5,16,1,8,128]{4,0,3,2,1:T(8,128)S(1)}, u32[]{:S(2)}, u32[]{:S(2)}) collective-permute-start(f32[5,16,1,8,128]{4,0,3,2,1:T(8,128)S(1)} %get-tuple-element.24), channel_id=1, source_target_pairs={{0,4},{4,8},{8,12},{12,16},{16,20},{20,24},{24,28},{1,5},{5,9},{9,... | collective-permute-start | bytes 983048 | tf_op jit(solution)/shard_map/ppermute | solution.py:26
  387.9 19.3 %collective-permute-start.28 = (f32[5,16,1,8,128]{4,0,3,2,1:T(8,128)S(1)}, f32[5,16,1,8,128]{4,0,3,2,1:T(8,128)S(1)}, u32[]{:S(2)}, u32[]{:S(2)}) collective-permute-start(f32[5,16,1,8,128]{4,0,3,2,1:T(8,128)S(1)} %get-tuple-element.25), channel_id=1, source_target_pairs={{4,0},{8,4},{12,8},{16,12},{20,16},{24,20},{28,24},{5,1},{9,5},{13... | collective-permute-start | bytes 983048 | tf_op jit(solution)/shard_map/ppermute | solution.py:27
  407.3 10.8 %collective-permute-start.31 = (f32[5,16,6,1,128]{4,0,3,2,1:T(8,128)S(1)}, f32[5,16,6,1,128]{4,0,3,2,1:T(8,128)S(1)}, u32[]{:S(2)}, u32[]{:S(2)}) collective-permute-start(f32[5,16,6,1,128]{4,0,3,2,1:T(8,128)S(1)} %get-tuple-element.8), channel_id=1, source_target_pairs={{0,1},{1,2},{2,3},{4,5},{5,6},{6,7},{8,9},{9,10},{10,11},{12,13},{... | collective-permute-start | bytes 737288 | tf_op jit(solution)/shard_map/ppermute | solution.py:26
  413.9 4.6 collective-permute-start.30
  (15 other events, 91.1 us)
where the time goes:
time: 511 us; the launch traced here: 502 us
  waiting for transfers between devices  118 us (23%)
  matrix products  117 us (23%)
  blocking collectives  115 us (23%)
  starting transfers between devices  112 us (22%)
  local copies, waits for them, and re-layouts  29.7 us (6%)
  other arithmetic  7.58 us (1%)
    ppermute x16, starting transfers between devices, padded_2(): before = lax.ppermute(last, axis, up)  89.8 us
    ppermute x16, waiting for transfers between devices, padded_2(): after = lax.ppermute(initial, axis, down)  79.9 us
    all_gather x1, blocking collectives, local(): lax.all_gather(mode_shapes, ('gx', 'gy'), axis=1, tiled=True)  62.8 us
    dot_general x8, matrix products, rates(): jnp.einsum('fg,gmxyz->fmxyz', jacobian[0], east_side - west_side, precisi...  56 us
    psum x1, blocking collectives, local(): gram_matrix = lax.psum(local_gram, ('gx', 'gy')) / rows_total  52.5 us
    ppermute x16, waiting for transfers between devices, padded_2(): before = lax.ppermute(last, axis, up)  37.9 us
    dot_general x8, matrix products, rates(): jnp.einsum('fg,gmxyz->fmxyz', jacobian[2], upper_side - lower_side, preci...  26.5 us
    dot_general x8, matrix products, rates(): jnp.einsum('fg,gmxyz->fmxyz', jacobian[1], north_side - south_side, preci...  23.8 us
  transfers between devices with their start and end apart: 32, of which 17 were waited for; matrix products, arithmetic and copies ran while one was open for 10% of the time, Pallas kernels for 0%

commit v1 on v0

v1 whole, which is shorter than its diff:
```python
import functools
import math

import jax
import jax.numpy as jnp
from jax import lax
from jax.experimental import pallas as pl
from jax.experimental.pallas import tpu as pltpu
from jax.sharding import PartitionSpec as P

STEPS = 2
NU_DAMP = 0.25
DT_STEP = 0.4
PULSE_MID = 0.8
PULSE_WIDTH = 0.5

AXES = ("gx", "gy")
FIELDS = 5
DEEP = 4
MEMBERS = 8
ROWS = 8
LANES = 128
TABLE = FIELDS * 2 * DEEP
F32 = jnp.float32

VMEM = pl.BlockSpec(memory_space=pltpu.VMEM)
SMEM = pl.BlockSpec(memory_space=pltpu.SMEM)
PARAMS = pltpu.CompilerParams(vmem_limit_bytes=48 * 1024 * 1024)


def pulse(time_now):
    return math.exp(-(((time_now - PULSE_MID) / PULSE_WIDTH) ** 2))


def step_scales(step):
    start = step * DT_STEP
    p0, ph, p1 = pulse(start), pulse(start + 0.5 * DT_STEP), pulse(start + DT_STEP)
    return (
        (DT_STEP / 4.0, p0),
        (DT_STEP / 3.0, (p0 + ph) / 2.0),
        (DT_STEP / 2.0, (p0 + 2.0 * ph) / 3.0),
        (DT_STEP, (p0 + 4.0 * ph + p1) / 6.0),
    )


def position():
    along_x = lax.axis_index("gx")
    return along_x // 2, (along_x % 2) * 4 + lax.axis_index("gy")


def pack_kernel(state_ref, sponge_ref, nodes_ref, weights_ref, count_ref, *pieces):
    _, member = position()
    row = member % 4
    lane = lax.broadcasted_iota(jnp.int32, (1, LANES), 1)
    table = [nodes_ref[row].astype(F32)]
    for x in range(DEEP):
        kept = jnp.where(lane < count_ref[x], 1.0, 0.0)
        table.append(weights_ref[row, pl.ds(x, 1), :] * kept)
    table = jnp.concatenate(table, axis=0)
    for d, piece in enumerate(pieces):
        other = member ^ d
        for f in range(FIELDS):
            for j in range(2):
                for x in range(DEEP):
                    piece[(f * 2 + j) * DEEP + x] = state_ref[f, 2 * other + j, x]
        piece[TABLE] = table
        for x in range(DEEP):
            piece[TABLE + 1 + x] = sponge_ref[x]


def pack(state_in, sponge, nodes, weights, count):
    shape = jax.ShapeDtypeStruct((TABLE + 1 + DEEP, ROWS, LANES), F32)
    return pl.pallas_call(
        pack_kernel,
        out_shape=[shape] * MEMBERS,
        in_specs=[VMEM, VMEM, VMEM, VMEM, SMEM],
        out_specs=[VMEM] * MEMBERS,
        compiler_params=PARAMS,
        name="pack",
    )(state_in, sponge, nodes, weights, count)


def shifted_rows(tiles, sub):
    ahead = [pltpu.roll(t, ROWS - 1, 0) for t in tiles]
    behind = [pltpu.roll(t, 1, 0) for t in tiles]
    zero = jnp.zeros_like(tiles[0])
    last, first = sub == ROWS - 1, sub == 0
    count = len(tiles)
    north = [jnp.where(last, ahead[t + 1] if t + 1 < count else zero, ahead[t]) for t in range(count)]
    south = [jnp.where(first, behind[t - 1] if t > 0 else zero, behind[t]) for t in range(count)]
    return north, south


def run_stage(src, base, dst, shift, sponge_ref, wall_ref, vel, wall_vec, h, scale, low, high):
    lane = lax.broadcasted_iota(jnp.int32, (ROWS, LANES), 1)
    sub = lax.broadcasted_iota(jnp.int32, (ROWS, LANES), 0)
    plus = [h * (NU_DAMP - 0.5 * v) for v in vel]
    minus = [h * (NU_DAMP + 0.5 * v) for v in vel]
    not_top, not_low = lane < LANES - 1, lane > 0
    plus_z = jnp.where(not_top, plus[2], 0.0)
    minus_z = jnp.where(not_low, minus[2], 0.0)
    flux = -0.5 * h
    flux_up = jnp.where(not_top, flux, 0.0)
    flux_low = jnp.where(not_low, flux, 0.0)
    tiles = range(4)

    def plane(i, carry):
        damp = [-h * (6.0 * NU_DAMP + sponge_ref[i, pl.ds(ROWS * t, ROWS), :]) for t in tiles]
        for j in range(2):
            def load(ref, f, at):
                return [ref[f, j, at, pl.ds(ROWS * t, ROWS), :] for t in tiles]

            new, d1, d2, d3, d4 = [], None, None, None, None
            for f in range(FIELDS):
                center = load(src, f, i)
                east, west = load(src, f, i + 1), load(src, f, i - 1)
                north, south = shifted_rows(center, sub)
                upper = [pltpu.roll(c, LANES - 1, 1) for c in center]
                lower = [pltpu.roll(c, 1, 1) for c in center]
                old = load(base, f, i)
                out = []
                for t in tiles:
                    acc = old[t] + damp[t] * center[t]
                    acc += plus[0] * east[t] + minus[0] * west[t]
                    acc += plus[1] * north[t] + minus[1] * south[t]
                    acc += plus_z * upper[t] + minus_z * lower[t]
                    if t == 0:
                        acc += (h * scale * wall_vec[f]) * wall_ref[j, i]
                    out.append(acc)
                new.append(out)
                if f == 1:
                    d1 = [flux * (east[t] - west[t]) for t in tiles]
                elif f == 2:
                    d2 = [flux * (north[t] - south[t]) for t in tiles]
                elif f == 3:
                    d3 = [flux_up * upper[t] - flux_low * lower[t] for t in tiles]
                elif f == 4:
                    d4 = [
                        (
                            flux * (east[t] - west[t]),
                            flux * (north[t] - south[t]),
                            flux_up * upper[t] - flux_low * lower[t],
                        )
                        for t in tiles
                    ]
            for t in tiles:
                spread = d1[t] + d2[t] + d3[t]
                new[0][t] += spread
                new[4][t] += spread
                for d in range(3):
                    new[1 + d][t] += d4[t][d]
            for f in range(FIELDS):
                for t in tiles:
                    dst[f, j, i - shift, pl.ds(ROWS * t, ROWS), :] = new[f][t]
        return carry

    lax.fori_loop(low, high, plane, 0)


def run_step(step, base, va, vb, q_low, q_high, sponge_ref, wall_ref, vel, wall_vec, has_low, has_high):
    zero = jnp.zeros((ROWS, LANES), F32)
    for buffer in (va, vb):
        for f in range(FIELDS):
            for j in range(2):
                for t in range(4):
                    buffer[f, j, DEEP - 1, pl.ds(ROWS * t, ROWS), :] = zero
                    buffer[f, j, 3 * DEEP, pl.ds(ROWS * t, ROWS), :] = zero
    scales = step_scales(step)
    src = base
    for k in range(4):
        h, scale = scales[k]
        args = (sponge_ref, wall_ref, vel, wall_vec, h, scale)
        if k < 3:
            dst = va if k % 2 == 0 else vb
            low = jnp.where(has_low, k + 1, DEEP)
            high = jnp.where(has_high, 4 * DEEP - 1 - k, 3 * DEEP)
            run_stage(src, base, dst, 0, *args, low, high)
            src = dst
        else:
            run_stage(src, base, q_low, DEEP, *args, DEEP, 2 * DEEP)
            run_stage(src, base, q_high, 2 * DEEP, *args, 2 * DEEP, 3 * DEEP)


def write_pieces(q_low, q_high, pieces, member):
    for d, piece in enumerate(pieces):
        other = member ^ d
        row = pl.multiple_of((other % 4) * ROWS, ROWS)

        def copy(source):
            for f in range(FIELDS):
                for j in range(2):
                    for x in range(DEEP):
                        piece[j, f, x] = source[f, j, x, pl.ds(row, ROWS), :]

        @pl.when(other < 4)
        def _():
            copy(q_low)

        @pl.when(other >= 4)
        def _():
            copy(q_high)


def gather_forcing(tables, shapes_ref, wall_ref):
    low_part, high_part, weights = [], [], []
    for table in tables:
        low_part.append(table[0] & (LANES - 1))
        high_part.append(table[0] // LANES)
        weights.append(table[1])
    count = len(tables)
    rows = shapes_ref.shape[1]

    def body(r, taken):
        out = [list(taken[j]) for j in range(2)]
        for j in range(2):
            line = jnp.broadcast_to(shapes_ref[j, pl.ds(r, 1), :], (ROWS, LANES))
            for b in range(count):
                value = jnp.take_along_axis(line, low_part[b], axis=1)
                out[j][b] = jnp.where(high_part[b] == r, value, taken[j][b])
        return tuple(tuple(o) for o in out)

    zero = jnp.zeros((ROWS, LANES), F32)
    taken = lax.fori_loop(0, rows, body, tuple(tuple(zero for _ in range(count)) for _ in range(2)))
    return [[taken[j][b] * weights[b] for b in range(count)] for j in range(2)]


def first_kernel(groups, vel_ref, vec_ref, shapes_ref, *refs):
    own, halo = refs[:MEMBERS], refs[MEMBERS : 2 * MEMBERS]
    q_low, q_high, wall_ref, sponge_ref = refs[2 * MEMBERS : 2 * MEMBERS + 4]
    pieces = refs[2 * MEMBERS + 4 : 3 * MEMBERS + 4]
    base, va, vb, tab = refs[3 * MEMBERS + 4 :]
    group, member = position()
    for d in range(MEMBERS):
        other = member ^ d
        row = pl.multiple_of((other % 4) * ROWS, ROWS)
        upper = other // 4
        for piece, start in ((own[d], DEEP + DEEP * upper), (halo[d], 3 * DEEP * (1 - upper))):
            for f in range(FIELDS):
                for j in range(2):
                    for x in range(DEEP):
                        base[f, j, start + x, pl.ds(row, ROWS), :] = piece[(f * 2 + j) * DEEP + x]
            for x in range(DEEP):
                sponge_ref[start + x, pl.ds(row, ROWS), :] = piece[TABLE + 1 + x]
            tab[other % 4, start // DEEP] = piece[TABLE]
    tables = []
    for block in range(4):
        for half in range(2):
            two = [tab[2 * half + n, block] for n in range(2)]
            index = jnp.concatenate([two[0][:DEEP], two[1][:DEEP]], axis=0).astype(jnp.int32)
            weight = jnp.concatenate([two[0][DEEP:], two[1][DEEP:]], axis=0)
            tables.append((index, weight))
    forced = gather_forcing(tables, shapes_ref, wall_ref)
    sub = lax.broadcasted_iota(jnp.int32, (ROWS, LANES), 0)
    for j in range(2):
        for block in range(4):
            total = forced[j][2 * block] + forced[j][2 * block + 1]
            total = total[:DEEP] + total[DEEP:]
            for x in range(DEEP):
                line = jnp.broadcast_to(total[x : x + 1], (ROWS, LANES))
                wall_ref[j, DEEP * block + x] = jnp.where(sub == 0, line, 0.0)
    vel = [vel_ref[d] for d in range(3)]
    vec = [vec_ref[f] for f in range(FIELDS)]
    run_step(0, base, va, vb, q_low, q_high, sponge_ref, wall_ref, vel, vec, group > 0, group < groups - 1)
    write_pieces(q_low, q_high, pieces, member)


def second_kernel(groups, vel_ref, vec_ref, sponge_ref, wall_ref, below, q_low, q_high, above, *refs):
    pieces = refs[:MEMBERS]
    r_low, r_high, base, va, vb = refs[MEMBERS:]
    group, member = position()
    for n, source in enumerate((below, q_low, q_high, above)):
        for f in range(FIELDS):
            for j in range(2):
                for x in range(DEEP):
                    for t in range(4):
                        rows = pl.ds(ROWS * t, ROWS)
                        base[f, j, DEEP * n + x, rows, :] = source[f, j, x, rows, :]
    vel = [vel_ref[d] for d in range(3)]
    vec = [vec_ref[f] for f in range(FIELDS)]
    run_step(1, base, va, vb, r_low, r_high, sponge_ref, wall_ref, vel, vec, group > 0, group < groups - 1)
    write_pieces(r_low, r_high, pieces, member)


def gram_kernel(total, *refs):
    parts = (refs[:MEMBERS], refs[MEMBERS : 2 * MEMBERS])
    state_ref, gram_ref, columns = refs[2 * MEMBERS :]
    _, member = position()
    tiles = FIELDS * DEEP
    for d in range(MEMBERS):
        other = member ^ d
        for n in range(STEPS):
            for j in range(2):
                for f in range(FIELDS):
                    for x in range(DEEP):
                        value = parts[n][d][j, f, x]
                        start = pl.multiple_of(
                            (n * 2 * MEMBERS + 2 * other + j) * tiles * ROWS, ROWS
                        ) + (f * DEEP + x) * ROWS
                        columns[pl.ds(pl.multiple_of(start, ROWS), ROWS), :] = value
                        if n == STEPS - 1:
                            state_ref[f, 2 * other + j, x] = value
    size = STEPS * 2 * MEMBERS
    stride = tiles * ROWS

    def body(r, acc):
        a = jnp.concatenate(
            [columns[pl.ds(4 * r + n, size, stride=stride), :] for n in range(4)], axis=1
        )
        return acc + lax.dot_general(
            a, a, (((1,), (1,)), ((), ())),
            precision=lax.Precision.HIGHEST, preferred_element_type=F32,
        )

    gram = lax.fori_loop(0, stride // 4, body, jnp.zeros((size, size), F32), unroll=4)
    tile = jnp.concatenate([gram[ROWS * n : ROWS * n + ROWS] for n in range(4)], axis=1)
    for n in range(gram_ref.shape[0]):
        gram_ref[n] = tile


def sum_kernel(total, parts_ref, gram_ref):
    acc = parts_ref[0]
    for n in range(1, parts_ref.shape[0]):
        acc = acc + parts_ref[n]
    acc = acc / total
    for n in range(4):
        gram_ref[pl.ds(ROWS * n, ROWS), :] = acc[:, 32 * n : 32 * n + 32]


def local(state_in, sponge, mean_velocity, wall_vector, mode_shapes, wall_nodes, wall_weights, wall_count):
    gx_size, gy_size = lax.axis_size("gx"), lax.axis_size("gy")
    groups = gx_size // 2
    devices = gx_size * gy_size
    cells_x, cells_y, cells_z = state_in.shape[2:]
    def inside(d):
        return [(i, i ^ d) for i in range(devices)]

    def across(d):
        moves = []
        for i in range(devices):
            g, m = divmod(i, MEMBERS)
            target = g + 1 if m >= 4 else g - 1
            if 0 <= target < groups:
                moves.append((i, target * MEMBERS + (m ^ d)))
        return moves

    up = [(i, i + MEMBERS) for i in range(devices - MEMBERS)]
    down = [(j, i) for i, j in up]

    pieces = pack(state_in, sponge, wall_nodes, wall_weights, wall_count)
    own = [pieces[0]] + [lax.ppermute(pieces[d], AXES, inside(d)) for d in range(1, MEMBERS)]
    halo = [lax.ppermute(pieces[d], AXES, across(d)) for d in range(MEMBERS)]

    nodes_here = mode_shapes.shape[1]
    sent = jnp.tile(mode_shapes.reshape(MEMBERS, 2 * nodes_here // LANES, LANES), (groups, 1, 1))
    got = lax.all_to_all(sent, AXES, 0, 0)
    shapes = got.reshape(devices, 2, nodes_here // LANES, LANES).transpose(1, 0, 2, 3)
    shapes = shapes.reshape(2, devices * nodes_here // LANES, LANES)

    border = jax.ShapeDtypeStruct((FIELDS, 2, DEEP, 4 * ROWS, LANES), F32)
    piece = jax.ShapeDtypeStruct((2, FIELDS, DEEP, ROWS, LANES), F32)
    wall = jax.ShapeDtypeStruct((2, 4 * DEEP, ROWS, LANES), F32)
    field = pltpu.VMEM((FIELDS, 2, 4 * DEEP, 4 * ROWS, LANES), F32)
    damping = jax.ShapeDtypeStruct((4 * DEEP, 4 * ROWS, LANES), F32)
    q_low, q_high, wall_rows, sponge_ext, *first = pl.pallas_call(
        functools.partial(first_kernel, groups),
        out_shape=[border, border, wall, damping] + [piece] * MEMBERS,
        in_specs=[SMEM, SMEM, VMEM] + [VMEM] * (2 * MEMBERS),
        out_specs=[VMEM] * (4 + MEMBERS),
        scratch_shapes=[field, field, field, pltpu.VMEM((4, 4, ROWS, LANES), F32)],
        compiler_params=PARAMS,
        name="first_step",
    )(mean_velocity, wall_vector, shapes, *own, *halo)

    below = lax.ppermute(q_high, AXES, up)
    above = lax.ppermute(q_low, AXES, down)
    first = [first[0]] + [lax.ppermute(first[d], AXES, inside(d)) for d in range(1, MEMBERS)]

    half = pltpu.VMEM((FIELDS, 2, DEEP, 4 * ROWS, LANES), F32)
    second = pl.pallas_call(
        functools.partial(second_kernel, groups),
        out_shape=[piece] * MEMBERS,
        in_specs=[SMEM, SMEM] + [VMEM] * 6,
        out_specs=[VMEM] * MEMBERS,
        scratch_shapes=[half, half, field, field, field],
        compiler_params=PARAMS,
        name="second_step",
    )(mean_velocity, wall_vector, sponge_ext, wall_rows, below, q_low, q_high, above)
    second = [second[0]] + [lax.ppermute(second[d], AXES, inside(d)) for d in range(1, MEMBERS)]

    rows_total = float(FIELDS * cells_x * gx_size * cells_y * gy_size * cells_z)
    snap_count = STEPS * 2 * MEMBERS
    state_out, grams = pl.pallas_call(
        functools.partial(gram_kernel, rows_total),
        out_shape=[
            jax.ShapeDtypeStruct(state_in.shape, F32),
            jax.ShapeDtypeStruct((devices, ROWS, LANES), F32),
        ],
        in_specs=[VMEM] * (2 * MEMBERS),
        out_specs=[VMEM, VMEM],
        scratch_shapes=[pltpu.VMEM((snap_count * FIELDS * DEEP * ROWS, LANES), F32)],
        compiler_params=PARAMS,
        name="gram",
    )(*first, *second)
    grams = lax.all_to_all(grams, AXES, 0, 0)
    gram_matrix = pl.pallas_call(
        functools.partial(sum_kernel, rows_total),
        out_shape=jax.ShapeDtypeStruct((snap_count, snap_count), F32),
        in_specs=[VMEM],
        out_specs=VMEM,
        compiler_params=PARAMS,
        name="gram_sum",
    )(grams)
    return state_out, jnp.linalg.cholesky(gram_matrix).T


def solution(mesh):
    placed = (
        P(None, None, "gx", "gy", None),
        P("gx", "gy", None),
        P(),
        P(),
        P(None, ("gx", "gy")),
        P(None, "gx", None),
        P(None, "gx", None),
        P("gx"),
    )
    return jax.shard_map(
        local,
        mesh=mesh,
        in_specs=placed,
        out_specs=(P(None, None, "gx", "gy", None), P()),
        check_vma=False,
    )
```

time: 511 us -> 152 us (0.30); the launches traced: 502 us -> 152 us
  matrix products: 117 us -> 0 us
  blocking collectives: 115 us -> 22.1 us
  waiting for transfers between devices: 118 us -> 37 us
  starting transfers between devices: 112 us -> 55.2 us
  Pallas kernels: 0 us -> 27.6 us
  local copies, waits for them, and re-layouts: 29.7 us -> 4.92 us
    dot_general x25 -> x0, matrix products: 117 us -> none  [the longest x8 56 us: rates(): jnp.einsum('fg,gmxyz->fmxyz', jacobian[0], east_side - west_side, precisi...]
    ppermute x32 -> x31, waiting for transfers between devices: 118 us -> 37 us  [the longest x7 12.2 us: local(): lax.ppermute(second[d], AXES, inside(d))]
    all_gather x1 -> x0, blocking collectives: 62.8 us -> none  [local(): lax.all_gather(mode_shapes, ('gx', 'gy'), axis=1, tiled=True)]
    ppermute x32 -> x31, starting transfers between devices: 112 us -> 55.2 us  [the longest x7 25.2 us: local(): lax.ppermute(pieces[d], AXES, inside(d))]
    psum x1 -> x0, blocking collectives: 52.5 us -> none  [local(): gram_matrix = lax.psum(local_gram, ('gx', 'gy')) / rows_total]
    pallas_call x0 -> x5, Pallas kernels: none -> 27.6 us  [the longest x1 14.7 us: local(): pl.pallas_call(functools.partial(first_kernel, groups), out_shape=[border...]
    all_to_all x0 -> x2, blocking collectives: none -> 22.1 us  [the longest x1 12 us: local(): got = lax.all_to_all(sent, AXES, 0, 0)]
    slice x18 -> x0, local copies, waits for them, and re-layouts: 11.7 us -> none  [the longest x8 8.43 us: rates(): upper_side = jnp.concatenate([center[..., 1:], zero_plane], axis=4)]
  transfers between devices with their start and end apart: 32 -> 31, of which waited for: 17 -> 11; matrix products, arithmetic and copies ran while one was open for 10% -> 0% of each run, Pallas kernels for 0% -> 5%
where the time goes in v1:
time: 152 us
  starting transfers between devices  55.2 us (36%)
  waiting for transfers between devices  37 us (24%)
  Pallas kernels  27.6 us (18%)
  blocking collectives  22.1 us (15%)
  local copies, waits for them, and re-layouts  4.92 us (3%)
  other arithmetic  4.25 us (3%)
    ppermute x7, starting transfers between devices, local(): lax.ppermute(pieces[d], AXES, inside(d))  25.2 us
    pallas_call x1, Pallas kernels, local(): pl.pallas_call(functools.partial(first_kernel, groups), out_shape=[border...  14.7 us
    ppermute x7, waiting for transfers between devices, local(): lax.ppermute(second[d], AXES, inside(d))  12.2 us
    all_to_all x1, blocking collectives, local(): got = lax.all_to_all(sent, AXES, 0, 0)  12 us
    ppermute x1, waiting for transfers between devices, local(): below = lax.ppermute(q_high, AXES, up)  11.2 us
    all_to_all x1, blocking collectives, local(): grams = lax.all_to_all(grams, AXES, 0, 0)  10.2 us
    ppermute x7, starting transfers between devices, local(): lax.ppermute(first[d], AXES, inside(d))  9.1 us
    ppermute x8, starting transfers between devices, local(): halo = [lax.ppermute(pieces[d], AXES, across(d)) for d in range(MEMBERS)]  7.79 us
  transfers between devices with their start and end apart: 31, of which 11 were waited for; matrix products, arithmetic and copies ran while one was open for 0% of the time, Pallas kernels for 5%

profile of v1, /device:TPU:0, one launch (start us, length us, event | category | flops | bytes accessed | tf_op | source)
XLA Modules:
  0.0 151.9 jit_solution(293596153154500752)
XLA Ops:
  0.6 1.3 copy-done
  5.4 1.3 collective-permute-start.7
  6.7 1.3 collective-permute-start.8
  9.8 2.6 %collective-permute-start.1 = (f32[45,8,128]{2,1,0:T(8,128)S(1)}, f32[45,8,128]{2,1,0:T(8,128)S(1)}, u32[]{:S(2)}, u32[]{:S(2)}) collective-permute-start(f32[45,8,128]{2,1,0:T(8,128)S(1)} %get-tuple-element.34), channel_id=1, source_target_pairs={{0,2},{1,3},{2,0},{3,1},{4,6},{5,7},{6,4},{7,5},{8,10},{9,11},{10,... | collective-permute-start | bytes 552968 | tf_op jit(solution)/shard_map/ppermute | solution.py:350
  12.4 3.4 %collective-permute-done.7.refs_8_ = f32[45,8,128]{2,1,0:T(8,128)S(1)} collective-permute-done((f32[45,8,128]{2,1,0:T(8,128)S(1)}, f32[45,8,128]{2,1,0:T(8,128)S(1)}, u32[]{:S(2)}, u32[]{:S(2)}) %collective-permute-start.7) | collective-permute-done | bytes 184352 | tf_op jit(solution)/shard_map/ppermute | solution.py:351
  15.8 1.3 collective-permute-start.10
  18.1 3.3 %collective-permute-start.2 = (f32[45,8,128]{2,1,0:T(8,128)S(1)}, f32[45,8,128]{2,1,0:T(8,128)S(1)}, u32[]{:S(2)}, u32[]{:S(2)}) collective-permute-start(f32[45,8,128]{2,1,0:T(8,128)S(1)} %get-tuple-element.35), channel_id=1, source_target_pairs={{0,3},{1,2},{2,1},{3,0},{4,7},{5,6},{6,5},{7,4},{8,11},{9,10},{10,... | collective-permute-start | bytes 552968 | tf_op jit(solution)/shard_map/ppermute | solution.py:350
  22.1 3.1 %collective-permute-done.9.refs_10_ = f32[45,8,128]{2,1,0:T(8,128)S(1)} collective-permute-done((f32[45,8,128]{2,1,0:T(8,128)S(1)}, f32[45,8,128]{2,1,0:T(8,128)S(1)}, u32[]{:S(2)}, u32[]{:S(2)}) %collective-permute-start.9) | collective-permute-done | bytes 184352 | tf_op jit(solution)/shard_map/ppermute | solution.py:351
  26.9 5.4 %collective-permute-start.4 = (f32[45,8,128]{2,1,0:T(8,128)S(1)}, f32[45,8,128]{2,1,0:T(8,128)S(1)}, u32[]{:S(2)}, u32[]{:S(2)}) collective-permute-start(f32[45,8,128]{2,1,0:T(8,128)S(1)} %get-tuple-element.37), channel_id=1, source_target_pairs={{0,5},{1,4},{2,7},{3,6},{4,1},{5,0},{6,3},{7,2},{8,13},{9,12},{10,... | collective-permute-start | bytes 552968 | tf_op jit(solution)/shard_map/ppermute | solution.py:350
  33.0 7.6 %collective-permute-start.5 = (f32[45,8,128]{2,1,0:T(8,128)S(1)}, f32[45,8,128]{2,1,0:T(8,128)S(1)}, u32[]{:S(2)}, u32[]{:S(2)}) collective-permute-start(f32[45,8,128]{2,1,0:T(8,128)S(1)} %get-tuple-element.38), channel_id=1, source_target_pairs={{0,6},{1,7},{2,4},{3,5},{4,2},{5,3},{6,0},{7,1},{8,14},{9,15},{10,... | collective-permute-start | bytes 552968 | tf_op jit(solution)/shard_map/ppermute | solution.py:350
  41.3 4.7 %collective-permute-start.6 = (f32[45,8,128]{2,1,0:T(8,128)S(1)}, f32[45,8,128]{2,1,0:T(8,128)S(1)}, u32[]{:S(2)}, u32[]{:S(2)}) collective-permute-start(f32[45,8,128]{2,1,0:T(8,128)S(1)} %get-tuple-element.39), channel_id=1, source_target_pairs={{0,7},{1,6},{2,5},{3,4},{4,3},{5,2},{6,1},{7,0},{8,15},{9,14},{10,... | collective-permute-start | bytes 552968 | tf_op jit(solution)/shard_map/ppermute | solution.py:350
  46.0 12.0 %all_to_all.10 = f32[32,4,128]{2,1,0:T(4,128)S(1)} all-to-all(f32[32,4,128]{2,1,0:T(4,128)S(1)} %bitcast.12), channel_id=1, replica_groups=mesh['gx'=8,'gy'=4] {'gx','gy'}, dimensions={0} | all-to-all | bytes 131072 | tf_op jit(solution)/shard_map/all_to_all | solution.py:355
  58.1 14.7 %first_step.1 = (f32[5,2,4,32,128]{4,3,2,1,0:T(8,128)S(1)}, f32[5,2,4,32,128]{4,3,2,1,0:T(8,128)S(1)}, f32[2,16,8,128]{3,2,1,0:T(8,128)S(1)}, f32[16,32,128]{2,1...) custom-call(f32[3]{0:T(128)S(1)} %copy-done.4, ...), custom_call_target="tpu_custom_call" | custom-call | tf_op jit(solution)/shard_map/first_step/pallas_call | solution.py:364
  72.8 6.6 %collective-permute-start.22 = (f32[5,2,4,32,128]{4,3,2,1,0:T(8,128)S(1)}, f32[5,2,4,32,128]{4,3,2,1,0:T(8,128)S(1)}, u32[]{:S(2)}, u32[]{:S(2)}) collective-permute-start(f32[5,2,4,32,128]{4,3,2,1,0:T(8,128)S(1)} %get-tuple-element.50.q_high), channel_id=1, source_target_pairs={{0,8},{1,9},{2,10},{3,11},{4,12},{5,13},{6,14},{7,15},{8,16},{9,17... | collective-permute-start | bytes 1966088 | tf_op jit(solution)/shard_map/ppermute | solution.py:374
  79.4 1.3 collective-permute-start.23
  80.8 1.4 collective-permute-start.16
  82.6 11.2 %collective-permute-done.22.below = f32[5,2,4,32,128]{4,3,2,1,0:T(8,128)S(1)} collective-permute-done((f32[5,2,4,32,128]{4,3,2,1,0:T(8,128)S(1)}, f32[5,2,4,32,128]{4,3,2,1,0:T(8,128)S(1)}, u32[]{:S(2)}, u32[]{:S(2)}) %collective-permute-start.22) | collective-permute-done | bytes 655392 | tf_op jit(solution)/shard_map/ppermute | solution.py:374
  93.8 2.4 %collective-permute-start.18 = (f32[2,5,4,8,128]{4,3,2,1,0:T(8,128)S(1)}, f32[2,5,4,8,128]{4,3,2,1,0:T(8,128)S(1)}, u32[]{:S(2)}, u32[]{:S(2)}) collective-permute-start(f32[2,5,4,8,128]{4,3,2,1,0:T(8,128)S(1)} %get-tuple-element.44), channel_id=1, source_target_pairs={{0,4},{1,5},{2,6},{3,7},{4,0},{5,1},{6,2},{7,3},{8,12},{9,13},{10,... | collective-permute-start | bytes 491528 | tf_op jit(solution)/shard_map/ppermute | solution.py:376
  96.1 1.8 %collective-permute-done.23.above = f32[5,2,4,32,128]{4,3,2,1,0:T(8,128)S(1)} collective-permute-done((f32[5,2,4,32,128]{4,3,2,1,0:T(8,128)S(1)}, f32[5,2,4,32,128]{4,3,2,1,0:T(8,128)S(1)}, u32[]{:S(2)}, u32[]{:S(2)}) %collective-permute-start.23) | collective-permute-done | bytes 655392 | tf_op jit(solution)/shard_map/ppermute | solution.py:375
  98.8 7.2 %second_step.1 = (f32[2,5,4,8,128]{4,3,2,1,0:T(8,128)S(1)}, f32[2,5,4,8,128]{4,3,2,1,0:T(8,128)S(1)}, f32[2,5,4,8,128]{4,3,2,1,0:T(8,128)S(1)}, f32[2,5,4,8,128]...) custom-call(f32[3]{0:T(128)S(1)} %copy-done.4, ...), custom_call_target="tpu_custom_call" | custom-call | tf_op jit(solution)/shard_map/second_step/pallas_call | solution.py:379
  106.0 1.5 collective-permute-start.20
  107.5 2.4 %collective-permute-start.21 = (f32[2,5,4,8,128]{4,3,2,1,0:T(8,128)S(1)}, f32[2,5,4,8,128]{4,3,2,1,0:T(8,128)S(1)}, u32[]{:S(2)}, u32[]{:S(2)}) collective-permute-start(f32[2,5,4,8,128]{4,3,2,1,0:T(8,128)S(1)} %get-tuple-element.47), channel_id=1, source_target_pairs={{0,7},{1,6},{2,5},{3,4},{4,3},{5,2},{6,1},{7,0},{8,15},{9,14},{10,... | collective-permute-start | bytes 491528 | tf_op jit(solution)/shard_map/ppermute | solution.py:376
  110.6 1.3 collective-permute-start.26
  111.8 1.7 %collective-permute-done.20.refs_6_ = f32[2,5,4,8,128]{4,3,2,1,0:T(8,128)S(1)} collective-permute-done((f32[2,5,4,8,128]{4,3,2,1,0:T(8,128)S(1)}, f32[2,5,4,8,128]{4,3,2,1,0:T(8,128)S(1)}, u32[]{:S(2)}, u32[]{:S(2)}) %collective-permute-start.20) | collective-permute-done | bytes 163872 | tf_op jit(solution)/shard_map/ppermute | solution.py:376
  113.5 2.1 %collective-permute-start.27 = (f32[2,5,4,8,128]{4,3,2,1,0:T(8,128)S(1)}, f32[2,5,4,8,128]{4,3,2,1,0:T(8,128)S(1)}, u32[]{:S(2)}, u32[]{:S(2)}) collective-permute-start(f32[2,5,4,8,128]{4,3,2,1,0:T(8,128)S(1)} %get-tuple-element.56), channel_id=1, source_target_pairs={{0,4},{1,5},{2,6},{3,7},{4,0},{5,1},{6,2},{7,3},{8,12},{9,13},{10,... | collective-permute-start | bytes 491528 | tf_op jit(solution)/shard_map/ppermute | solution.py:388
  115.6 2.6 %collective-permute-done.21.refs_7_ = f32[2,5,4,8,128]{4,3,2,1,0:T(8,128)S(1)} collective-permute-done((f32[2,5,4,8,128]{4,3,2,1,0:T(8,128)S(1)}, f32[2,5,4,8,128]{4,3,2,1,0:T(8,128)S(1)}, u32[]{:S(2)}, u32[]{:S(2)}) %collective-permute-start.21) | collective-permute-done | bytes 163872 | tf_op jit(solution)/shard_map/ppermute | solution.py:376
  118.7 2.5 %collective-permute-done.25.refs_10_ = f32[2,5,4,8,128]{4,3,2,1,0:T(8,128)S(1)} collective-permute-done((f32[2,5,4,8,128]{4,3,2,1,0:T(8,128)S(1)}, f32[2,5,4,8,128]{4,3,2,1,0:T(8,128)S(1)}, u32[]{:S(2)}, u32[]{:S(2)}) %collective-permute-start.25) | collective-permute-done | bytes 163872 | tf_op jit(solution)/shard_map/ppermute | solution.py:388
  122.6 7.2 %collective-permute-done.28.refs_13_ = f32[2,5,4,8,128]{4,3,2,1,0:T(8,128)S(1)} collective-permute-done((f32[2,5,4,8,128]{4,3,2,1,0:T(8,128)S(1)}, f32[2,5,4,8,128]{4,3,2,1,0:T(8,128)S(1)}, u32[]{:S(2)}, u32[]{:S(2)}) %collective-permute-start.28) | collective-permute-done | bytes 163872 | tf_op jit(solution)/shard_map/ppermute | solution.py:388
  129.8 1.8 %collective-permute-done.30.refs_15_ = f32[2,5,4,8,128]{4,3,2,1,0:T(8,128)S(1)} collective-permute-done((f32[2,5,4,8,128]{4,3,2,1,0:T(8,128)S(1)}, f32[2,5,4,8,128]{4,3,2,1,0:T(8,128)S(1)}, u32[]{:S(2)}, u32[]{:S(2)}) %collective-permute-start.30) | collective-permute-done | bytes 163872 | tf_op jit(solution)/shard_map/ppermute | solution.py:388
  131.7 4.9 %gram.1 = (f32[5,16,4,8,128]{4,3,2,1,0:T(8,128)}, f32[32,8,128]{2,1,0:T(8,128)S(1)}) custom-call(f32[2,5,4,8,128]{4,3,2,1,0:T(8,128)S(1)} %get-tuple-element.40.refs_0_, f32[2,5,4,8,128]{4,3,2,1,0:T(8,128)S(1)} %collective-permute-done.15.refs_1_, f32[2,5,4,8,128]{4,3,2,1,0:T(8,128)S(1)} %collective-permute-done.16.refs_2_, ...), custom_call_target="tpu_custom_call" | custom-call | tf_op jit(solution)/shard_map/gram/pallas_call | solution.py:392
  136.6 10.2 %all_to_all.11.parts_ref = f32[32,8,128]{2,1,0:T(8,128)S(1)} all-to-all(f32[32,8,128]{2,1,0:T(8,128)S(1)} %get-tuple-element.61), channel_id=1, replica_groups=mesh['gx'=8,'gy'=4] {'gx','gy'}, dimensions={0} | all-to-all | bytes 262144 | tf_op jit(solution)/shard_map/all_to_all | solution.py:404
  146.9 2.9 %cholesky.18 = f32[32,32]{1,0:T(8,128)S(1)} custom-call(f32[32,32]{1,0:T(8,128)S(1)} %fusion), custom_call_target="Cholesky" | custom-call | tf_op jit(solution)/shard_map/jit(cholesky)/cholesky | solution.py:413
  (64 shorter events, 16.2 us)
Async XLA Ops:
  4.7 53.4 %copy-start.5 = (f32[5]{0:T(128)S(1)}, f32[5]{0:T(128)}, u32[]{:S(2)}) copy-start(f32[5]{0:T(128)} %vec_ref.3) | copy-start | bytes 64
  5.4 10.4 %collective-permute-start.7 = (f32[45,8,128]{2,1,0:T(8,128)S(1)}, f32[45,8,128]{2,1,0:T(8,128)S(1)}, u32[]{:S(2)}, u32[]{:S(2)}) collective-permute-start(f32[45,8,128]{2,1,0:T(8,128)S(1)} %get-tuple-element.32.refs_0_), channel_id=1, source_target_pairs={{4,12},{5,13},{6,14},{7,15},{8,0},{9,1},{10,2},{11,3},{12,20},{13,... | collective-permute-start | bytes 552968 | tf_op jit(solution)/shard_map/ppermute | solution.py:351
  6.7 11.4 %collective-permute-start.8 = (f32[45,8,128]{2,1,0:T(8,128)S(1)}, f32[45,8,128]{2,1,0:T(8,128)S(1)}, u32[]{:S(2)}, u32[]{:S(2)}) collective-permute-start(f32[45,8,128]{2,1,0:T(8,128)S(1)} %get-tuple-element.33), channel_id=1, source_target_pairs={{4,13},{5,12},{6,15},{7,14},{8,1},{9,0},{10,3},{11,2},{12,21},{13,... | collective-permute-start | bytes 552968 | tf_op jit(solution)/shard_map/ppermute | solution.py:351
  8.0 13.4 %collective-permute-start = (f32[45,8,128]{2,1,0:T(8,128)S(1)}, f32[45,8,128]{2,1,0:T(8,128)S(1)}, u32[]{:S(2)}, u32[]{:S(2)}) collective-permute-start(f32[45,8,128]{2,1,0:T(8,128)S(1)} %get-tuple-element.33), channel_id=1, source_target_pairs={{0,1},{1,0},{2,3},{3,2},{4,5},{5,4},{6,7},{7,6},{8,9},{9,8},{10,11... | collective-permute-start | bytes 552968 | tf_op jit(solution)/shard_map/ppermute | solution.py:350
  8.5 16.7 %collective-permute-start.9 = (f32[45,8,128]{2,1,0:T(8,128)S(1)}, f32[45,8,128]{2,1,0:T(8,128)S(1)}, u32[]{:S(2)}, u32[]{:S(2)}) collective-permute-start(f32[45,8,128]{2,1,0:T(8,128)S(1)} %get-tuple-element.34), channel_id=1, source_target_pairs={{4,14},{5,15},{6,12},{7,13},{8,2},{9,3},{10,0},{11,1},{12,22},{13,... | collective-permute-start | bytes 552968 | tf_op jit(solution)/shard_map/ppermute | solution.py:351
  9.8 16.5 %collective-permute-start.1 = (f32[45,8,128]{2,1,0:T(8,128)S(1)}, f32[45,8,128]{2,1,0:T(8,128)S(1)}, u32[]{:S(2)}, u32[]{:S(2)}) collective-permute-start(f32[45,8,128]{2,1,0:T(8,128)S(1)} %get-tuple-element.34), channel_id=1, source_target_pairs={{0,2},{1,3},{2,0},{3,1},{4,6},{5,7},{6,4},{7,5},{8,10},{9,11},{10,... | collective-permute-start | bytes 552968 | tf_op jit(solution)/shard_map/ppermute | solution.py:350
  15.8 11.1 %collective-permute-start.10 = (f32[45,8,128]{2,1,0:T(8,128)S(1)}, f32[45,8,128]{2,1,0:T(8,128)S(1)}, u32[]{:S(2)}, u32[]{:S(2)}) collective-permute-start(f32[45,8,128]{2,1,0:T(8,128)S(1)} %get-tuple-element.35), channel_id=1, source_target_pairs={{4,15},{5,14},{6,13},{7,12},{8,3},{9,2},{10,1},{11,0},{12,23},{13,... | collective-permute-start | bytes 552968 | tf_op jit(solution)/shard_map/ppermute | solution.py:351
  18.1 14.2 %collective-permute-start.2 = (f32[45,8,128]{2,1,0:T(8,128)S(1)}, f32[45,8,128]{2,1,0:T(8,128)S(1)}, u32[]{:S(2)}, u32[]{:S(2)}) collective-permute-start(f32[45,8,128]{2,1,0:T(8,128)S(1)} %get-tuple-element.35), channel_id=1, source_target_pairs={{0,3},{1,2},{2,1},{3,0},{4,7},{5,6},{6,5},{7,4},{8,11},{9,10},{10,... | collective-permute-start | bytes 552968 | tf_op jit(solution)/shard_map/ppermute | solution.py:350
  21.4 11.5 %collective-permute-start.11 = (f32[45,8,128]{2,1,0:T(8,128)S(1)}, f32[45,8,128]{2,1,0:T(8,128)S(1)}, u32[]{:S(2)}, u32[]{:S(2)}) collective-permute-start(f32[45,8,128]{2,1,0:T(8,128)S(1)} %get-tuple-element.36), channel_id=1, source_target_pairs={{4,8},{5,9},{6,10},{7,11},{8,4},{9,5},{10,6},{11,7},{12,16},{13,17... | collective-permute-start | bytes 552968 | tf_op jit(solution)/shard_map/ppermute | solution.py:351
  25.2 15.4 %collective-permute-start.3 = (f32[45,8,128]{2,1,0:T(8,128)S(1)}, f32[45,8,128]{2,1,0:T(8,128)S(1)}, u32[]{:S(2)}, u32[]{:S(2)}) collective-permute-start(f32[45,8,128]{2,1,0:T(8,128)S(1)} %get-tuple-element.36), channel_id=1, source_target_pairs={{0,4},{1,5},{2,6},{3,7},{4,0},{5,1},{6,2},{7,3},{8,12},{9,13},{10,... | collective-permute-start | bytes 552968 | tf_op jit(solution)/shard_map/ppermute | solution.py:350
  26.2 15.0 %collective-permute-start.12 = (f32[45,8,128]{2,1,0:T(8,128)S(1)}, f32[45,8,128]{2,1,0:T(8,128)S(1)}, u32[]{:S(2)}, u32[]{:S(2)}) collective-permute-start(f32[45,8,128]{2,1,0:T(8,128)S(1)} %get-tuple-element.37), channel_id=1, source_target_pairs={{4,9},{5,8},{6,11},{7,10},{8,5},{9,4},{10,7},{11,6},{12,17},{13,16... | collective-permute-start | bytes 552968 | tf_op jit(solution)/shard_map/ppermute | solution.py:351
  26.9 31.1 %collective-permute-start.4 = (f32[45,8,128]{2,1,0:T(8,128)S(1)}, f32[45,8,128]{2,1,0:T(8,128)S(1)}, u32[]{:S(2)}, u32[]{:S(2)}) collective-permute-start(f32[45,8,128]{2,1,0:T(8,128)S(1)} %get-tuple-element.37), channel_id=1, source_target_pairs={{0,5},{1,4},{2,7},{3,6},{4,1},{5,0},{6,3},{7,2},{8,13},{9,12},{10,... | collective-permute-start | bytes 552968 | tf_op jit(solution)/shard_map/ppermute | solution.py:350
  32.3 25.7 %collective-permute-start.13 = (f32[45,8,128]{2,1,0:T(8,128)S(1)}, f32[45,8,128]{2,1,0:T(8,128)S(1)}, u32[]{:S(2)}, u32[]{:S(2)}) collective-permute-start(f32[45,8,128]{2,1,0:T(8,128)S(1)} %get-tuple-element.38), channel_id=1, source_target_pairs={{4,10},{5,11},{6,8},{7,9},{8,6},{9,7},{10,4},{11,5},{12,18},{13,19... | collective-permute-start | bytes 552968 | tf_op jit(solution)/shard_map/ppermute | solution.py:351
  33.0 25.1 %collective-permute-start.5 = (f32[45,8,128]{2,1,0:T(8,128)S(1)}, f32[45,8,128]{2,1,0:T(8,128)S(1)}, u32[]{:S(2)}, u32[]{:S(2)}) collective-permute-start(f32[45,8,128]{2,1,0:T(8,128)S(1)} %get-tuple-element.38), channel_id=1, source_target_pairs={{0,6},{1,7},{2,4},{3,5},{4,2},{5,3},{6,0},{7,1},{8,14},{9,15},{10,... | collective-permute-start | bytes 552968 | tf_op jit(solution)/shard_map/ppermute | solution.py:350
  40.6 17.4 %collective-permute-start.14 = (f32[45,8,128]{2,1,0:T(8,128)S(1)}, f32[45,8,128]{2,1,0:T(8,128)S(1)}, u32[]{:S(2)}, u32[]{:S(2)}) collective-permute-start(f32[45,8,128]{2,1,0:T(8,128)S(1)} %get-tuple-element.39), channel_id=1, source_target_pairs={{4,11},{5,10},{6,9},{7,8},{8,7},{9,6},{10,5},{11,4},{12,19},{13,18... | collective-permute-start | bytes 552968 | tf_op jit(solution)/shard_map/ppermute | solution.py:351
  41.3 16.8 %collective-permute-start.6 = (f32[45,8,128]{2,1,0:T(8,128)S(1)}, f32[45,8,128]{2,1,0:T(8,128)S(1)}, u32[]{:S(2)}, u32[]{:S(2)}) collective-permute-start(f32[45,8,128]{2,1,0:T(8,128)S(1)} %get-tuple-element.39), channel_id=1, source_target_pairs={{0,7},{1,6},{2,5},{3,4},{4,3},{5,2},{6,1},{7,0},{8,15},{9,14},{10,... | collective-permute-start | bytes 552968 | tf_op jit(solution)/shard_map/ppermute | solution.py:350
  72.8 21.0 %collective-permute-start.22 = (f32[5,2,4,32,128]{4,3,2,1,0:T(8,128)S(1)}, f32[5,2,4,32,128]{4,3,2,1,0:T(8,128)S(1)}, u32[]{:S(2)}, u32[]{:S(2)}) collective-permute-start(f32[5,2,4,32,128]{4,3,2,1,0:T(8,128)S(1)} %get-tuple-element.50.q_high), channel_id=1, source_target_pairs={{0,8},{1,9},{2,10},{3,11},{4,12},{5,13},{6,14},{7,15},{8,16},{9,17... | collective-permute-start | bytes 1966088 | tf_op jit(solution)/shard_map/ppermute | solution.py:374
  79.4 18.6 %collective-permute-start.23 = (f32[5,2,4,32,128]{4,3,2,1,0:T(8,128)S(1)}, f32[5,2,4,32,128]{4,3,2,1,0:T(8,128)S(1)}, u32[]{:S(2)}, u32[]{:S(2)}) collective-permute-start(f32[5,2,4,32,128]{4,3,2,1,0:T(8,128)S(1)} %get-tuple-element.51.q_low), channel_id=1, source_target_pairs={{8,0},{9,1},{10,2},{11,3},{12,4},{13,5},{14,6},{15,7},{16,8},{17,9... | collective-permute-start | bytes 1966088 | tf_op jit(solution)/shard_map/ppermute | solution.py:375
  80.7 25.4 %collective-permute-start.15 = (f32[2,5,4,8,128]{4,3,2,1,0:T(8,128)S(1)}, f32[2,5,4,8,128]{4,3,2,1,0:T(8,128)S(1)}, u32[]{:S(2)}, u32[]{:S(2)}) collective-permute-start(f32[2,5,4,8,128]{4,3,2,1,0:T(8,128)S(1)} %get-tuple-element.41), channel_id=1, source_target_pairs={{0,1},{1,0},{2,3},{3,2},{4,5},{5,4},{6,7},{7,6},{8,9},{9,8},{10,11... | collective-permute-start | bytes 491528 | tf_op jit(solution)/shard_map/ppermute | solution.py:376
  80.8 26.8 %collective-permute-start.16 = (f32[2,5,4,8,128]{4,3,2,1,0:T(8,128)S(1)}, f32[2,5,4,8,128]{4,3,2,1,0:T(8,128)S(1)}, u32[]{:S(2)}, u32[]{:S(2)}) collective-permute-start(f32[2,5,4,8,128]{4,3,2,1,0:T(8,128)S(1)} %get-tuple-element.42), channel_id=1, source_target_pairs={{0,2},{1,3},{2,0},{3,1},{4,6},{5,7},{6,4},{7,5},{8,10},{9,11},{10,... | collective-permute-start | bytes 491528 | tf_op jit(solution)/shard_map/ppermute | solution.py:376
  82.2 27.8 %collective-permute-start.17 = (f32[2,5,4,8,128]{4,3,2,1,0:T(8,128)S(1)}, f32[2,5,4,8,128]{4,3,2,1,0:T(8,128)S(1)}, u32[]{:S(2)}, u32[]{:S(2)}) collective-permute-start(f32[2,5,4,8,128]{4,3,2,1,0:T(8,128)S(1)} %get-tuple-element.43), channel_id=1, source_target_pairs={{0,3},{1,2},{2,1},{3,0},{4,7},{5,6},{6,5},{7,4},{8,11},{9,10},{10,... | collective-permute-start | bytes 491528 | tf_op jit(solution)/shard_map/ppermute | solution.py:376
  93.8 16.2 %collective-permute-start.18 = (f32[2,5,4,8,128]{4,3,2,1,0:T(8,128)S(1)}, f32[2,5,4,8,128]{4,3,2,1,0:T(8,128)S(1)}, u32[]{:S(2)}, u32[]{:S(2)}) collective-permute-start(f32[2,5,4,8,128]{4,3,2,1,0:T(8,128)S(1)} %get-tuple-element.44), channel_id=1, source_target_pairs={{0,4},{1,5},{2,6},{3,7},{4,0},{5,1},{6,2},{7,3},{8,12},{9,13},{10,... | collective-permute-start | bytes 491528 | tf_op jit(solution)/shard_map/ppermute | solution.py:376
  97.9 12.6 %collective-permute-start.19 = (f32[2,5,4,8,128]{4,3,2,1,0:T(8,128)S(1)}, f32[2,5,4,8,128]{4,3,2,1,0:T(8,128)S(1)}, u32[]{:S(2)}, u32[]{:S(2)}) collective-permute-start(f32[2,5,4,8,128]{4,3,2,1,0:T(8,128)S(1)} %get-tuple-element.45), channel_id=1, source_target_pairs={{0,5},{1,4},{2,7},{3,6},{4,1},{5,0},{6,3},{7,2},{8,13},{9,12},{10,... | collective-permute-start | bytes 491528 | tf_op jit(solution)/shard_map/ppermute | solution.py:376
  106.0 7.5 %collective-permute-start.20 = (f32[2,5,4,8,128]{4,3,2,1,0:T(8,128)S(1)}, f32[2,5,4,8,128]{4,3,2,1,0:T(8,128)S(1)}, u32[]{:S(2)}, u32[]{:S(2)}) collective-permute-start(f32[2,5,4,8,128]{4,3,2,1,0:T(8,128)S(1)} %get-tuple-element.46), channel_id=1, source_target_pairs={{0,6},{1,7},{2,4},{3,5},{4,2},{5,3},{6,0},{7,1},{8,14},{9,15},{10,... | collective-permute-start | bytes 491528 | tf_op jit(solution)/shard_map/ppermute | solution.py:376
  107.5 10.6 %collective-permute-start.21 = (f32[2,5,4,8,128]{4,3,2,1,0:T(8,128)S(1)}, f32[2,5,4,8,128]{4,3,2,1,0:T(8,128)S(1)}, u32[]{:S(2)}, u32[]{:S(2)}) collective-permute-start(f32[2,5,4,8,128]{4,3,2,1,0:T(8,128)S(1)} %get-tuple-element.47), channel_id=1, source_target_pairs={{0,7},{1,6},{2,5},{3,4},{4,3},{5,2},{6,1},{7,0},{8,15},{9,14},{10,... | collective-permute-start | bytes 491528 | tf_op jit(solution)/shard_map/ppermute | solution.py:376
  110.0 8.6 %collective-permute-start.24 = (f32[2,5,4,8,128]{4,3,2,1,0:T(8,128)S(1)}, f32[2,5,4,8,128]{4,3,2,1,0:T(8,128)S(1)}, u32[]{:S(2)}, u32[]{:S(2)}) collective-permute-start(f32[2,5,4,8,128]{4,3,2,1,0:T(8,128)S(1)} %get-tuple-element.53), channel_id=1, source_target_pairs={{0,1},{1,0},{2,3},{3,2},{4,5},{5,4},{6,7},{7,6},{8,9},{9,8},{10,11... | collective-permute-start | bytes 491528 | tf_op jit(solution)/shard_map/ppermute | solution.py:388
  110.0 11.2 %collective-permute-start.25 = (f32[2,5,4,8,128]{4,3,2,1,0:T(8,128)S(1)}, f32[2,5,4,8,128]{4,3,2,1,0:T(8,128)S(1)}, u32[]{:S(2)}, u32[]{:S(2)}) collective-permute-start(f32[2,5,4,8,128]{4,3,2,1,0:T(8,128)S(1)} %get-tuple-element.54), channel_id=1, source_target_pairs={{0,2},{1,3},{2,0},{3,1},{4,6},{5,7},{6,4},{7,5},{8,10},{9,11},{10,... | collective-permute-start | bytes 491528 | tf_op jit(solution)/shard_map/ppermute | solution.py:388
  110.6 12.0 %collective-permute-start.26 = (f32[2,5,4,8,128]{4,3,2,1,0:T(8,128)S(1)}, f32[2,5,4,8,128]{4,3,2,1,0:T(8,128)S(1)}, u32[]{:S(2)}, u32[]{:S(2)}) collective-permute-start(f32[2,5,4,8,128]{4,3,2,1,0:T(8,128)S(1)} %get-tuple-element.55), channel_id=1, source_target_pairs={{0,3},{1,2},{2,1},{3,0},{4,7},{5,6},{6,5},{7,4},{8,11},{9,10},{10,... | collective-permute-start | bytes 491528 | tf_op jit(solution)/shard_map/ppermute | solution.py:388
  113.5 9.1 %collective-permute-start.27 = (f32[2,5,4,8,128]{4,3,2,1,0:T(8,128)S(1)}, f32[2,5,4,8,128]{4,3,2,1,0:T(8,128)S(1)}, u32[]{:S(2)}, u32[]{:S(2)}) collective-permute-start(f32[2,5,4,8,128]{4,3,2,1,0:T(8,128)S(1)} %get-tuple-element.56), channel_id=1, source_target_pairs={{0,4},{1,5},{2,6},{3,7},{4,0},{5,1},{6,2},{7,3},{8,12},{9,13},{10,... | collective-permute-start | bytes 491528 | tf_op jit(solution)/shard_map/ppermute | solution.py:388
  118.2 11.7 %collective-permute-start.28 = (f32[2,5,4,8,128]{4,3,2,1,0:T(8,128)S(1)}, f32[2,5,4,8,128]{4,3,2,1,0:T(8,128)S(1)}, u32[]{:S(2)}, u32[]{:S(2)}) collective-permute-start(f32[2,5,4,8,128]{4,3,2,1,0:T(8,128)S(1)} %get-tuple-element.57), channel_id=1, source_target_pairs={{0,5},{1,4},{2,7},{3,6},{4,1},{5,0},{6,3},{7,2},{8,13},{9,12},{10,... | collective-permute-start | bytes 491528 | tf_op jit(solution)/shard_map/ppermute | solution.py:388
  118.5 11.3 %collective-permute-start.29 = (f32[2,5,4,8,128]{4,3,2,1,0:T(8,128)S(1)}, f32[2,5,4,8,128]{4,3,2,1,0:T(8,128)S(1)}, u32[]{:S(2)}, u32[]{:S(2)}) collective-permute-start(f32[2,5,4,8,128]{4,3,2,1,0:T(8,128)S(1)} %get-tuple-element.58), channel_id=1, source_target_pairs={{0,6},{1,7},{2,4},{3,5},{4,2},{5,3},{6,0},{7,1},{8,14},{9,15},{10,... | collective-permute-start | bytes 491528 | tf_op jit(solution)/shard_map/ppermute | solution.py:388
  121.2 10.5 %collective-permute-start.30 = (f32[2,5,4,8,128]{4,3,2,1,0:T(8,128)S(1)}, f32[2,5,4,8,128]{4,3,2,1,0:T(8,128)S(1)}, u32[]{:S(2)}, u32[]{:S(2)}) collective-permute-start(f32[2,5,4,8,128]{4,3,2,1,0:T(8,128)S(1)} %get-tuple-element.59), channel_id=1, source_target_pairs={{0,7},{1,6},{2,5},{3,4},{4,3},{5,2},{6,1},{7,0},{8,15},{9,14},{10,... | collective-permute-start | bytes 491528 | tf_op jit(solution)/shard_map/ppermute | solution.py:388
  (7 other events, 98.7 us)

commit v2 on v0

v2 whole, which is shorter than its diff:
```python
import functools
import math

import jax
import jax.numpy as jnp
from jax import lax
from jax.experimental import pallas as pl
from jax.experimental.pallas import tpu as pltpu
from jax.sharding import PartitionSpec as P

STEPS = 2
NU_DAMP = 0.25
DT_STEP = 0.4
PULSE_MID = 0.8
PULSE_WIDTH = 0.5

AXES = ("gx", "gy")
FIELDS = 5
DEEP = 4
MEMBERS = 8
ROWS = 8
LANES = 128
STATE = FIELDS * DEEP
SPONGE = 2 * STATE
PIECE = SPONGE + DEEP
F32 = jnp.float32

VMEM = pl.BlockSpec(memory_space=pltpu.VMEM)
SMEM = pl.BlockSpec(memory_space=pltpu.SMEM)
HBM = pl.BlockSpec(memory_space=pltpu.HBM)
PARAMS = pltpu.CompilerParams(vmem_limit_bytes=48 * 1024 * 1024)


def cost(micros):
    return pl.CostEstimate(flops=0, transcendentals=0, bytes_accessed=int(3.0e6 * micros))


def pulse(time_now):
    return math.exp(-(((time_now - PULSE_MID) / PULSE_WIDTH) ** 2))


def step_scales(step):
    start = step * DT_STEP
    p0, ph, p1 = pulse(start), pulse(start + 0.5 * DT_STEP), pulse(start + DT_STEP)
    return (
        (DT_STEP / 4.0, p0),
        (DT_STEP / 3.0, (p0 + ph) / 2.0),
        (DT_STEP / 2.0, (p0 + 2.0 * ph) / 3.0),
        (DT_STEP, (p0 + 4.0 * ph + p1) / 6.0),
    )


def position():
    along_x = lax.axis_index("gx")
    return along_x // 2, (along_x % 2) * 4 + lax.axis_index("gy")


def pack_kernel(groups, state_hbm, sponge_hbm, nodes_hbm, weights_hbm, count_hbm, shapes_hbm, *refs):
    pieces, wall = refs[:MEMBERS], refs[MEMBERS]
    sponge_ref, nodes_ref, weights_ref, count_ref, shapes_ref, sems = refs[MEMBERS + 1 :]
    _, member = position()
    row = member % 4
    small = [
        pltpu.make_async_copy(count_hbm, count_ref, sems.at[0]),
        pltpu.make_async_copy(nodes_hbm.at[row], nodes_ref, sems.at[1]),
        pltpu.make_async_copy(weights_hbm.at[row], weights_ref, sems.at[2]),
        pltpu.make_async_copy(sponge_hbm, sponge_ref, sems.at[3]),
        pltpu.make_async_copy(shapes_hbm, shapes_ref, sems.at[4]),
    ]
    large = []
    for d, piece in enumerate(pieces):
        for f in range(FIELDS):
            large.append(
                pltpu.make_async_copy(
                    state_hbm.at[f, pl.ds(2 * DEEP * (member ^ d), 2 * DEEP)],
                    piece.at[pl.ds(2 * DEEP * f, 2 * DEEP)],
                    sems.at[5 + d * FIELDS + f],
                )
            )
    for copy in small + large:
        copy.start()
    for copy in small:
        copy.wait()
    lane = lax.broadcasted_iota(jnp.int32, (1, LANES), 1)
    table = [nodes_ref[...].astype(F32)]
    for x in range(DEEP):
        kept = jnp.where(lane < count_ref[x], 1.0, 0.0)
        table.append(weights_ref[pl.ds(x, 1), :] * kept)
    table = jnp.concatenate(table, axis=0)
    for piece in pieces:
        for x in range(DEEP):
            piece[SPONGE + x] = sponge_ref[x]
    for m in range(MEMBERS):
        two = shapes_ref[2 * m : 2 * m + 2, :]
        lines = jnp.concatenate([two[:, :LANES], two[:, LANES:]] * 2, axis=0)
        for g in range(groups):
            wall[g * MEMBERS + m, 0] = lines
            wall[g * MEMBERS + m, 1] = table
    for copy in large:
        copy.wait()


def pack(groups, state_in, sponge, nodes, weights, count, shapes):
    inputs = (
        state_in.reshape(FIELDS, 2 * MEMBERS * DEEP, ROWS, LANES),
        sponge, nodes, weights, count, shapes,
    )
    return pl.pallas_call(
        functools.partial(pack_kernel, groups),
        out_shape=[jax.ShapeDtypeStruct((PIECE, ROWS, LANES), F32)] * MEMBERS
        + [jax.ShapeDtypeStruct((groups * MEMBERS, 2, ROWS, LANES), F32)],
        in_specs=[HBM] * 6,
        out_specs=[VMEM] * (MEMBERS + 1),
        scratch_shapes=[
            pltpu.VMEM(sponge.shape, F32),
            pltpu.VMEM(nodes.shape[1:], jnp.int32),
            pltpu.VMEM(weights.shape[1:], F32),
            pltpu.SMEM(count.shape, jnp.int32),
            pltpu.VMEM(shapes.shape, F32),
            pltpu.SemaphoreType.DMA((5 + MEMBERS * FIELDS,)),
        ],
        compiler_params=PARAMS,
        cost_estimate=cost(2),
        name="pack",
    )(*[pltpu.with_memory_space_constraint(x, pltpu.HBM) for x in inputs])


def assemble_kernel(*refs):
    pieces, targets = refs[:MEMBERS], refs[MEMBERS:]
    group, member = position()
    even = group % 2 == 0
    for d, piece in enumerate(pieces):
        other = member ^ d
        is_first = (other >= 4) == even

        def copy(modes):
            for f in range(FIELDS):
                for j in range(2):
                    for x in range(DEEP):
                        modes[j][other % 4, f * DEEP + x] = piece[(f * 2 + j) * DEEP + x]
            for x in range(DEEP):
                modes[0][other % 4, STATE + x] = piece[SPONGE + x]

        @pl.when(is_first)
        def _():
            copy(targets[0::2])

        @pl.when(jnp.logical_not(is_first))
        def _():
            copy(targets[1::2])


def shifted_rows(tiles, sub):
    ahead = [pltpu.roll(t, ROWS - 1, 0) for t in tiles]
    behind = [pltpu.roll(t, 1, 0) for t in tiles]
    zero = jnp.zeros_like(tiles[0])
    last, first = sub == ROWS - 1, sub == 0
    count = len(tiles)
    north = [jnp.where(last, ahead[t + 1] if t + 1 < count else zero, ahead[t]) for t in range(count)]
    south = [jnp.where(first, behind[t - 1] if t > 0 else zero, behind[t]) for t in range(count)]
    return north, south


def run_stage(src, base, dst, sponge_ref, wall_ref, vel, wall_vec, h, scale, low, high):
    lane = lax.broadcasted_iota(jnp.int32, (ROWS, LANES), 1)
    sub = lax.broadcasted_iota(jnp.int32, (ROWS, LANES), 0)
    plus = [h * (NU_DAMP - 0.5 * v) for v in vel]
    minus = [h * (NU_DAMP + 0.5 * v) for v in vel]
    not_top, not_low = lane < LANES - 1, lane > 0
    plus_z = jnp.where(not_top, plus[2], 0.0)
    minus_z = jnp.where(not_low, minus[2], 0.0)
    flux = -0.5 * h
    flux_up = jnp.where(not_top, flux, 0.0)
    flux_low = jnp.where(not_low, flux, 0.0)
    tiles = range(4)

    def plane(i, carry):
        def load(ref, f, at):
            return [ref[f, at, pl.ds(ROWS * t, ROWS), :] for t in tiles]

        damp = [-h * (6.0 * NU_DAMP + sponge_ref[i, pl.ds(ROWS * t, ROWS), :]) for t in tiles]
        new = []
        for f in range(FIELDS):
            center = load(src, f, i)
            east, west = load(src, f, i + 1), load(src, f, i - 1)
            north, south = shifted_rows(center, sub)
            upper = [pltpu.roll(c, LANES - 1, 1) for c in center]
            lower = [pltpu.roll(c, 1, 1) for c in center]
            old = load(base, f, i)
            out = []
            for t in tiles:
                acc = old[t] + damp[t] * center[t]
                acc += plus[0] * east[t] + minus[0] * west[t]
                acc += plus[1] * north[t] + minus[1] * south[t]
                acc += plus_z * upper[t] + minus_z * lower[t]
                if t == 0:
                    acc += (h * scale * wall_vec[f]) * wall_ref[i]
                out.append(acc)
            new.append(out)
            if f == 1:
                d1 = [east[t] - west[t] for t in tiles]
            elif f == 2:
                d2 = [north[t] - south[t] for t in tiles]
            elif f == 3:
                d3 = [flux_up * upper[t] - flux_low * lower[t] for t in tiles]
            elif f == 4:
                for t in tiles:
                    new[1][t] += flux * (east[t] - west[t])
                    new[2][t] += flux * (north[t] - south[t])
                    new[3][t] += flux_up * upper[t] - flux_low * lower[t]
        for t in tiles:
            spread = flux * (d1[t] + d2[t]) + d3[t]
            new[0][t] += spread
            new[4][t] += spread
        for f in range(FIELDS):
            for t in tiles:
                dst[f, i, pl.ds(ROWS * t, ROWS), :] = new[f][t]
        return carry

    def two_planes(n, carry):
        plane(low + 2 * n, carry)
        return plane(low + 2 * n + 1, carry)

    lax.fori_loop(0, (high - low) // 2, two_planes, 0)


def run_step(step, base, va, vb, sponge_ref, wall_ref, vel, wall_vec, has_low, has_high):
    zero = jnp.zeros((ROWS, LANES), F32)
    src = base
    for k, (h, scale) in enumerate(step_scales(step)):
        dst = va if k % 2 == 0 else vb
        low, high = k + 1, 4 * DEEP - 1 - k
        run_stage(src, base, dst, sponge_ref, wall_ref, vel, wall_vec, h, scale, low, high)
        if k < 3:
            for there, at in ((has_low, DEEP - 1), (has_high, 3 * DEEP)):

                @pl.when(jnp.logical_not(there))
                def _():
                    for f in range(FIELDS):
                        for t in range(4):
                            dst[f, at, pl.ds(ROWS * t, ROWS), :] = zero

        src = dst


def write_pieces(sources, pieces):
    for m in range(MEMBERS):
        row = ROWS * (m % 4)
        for j, (ref, starts) in enumerate(sources):
            for f in range(FIELDS):
                for x in range(DEEP):
                    pieces[m, j, f, x] = ref[f, starts[m // 4] + x, row : row + ROWS, :]


def block_starts(group):
    even = group % 2 == 0
    return (
        jnp.where(even, 2 * DEEP, DEEP),
        jnp.where(even, DEEP, 2 * DEEP),
        jnp.where(even, 3 * DEEP, 0),
        jnp.where(even, 0, 3 * DEEP),
    )


def forcing_kernel(groups, parts, *walls):
    group, member = position()
    last = groups - 1
    tab = []
    for block in range(4):
        side = jnp.clip(group + (-1, 0, 0, 1)[block], 0, last)
        there = (group > 0, True, True, group < last)[block]
        for half in range(2):
            two = [parts[side * MEMBERS + (4, 0, 4, 0)[block] + 2 * half + n, 1] for n in range(2)]
            tab.append((two, there))
    zero = jnp.zeros((ROWS, LANES), F32)
    low_part, high_part, weights = [], [], []
    for two, there in tab:
        index = jnp.concatenate([two[0][:DEEP], two[1][:DEEP]], axis=0).astype(jnp.int32)
        weight = jnp.concatenate([two[0][DEEP:], two[1][DEEP:]], axis=0)
        weights.append(weight if there is True else jnp.where(there, weight, 0.0))
        low_part.append(index & (LANES - 1))
        high_part.append(index // LANES)
    count = len(weights)

    def body(q, taken):
        taken = [list(taken[j]) for j in range(2)]
        tile = parts[q, 0]
        for s in range(2):
            for j in range(2):
                line = jnp.broadcast_to(tile[2 * s + j : 2 * s + j + 1], (ROWS, LANES))
                for b in range(count):
                    value = jnp.take_along_axis(line, low_part[b], axis=1)
                    taken[j][b] = jnp.where(high_part[b] == 2 * q + s, value, taken[j][b])
        return tuple(tuple(t) for t in taken)

    start = tuple(tuple(zero for _ in range(count)) for _ in range(2))
    taken = lax.fori_loop(0, groups * MEMBERS, body, start)
    sub = lax.broadcasted_iota(jnp.int32, (ROWS, LANES), 0)
    for j in range(2):
        for block in range(4):
            total = sum(taken[j][2 * block + n] * weights[2 * block + n] for n in range(2))
            total = total[:DEEP] + total[DEEP:]
            for x in range(DEEP):
                line = jnp.broadcast_to(total[x : x + 1], (ROWS, LANES))
                walls[j][DEEP * block + x] = jnp.where(sub == 0, line, 0.0)


def first_kernel(groups, mode, vel_ref, vec_ref, wall_ref, *refs):
    blocks, refs = refs[:4], refs[4:]
    if mode == 0:
        a_ref, b_ref, sponge_ref, base, va, vb = refs
    else:
        sponge_ref, a_other, b_other, a_ref, b_ref = refs[:5]
        pieces, base, va, vb = refs[5:]
    group, member = position()
    starts = block_starts(group)
    for source, start in zip(blocks, starts):
        for y in range(4):
            rows = pl.ds(ROWS * y, ROWS)
            for f in range(FIELDS):
                for x in range(DEEP):
                    base[f, start + x, rows, :] = source[y, f * DEEP + x]
            if mode == 0:
                for x in range(DEEP):
                    sponge_ref[start + x, rows, :] = source[y, STATE + x]
    vel = [vel_ref[d] for d in range(3)]
    vec = [vec_ref[f] for f in range(FIELDS)]
    run_step(0, base, va, vb, sponge_ref, wall_ref, vel, vec, group > 0, group < groups - 1)
    for target, start in zip((a_ref, b_ref), starts):
        for f in range(FIELDS):
            for x in range(DEEP):
                target[f, x] = vb[f, start + x]
    if mode == 1:
        for f in range(FIELDS):
            for x in range(DEEP):
                va[f, starts[0] + x] = a_other[f, x]
                va[f, starts[1] + x] = b_other[f, x]
        write_pieces([(va, (DEEP, 2 * DEEP)), (vb, (DEEP, 2 * DEEP))], pieces)


def second_kernel(groups, mode, vel_ref, vec_ref, wall_ref, *refs):
    blocks, refs = refs[:4], refs[4:]
    if mode == 0:
        sponge_ref, target, base, va, vb = refs
    else:
        sponge_ref, other = refs[:2]
        pieces = refs[2 : 2 + MEMBERS]
        base, va, vb = refs[2 + MEMBERS :]
    group, member = position()
    for source, start in zip(blocks, block_starts(group)):
        for f in range(FIELDS):
            for x in range(DEEP):
                base[f, start + x] = source[f, x]
    vel = [vel_ref[d] for d in range(3)]
    vec = [vec_ref[f] for f in range(FIELDS)]
    run_step(1, base, va, vb, sponge_ref, wall_ref, vel, vec, group > 0, group < groups - 1)
    if mode == 0:
        for f in range(FIELDS):
            for x in range(2 * DEEP):
                target[f, x] = vb[f, DEEP + x]
    else:
        for d in range(MEMBERS):
            to = member ^ d
            row = pl.multiple_of((to % 4) * ROWS, ROWS)
            start = DEEP * (to // 4)
            for f in range(FIELDS):
                for x in range(DEEP):
                    pieces[d][0, f, x] = other[f, start + x, pl.ds(row, ROWS), :]
                    pieces[d][1, f, x] = vb[f, DEEP + start + x, pl.ds(row, ROWS), :]


def gram_kernel(total, *refs):
    first, second = refs[0], refs[1 : 1 + MEMBERS]
    state_ref, gram_ref, columns = refs[1 + MEMBERS :]
    _, member = position()
    tiles = FIELDS * DEEP
    for d in range(MEMBERS):
        other = member ^ d
        for j in range(2):
            here = (2 * d + j) * tiles * ROWS
            there = pl.multiple_of((2 * MEMBERS + 2 * other + j) * tiles * ROWS, ROWS)
            for f in range(FIELDS):
                for x in range(DEEP):
                    n = (f * DEEP + x) * ROWS
                    columns[here + n : here + n + ROWS, :] = first[d, j, f, x]
                    value = second[d][j, f, x]
                    columns[pl.ds(pl.multiple_of(there + n, ROWS), ROWS), :] = value
                    state_ref[f, 2 * other + j, x] = value
    size = STEPS * 2 * MEMBERS
    stride = tiles * ROWS

    def body(r, acc):
        a = jnp.concatenate(
            [columns[pl.ds(4 * r + n, size, stride=stride), :] for n in range(4)], axis=1
        )
        return acc + lax.dot_general(
            a, a, (((1,), (1,)), ((), ())),
            precision=lax.Precision.HIGHEST, preferred_element_type=F32,
        )

    gram = lax.fori_loop(0, stride // 4, body, jnp.zeros((size, size), F32), unroll=4)
    tile = jnp.concatenate([gram[ROWS * n : ROWS * n + ROWS] for n in range(4)], axis=1)
    for n in range(gram_ref.shape[0]):
        gram_ref[n] = tile


def factor_kernel(total, parts_ref, factor_ref):
    acc = parts_ref[0]
    for n in range(1, parts_ref.shape[0]):
        acc = acc + parts_ref[n]
    acc = acc / total
    size = factor_ref.shape[0]
    a = jnp.concatenate([acc[:, size * n : size * n + size] for n in range(4)], axis=0)
    lines = []
    for k in range(size):
        inverse = 1.0 / jnp.sqrt(a[k : k + 1, k : k + 1])
        line = a[k : k + 1, :] * inverse
        lines.append(line)
        if k < size - 1:
            a = a - (a[:, k : k + 1] * inverse) * line
    factor = jnp.concatenate(lines, axis=0)
    row = lax.broadcasted_iota(jnp.int32, (size, size), 0)
    col = lax.broadcasted_iota(jnp.int32, (size, size), 1)
    factor_ref[...] = jnp.where(col >= row, factor, 0.0)


def local(state_in, sponge, mean_velocity, wall_vector, mode_shapes, wall_nodes, wall_weights, wall_count):
    gx_size, gy_size = lax.axis_size("gx"), lax.axis_size("gy")
    groups = gx_size // 2
    devices = gx_size * gy_size
    cells_x, cells_y, cells_z = state_in.shape[2:]
    def inside(d):
        return [(i, i ^ d) for i in range(devices)]

    def swap(first):
        moves = []
        for i in range(devices):
            g = i // MEMBERS
            target = g + 1 if (g % 2 == 0) == first else g - 1
            if 0 <= target < groups:
                moves.append((i, i + (target - g) * MEMBERS))
        return moves

    def exchange(a, b):
        return a, b, lax.ppermute(a, AXES, swap(True)), lax.ppermute(b, AXES, swap(False))

    def spread(pieces):
        got = {0: pieces[0]}
        for d in (4, 2, 5, 3, 6, 7, 1):
            got[d] = lax.ppermute(pieces[d], AXES, inside(d))
        return [got[d] for d in range(MEMBERS)]

    def call(kernel, name, micros, out_shape, inputs, scratch=(), scalars=0):
        return pl.pallas_call(
            kernel,
            out_shape=out_shape,
            in_specs=[SMEM] * scalars + [VMEM] * (len(inputs) - scalars),
            out_specs=[VMEM] * len(out_shape),
            scratch_shapes=scratch,
            compiler_params=PARAMS,
            cost_estimate=cost(micros),
            name=name,
        )(*inputs)

    def shape(*sizes):
        return jax.ShapeDtypeStruct(sizes, F32)

    *pieces, wall = pack(groups, state_in, sponge, wall_nodes, wall_weights, wall_count, mode_shapes)
    pieces = spread(pieces)
    wall, pieces[1] = lax.optimization_barrier((wall, pieces[1]))
    wall = lax.all_to_all(wall, AXES, 0, 0)
    messages = call(
        assemble_kernel,
        "assemble",
        1,
        [shape(4, STATE + DEEP, ROWS, LANES)] * 2 + [shape(4, STATE, ROWS, LANES)] * 2,
        pieces,
    )
    blocks = [exchange(*messages[:2]), exchange(*messages[2:])]
    walls = call(
        functools.partial(forcing_kernel, groups),
        "forcing",
        5.0,
        [shape(4 * DEEP, ROWS, LANES)] * 2,
        [wall],
    )
    field = [pltpu.VMEM((FIELDS, 4 * DEEP, 4 * ROWS, LANES), F32)] * 3
    border = shape(FIELDS, DEEP, 4 * ROWS, LANES)
    piece = shape(2, FIELDS, DEEP, ROWS, LANES)
    constants = (mean_velocity, wall_vector)
    a0, b0, sponge_ext = call(
        functools.partial(first_kernel, groups, 0),
        "first_step_0",
        5.0,
        [border, border, shape(4 * DEEP, 4 * ROWS, LANES)],
        (*constants, walls[0], *blocks[0]),
        field,
        2,
    )
    next_blocks = [exchange(a0, b0)]
    a1, b1, first = call(
        functools.partial(first_kernel, groups, 1),
        "first_step_1",
        5.0,
        [border, border, shape(MEMBERS, 2, FIELDS, DEEP, ROWS, LANES)],
        (*constants, walls[1], *blocks[1], sponge_ext, a0, b0),
        field,
        2,
    )
    next_blocks.append(exchange(a1, b1))
    members = [[g * MEMBERS + m for m in range(MEMBERS)] for g in range(groups)]
    first = lax.all_to_all(first, AXES, 0, 0, axis_index_groups=members)
    (second_0,) = call(
        functools.partial(second_kernel, groups, 0),
        "second_step_0",
        5.0,
        [shape(FIELDS, 2 * DEEP, 4 * ROWS, LANES)],
        (*constants, walls[0], *next_blocks[0], sponge_ext),
        field,
        2,
    )
    second = call(
        functools.partial(second_kernel, groups, 1),
        "second_step_1",
        5.0,
        [piece] * MEMBERS,
        (*constants, walls[1], *next_blocks[1], sponge_ext, second_0),
        field,
        2,
    )
    second = spread(second)

    rows_total = float(FIELDS * cells_x * gx_size * cells_y * gy_size * cells_z)
    snap_count = STEPS * 2 * MEMBERS
    state_out, grams = pl.pallas_call(
        functools.partial(gram_kernel, rows_total),
        out_shape=[
            jax.ShapeDtypeStruct(state_in.shape, F32),
            jax.ShapeDtypeStruct((devices, ROWS, LANES), F32),
        ],
        in_specs=[VMEM] * (1 + MEMBERS),
        out_specs=[VMEM, VMEM],
        scratch_shapes=[pltpu.VMEM((snap_count * FIELDS * DEEP * ROWS, LANES), F32)],
        compiler_params=PARAMS,
        name="gram",
    )(first, *second)
    grams = lax.all_to_all(grams, AXES, 0, 0)
    factor = pl.pallas_call(
        functools.partial(factor_kernel, rows_total),
        out_shape=jax.ShapeDtypeStruct((snap_count, snap_count), F32),
        in_specs=[VMEM],
        out_specs=VMEM,
        compiler_params=PARAMS,
        name="factor",
    )(grams)
    return state_out, factor


def solution(mesh):
    placed = (
        P(None, None, "gx", "gy", None),
        P("gx", "gy", None),
        P(),
        P(),
        P(None, ("gx", "gy")),
        P(None, "gx", None),
        P(None, "gx", None),
        P("gx"),
    )
    return jax.shard_map(
        local,
        mesh=mesh,
        in_specs=placed,
        out_specs=(P(None, None, "gx", "gy", None), P()),
        check_vma=False,
    )
```

time: 511 us -> 124 us (0.24); the launches traced: 502 us -> 123 us
  matrix products: 117 us -> 0 us
  blocking collectives: 115 us -> 15.5 us
  waiting for transfers between devices: 118 us -> 27.5 us
  starting transfers between devices: 112 us -> 42.8 us
  Pallas kernels: 0 us -> 36.6 us
  local copies, waits for them, and re-layouts: 29.7 us -> 0.01 us
  other arithmetic: 7.58 us -> 0 us
    dot_general x25 -> x0, matrix products: 117 us -> none  [the longest x8 56 us: rates(): jnp.einsum('fg,gmxyz->fmxyz', jacobian[0], east_side - west_side, precisi...]
    ppermute x32 -> x22, waiting for transfers between devices: 118 us -> 27.5 us  [the longest x14 19.6 us: spread(): got[d] = lax.ppermute(pieces[d], AXES, inside(d))]
    ppermute x32 -> x22, starting transfers between devices: 112 us -> 34.1 us  [the longest x14 16.8 us: spread(): got[d] = lax.ppermute(pieces[d], AXES, inside(d))]
    all_gather x1 -> x0, blocking collectives: 62.8 us -> none  [local(): lax.all_gather(mode_shapes, ('gx', 'gy'), axis=1, tiled=True)]
    psum x1 -> x0, blocking collectives: 52.5 us -> none  [local(): gram_matrix = lax.psum(local_gram, ('gx', 'gy')) / rows_total]
    pallas_call x0 -> x9, Pallas kernels: none -> 36.6 us  [the longest x6 25.5 us: call(): pl.pallas_call(kernel, out_shape=out_shape, in_specs=[SMEM] * scalars + [...]
    all_to_all x0 -> x1, blocking collectives: none -> 15.5 us  [local(): grams = lax.all_to_all(grams, AXES, 0, 0)]
    slice x18 -> x0, local copies, waits for them, and re-layouts: 11.7 us -> none  [the longest x8 8.43 us: rates(): upper_side = jnp.concatenate([center[..., 1:], zero_plane], axis=4)]
  transfers between devices with their start and end apart: 32 -> 24, of which waited for: 17 -> 8; matrix products, arithmetic and copies ran while one was open for 10% -> 0% of each run, Pallas kernels for 0% -> 16%
where the time goes in v2:
time: 124 us; the launch traced here: 123 us
  starting transfers between devices  42.8 us (35%)
  Pallas kernels  36.6 us (30%)
  waiting for transfers between devices  27.5 us (22%)
  blocking collectives  15.5 us (12%)
    pallas_call x6, Pallas kernels, call(): pl.pallas_call(kernel, out_shape=out_shape, in_specs=[SMEM] * scalars + [...  25.5 us
    ppermute x14, waiting for transfers between devices, spread(): got[d] = lax.ppermute(pieces[d], AXES, inside(d))  19.6 us
    ppermute x14, starting transfers between devices, spread(): got[d] = lax.ppermute(pieces[d], AXES, inside(d))  16.8 us
    all_to_all x1, blocking collectives, local(): grams = lax.all_to_all(grams, AXES, 0, 0)  15.5 us
    ppermute x4, starting transfers between devices, exchange(): lax.ppermute(a, AXES, swap(True))  13.9 us
    ppermute x4, waiting for transfers between devices, exchange(): lax.ppermute(a, AXES, swap(True))  7.84 us
    pallas_call x1, Pallas kernels, local(): pl.pallas_call(functools.partial(gram_kernel, rows_total), out_shape=[jax...  5.07 us
    all_to_all x1, starting transfers between devices, local(): wall = lax.all_to_all(wall, AXES, 0, 0)  4.87 us
  transfers between devices with their start and end apart: 24, of which 8 were waited for; matrix products, arithmetic and copies ran while one was open for 0% of the time, Pallas kernels for 16%

profile of v2, /device:TPU:0, one launch (start us, length us, event | category | flops | bytes accessed | tf_op | source)
XLA Modules:
  0.0 123.1 jit_solution(8017681742612793764)
XLA Ops:
  0.6 2.4 %pack.1 = (f32[44,8,128]{2,1,0:T(8,128)S(1)}, f32[44,8,128]{2,1,0:T(8,128)S(1)}, f32[44,8,128]{2,1,0:T(8,128)S(1)}, f32[44,8,128]{2,1,0:T(8,128)S(1)}, f32[44,8,...) custom-call(f32[5,64,8,128]{3,2,1,0:T(8,128)} %bitcast.1, ...), custom_call_target="tpu_custom_call" | custom-call | bytes 6000000 | tf_op jit(solution)/shard_map/pack/pallas_call | solution.py:108
  3.6 2.6 %collective-permute-start.1 = (f32[44,8,128]{2,1,0:T(8,128)S(1)}, f32[44,8,128]{2,1,0:T(8,128)S(1)}, u32[]{:S(2)}, u32[]{:S(2)}) collective-permute-start(f32[44,8,128]{2,1,0:T(8,128)S(1)} %get-tuple-element.41), channel_id=1, source_target_pairs={{0,2},{1,3},{2,0},{3,1},{4,6},{5,7},{6,4},{7,5},{8,10},{9,11},{10,... | collective-permute-start | bytes 540680 | tf_op jit(solution)/shard_map/ppermute | solution.py:450
  6.2 1.8 %collective-permute-start.3 = (f32[44,8,128]{2,1,0:T(8,128)S(1)}, f32[44,8,128]{2,1,0:T(8,128)S(1)}, u32[]{:S(2)}, u32[]{:S(2)}) collective-permute-start(f32[44,8,128]{2,1,0:T(8,128)S(1)} %get-tuple-element.43), channel_id=1, source_target_pairs={{0,4},{1,5},{2,6},{3,7},{4,0},{5,1},{6,2},{7,3},{8,12},{9,13},{10,... | collective-permute-start | bytes 540680 | tf_op jit(solution)/shard_map/ppermute | solution.py:450
  8.0 2.6 %collective-permute-start.5 = (f32[44,8,128]{2,1,0:T(8,128)S(1)}, f32[44,8,128]{2,1,0:T(8,128)S(1)}, u32[]{:S(2)}, u32[]{:S(2)}) collective-permute-start(f32[44,8,128]{2,1,0:T(8,128)S(1)} %get-tuple-element.45), channel_id=1, source_target_pairs={{0,6},{1,7},{2,4},{3,5},{4,2},{5,3},{6,0},{7,1},{8,14},{9,15},{10,... | collective-permute-start | bytes 540680 | tf_op jit(solution)/shard_map/ppermute | solution.py:450
  10.6 0.9 collective-permute-done.1.refs_2_
  11.6 1.7 %collective-permute-start.6 = (f32[44,8,128]{2,1,0:T(8,128)S(1)}, f32[44,8,128]{2,1,0:T(8,128)S(1)}, u32[]{:S(2)}, u32[]{:S(2)}) collective-permute-start(f32[44,8,128]{2,1,0:T(8,128)S(1)} %get-tuple-element.46), channel_id=1, source_target_pairs={{0,7},{1,6},{2,5},{3,4},{4,3},{5,2},{6,1},{7,0},{8,15},{9,14},{10,... | collective-permute-start | bytes 540680 | tf_op jit(solution)/shard_map/ppermute | solution.py:450
  13.3 4.9 %all-to-all-start = ((f32[32,2,8,128]{3,2,1,0:T(8,128)}), f32[32,2,8,128]{3,2,1,0:T(8,128)S(1)}, u32[]{:S(2)}, u32[]{:S(2)}) async-start(f32[32,2,8,128]{3,2,1,0:T(8,128)} %get-tuple-element.37), calls=%async_computation | async-start | bytes 524288 | tf_op jit(solution)/shard_map/all_to_all | solution.py:471
  18.2 8.1 %collective-permute-done.4.refs_5_ = f32[44,8,128]{2,1,0:T(8,128)S(1)} collective-permute-done((f32[44,8,128]{2,1,0:T(8,128)S(1)}, f32[44,8,128]{2,1,0:T(8,128)S(1)}, u32[]{:S(2)}, u32[]{:S(2)}) %collective-permute-start.4) | collective-permute-done | bytes 180256 | tf_op jit(solution)/shard_map/ppermute | solution.py:450
  26.3 0.9 assemble.1
  27.3 1.8 %collective-permute-start.9 = (f32[4,24,8,128]{3,2,1,0:T(8,128)S(1)}, f32[4,24,8,128]{3,2,1,0:T(8,128)S(1)}, u32[]{:S(2)}, u32[]{:S(2)}) collective-permute-start(f32[4,24,8,128]{3,2,1,0:T(8,128)S(1)} %get-tuple-element.50.refs_0_), channel_id=1, source_target_pairs={{0,8},{1,9},{2,10},{3,11},{4,12},{5,13},{6,14},{7,15},{8,0},{9,1},... | collective-permute-start | bytes 1179656 | tf_op jit(solution)/shard_map/ppermute | solution.py:445
  29.8 4.4 %collective-permute-start.7 = (f32[4,20,8,128]{3,2,1,0:T(8,128)S(1)}, f32[4,20,8,128]{3,2,1,0:T(8,128)}, u32[]{:S(2)}, u32[]{:S(2)}) collective-permute-start(f32[4,20,8,128]{3,2,1,0:T(8,128)S(1)} %get-tuple-element.47.refs_0_), channel_id=1, source_target_pairs={{0,8},{1,9},{2,10},{3,11},{4,12},{5,13},{6,14},{7,15},{8,0},{9,1},... | collective-permute-start | bytes 983048 | tf_op jit(solution)/shard_map/ppermute | solution.py:445
  34.2 1.4 %collective-permute-start.8 = (f32[4,20,8,128]{3,2,1,0:T(8,128)}, f32[4,20,8,128]{3,2,1,0:T(8,128)}, u32[]{:S(2)}, u32[]{:S(2)}) collective-permute-start(f32[4,20,8,128]{3,2,1,0:T(8,128)} %get-tuple-element.48.refs_1_), channel_id=1, source_target_pairs={{8,16},{9,17},{10,18},{11,19},{12,20},{13,21},{14,22},{15,23},{16,... | collective-permute-start | bytes 983048 | tf_op jit(solution)/shard_map/ppermute | solution.py:445
  35.6 5.1 %forcing.1 = (f32[16,8,128]{2,1,0:T(8,128)S(1)}, f32[16,8,128]{2,1,0:T(8,128)S(1)}) custom-call(f32[32,2,8,128]{3,2,1,0:T(8,128)S(1)} %all-to-all-done.parts), custom_call_target="tpu_custom_call" | custom-call | bytes 15000000 | tf_op jit(solution)/shard_map/forcing/pallas_call | solution.py:454
  40.7 4.4 %first_step_0.1 = (f32[5,4,32,128]{3,2,1,0:T(8,128)S(1)}, f32[5,4,32,128]{3,2,1,0:T(8,128)S(1)}, f32[16,32,128]{2,1,0:T(8,128)S(1)}) custom-call(f32[3]{0:T(128)S(1)} %copy-done, f32[5]{0:T(128)S(1)} %copy-done.1, f32[16,8,128]{2,1,0:T(8,128)S(1)} %get-tuple-element.49.wall_ref, f32[4,24,8,128]{3,2,1,0:T(8,128)S(1)} %get-tuple-element.50.refs_0_, ...), custom_call_target="tpu_custom_call" | custom-call | bytes 15000000 | tf_op jit(solution)/shard_map/first_step_0/pallas_call | solution.py:454
  45.1 1.2 collective-permute-done.7.refs_2_
  46.3 6.2 %first_step_1.1 = (f32[5,4,32,128]{3,2,1,0:T(8,128)S(1)}, f32[5,4,32,128]{3,2,1,0:T(8,128)S(1)}, f32[8,2,5,4,8,128]{5,4,3,2,1,0:T(8,128)}) custom-call(f32[3]{0:T(128)S(1)} %copy-done, f32[5]{0:T(128)S(1)} %copy-done.1, f32[16,8,128]{2,1,0:T(8,128)S(1)} %get-tuple-element.38.wall_ref, f32[4,20,8,128]{3,2,1,0:T(8,128)S(1)} %get-tuple-element.47.refs_0_, ...), custom_call_target="tpu_custom_call" | custom-call | bytes 15000000 | tf_op jit(solution)/shard_map/first_step_1/pallas_call | solution.py:454
  52.5 3.8 %all-to-all-start.1 = ((f32[8,2,5,4,8,128]{5,4,3,2,1,0:T(8,128)}), f32[8,2,5,4,8,128]{5,4,3,2,1,0:T(8,128)S(1)}, u32[]{:S(2)}, u32[]{:S(2)}) async-start(f32[8,2,5,4,8,128]{5,4,3,2,1,0:T(8,128)} %get-tuple-element.55), calls=%async_computation.1 | async-start | bytes 2621440 | tf_op jit(solution)/shard_map/all_to_all | solution.py:512
  56.3 4.6 %collective-permute-start.13 = (f32[5,4,32,128]{3,2,1,0:T(8,128)S(1)}, f32[5,4,32,128]{3,2,1,0:T(8,128)S(1)}, u32[]{:S(2)}, u32[]{:S(2)}) collective-permute-start(f32[5,4,32,128]{3,2,1,0:T(8,128)S(1)} %get-tuple-element.53.refs_5_.refs_0_), channel_id=1, source_target_pairs={{0,8},{1,9},{2,10},{3,11},{4,12},{5,13},{6,14},{7,15},{8,0},{9,1},... | collective-permute-start | bytes 983048 | tf_op jit(solution)/shard_map/ppermute | solution.py:445
  61.6 3.0 %collective-permute-start.11 = (f32[5,4,32,128]{3,2,1,0:T(8,128)S(1)}, f32[5,4,32,128]{3,2,1,0:T(8,128)S(1)}, u32[]{:S(2)}, u32[]{:S(2)}) collective-permute-start(f32[5,4,32,128]{3,2,1,0:T(8,128)S(1)} %get-tuple-element.56.refs_0_), channel_id=1, source_target_pairs={{0,8},{1,9},{2,10},{3,11},{4,12},{5,13},{6,14},{7,15},{8,0},{9,1},... | collective-permute-start | bytes 983048 | tf_op jit(solution)/shard_map/ppermute | solution.py:445
  65.3 4.2 %collective-permute-done.13.refs_2_ = f32[5,4,32,128]{3,2,1,0:T(8,128)S(1)} collective-permute-done((f32[5,4,32,128]{3,2,1,0:T(8,128)S(1)}, f32[5,4,32,128]{3,2,1,0:T(8,128)S(1)}, u32[]{:S(2)}, u32[]{:S(2)}) %collective-permute-start.13) | collective-permute-done | bytes 327712 | tf_op jit(solution)/shard_map/ppermute | solution.py:445
  69.5 4.3 %second_step_0.1.refs_5_ = f32[5,8,32,128]{3,2,1,0:T(8,128)S(1)} custom-call(f32[3]{0:T(128)S(1)} %copy-done, f32[5]{0:T(128)S(1)} %copy-done.1, f32[16,8,128]{2,1,0:T(8,128)S(1)} %get-tuple-element.49.wall_ref, f32[5,4,32,128]{3,2,1,0:T(8,128)S(1)} %get-tuple-element.53.refs_5_.refs_0_, f32[5,4,32,128]{3,2,1,0:T(8,128)S(1)} %get-tuple-element.54.refs_6_.refs_1_, ...), custom_call_target="tpu_custom_call" | custom-call | bytes 15000000 | tf_op jit(solution)/shard_map/second_step_0/pallas_call | solution.py:454
  73.9 2.5 %collective-permute-done.11.refs_2_ = f32[5,4,32,128]{3,2,1,0:T(8,128)S(1)} collective-permute-done((f32[5,4,32,128]{3,2,1,0:T(8,128)S(1)}, f32[5,4,32,128]{3,2,1,0:T(8,128)S(1)}, u32[]{:S(2)}, u32[]{:S(2)}) %collective-permute-start.11) | collective-permute-done | bytes 327712 | tf_op jit(solution)/shard_map/ppermute | solution.py:445
  76.3 4.5 %second_step_1.1 = (f32[2,5,4,8,128]{4,3,2,1,0:T(8,128)S(1)}, f32[2,5,4,8,128]{4,3,2,1,0:T(8,128)S(1)}, f32[2,5,4,8,128]{4,3,2,1,0:T(8,128)S(1)}, f32[2,5,4,8,12...) custom-call(f32[3]{0:T(128)S(1)} %copy-done, ...), custom_call_target="tpu_custom_call" | custom-call | bytes 15000000 | tf_op jit(solution)/shard_map/second_step_1/pallas_call | solution.py:454
  80.9 1.7 %collective-permute-start.16 = (f32[2,5,4,8,128]{4,3,2,1,0:T(8,128)S(1)}, f32[2,5,4,8,128]{4,3,2,1,0:T(8,128)S(1)}, u32[]{:S(2)}, u32[]{:S(2)}) collective-permute-start(f32[2,5,4,8,128]{4,3,2,1,0:T(8,128)S(1)} %get-tuple-element.60), channel_id=1, source_target_pairs={{0,2},{1,3},{2,0},{3,1},{4,6},{5,7},{6,4},{7,5},{8,10},{9,11},{10,... | collective-permute-start | bytes 491528 | tf_op jit(solution)/shard_map/ppermute | solution.py:450
  82.8 1.7 %collective-permute-start.18 = (f32[2,5,4,8,128]{4,3,2,1,0:T(8,128)S(1)}, f32[2,5,4,8,128]{4,3,2,1,0:T(8,128)S(1)}, u32[]{:S(2)}, u32[]{:S(2)}) collective-permute-start(f32[2,5,4,8,128]{4,3,2,1,0:T(8,128)S(1)} %get-tuple-element.62), channel_id=1, source_target_pairs={{0,4},{1,5},{2,6},{3,7},{4,0},{5,1},{6,2},{7,3},{8,12},{9,13},{10,... | collective-permute-start | bytes 491528 | tf_op jit(solution)/shard_map/ppermute | solution.py:450
  84.5 2.6 %collective-permute-start.20 = (f32[2,5,4,8,128]{4,3,2,1,0:T(8,128)S(1)}, f32[2,5,4,8,128]{4,3,2,1,0:T(8,128)S(1)}, u32[]{:S(2)}, u32[]{:S(2)}) collective-permute-start(f32[2,5,4,8,128]{4,3,2,1,0:T(8,128)S(1)} %get-tuple-element.64), channel_id=1, source_target_pairs={{0,6},{1,7},{2,4},{3,5},{4,2},{5,3},{6,0},{7,1},{8,14},{9,15},{10,... | collective-permute-start | bytes 491528 | tf_op jit(solution)/shard_map/ppermute | solution.py:450
  88.0 1.4 %collective-permute-start.21 = (f32[2,5,4,8,128]{4,3,2,1,0:T(8,128)S(1)}, f32[2,5,4,8,128]{4,3,2,1,0:T(8,128)S(1)}, u32[]{:S(2)}, u32[]{:S(2)}) collective-permute-start(f32[2,5,4,8,128]{4,3,2,1,0:T(8,128)S(1)} %get-tuple-element.65), channel_id=1, source_target_pairs={{0,7},{1,6},{2,5},{3,4},{4,3},{5,2},{6,1},{7,0},{8,15},{9,14},{10,... | collective-permute-start | bytes 491528 | tf_op jit(solution)/shard_map/ppermute | solution.py:450
  89.4 1.3 %collective-permute-done.17.refs_4_ = f32[2,5,4,8,128]{4,3,2,1,0:T(8,128)S(1)} collective-permute-done((f32[2,5,4,8,128]{4,3,2,1,0:T(8,128)S(1)}, f32[2,5,4,8,128]{4,3,2,1,0:T(8,128)S(1)}, u32[]{:S(2)}, u32[]{:S(2)}) %collective-permute-start.17) | collective-permute-done | bytes 163872 | tf_op jit(solution)/shard_map/ppermute | solution.py:450
  90.7 8.3 %collective-permute-done.19.refs_6_ = f32[2,5,4,8,128]{4,3,2,1,0:T(8,128)S(1)} collective-permute-done((f32[2,5,4,8,128]{4,3,2,1,0:T(8,128)S(1)}, f32[2,5,4,8,128]{4,3,2,1,0:T(8,128)S(1)}, u32[]{:S(2)}, u32[]{:S(2)}) %collective-permute-start.19) | collective-permute-done | bytes 163872 | tf_op jit(solution)/shard_map/ppermute | solution.py:450
  99.0 5.1 %gram.1 = (f32[5,16,4,8,128]{4,3,2,1,0:T(8,128)}, f32[32,8,128]{2,1,0:T(8,128)S(1)}) custom-call(f32[8,2,5,4,8,128]{5,4,3,2,1,0:T(8,128)S(1)} %all-to-all-done.1.refs_0_, f32[2,5,4,8,128]{4,3,2,1,0:T(8,128)S(1)} %get-tuple-element.58.refs_1_, f32[2,5,4,8,128]{4,3,2,1,0:T(8,128)S(1)} %collective-permute-done.15.refs_2_, ...), custom_call_target="tpu_custom_call" | custom-call | tf_op jit(solution)/shard_map/gram/pallas_call | solution.py:535
  104.0 15.5 %all_to_all.15.parts_ref = f32[32,8,128]{2,1,0:T(8,128)S(1)} all-to-all(f32[32,8,128]{2,1,0:T(8,128)S(1)} %get-tuple-element.67), channel_id=1, replica_groups=mesh['gx'=8,'gy'=4] {'gx','gy'}, dimensions={0} | all-to-all | bytes 262144 | tf_op jit(solution)/shard_map/all_to_all | solution.py:547
  119.5 3.6 %factor.1 = f32[32,32]{1,0:T(8,128)} custom-call(f32[32,8,128]{2,1,0:T(8,128)S(1)} %all_to_all.15.parts_ref), custom_call_target="tpu_custom_call" | custom-call | tf_op jit(solution)/shard_map/factor/pallas_call | solution.py:548
  (30 shorter events, 3.8 us)
Async XLA Ops:
  3.1 37.6 %copy-start = (f32[3]{0:T(128)S(1)}, f32[3]{0:T(128)}, u32[]{:S(2)}) copy-start(f32[3]{0:T(128)} %vel_ref.7) | copy-start | bytes 40
  3.1 37.6 %copy-start.1 = (f32[5]{0:T(128)S(1)}, f32[5]{0:T(128)}, u32[]{:S(2)}) copy-start(f32[5]{0:T(128)} %vec_ref.7) | copy-start | bytes 64
  3.1 4.9 %collective-permute-start = (f32[44,8,128]{2,1,0:T(8,128)S(1)}, f32[44,8,128]{2,1,0:T(8,128)S(1)}, u32[]{:S(2)}, u32[]{:S(2)}) collective-permute-start(f32[44,8,128]{2,1,0:T(8,128)S(1)} %get-tuple-element.36), channel_id=1, source_target_pairs={{0,1},{1,0},{2,3},{3,2},{4,5},{5,4},{6,7},{7,6},{8,9},{9,8},{10,11... | collective-permute-start | bytes 540680 | tf_op jit(solution)/shard_map/ppermute | solution.py:450
  3.6 8.0 %collective-permute-start.1 = (f32[44,8,128]{2,1,0:T(8,128)S(1)}, f32[44,8,128]{2,1,0:T(8,128)S(1)}, u32[]{:S(2)}, u32[]{:S(2)}) collective-permute-start(f32[44,8,128]{2,1,0:T(8,128)S(1)} %get-tuple-element.41), channel_id=1, source_target_pairs={{0,2},{1,3},{2,0},{3,1},{4,6},{5,7},{6,4},{7,5},{8,10},{9,11},{10,... | collective-permute-start | bytes 540680 | tf_op jit(solution)/shard_map/ppermute | solution.py:450
  6.2 12.0 %collective-permute-start.2 = (f32[44,8,128]{2,1,0:T(8,128)S(1)}, f32[44,8,128]{2,1,0:T(8,128)S(1)}, u32[]{:S(2)}, u32[]{:S(2)}) collective-permute-start(f32[44,8,128]{2,1,0:T(8,128)S(1)} %get-tuple-element.42), channel_id=1, source_target_pairs={{0,3},{1,2},{2,1},{3,0},{4,7},{5,6},{6,5},{7,4},{8,11},{9,10},{10,... | collective-permute-start | bytes 540680 | tf_op jit(solution)/shard_map/ppermute | solution.py:450
  6.2 11.9 %collective-permute-start.3 = (f32[44,8,128]{2,1,0:T(8,128)S(1)}, f32[44,8,128]{2,1,0:T(8,128)S(1)}, u32[]{:S(2)}, u32[]{:S(2)}) collective-permute-start(f32[44,8,128]{2,1,0:T(8,128)S(1)} %get-tuple-element.43), channel_id=1, source_target_pairs={{0,4},{1,5},{2,6},{3,7},{4,0},{5,1},{6,2},{7,3},{8,12},{9,13},{10,... | collective-permute-start | bytes 540680 | tf_op jit(solution)/shard_map/ppermute | solution.py:450
  8.0 18.3 %collective-permute-start.4 = (f32[44,8,128]{2,1,0:T(8,128)S(1)}, f32[44,8,128]{2,1,0:T(8,128)S(1)}, u32[]{:S(2)}, u32[]{:S(2)}) collective-permute-start(f32[44,8,128]{2,1,0:T(8,128)S(1)} %get-tuple-element.44), channel_id=1, source_target_pairs={{0,5},{1,4},{2,7},{3,6},{4,1},{5,0},{6,3},{7,2},{8,13},{9,12},{10,... | collective-permute-start | bytes 540680 | tf_op jit(solution)/shard_map/ppermute | solution.py:450
  8.0 18.3 %collective-permute-start.5 = (f32[44,8,128]{2,1,0:T(8,128)S(1)}, f32[44,8,128]{2,1,0:T(8,128)S(1)}, u32[]{:S(2)}, u32[]{:S(2)}) collective-permute-start(f32[44,8,128]{2,1,0:T(8,128)S(1)} %get-tuple-element.45), channel_id=1, source_target_pairs={{0,6},{1,7},{2,4},{3,5},{4,2},{5,3},{6,0},{7,1},{8,14},{9,15},{10,... | collective-permute-start | bytes 540680 | tf_op jit(solution)/shard_map/ppermute | solution.py:450
  11.6 14.8 %collective-permute-start.6 = (f32[44,8,128]{2,1,0:T(8,128)S(1)}, f32[44,8,128]{2,1,0:T(8,128)S(1)}, u32[]{:S(2)}, u32[]{:S(2)}) collective-permute-start(f32[44,8,128]{2,1,0:T(8,128)S(1)} %get-tuple-element.46), channel_id=1, source_target_pairs={{0,7},{1,6},{2,5},{3,4},{4,3},{5,2},{6,1},{7,0},{8,15},{9,14},{10,... | collective-permute-start | bytes 540680 | tf_op jit(solution)/shard_map/ppermute | solution.py:450
  13.3 22.3 %all-to-all-start = ((f32[32,2,8,128]{3,2,1,0:T(8,128)}), f32[32,2,8,128]{3,2,1,0:T(8,128)S(1)}, u32[]{:S(2)}, u32[]{:S(2)}) async-start(f32[32,2,8,128]{3,2,1,0:T(8,128)} %get-tuple-element.37), calls=%async_computation | async-start | bytes 524288 | tf_op jit(solution)/shard_map/all_to_all | solution.py:471
  27.3 13.4 %collective-permute-start.9 = (f32[4,24,8,128]{3,2,1,0:T(8,128)S(1)}, f32[4,24,8,128]{3,2,1,0:T(8,128)S(1)}, u32[]{:S(2)}, u32[]{:S(2)}) collective-permute-start(f32[4,24,8,128]{3,2,1,0:T(8,128)S(1)} %get-tuple-element.50.refs_0_), channel_id=1, source_target_pairs={{0,8},{1,9},{2,10},{3,11},{4,12},{5,13},{6,14},{7,15},{8,0},{9,1},... | collective-permute-start | bytes 1179656 | tf_op jit(solution)/shard_map/ppermute | solution.py:445
  29.1 11.6 %collective-permute-start.10 = (f32[4,24,8,128]{3,2,1,0:T(8,128)S(1)}, f32[4,24,8,128]{3,2,1,0:T(8,128)S(1)}, u32[]{:S(2)}, u32[]{:S(2)}) collective-permute-start(f32[4,24,8,128]{3,2,1,0:T(8,128)S(1)} %get-tuple-element.51.refs_1_), channel_id=1, source_target_pairs={{8,16},{9,17},{10,18},{11,19},{12,20},{13,21},{14,22},{15,23},{16,... | collective-permute-start | bytes 1179656 | tf_op jit(solution)/shard_map/ppermute | solution.py:445
  29.8 16.6 %collective-permute-start.7 = (f32[4,20,8,128]{3,2,1,0:T(8,128)S(1)}, f32[4,20,8,128]{3,2,1,0:T(8,128)}, u32[]{:S(2)}, u32[]{:S(2)}) collective-permute-start(f32[4,20,8,128]{3,2,1,0:T(8,128)S(1)} %get-tuple-element.47.refs_0_), channel_id=1, source_target_pairs={{0,8},{1,9},{2,10},{3,11},{4,12},{5,13},{6,14},{7,15},{8,0},{9,1},... | collective-permute-start | bytes 983048 | tf_op jit(solution)/shard_map/ppermute | solution.py:445
  34.2 12.2 %collective-permute-start.8 = (f32[4,20,8,128]{3,2,1,0:T(8,128)}, f32[4,20,8,128]{3,2,1,0:T(8,128)}, u32[]{:S(2)}, u32[]{:S(2)}) collective-permute-start(f32[4,20,8,128]{3,2,1,0:T(8,128)} %get-tuple-element.48.refs_1_), channel_id=1, source_target_pairs={{8,16},{9,17},{10,18},{11,19},{12,20},{13,21},{14,22},{15,23},{16,... | collective-permute-start | bytes 983048 | tf_op jit(solution)/shard_map/ppermute | solution.py:445
  52.5 46.4 %all-to-all-start.1 = ((f32[8,2,5,4,8,128]{5,4,3,2,1,0:T(8,128)}), f32[8,2,5,4,8,128]{5,4,3,2,1,0:T(8,128)S(1)}, u32[]{:S(2)}, u32[]{:S(2)}) async-start(f32[8,2,5,4,8,128]{5,4,3,2,1,0:T(8,128)} %get-tuple-element.55), calls=%async_computation.1 | async-start | bytes 2621440 | tf_op jit(solution)/shard_map/all_to_all | solution.py:512
  56.3 13.2 %collective-permute-start.13 = (f32[5,4,32,128]{3,2,1,0:T(8,128)S(1)}, f32[5,4,32,128]{3,2,1,0:T(8,128)S(1)}, u32[]{:S(2)}, u32[]{:S(2)}) collective-permute-start(f32[5,4,32,128]{3,2,1,0:T(8,128)S(1)} %get-tuple-element.53.refs_5_.refs_0_), channel_id=1, source_target_pairs={{0,8},{1,9},{2,10},{3,11},{4,12},{5,13},{6,14},{7,15},{8,0},{9,1},... | collective-permute-start | bytes 983048 | tf_op jit(solution)/shard_map/ppermute | solution.py:445
  60.9 8.6 %collective-permute-start.14 = (f32[5,4,32,128]{3,2,1,0:T(8,128)S(1)}, f32[5,4,32,128]{3,2,1,0:T(8,128)S(1)}, u32[]{:S(2)}, u32[]{:S(2)}) collective-permute-start(f32[5,4,32,128]{3,2,1,0:T(8,128)S(1)} %get-tuple-element.54.refs_6_.refs_1_), channel_id=1, source_target_pairs={{8,16},{9,17},{10,18},{11,19},{12,20},{13,21},{14,22},{15,23},{16,... | collective-permute-start | bytes 983048 | tf_op jit(solution)/shard_map/ppermute | solution.py:445
  61.6 14.7 %collective-permute-start.11 = (f32[5,4,32,128]{3,2,1,0:T(8,128)S(1)}, f32[5,4,32,128]{3,2,1,0:T(8,128)S(1)}, u32[]{:S(2)}, u32[]{:S(2)}) collective-permute-start(f32[5,4,32,128]{3,2,1,0:T(8,128)S(1)} %get-tuple-element.56.refs_0_), channel_id=1, source_target_pairs={{0,8},{1,9},{2,10},{3,11},{4,12},{5,13},{6,14},{7,15},{8,0},{9,1},... | collective-permute-start | bytes 983048 | tf_op jit(solution)/shard_map/ppermute | solution.py:445
  64.7 11.7 %collective-permute-start.12 = (f32[5,4,32,128]{3,2,1,0:T(8,128)S(1)}, f32[5,4,32,128]{3,2,1,0:T(8,128)S(1)}, u32[]{:S(2)}, u32[]{:S(2)}) collective-permute-start(f32[5,4,32,128]{3,2,1,0:T(8,128)S(1)} %get-tuple-element.57.refs_1_), channel_id=1, source_target_pairs={{8,16},{9,17},{10,18},{11,19},{12,20},{13,21},{14,22},{15,23},{16,... | collective-permute-start | bytes 983048 | tf_op jit(solution)/shard_map/ppermute | solution.py:445
  80.8 3.7 %collective-permute-start.15 = (f32[2,5,4,8,128]{4,3,2,1,0:T(8,128)S(1)}, f32[2,5,4,8,128]{4,3,2,1,0:T(8,128)S(1)}, u32[]{:S(2)}, u32[]{:S(2)}) collective-permute-start(f32[2,5,4,8,128]{4,3,2,1,0:T(8,128)S(1)} %get-tuple-element.59), channel_id=1, source_target_pairs={{0,1},{1,0},{2,3},{3,2},{4,5},{5,4},{6,7},{7,6},{8,9},{9,8},{10,11... | collective-permute-start | bytes 491528 | tf_op jit(solution)/shard_map/ppermute | solution.py:450
  80.9 7.1 %collective-permute-start.16 = (f32[2,5,4,8,128]{4,3,2,1,0:T(8,128)S(1)}, f32[2,5,4,8,128]{4,3,2,1,0:T(8,128)S(1)}, u32[]{:S(2)}, u32[]{:S(2)}) collective-permute-start(f32[2,5,4,8,128]{4,3,2,1,0:T(8,128)S(1)} %get-tuple-element.60), channel_id=1, source_target_pairs={{0,2},{1,3},{2,0},{3,1},{4,6},{5,7},{6,4},{7,5},{8,10},{9,11},{10,... | collective-permute-start | bytes 491528 | tf_op jit(solution)/shard_map/ppermute | solution.py:450
  82.6 8.0 %collective-permute-start.17 = (f32[2,5,4,8,128]{4,3,2,1,0:T(8,128)S(1)}, f32[2,5,4,8,128]{4,3,2,1,0:T(8,128)S(1)}, u32[]{:S(2)}, u32[]{:S(2)}) collective-permute-start(f32[2,5,4,8,128]{4,3,2,1,0:T(8,128)S(1)} %get-tuple-element.61), channel_id=1, source_target_pairs={{0,3},{1,2},{2,1},{3,0},{4,7},{5,6},{6,5},{7,4},{8,11},{9,10},{10,... | collective-permute-start | bytes 491528 | tf_op jit(solution)/shard_map/ppermute | solution.py:450
  82.8 7.9 %collective-permute-start.18 = (f32[2,5,4,8,128]{4,3,2,1,0:T(8,128)S(1)}, f32[2,5,4,8,128]{4,3,2,1,0:T(8,128)S(1)}, u32[]{:S(2)}, u32[]{:S(2)}) collective-permute-start(f32[2,5,4,8,128]{4,3,2,1,0:T(8,128)S(1)} %get-tuple-element.62), channel_id=1, source_target_pairs={{0,4},{1,5},{2,6},{3,7},{4,0},{5,1},{6,2},{7,3},{8,12},{9,13},{10,... | collective-permute-start | bytes 491528 | tf_op jit(solution)/shard_map/ppermute | solution.py:450
  84.4 14.5 %collective-permute-start.19 = (f32[2,5,4,8,128]{4,3,2,1,0:T(8,128)S(1)}, f32[2,5,4,8,128]{4,3,2,1,0:T(8,128)S(1)}, u32[]{:S(2)}, u32[]{:S(2)}) collective-permute-start(f32[2,5,4,8,128]{4,3,2,1,0:T(8,128)S(1)} %get-tuple-element.63), channel_id=1, source_target_pairs={{0,5},{1,4},{2,7},{3,6},{4,1},{5,0},{6,3},{7,2},{8,13},{9,12},{10,... | collective-permute-start | bytes 491528 | tf_op jit(solution)/shard_map/ppermute | solution.py:450
  84.5 14.5 %collective-permute-start.20 = (f32[2,5,4,8,128]{4,3,2,1,0:T(8,128)S(1)}, f32[2,5,4,8,128]{4,3,2,1,0:T(8,128)S(1)}, u32[]{:S(2)}, u32[]{:S(2)}) collective-permute-start(f32[2,5,4,8,128]{4,3,2,1,0:T(8,128)S(1)} %get-tuple-element.64), channel_id=1, source_target_pairs={{0,6},{1,7},{2,4},{3,5},{4,2},{5,3},{6,0},{7,1},{8,14},{9,15},{10,... | collective-permute-start | bytes 491528 | tf_op jit(solution)/shard_map/ppermute | solution.py:450
  88.0 11.0 %collective-permute-start.21 = (f32[2,5,4,8,128]{4,3,2,1,0:T(8,128)S(1)}, f32[2,5,4,8,128]{4,3,2,1,0:T(8,128)S(1)}, u32[]{:S(2)}, u32[]{:S(2)}) collective-permute-start(f32[2,5,4,8,128]{4,3,2,1,0:T(8,128)S(1)} %get-tuple-element.65), channel_id=1, source_target_pairs={{0,7},{1,6},{2,5},{3,4},{4,3},{5,2},{6,1},{7,0},{8,15},{9,14},{10,... | collective-permute-start | bytes 491528 | tf_op jit(solution)/shard_map/ppermute | solution.py:450

commit v3 on v2

--- a/solution.py
+++ b/solution.py
@@ -24,11 +24,12 @@
 SPONGE = 2 * STATE
 PIECE = SPONGE + DEEP
 F32 = jnp.float32
+TURNS = (0, 1, 4, 2, 5, 3, 6, 7)
 
 VMEM = pl.BlockSpec(memory_space=pltpu.VMEM)
 SMEM = pl.BlockSpec(memory_space=pltpu.SMEM)
 HBM = pl.BlockSpec(memory_space=pltpu.HBM)
-PARAMS = pltpu.CompilerParams(vmem_limit_bytes=48 * 1024 * 1024)
+PARAMS = pltpu.CompilerParams(vmem_limit_bytes=24 * 1024 * 1024)
 
 
 def cost(micros):
@@ -68,13 +69,13 @@
         pltpu.make_async_copy(shapes_hbm, shapes_ref, sems.at[4]),
     ]
     large = []
-    for d, piece in enumerate(pieces):
+    for n, piece in enumerate(pieces):
         for f in range(FIELDS):
             large.append(
                 pltpu.make_async_copy(
-                    state_hbm.at[f, pl.ds(2 * DEEP * (member ^ d), 2 * DEEP)],
+                    state_hbm.at[f, pl.ds(2 * DEEP * (member ^ TURNS[n]), 2 * DEEP)],
                     piece.at[pl.ds(2 * DEEP * f, 2 * DEEP)],
-                    sems.at[5 + d * FIELDS + f],
+                    sems.at[5 + n * FIELDS + f],
                 )
             )
     for copy in small + large:
@@ -129,7 +130,7 @@
     pieces, targets = refs[:MEMBERS], refs[MEMBERS:]
     group, member = position()
     even = group % 2 == 0
-    for d, piece in enumerate(pieces):
+    for d, piece in zip(TURNS, pieces):
         other = member ^ d
         is_first = (other >= 4) == even
 
@@ -360,7 +361,7 @@
                 target[f, x] = vb[f, DEEP + x]
     else:
         for d in range(MEMBERS):
-            to = member ^ d
+            to = member ^ TURNS[d]
             row = pl.multiple_of((to % 4) * ROWS, ROWS)
             start = DEEP * (to // 4)
             for f in range(FIELDS):
@@ -375,7 +376,7 @@
     _, member = position()
     tiles = FIELDS * DEEP
     for d in range(MEMBERS):
-        other = member ^ d
+        other = member ^ TURNS[d]
         for j in range(2):
             here = (2 * d + j) * tiles * ROWS
             there = pl.multiple_of((2 * MEMBERS + 2 * other + j) * tiles * ROWS, ROWS)
@@ -411,14 +412,19 @@
     acc = acc / total
     size = factor_ref.shape[0]
     a = jnp.concatenate([acc[:, size * n : size * n + size] for n in range(4)], axis=0)
-    lines = []
-    for k in range(size):
-        inverse = 1.0 / jnp.sqrt(a[k : k + 1, k : k + 1])
-        line = a[k : k + 1, :] * inverse
-        lines.append(line)
-        if k < size - 1:
-            a = a - (a[:, k : k + 1] * inverse) * line
-    factor = jnp.concatenate(lines, axis=0)
+    lines, pivots = [], []
+    for k in range(0, size, 2):
+        row0, row1 = a[k : k + 1, :], a[k + 1 : k + 2, :]
+        pivot0, side, corner = row0[:, k : k + 1], row0[:, k + 1 : k + 2], row1[:, k + 1 : k + 2]
+        ratio = side / pivot0
+        pivot1 = corner - side * ratio
+        row1 = row1 - ratio * row0
+        lines += [row0, row1]
+        pivots += [pivot0, pivot1]
+        if k < size - 2:
+            col0, col1 = a[:, k : k + 1], a[:, k + 1 : k + 2]
+            a = a - col0 * (row0 / pivot0) - (col1 - ratio * col0) * (row1 / pivot1)
+    factor = jnp.concatenate(lines, axis=0) / jnp.sqrt(jnp.concatenate(pivots, axis=0))
     row = lax.broadcasted_iota(jnp.int32, (size, size), 0)
     col = lax.broadcasted_iota(jnp.int32, (size, size), 1)
     factor_ref[...] = jnp.where(col >= row, factor, 0.0)
@@ -445,10 +451,8 @@
         return a, b, lax.ppermute(a, AXES, swap(True)), lax.ppermute(b, AXES, swap(False))
 
     def spread(pieces):
-        got = {0: pieces[0]}
-        for d in (4, 2, 5, 3, 6, 7, 1):
-            got[d] = lax.ppermute(pieces[d], AXES, inside(d))
-        return [got[d] for d in range(MEMBERS)]
+        sent = zip(pieces[1:], TURNS[1:])
+        return [pieces[0]] + [lax.ppermute(piece, AXES, inside(d)) for piece, d in sent]
 
     def call(kernel, name, micros, out_shape, inputs, scratch=(), scalars=0):
         return pl.pallas_call(
@@ -509,6 +513,7 @@
     )
     next_blocks.append(exchange(a1, b1))
     members = [[g * MEMBERS + m for m in range(MEMBERS)] for g in range(groups)]
+    first, _ = lax.optimization_barrier((first, next_blocks[0]))
     first = lax.all_to_all(first, AXES, 0, 0, axis_index_groups=members)
     (second_0,) = call(
         functools.partial(second_kernel, groups, 0),

time: 124 us -> 119 us (0.960)
  waiting for transfers between devices: 27.5 us -> 21.6 us
  local copies, waits for them, and re-layouts: 0.01 us -> 2.35 us
    ppermute x4, waiting for transfers between devices: 7.84 us -> 3.45 us  [exchange(): lax.ppermute(a, AXES, swap(True))]
    unnamed x4 -> x20, local copies, waits for them, and re-layouts: 0.01 us -> 2.35 us
    ppermute x14, waiting for transfers between devices: 19.6 us -> 18.1 us  [spread(): lax.ppermute(piece, AXES, inside(d))]
    ppermute x4, starting transfers between devices: 13.9 us -> 12.5 us  [exchange(): lax.ppermute(a, AXES, swap(True))]
  transfers between devices with their start and end apart: 24 -> 24, of which waited for: 8 -> 11; matrix products, arithmetic and copies ran while one was open for 0% -> 0% of each run, Pallas kernels for 16% -> 22%
where the time goes in v3:
time: 119 us; the launch traced here: 118 us
  starting transfers between devices  42 us (35%)
  Pallas kernels  36.3 us (31%)
  waiting for transfers between devices  21.6 us (18%)
  blocking collectives  15.2 us (13%)
  local copies, waits for them, and re-layouts  2.35 us (2%)
    pallas_call x6, Pallas kernels, call(): pl.pallas_call(kernel, out_shape=out_shape, in_specs=[SMEM] * scalars + [...  25.5 us
    ppermute x14, waiting for transfers between devices, spread(): lax.ppermute(piece, AXES, inside(d))  18.1 us
    ppermute x14, starting transfers between devices, spread(): lax.ppermute(piece, AXES, inside(d))  17.4 us
    all_to_all x1, blocking collectives, local(): grams = lax.all_to_all(grams, AXES, 0, 0)  15.2 us
    ppermute x4, starting transfers between devices, exchange(): lax.ppermute(a, AXES, swap(True))  12.5 us
    pallas_call x1, Pallas kernels, local(): pl.pallas_call(functools.partial(gram_kernel, rows_total), out_shape=[jax...  5.06 us
    all_to_all x1, starting transfers between devices, local(): wall = lax.all_to_all(wall, AXES, 0, 0)  4.87 us
    all_to_all x1, starting transfers between devices, local(): first = lax.all_to_all(first, AXES, 0, 0, axis_index_groups=members)  3.73 us
  transfers between devices with their start and end apart: 24, of which 11 were waited for; matrix products, arithmetic and copies ran while one was open for 0% of the time, Pallas kernels for 22%

profile of v3, /device:TPU:0, one launch (start us, length us, event | category | flops | bytes accessed | tf_op | source)
XLA Modules:
  0.0 118.2 jit_solution(5061511814449457153)
XLA Ops:
  0.6 2.4 %pack.1 = (f32[44,8,128]{2,1,0:T(8,128)S(1)}, f32[44,8,128]{2,1,0:T(8,128)S(1)}, f32[44,8,128]{2,1,0:T(8,128)S(1)}, f32[44,8,128]{2,1,0:T(8,128)S(1)}, f32[44,8,...) custom-call(f32[5,64,8,128]{3,2,1,0:T(8,128)} %bitcast.1, ...), custom_call_target="tpu_custom_call" | custom-call | bytes 6000000 | tf_op jit(solution)/shard_map/pack/pallas_call | solution.py:109
  3.6 2.6 %collective-permute-start.1 = (f32[44,8,128]{2,1,0:T(8,128)S(1)}, f32[44,8,128]{2,1,0:T(8,128)S(1)}, u32[]{:S(2)}, u32[]{:S(2)}) collective-permute-start(f32[44,8,128]{2,1,0:T(8,128)S(1)} %get-tuple-element.42), channel_id=1, source_target_pairs={{0,4},{1,5},{2,6},{3,7},{4,0},{5,1},{6,2},{7,3},{8,12},{9,13},{10,... | collective-permute-start | bytes 540680 | tf_op jit(solution)/shard_map/ppermute | solution.py:455
  6.2 1.5 %collective-permute-start.2 = (f32[44,8,128]{2,1,0:T(8,128)S(1)}, f32[44,8,128]{2,1,0:T(8,128)S(1)}, u32[]{:S(2)}, u32[]{:S(2)}) collective-permute-start(f32[44,8,128]{2,1,0:T(8,128)S(1)} %get-tuple-element.43), channel_id=1, source_target_pairs={{0,2},{1,3},{2,0},{3,1},{4,6},{5,7},{6,4},{7,5},{8,10},{9,11},{10,... | collective-permute-start | bytes 540680 | tf_op jit(solution)/shard_map/ppermute | solution.py:455
  8.0 2.9 %collective-permute-start.5 = (f32[44,8,128]{2,1,0:T(8,128)S(1)}, f32[44,8,128]{2,1,0:T(8,128)S(1)}, u32[]{:S(2)}, u32[]{:S(2)}) collective-permute-start(f32[44,8,128]{2,1,0:T(8,128)S(1)} %get-tuple-element.46), channel_id=1, source_target_pairs={{0,6},{1,7},{2,4},{3,5},{4,2},{5,3},{6,0},{7,1},{8,14},{9,15},{10,... | collective-permute-start | bytes 540680 | tf_op jit(solution)/shard_map/ppermute | solution.py:455
  11.6 1.7 %collective-permute-start.6 = (f32[44,8,128]{2,1,0:T(8,128)S(1)}, f32[44,8,128]{2,1,0:T(8,128)S(1)}, u32[]{:S(2)}, u32[]{:S(2)}) collective-permute-start(f32[44,8,128]{2,1,0:T(8,128)S(1)} %get-tuple-element.47), channel_id=1, source_target_pairs={{0,7},{1,6},{2,5},{3,4},{4,3},{5,2},{6,1},{7,0},{8,15},{9,14},{10,... | collective-permute-start | bytes 540680 | tf_op jit(solution)/shard_map/ppermute | solution.py:455
  13.3 4.9 %all-to-all-start = ((f32[32,2,8,128]{3,2,1,0:T(8,128)}), f32[32,2,8,128]{3,2,1,0:T(8,128)S(1)}, u32[]{:S(2)}, u32[]{:S(2)}) async-start(f32[32,2,8,128]{3,2,1,0:T(8,128)} %get-tuple-element.38), calls=%async_computation | async-start | bytes 524288 | tf_op jit(solution)/shard_map/all_to_all | solution.py:475
  18.2 2.6 %collective-permute-done.5.refs_6_ = f32[44,8,128]{2,1,0:T(8,128)S(1)} collective-permute-done((f32[44,8,128]{2,1,0:T(8,128)S(1)}, f32[44,8,128]{2,1,0:T(8,128)S(1)}, u32[]{:S(2)}, u32[]{:S(2)}) %collective-permute-start.5) | collective-permute-done | bytes 180256 | tf_op jit(solution)/shard_map/ppermute | solution.py:455
  20.8 4.9 %collective-permute-done.6.refs_7_ = f32[44,8,128]{2,1,0:T(8,128)S(1)} collective-permute-done((f32[44,8,128]{2,1,0:T(8,128)S(1)}, f32[44,8,128]{2,1,0:T(8,128)S(1)}, u32[]{:S(2)}, u32[]{:S(2)}) %collective-permute-start.6) | collective-permute-done | bytes 180256 | tf_op jit(solution)/shard_map/ppermute | solution.py:455
  26.7 1.7 %collective-permute-start.9 = (f32[4,24,8,128]{3,2,1,0:T(8,128)S(1)}, f32[4,24,8,128]{3,2,1,0:T(8,128)S(1)}, u32[]{:S(2)}, u32[]{:S(2)}) collective-permute-start(f32[4,24,8,128]{3,2,1,0:T(8,128)S(1)} %get-tuple-element.51.refs_0_), channel_id=1, source_target_pairs={{0,8},{1,9},{2,10},{3,11},{4,12},{5,13},{6,14},{7,15},{8,0},{9,1},... | collective-permute-start | bytes 1179656 | tf_op jit(solution)/shard_map/ppermute | solution.py:451
  29.1 4.4 %collective-permute-start.7 = (f32[4,20,8,128]{3,2,1,0:T(8,128)S(1)}, f32[4,20,8,128]{3,2,1,0:T(8,128)}, u32[]{:S(2)}, u32[]{:S(2)}) collective-permute-start(f32[4,20,8,128]{3,2,1,0:T(8,128)S(1)} %get-tuple-element.48.refs_0_), channel_id=1, source_target_pairs={{0,8},{1,9},{2,10},{3,11},{4,12},{5,13},{6,14},{7,15},{8,0},{9,1},... | collective-permute-start | bytes 983048 | tf_op jit(solution)/shard_map/ppermute | solution.py:451
  33.5 1.4 %collective-permute-start.8 = (f32[4,20,8,128]{3,2,1,0:T(8,128)}, f32[4,20,8,128]{3,2,1,0:T(8,128)}, u32[]{:S(2)}, u32[]{:S(2)}) collective-permute-start(f32[4,20,8,128]{3,2,1,0:T(8,128)} %get-tuple-element.49.refs_1_), channel_id=1, source_target_pairs={{8,16},{9,17},{10,18},{11,19},{12,20},{13,21},{14,22},{15,23},{16,... | collective-permute-start | bytes 983048 | tf_op jit(solution)/shard_map/ppermute | solution.py:451
  34.9 5.1 %forcing.1 = (f32[16,8,128]{2,1,0:T(8,128)S(1)}, f32[16,8,128]{2,1,0:T(8,128)S(1)}) custom-call(f32[32,2,8,128]{3,2,1,0:T(8,128)S(1)} %all-to-all-done.parts), custom_call_target="tpu_custom_call" | custom-call | bytes 15000000 | tf_op jit(solution)/shard_map/forcing/pallas_call | solution.py:458
  40.0 4.4 %first_step_0.1 = (f32[5,4,32,128]{3,2,1,0:T(8,128)S(1)}, f32[5,4,32,128]{3,2,1,0:T(8,128)S(1)}, f32[16,32,128]{2,1,0:T(8,128)S(1)}) custom-call(f32[3]{0:T(128)S(1)} %copy-done.8, f32[5]{0:T(128)S(1)} %copy-done.9, f32[16,8,128]{2,1,0:T(8,128)S(1)} %get-tuple-element.50.wall_ref, f32[4,24,8,128]{3,2,1,0:T(8,128)S(1)} %get-tuple-element.51.refs_0_, ...), custom_call_target="tpu_custom_call" | custom-call | bytes 15000000 | tf_op jit(solution)/shard_map/first_step_0/pallas_call | solution.py:458
  44.5 3.4 %collective-permute-start.11 = (f32[5,4,32,128]{3,2,1,0:T(8,128)S(1)}, f32[5,4,32,128]{3,2,1,0:T(8,128)S(1)}, u32[]{:S(2)}, u32[]{:S(2)}) collective-permute-start(f32[5,4,32,128]{3,2,1,0:T(8,128)S(1)} %get-tuple-element.54.refs_5_.refs_0_), channel_id=1, source_target_pairs={{0,8},{1,9},{2,10},{3,11},{4,12},{5,13},{6,14},{7,15},{8,0},{9,1},... | collective-permute-start | bytes 983048 | tf_op jit(solution)/shard_map/ppermute | solution.py:451
  48.6 6.2 %first_step_1.1 = (f32[5,4,32,128]{3,2,1,0:T(8,128)S(1)}, f32[5,4,32,128]{3,2,1,0:T(8,128)S(1)}, f32[8,2,5,4,8,128]{5,4,3,2,1,0:T(8,128)}) custom-call(f32[3]{0:T(128)S(1)} %copy-done.8, f32[5]{0:T(128)S(1)} %copy-done.9, f32[16,8,128]{2,1,0:T(8,128)S(1)} %get-tuple-element.39.wall_ref, f32[4,20,8,128]{3,2,1,0:T(8,128)S(1)} %get-tuple-element.48.refs_0_, ...), custom_call_target="tpu_custom_call" | custom-call | bytes 15000000 | tf_op jit(solution)/shard_map/first_step_1/pallas_call | solution.py:458
  54.8 1.0 collective-permute-done.11.refs_2_
  57.4 3.7 %all-to-all-start.1 = ((f32[8,2,5,4,8,128]{5,4,3,2,1,0:T(8,128)}), f32[8,2,5,4,8,128]{5,4,3,2,1,0:T(8,128)S(1)}, u32[]{:S(2)}, u32[]{:S(2)}) async-start(f32[8,2,5,4,8,128]{5,4,3,2,1,0:T(8,128)} %get-tuple-element.57), calls=%async_computation.1 | async-start | bytes 2621440 | tf_op jit(solution)/shard_map/all_to_all | solution.py:517
  61.1 3.0 %collective-permute-start.13 = (f32[5,4,32,128]{3,2,1,0:T(8,128)S(1)}, f32[5,4,32,128]{3,2,1,0:T(8,128)S(1)}, u32[]{:S(2)}, u32[]{:S(2)}) collective-permute-start(f32[5,4,32,128]{3,2,1,0:T(8,128)S(1)} %get-tuple-element.58.refs_0_), channel_id=1, source_target_pairs={{0,8},{1,9},{2,10},{3,11},{4,12},{5,13},{6,14},{7,15},{8,0},{9,1},... | collective-permute-start | bytes 983048 | tf_op jit(solution)/shard_map/ppermute | solution.py:451
  65.6 4.3 %second_step_0.1.refs_5_ = f32[5,8,32,128]{3,2,1,0:T(8,128)S(1)} custom-call(f32[3]{0:T(128)S(1)} %copy-done.8, f32[5]{0:T(128)S(1)} %copy-done.9, f32[16,8,128]{2,1,0:T(8,128)S(1)} %copy-done.7, f32[5,4,32,128]{3,2,1,0:T(8,128)S(1)} %get-tuple-element.54.refs_5_.refs_0_, f32[5,4,32,128]{3,2,1,0:T(8,128)S(1)} %get-tuple-element.55.refs_6_.refs_1_, ...), custom_call_target="tpu_custom_call" | custom-call | bytes 15000000 | tf_op jit(solution)/shard_map/second_step_0/pallas_call | solution.py:458
  69.9 2.4 %collective-permute-done.13.refs_2_ = f32[5,4,32,128]{3,2,1,0:T(8,128)S(1)} collective-permute-done((f32[5,4,32,128]{3,2,1,0:T(8,128)S(1)}, f32[5,4,32,128]{3,2,1,0:T(8,128)S(1)}, u32[]{:S(2)}, u32[]{:S(2)}) %collective-permute-start.13) | collective-permute-done | bytes 327712 | tf_op jit(solution)/shard_map/ppermute | solution.py:451
  72.4 4.5 %second_step_1.1 = (f32[2,5,4,8,128]{4,3,2,1,0:T(8,128)S(1)}, f32[2,5,4,8,128]{4,3,2,1,0:T(8,128)S(1)}, f32[2,5,4,8,128]{4,3,2,1,0:T(8,128)S(1)}, f32[2,5,4,8,12...) custom-call(f32[3]{0:T(128)S(1)} %copy-done.8, ...), custom_call_target="tpu_custom_call" | custom-call | bytes 15000000 | tf_op jit(solution)/shard_map/second_step_1/pallas_call | solution.py:458
  76.9 1.7 %collective-permute-start.16 = (f32[2,5,4,8,128]{4,3,2,1,0:T(8,128)S(1)}, f32[2,5,4,8,128]{4,3,2,1,0:T(8,128)S(1)}, u32[]{:S(2)}, u32[]{:S(2)}) collective-permute-start(f32[2,5,4,8,128]{4,3,2,1,0:T(8,128)S(1)} %get-tuple-element.62), channel_id=1, source_target_pairs={{0,4},{1,5},{2,6},{3,7},{4,0},{5,1},{6,2},{7,3},{8,12},{9,13},{10,... | collective-permute-start | bytes 491528 | tf_op jit(solution)/shard_map/ppermute | solution.py:455
  78.7 1.5 %collective-permute-start.17 = (f32[2,5,4,8,128]{4,3,2,1,0:T(8,128)S(1)}, f32[2,5,4,8,128]{4,3,2,1,0:T(8,128)S(1)}, u32[]{:S(2)}, u32[]{:S(2)}) collective-permute-start(f32[2,5,4,8,128]{4,3,2,1,0:T(8,128)S(1)} %get-tuple-element.63), channel_id=1, source_target_pairs={{0,2},{1,3},{2,0},{3,1},{4,6},{5,7},{6,4},{7,5},{8,10},{9,11},{10,... | collective-permute-start | bytes 491528 | tf_op jit(solution)/shard_map/ppermute | solution.py:455
  80.8 2.6 %collective-permute-start.20 = (f32[2,5,4,8,128]{4,3,2,1,0:T(8,128)S(1)}, f32[2,5,4,8,128]{4,3,2,1,0:T(8,128)S(1)}, u32[]{:S(2)}, u32[]{:S(2)}) collective-permute-start(f32[2,5,4,8,128]{4,3,2,1,0:T(8,128)S(1)} %get-tuple-element.66), channel_id=1, source_target_pairs={{0,6},{1,7},{2,4},{3,5},{4,2},{5,3},{6,0},{7,1},{8,14},{9,15},{10,... | collective-permute-start | bytes 491528 | tf_op jit(solution)/shard_map/ppermute | solution.py:455
  83.9 1.5 %collective-permute-start.21 = (f32[2,5,4,8,128]{4,3,2,1,0:T(8,128)S(1)}, f32[2,5,4,8,128]{4,3,2,1,0:T(8,128)S(1)}, u32[]{:S(2)}, u32[]{:S(2)}) collective-permute-start(f32[2,5,4,8,128]{4,3,2,1,0:T(8,128)S(1)} %get-tuple-element.67), channel_id=1, source_target_pairs={{0,7},{1,6},{2,5},{3,4},{4,3},{5,2},{6,1},{7,0},{8,15},{9,14},{10,... | collective-permute-start | bytes 491528 | tf_op jit(solution)/shard_map/ppermute | solution.py:455
  85.7 1.0 collective-permute-done.18.refs_5_
  86.7 1.5 %collective-permute-done.19.refs_6_ = f32[2,5,4,8,128]{4,3,2,1,0:T(8,128)S(1)} collective-permute-done((f32[2,5,4,8,128]{4,3,2,1,0:T(8,128)S(1)}, f32[2,5,4,8,128]{4,3,2,1,0:T(8,128)S(1)}, u32[]{:S(2)}, u32[]{:S(2)}) %collective-permute-start.19) | collective-permute-done | bytes 163872 | tf_op jit(solution)/shard_map/ppermute | solution.py:455
  88.2 4.1 %collective-permute-done.20.refs_7_ = f32[2,5,4,8,128]{4,3,2,1,0:T(8,128)S(1)} collective-permute-done((f32[2,5,4,8,128]{4,3,2,1,0:T(8,128)S(1)}, f32[2,5,4,8,128]{4,3,2,1,0:T(8,128)S(1)}, u32[]{:S(2)}, u32[]{:S(2)}) %collective-permute-start.20) | collective-permute-done | bytes 163872 | tf_op jit(solution)/shard_map/ppermute | solution.py:455
  92.4 2.3 %collective-permute-done.21.refs_8_ = f32[2,5,4,8,128]{4,3,2,1,0:T(8,128)S(1)} collective-permute-done((f32[2,5,4,8,128]{4,3,2,1,0:T(8,128)S(1)}, f32[2,5,4,8,128]{4,3,2,1,0:T(8,128)S(1)}, u32[]{:S(2)}, u32[]{:S(2)}) %collective-permute-start.21) | collective-permute-done | bytes 163872 | tf_op jit(solution)/shard_map/ppermute | solution.py:455
  94.7 5.1 %gram.1 = (f32[5,16,4,8,128]{4,3,2,1,0:T(8,128)}, f32[32,8,128]{2,1,0:T(8,128)S(1)}) custom-call(f32[8,2,5,4,8,128]{5,4,3,2,1,0:T(8,128)S(1)} %all-to-all-done.1.refs_0_, f32[2,5,4,8,128]{4,3,2,1,0:T(8,128)S(1)} %get-tuple-element.60.refs_1_, f32[2,5,4,8,128]{4,3,2,1,0:T(8,128)S(1)} %collective-permute-done.15.refs_2_, ...), custom_call_target="tpu_custom_call" | custom-call | tf_op jit(solution)/shard_map/gram/pallas_call | solution.py:540
  99.7 15.2 %all_to_all.15.parts_ref = f32[32,8,128]{2,1,0:T(8,128)S(1)} all-to-all(f32[32,8,128]{2,1,0:T(8,128)S(1)} %get-tuple-element.69), channel_id=1, replica_groups=mesh['gx'=8,'gy'=4] {'gx','gy'}, dimensions={0} | all-to-all | bytes 262144 | tf_op jit(solution)/shard_map/all_to_all | solution.py:552
  114.9 3.3 %factor.1 = f32[32,32]{1,0:T(8,128)} custom-call(f32[32,8,128]{2,1,0:T(8,128)S(1)} %all_to_all.15.parts_ref), custom_call_target="tpu_custom_call" | custom-call | tf_op jit(solution)/shard_map/factor/pallas_call | solution.py:553
  (46 shorter events, 8.5 us)
Async XLA Ops:
  3.1 37.0 %copy-start.8 = (f32[3]{0:T(128)S(1)}, f32[3]{0:T(128)}, u32[]{:S(2)}) copy-start(f32[3]{0:T(128)} %vel_ref.7) | copy-start | bytes 40
  3.1 37.0 %copy-start.9 = (f32[5]{0:T(128)S(1)}, f32[5]{0:T(128)}, u32[]{:S(2)}) copy-start(f32[5]{0:T(128)} %vec_ref.7) | copy-start | bytes 64
  3.1 4.9 %collective-permute-start = (f32[44,8,128]{2,1,0:T(8,128)S(1)}, f32[44,8,128]{2,1,0:T(8,128)S(1)}, u32[]{:S(2)}, u32[]{:S(2)}) collective-permute-start(f32[44,8,128]{2,1,0:T(8,128)S(1)} %get-tuple-element.37), channel_id=1, source_target_pairs={{0,1},{1,0},{2,3},{3,2},{4,5},{5,4},{6,7},{7,6},{8,9},{9,8},{10,11... | collective-permute-start | bytes 540680 | tf_op jit(solution)/shard_map/ppermute | solution.py:455
  3.6 8.0 %collective-permute-start.1 = (f32[44,8,128]{2,1,0:T(8,128)S(1)}, f32[44,8,128]{2,1,0:T(8,128)S(1)}, u32[]{:S(2)}, u32[]{:S(2)}) collective-permute-start(f32[44,8,128]{2,1,0:T(8,128)S(1)} %get-tuple-element.42), channel_id=1, source_target_pairs={{0,4},{1,5},{2,6},{3,7},{4,0},{5,1},{6,2},{7,3},{8,12},{9,13},{10,... | collective-permute-start | bytes 540680 | tf_op jit(solution)/shard_map/ppermute | solution.py:455
  6.2 12.0 %collective-permute-start.2 = (f32[44,8,128]{2,1,0:T(8,128)S(1)}, f32[44,8,128]{2,1,0:T(8,128)S(1)}, u32[]{:S(2)}, u32[]{:S(2)}) collective-permute-start(f32[44,8,128]{2,1,0:T(8,128)S(1)} %get-tuple-element.43), channel_id=1, source_target_pairs={{0,2},{1,3},{2,0},{3,1},{4,6},{5,7},{6,4},{7,5},{8,10},{9,11},{10,... | collective-permute-start | bytes 540680 | tf_op jit(solution)/shard_map/ppermute | solution.py:455
  7.7 10.5 %collective-permute-start.3 = (f32[44,8,128]{2,1,0:T(8,128)S(1)}, f32[44,8,128]{2,1,0:T(8,128)S(1)}, u32[]{:S(2)}, u32[]{:S(2)}) collective-permute-start(f32[44,8,128]{2,1,0:T(8,128)S(1)} %get-tuple-element.44), channel_id=1, source_target_pairs={{0,5},{1,4},{2,7},{3,6},{4,1},{5,0},{6,3},{7,2},{8,13},{9,12},{10,... | collective-permute-start | bytes 540680 | tf_op jit(solution)/shard_map/ppermute | solution.py:455
  7.7 10.5 %collective-permute-start.4 = (f32[44,8,128]{2,1,0:T(8,128)S(1)}, f32[44,8,128]{2,1,0:T(8,128)S(1)}, u32[]{:S(2)}, u32[]{:S(2)}) collective-permute-start(f32[44,8,128]{2,1,0:T(8,128)S(1)} %get-tuple-element.45), channel_id=1, source_target_pairs={{0,3},{1,2},{2,1},{3,0},{4,7},{5,6},{6,5},{7,4},{8,11},{9,10},{10,... | collective-permute-start | bytes 540680 | tf_op jit(solution)/shard_map/ppermute | solution.py:455
  8.0 12.8 %collective-permute-start.5 = (f32[44,8,128]{2,1,0:T(8,128)S(1)}, f32[44,8,128]{2,1,0:T(8,128)S(1)}, u32[]{:S(2)}, u32[]{:S(2)}) collective-permute-start(f32[44,8,128]{2,1,0:T(8,128)S(1)} %get-tuple-element.46), channel_id=1, source_target_pairs={{0,6},{1,7},{2,4},{3,5},{4,2},{5,3},{6,0},{7,1},{8,14},{9,15},{10,... | collective-permute-start | bytes 540680 | tf_op jit(solution)/shard_map/ppermute | solution.py:455
  11.6 14.1 %collective-permute-start.6 = (f32[44,8,128]{2,1,0:T(8,128)S(1)}, f32[44,8,128]{2,1,0:T(8,128)S(1)}, u32[]{:S(2)}, u32[]{:S(2)}) collective-permute-start(f32[44,8,128]{2,1,0:T(8,128)S(1)} %get-tuple-element.47), channel_id=1, source_target_pairs={{0,7},{1,6},{2,5},{3,4},{4,3},{5,2},{6,1},{7,0},{8,15},{9,14},{10,... | collective-permute-start | bytes 540680 | tf_op jit(solution)/shard_map/ppermute | solution.py:455
  13.3 21.6 %all-to-all-start = ((f32[32,2,8,128]{3,2,1,0:T(8,128)}), f32[32,2,8,128]{3,2,1,0:T(8,128)S(1)}, u32[]{:S(2)}, u32[]{:S(2)}) async-start(f32[32,2,8,128]{3,2,1,0:T(8,128)} %get-tuple-element.38), calls=%async_computation | async-start | bytes 524288 | tf_op jit(solution)/shard_map/all_to_all | solution.py:475
  26.7 13.3 %collective-permute-start.9 = (f32[4,24,8,128]{3,2,1,0:T(8,128)S(1)}, f32[4,24,8,128]{3,2,1,0:T(8,128)S(1)}, u32[]{:S(2)}, u32[]{:S(2)}) collective-permute-start(f32[4,24,8,128]{3,2,1,0:T(8,128)S(1)} %get-tuple-element.51.refs_0_), channel_id=1, source_target_pairs={{0,8},{1,9},{2,10},{3,11},{4,12},{5,13},{6,14},{7,15},{8,0},{9,1},... | collective-permute-start | bytes 1179656 | tf_op jit(solution)/shard_map/ppermute | solution.py:451
  28.4 11.6 %collective-permute-start.10 = (f32[4,24,8,128]{3,2,1,0:T(8,128)S(1)}, f32[4,24,8,128]{3,2,1,0:T(8,128)S(1)}, u32[]{:S(2)}, u32[]{:S(2)}) collective-permute-start(f32[4,24,8,128]{3,2,1,0:T(8,128)S(1)} %get-tuple-element.52.refs_1_), channel_id=1, source_target_pairs={{8,16},{9,17},{10,18},{11,19},{12,20},{13,21},{14,22},{15,23},{16,... | collective-permute-start | bytes 1179656 | tf_op jit(solution)/shard_map/ppermute | solution.py:451
  29.1 19.5 %collective-permute-start.7 = (f32[4,20,8,128]{3,2,1,0:T(8,128)S(1)}, f32[4,20,8,128]{3,2,1,0:T(8,128)}, u32[]{:S(2)}, u32[]{:S(2)}) collective-permute-start(f32[4,20,8,128]{3,2,1,0:T(8,128)S(1)} %get-tuple-element.48.refs_0_), channel_id=1, source_target_pairs={{0,8},{1,9},{2,10},{3,11},{4,12},{5,13},{6,14},{7,15},{8,0},{9,1},... | collective-permute-start | bytes 983048 | tf_op jit(solution)/shard_map/ppermute | solution.py:451
  33.5 15.1 %collective-permute-start.8 = (f32[4,20,8,128]{3,2,1,0:T(8,128)}, f32[4,20,8,128]{3,2,1,0:T(8,128)}, u32[]{:S(2)}, u32[]{:S(2)}) collective-permute-start(f32[4,20,8,128]{3,2,1,0:T(8,128)} %get-tuple-element.49.refs_1_), channel_id=1, source_target_pairs={{8,16},{9,17},{10,18},{11,19},{12,20},{13,21},{14,22},{15,23},{16,... | collective-permute-start | bytes 983048 | tf_op jit(solution)/shard_map/ppermute | solution.py:451
  40.0 14.9 %copy-start.4 = (f32[16,8,128]{2,1,0:T(8,128)}, f32[16,8,128]{2,1,0:T(8,128)S(1)}, u32[]{:S(2)}) copy-start(f32[16,8,128]{2,1,0:T(8,128)S(1)} %get-tuple-element.39.wall_ref) | copy-start | bytes 196612
  40.0 14.9 %copy-start.6 = (f32[16,8,128]{2,1,0:T(8,128)}, f32[16,8,128]{2,1,0:T(8,128)S(1)}, u32[]{:S(2)}) copy-start(f32[16,8,128]{2,1,0:T(8,128)S(1)} %get-tuple-element.50.wall_ref) | copy-start | bytes 196612
  44.5 11.4 %collective-permute-start.11 = (f32[5,4,32,128]{3,2,1,0:T(8,128)S(1)}, f32[5,4,32,128]{3,2,1,0:T(8,128)S(1)}, u32[]{:S(2)}, u32[]{:S(2)}) collective-permute-start(f32[5,4,32,128]{3,2,1,0:T(8,128)S(1)} %get-tuple-element.54.refs_5_.refs_0_), channel_id=1, source_target_pairs={{0,8},{1,9},{2,10},{3,11},{4,12},{5,13},{6,14},{7,15},{8,0},{9,1},... | collective-permute-start | bytes 983048 | tf_op jit(solution)/shard_map/ppermute | solution.py:451
  47.9 8.7 %collective-permute-start.12 = (f32[5,4,32,128]{3,2,1,0:T(8,128)S(1)}, f32[5,4,32,128]{3,2,1,0:T(8,128)S(1)}, u32[]{:S(2)}, u32[]{:S(2)}) collective-permute-start(f32[5,4,32,128]{3,2,1,0:T(8,128)S(1)} %get-tuple-element.55.refs_6_.refs_1_), channel_id=1, source_target_pairs={{8,16},{9,17},{10,18},{11,19},{12,20},{13,21},{14,22},{15,23},{16,... | collective-permute-start | bytes 983048 | tf_op jit(solution)/shard_map/ppermute | solution.py:451
  57.4 7.4 %copy-start.1 = (f32[5,4,32,128]{3,2,1,0:T(8,128)S(1)}, f32[5,4,32,128]{3,2,1,0:T(8,128)}, u32[]{:S(2)}) copy-start(f32[5,4,32,128]{3,2,1,0:T(8,128)} %copy-done) | copy-start | bytes 983044
  57.4 7.4 %copy-start.3 = (f32[5,4,32,128]{3,2,1,0:T(8,128)S(1)}, f32[5,4,32,128]{3,2,1,0:T(8,128)}, u32[]{:S(2)}) copy-start(f32[5,4,32,128]{3,2,1,0:T(8,128)} %copy-done.2) | copy-start | bytes 983044
  57.4 37.3 %all-to-all-start.1 = ((f32[8,2,5,4,8,128]{5,4,3,2,1,0:T(8,128)}), f32[8,2,5,4,8,128]{5,4,3,2,1,0:T(8,128)S(1)}, u32[]{:S(2)}, u32[]{:S(2)}) async-start(f32[8,2,5,4,8,128]{5,4,3,2,1,0:T(8,128)} %get-tuple-element.57), calls=%async_computation.1 | async-start | bytes 2621440 | tf_op jit(solution)/shard_map/all_to_all | solution.py:517
  61.1 11.3 %copy-start.5 = (f32[16,8,128]{2,1,0:T(8,128)S(1)}, f32[16,8,128]{2,1,0:T(8,128)}, u32[]{:S(2)}) copy-start(f32[16,8,128]{2,1,0:T(8,128)} %copy-done.4) | copy-start | bytes 196612
  61.1 11.3 %collective-permute-start.13 = (f32[5,4,32,128]{3,2,1,0:T(8,128)S(1)}, f32[5,4,32,128]{3,2,1,0:T(8,128)S(1)}, u32[]{:S(2)}, u32[]{:S(2)}) collective-permute-start(f32[5,4,32,128]{3,2,1,0:T(8,128)S(1)} %get-tuple-element.58.refs_0_), channel_id=1, source_target_pairs={{0,8},{1,9},{2,10},{3,11},{4,12},{5,13},{6,14},{7,15},{8,0},{9,1},... | collective-permute-start | bytes 983048 | tf_op jit(solution)/shard_map/ppermute | solution.py:451
  64.1 8.3 %collective-permute-start.14 = (f32[5,4,32,128]{3,2,1,0:T(8,128)S(1)}, f32[5,4,32,128]{3,2,1,0:T(8,128)S(1)}, u32[]{:S(2)}, u32[]{:S(2)}) collective-permute-start(f32[5,4,32,128]{3,2,1,0:T(8,128)S(1)} %get-tuple-element.59.refs_1_), channel_id=1, source_target_pairs={{8,16},{9,17},{10,18},{11,19},{12,20},{13,21},{14,22},{15,23},{16,... | collective-permute-start | bytes 983048 | tf_op jit(solution)/shard_map/ppermute | solution.py:451
  64.8 0.8 copy-start.7
  76.9 3.9 %collective-permute-start.15 = (f32[2,5,4,8,128]{4,3,2,1,0:T(8,128)S(1)}, f32[2,5,4,8,128]{4,3,2,1,0:T(8,128)S(1)}, u32[]{:S(2)}, u32[]{:S(2)}) collective-permute-start(f32[2,5,4,8,128]{4,3,2,1,0:T(8,128)S(1)} %get-tuple-element.61), channel_id=1, source_target_pairs={{0,1},{1,0},{2,3},{3,2},{4,5},{5,4},{6,7},{7,6},{8,9},{9,8},{10,11... | collective-permute-start | bytes 491528 | tf_op jit(solution)/shard_map/ppermute | solution.py:455
  76.9 7.0 %collective-permute-start.16 = (f32[2,5,4,8,128]{4,3,2,1,0:T(8,128)S(1)}, f32[2,5,4,8,128]{4,3,2,1,0:T(8,128)S(1)}, u32[]{:S(2)}, u32[]{:S(2)}) collective-permute-start(f32[2,5,4,8,128]{4,3,2,1,0:T(8,128)S(1)} %get-tuple-element.62), channel_id=1, source_target_pairs={{0,4},{1,5},{2,6},{3,7},{4,0},{5,1},{6,2},{7,3},{8,12},{9,13},{10,... | collective-permute-start | bytes 491528 | tf_op jit(solution)/shard_map/ppermute | solution.py:455
  78.7 7.0 %collective-permute-start.17 = (f32[2,5,4,8,128]{4,3,2,1,0:T(8,128)S(1)}, f32[2,5,4,8,128]{4,3,2,1,0:T(8,128)S(1)}, u32[]{:S(2)}, u32[]{:S(2)}) collective-permute-start(f32[2,5,4,8,128]{4,3,2,1,0:T(8,128)S(1)} %get-tuple-element.63), channel_id=1, source_target_pairs={{0,2},{1,3},{2,0},{3,1},{4,6},{5,7},{6,4},{7,5},{8,10},{9,11},{10,... | collective-permute-start | bytes 491528 | tf_op jit(solution)/shard_map/ppermute | solution.py:455
  80.1 6.6 %collective-permute-start.18 = (f32[2,5,4,8,128]{4,3,2,1,0:T(8,128)S(1)}, f32[2,5,4,8,128]{4,3,2,1,0:T(8,128)S(1)}, u32[]{:S(2)}, u32[]{:S(2)}) collective-permute-start(f32[2,5,4,8,128]{4,3,2,1,0:T(8,128)S(1)} %get-tuple-element.64), channel_id=1, source_target_pairs={{0,5},{1,4},{2,7},{3,6},{4,1},{5,0},{6,3},{7,2},{8,13},{9,12},{10,... | collective-permute-start | bytes 491528 | tf_op jit(solution)/shard_map/ppermute | solution.py:455
  80.2 8.0 %collective-permute-start.19 = (f32[2,5,4,8,128]{4,3,2,1,0:T(8,128)S(1)}, f32[2,5,4,8,128]{4,3,2,1,0:T(8,128)S(1)}, u32[]{:S(2)}, u32[]{:S(2)}) collective-permute-start(f32[2,5,4,8,128]{4,3,2,1,0:T(8,128)S(1)} %get-tuple-element.65), channel_id=1, source_target_pairs={{0,3},{1,2},{2,1},{3,0},{4,7},{5,6},{6,5},{7,4},{8,11},{9,10},{10,... | collective-permute-start | bytes 491528 | tf_op jit(solution)/shard_map/ppermute | solution.py:455
  80.8 11.6 %collective-permute-start.20 = (f32[2,5,4,8,128]{4,3,2,1,0:T(8,128)S(1)}, f32[2,5,4,8,128]{4,3,2,1,0:T(8,128)S(1)}, u32[]{:S(2)}, u32[]{:S(2)}) collective-permute-start(f32[2,5,4,8,128]{4,3,2,1,0:T(8,128)S(1)} %get-tuple-element.66), channel_id=1, source_target_pairs={{0,6},{1,7},{2,4},{3,5},{4,2},{5,3},{6,0},{7,1},{8,14},{9,15},{10,... | collective-permute-start | bytes 491528 | tf_op jit(solution)/shard_map/ppermute | solution.py:455
  83.9 10.8 %collective-permute-start.21 = (f32[2,5,4,8,128]{4,3,2,1,0:T(8,128)S(1)}, f32[2,5,4,8,128]{4,3,2,1,0:T(8,128)S(1)}, u32[]{:S(2)}, u32[]{:S(2)}) collective-permute-start(f32[2,5,4,8,128]{4,3,2,1,0:T(8,128)S(1)} %get-tuple-element.67), channel_id=1, source_target_pairs={{0,7},{1,6},{2,5},{3,4},{4,3},{5,2},{6,1},{7,0},{8,15},{9,14},{10,... | collective-permute-start | bytes 491528 | tf_op jit(solution)/shard_map/ppermute | solution.py:455
  (2 other events, 1.5 us)

commit v4 on v3

--- a/solution.py
+++ b/solution.py
@@ -23,6 +23,7 @@
 STATE = FIELDS * DEEP
 SPONGE = 2 * STATE
 PIECE = SPONGE + DEEP
+CHUNK = 4
 F32 = jnp.float32
 TURNS = (0, 1, 4, 2, 5, 3, 6, 7)
 
@@ -370,37 +371,59 @@
                     pieces[d][1, f, x] = vb[f, DEEP + start + x, pl.ds(row, ROWS), :]
 
 
-def gram_kernel(total, *refs):
-    first, second = refs[0], refs[1 : 1 + MEMBERS]
-    state_ref, gram_ref, columns = refs[1 + MEMBERS :]
+def three_parts(a):
+    high = a.astype(jnp.bfloat16)
+    rest = a - high.astype(F32)
+    middle = rest.astype(jnp.bfloat16)
+    low = (rest - middle.astype(F32)).astype(jnp.bfloat16)
+    return jnp.concatenate([high, middle, low], axis=0)
+
+
+def chunk_of(ref, r):
+    stride = FIELDS * DEEP * ROWS
+    rows = [ref[pl.ds(CHUNK * r + n, 2 * MEMBERS, stride=stride), :] for n in range(CHUNK)]
+    return jnp.concatenate(rows, axis=1)
+
+
+def split_kernel(first, parts_ref):
+    def body(r, carry):
+        parts_ref[r] = three_parts(chunk_of(first, r))
+        return carry
+
+    lax.fori_loop(0, parts_ref.shape[0], body, 0, unroll=4)
+
+
+def gram_kernel(first_parts, *refs):
+    second, (state_ref, gram_ref, columns) = refs[:MEMBERS], refs[MEMBERS:]
     _, member = position()
     tiles = FIELDS * DEEP
     for d in range(MEMBERS):
         other = member ^ TURNS[d]
         for j in range(2):
-            here = (2 * d + j) * tiles * ROWS
-            there = pl.multiple_of((2 * MEMBERS + 2 * other + j) * tiles * ROWS, ROWS)
+            start = (2 * other + j) * tiles * ROWS
             for f in range(FIELDS):
                 for x in range(DEEP):
-                    n = (f * DEEP + x) * ROWS
-                    columns[here + n : here + n + ROWS, :] = first[d, j, f, x]
                     value = second[d][j, f, x]
-                    columns[pl.ds(pl.multiple_of(there + n, ROWS), ROWS), :] = value
+                    at = pl.multiple_of(start + (f * DEEP + x) * ROWS, ROWS)
+                    columns[pl.ds(at, ROWS), :] = value
                     state_ref[f, 2 * other + j, x] = value
-    size = STEPS * 2 * MEMBERS
-    stride = tiles * ROWS
+    modes = 2 * MEMBERS
 
     def body(r, acc):
-        a = jnp.concatenate(
-            [columns[pl.ds(4 * r + n, size, stride=stride), :] for n in range(4)], axis=1
+        parts = jnp.concatenate([first_parts[r], three_parts(chunk_of(columns, r))], axis=0)
+        return acc + lax.dot_general(
+            parts, parts, (((1,), (1,)), ((), ())), preferred_element_type=F32
         )
-        return acc + lax.dot_general(
-            a, a, (((1,), (1,)), ((), ())),
-            precision=lax.Precision.HIGHEST, preferred_element_type=F32,
-        )
-
-    gram = lax.fori_loop(0, stride // 4, body, jnp.zeros((size, size), F32), unroll=4)
-    tile = jnp.concatenate([gram[ROWS * n : ROWS * n + ROWS] for n in range(4)], axis=1)
+
+    acc = jnp.zeros((6 * modes, 6 * modes), F32)
+    acc = lax.fori_loop(0, first_parts.shape[0], body, acc, unroll=4)
+
+    def block(n, m):
+        part = [modes * (3 * n + i) for i in range(3)], [modes * (3 * m + i) for i in range(3)]
+        return sum(acc[r : r + modes, c : c + modes] for r in part[0] for c in part[1])
+
+    rows = [jnp.concatenate([block(n, m) for m in range(STEPS)], axis=1) for n in range(STEPS)]
+    tile = jnp.concatenate([line[ROWS * n : ROWS * n + ROWS] for line in rows for n in range(2)], axis=1)
     for n in range(gram_ref.shape[0]):
         gram_ref[n] = tile
 
@@ -535,20 +558,28 @@
     )
     second = spread(second)
 
+    row_count = FIELDS * DEEP * ROWS
+    (parts,) = call(
+        split_kernel,
+        "split",
+        2,
+        [jax.ShapeDtypeStruct((row_count // CHUNK, 6 * MEMBERS, CHUNK * LANES), jnp.bfloat16)],
+        [first.reshape(2 * MEMBERS * row_count, LANES)],
+    )
     rows_total = float(FIELDS * cells_x * gx_size * cells_y * gy_size * cells_z)
     snap_count = STEPS * 2 * MEMBERS
     state_out, grams = pl.pallas_call(
-        functools.partial(gram_kernel, rows_total),
+        gram_kernel,
         out_shape=[
             jax.ShapeDtypeStruct(state_in.shape, F32),
             jax.ShapeDtypeStruct((devices, ROWS, LANES), F32),
         ],
         in_specs=[VMEM] * (1 + MEMBERS),
         out_specs=[VMEM, VMEM],
-        scratch_shapes=[pltpu.VMEM((snap_count * FIELDS * DEEP * ROWS, LANES), F32)],
+        scratch_shapes=[pltpu.VMEM((2 * MEMBERS * row_count, LANES), F32)],
         compiler_params=PARAMS,
         name="gram",
-    )(first, *second)
+    )(parts, *second)
     grams = lax.all_to_all(grams, AXES, 0, 0)
     factor = pl.pallas_call(
         functools.partial(factor_kernel, rows_total),

time: 119 us -> 118 us (level)
    pallas_call x6 -> x7, Pallas kernels: 25.5 us -> 27 us  [call(): pl.pallas_call(kernel, out_shape=out_shape, in_specs=[SMEM] * scalars + [...]
    pallas_call x1, Pallas kernels: 5.06 us -> 3.79 us  [local(): pl.pallas_call(gram_kernel, out_shape=[jax.ShapeDtypeStruct(state_in.shap...]
  transfers between devices with their start and end apart: 24 -> 24, of which waited for: 11 -> 10; matrix products, arithmetic and copies ran while one was open for 0% -> 0% of each run, Pallas kernels for 22% -> 23%
where the time goes in v4:
time: 118 us
  starting transfers between devices  41.9 us (36%)
  Pallas kernels  36.6 us (31%)
  waiting for transfers between devices  20.8 us (18%)
  blocking collectives  15.3 us (13%)
  local copies, waits for them, and re-layouts  2.35 us (2%)
    pallas_call x7, Pallas kernels, call(): pl.pallas_call(kernel, out_shape=out_shape, in_specs=[SMEM] * scalars + [...  27 us
    ppermute x14, starting transfers between devices, spread(): lax.ppermute(piece, AXES, inside(d))  17.4 us
    ppermute x14, waiting for transfers between devices, spread(): lax.ppermute(piece, AXES, inside(d))  17.3 us
    all_to_all x1, blocking collectives, local(): grams = lax.all_to_all(grams, AXES, 0, 0)  15.3 us
    ppermute x4, starting transfers between devices, exchange(): lax.ppermute(a, AXES, swap(True))  12.5 us
    all_to_all x1, starting transfers between devices, local(): wall = lax.all_to_all(wall, AXES, 0, 0)  4.87 us
    pallas_call x1, Pallas kernels, local(): pl.pallas_call(gram_kernel, out_shape=[jax.ShapeDtypeStruct(state_in.shap...  3.79 us
    all_to_all x1, starting transfers between devices, local(): first = lax.all_to_all(first, AXES, 0, 0, axis_index_groups=members)  3.73 us
  transfers between devices with their start and end apart: 24, of which 10 were waited for; matrix products, arithmetic and copies ran while one was open for 0% of the time, Pallas kernels for 23%

profile of v4, /device:TPU:0, one launch (start us, length us, event | category | flops | bytes accessed | tf_op | source)
XLA Modules:
  0.0 117.7 jit_solution(8258666738964359909)
XLA Ops:
  0.6 2.4 %pack.1 = (f32[44,8,128]{2,1,0:T(8,128)S(1)}, f32[44,8,128]{2,1,0:T(8,128)S(1)}, f32[44,8,128]{2,1,0:T(8,128)S(1)}, f32[44,8,128]{2,1,0:T(8,128)S(1)}, f32[44,8,...) custom-call(f32[5,64,8,128]{3,2,1,0:T(8,128)} %bitcast.3, ...), custom_call_target="tpu_custom_call" | custom-call | bytes 6000000 | tf_op jit(solution)/shard_map/pack/pallas_call | solution.py:110
  3.6 2.6 %collective-permute-start.1 = (f32[44,8,128]{2,1,0:T(8,128)S(1)}, f32[44,8,128]{2,1,0:T(8,128)S(1)}, u32[]{:S(2)}, u32[]{:S(2)}) collective-permute-start(f32[44,8,128]{2,1,0:T(8,128)S(1)} %get-tuple-element.42), channel_id=1, source_target_pairs={{0,4},{1,5},{2,6},{3,7},{4,0},{5,1},{6,2},{7,3},{8,12},{9,13},{10,... | collective-permute-start | bytes 540680 | tf_op jit(solution)/shard_map/ppermute | solution.py:478
  6.2 1.5 %collective-permute-start.2 = (f32[44,8,128]{2,1,0:T(8,128)S(1)}, f32[44,8,128]{2,1,0:T(8,128)S(1)}, u32[]{:S(2)}, u32[]{:S(2)}) collective-permute-start(f32[44,8,128]{2,1,0:T(8,128)S(1)} %get-tuple-element.43), channel_id=1, source_target_pairs={{0,2},{1,3},{2,0},{3,1},{4,6},{5,7},{6,4},{7,5},{8,10},{9,11},{10,... | collective-permute-start | bytes 540680 | tf_op jit(solution)/shard_map/ppermute | solution.py:478
  8.0 2.9 %collective-permute-start.5 = (f32[44,8,128]{2,1,0:T(8,128)S(1)}, f32[44,8,128]{2,1,0:T(8,128)S(1)}, u32[]{:S(2)}, u32[]{:S(2)}) collective-permute-start(f32[44,8,128]{2,1,0:T(8,128)S(1)} %get-tuple-element.46), channel_id=1, source_target_pairs={{0,6},{1,7},{2,4},{3,5},{4,2},{5,3},{6,0},{7,1},{8,14},{9,15},{10,... | collective-permute-start | bytes 540680 | tf_op jit(solution)/shard_map/ppermute | solution.py:478
  11.6 1.7 %collective-permute-start.6 = (f32[44,8,128]{2,1,0:T(8,128)S(1)}, f32[44,8,128]{2,1,0:T(8,128)S(1)}, u32[]{:S(2)}, u32[]{:S(2)}) collective-permute-start(f32[44,8,128]{2,1,0:T(8,128)S(1)} %get-tuple-element.47), channel_id=1, source_target_pairs={{0,7},{1,6},{2,5},{3,4},{4,3},{5,2},{6,1},{7,0},{8,15},{9,14},{10,... | collective-permute-start | bytes 540680 | tf_op jit(solution)/shard_map/ppermute | solution.py:478
  13.3 4.9 %all-to-all-start = ((f32[32,2,8,128]{3,2,1,0:T(8,128)}), f32[32,2,8,128]{3,2,1,0:T(8,128)S(1)}, u32[]{:S(2)}, u32[]{:S(2)}) async-start(f32[32,2,8,128]{3,2,1,0:T(8,128)} %get-tuple-element.38), calls=%async_computation | async-start | bytes 524288 | tf_op jit(solution)/shard_map/all_to_all | solution.py:498
  18.2 2.6 %collective-permute-done.5.refs_6_ = f32[44,8,128]{2,1,0:T(8,128)S(1)} collective-permute-done((f32[44,8,128]{2,1,0:T(8,128)S(1)}, f32[44,8,128]{2,1,0:T(8,128)S(1)}, u32[]{:S(2)}, u32[]{:S(2)}) %collective-permute-start.5) | collective-permute-done | bytes 180256 | tf_op jit(solution)/shard_map/ppermute | solution.py:478
  20.8 4.9 %collective-permute-done.6.refs_7_ = f32[44,8,128]{2,1,0:T(8,128)S(1)} collective-permute-done((f32[44,8,128]{2,1,0:T(8,128)S(1)}, f32[44,8,128]{2,1,0:T(8,128)S(1)}, u32[]{:S(2)}, u32[]{:S(2)}) %collective-permute-start.6) | collective-permute-done | bytes 180256 | tf_op jit(solution)/shard_map/ppermute | solution.py:478
  25.7 0.9 assemble.1
  26.7 1.7 %collective-permute-start.9 = (f32[4,24,8,128]{3,2,1,0:T(8,128)S(1)}, f32[4,24,8,128]{3,2,1,0:T(8,128)S(1)}, u32[]{:S(2)}, u32[]{:S(2)}) collective-permute-start(f32[4,24,8,128]{3,2,1,0:T(8,128)S(1)} %get-tuple-element.51.refs_0_), channel_id=1, source_target_pairs={{0,8},{1,9},{2,10},{3,11},{4,12},{5,13},{6,14},{7,15},{8,0},{9,1},... | collective-permute-start | bytes 1179656 | tf_op jit(solution)/shard_map/ppermute | solution.py:474
  29.1 4.4 %collective-permute-start.7 = (f32[4,20,8,128]{3,2,1,0:T(8,128)S(1)}, f32[4,20,8,128]{3,2,1,0:T(8,128)}, u32[]{:S(2)}, u32[]{:S(2)}) collective-permute-start(f32[4,20,8,128]{3,2,1,0:T(8,128)S(1)} %get-tuple-element.48.refs_0_), channel_id=1, source_target_pairs={{0,8},{1,9},{2,10},{3,11},{4,12},{5,13},{6,14},{7,15},{8,0},{9,1},... | collective-permute-start | bytes 983048 | tf_op jit(solution)/shard_map/ppermute | solution.py:474
  33.5 1.4 %collective-permute-start.8 = (f32[4,20,8,128]{3,2,1,0:T(8,128)}, f32[4,20,8,128]{3,2,1,0:T(8,128)}, u32[]{:S(2)}, u32[]{:S(2)}) collective-permute-start(f32[4,20,8,128]{3,2,1,0:T(8,128)} %get-tuple-element.49.refs_1_), channel_id=1, source_target_pairs={{8,16},{9,17},{10,18},{11,19},{12,20},{13,21},{14,22},{15,23},{16,... | collective-permute-start | bytes 983048 | tf_op jit(solution)/shard_map/ppermute | solution.py:474
  34.9 5.1 %forcing.1 = (f32[16,8,128]{2,1,0:T(8,128)S(1)}, f32[16,8,128]{2,1,0:T(8,128)S(1)}) custom-call(f32[32,2,8,128]{3,2,1,0:T(8,128)S(1)} %all-to-all-done.parts), custom_call_target="tpu_custom_call" | custom-call | bytes 15000000 | tf_op jit(solution)/shard_map/forcing/pallas_call | solution.py:481
  40.0 4.4 %first_step_0.1 = (f32[5,4,32,128]{3,2,1,0:T(8,128)S(1)}, f32[5,4,32,128]{3,2,1,0:T(8,128)S(1)}, f32[16,32,128]{2,1,0:T(8,128)S(1)}) custom-call(f32[3]{0:T(128)S(1)} %copy-done.8, f32[5]{0:T(128)S(1)} %copy-done.9, f32[16,8,128]{2,1,0:T(8,128)S(1)} %get-tuple-element.50.wall_ref, f32[4,24,8,128]{3,2,1,0:T(8,128)S(1)} %get-tuple-element.51.refs_0_, ...), custom_call_target="tpu_custom_call" | custom-call | bytes 15000000 | tf_op jit(solution)/shard_map/first_step_0/pallas_call | solution.py:481
  44.5 3.4 %collective-permute-start.11 = (f32[5,4,32,128]{3,2,1,0:T(8,128)S(1)}, f32[5,4,32,128]{3,2,1,0:T(8,128)S(1)}, u32[]{:S(2)}, u32[]{:S(2)}) collective-permute-start(f32[5,4,32,128]{3,2,1,0:T(8,128)S(1)} %get-tuple-element.54.refs_5_.refs_0_), channel_id=1, source_target_pairs={{0,8},{1,9},{2,10},{3,11},{4,12},{5,13},{6,14},{7,15},{8,0},{9,1},... | collective-permute-start | bytes 983048 | tf_op jit(solution)/shard_map/ppermute | solution.py:474
  48.6 6.2 %first_step_1.1 = (f32[5,4,32,128]{3,2,1,0:T(8,128)S(1)}, f32[5,4,32,128]{3,2,1,0:T(8,128)S(1)}, f32[8,2,5,4,8,128]{5,4,3,2,1,0:T(8,128)}) custom-call(f32[3]{0:T(128)S(1)} %copy-done.8, f32[5]{0:T(128)S(1)} %copy-done.9, f32[16,8,128]{2,1,0:T(8,128)S(1)} %get-tuple-element.39.wall_ref, f32[4,20,8,128]{3,2,1,0:T(8,128)S(1)} %get-tuple-element.48.refs_0_, ...), custom_call_target="tpu_custom_call" | custom-call | bytes 15000000 | tf_op jit(solution)/shard_map/first_step_1/pallas_call | solution.py:481
  54.8 1.0 collective-permute-done.11.refs_2_
  57.4 3.7 %all-to-all-start.1 = ((f32[8,2,5,4,8,128]{5,4,3,2,1,0:T(8,128)}), f32[8,2,5,4,8,128]{5,4,3,2,1,0:T(8,128)S(1)}, u32[]{:S(2)}, u32[]{:S(2)}) async-start(f32[8,2,5,4,8,128]{5,4,3,2,1,0:T(8,128)} %get-tuple-element.57), calls=%async_computation.1 | async-start | bytes 2621440 | tf_op jit(solution)/shard_map/all_to_all | solution.py:540
  61.1 3.0 %collective-permute-start.13 = (f32[5,4,32,128]{3,2,1,0:T(8,128)S(1)}, f32[5,4,32,128]{3,2,1,0:T(8,128)S(1)}, u32[]{:S(2)}, u32[]{:S(2)}) collective-permute-start(f32[5,4,32,128]{3,2,1,0:T(8,128)S(1)} %get-tuple-element.58.refs_0_), channel_id=1, source_target_pairs={{0,8},{1,9},{2,10},{3,11},{4,12},{5,13},{6,14},{7,15},{8,0},{9,1},... | collective-permute-start | bytes 983048 | tf_op jit(solution)/shard_map/ppermute | solution.py:474
  65.6 4.3 %second_step_0.1.refs_5_ = f32[5,8,32,128]{3,2,1,0:T(8,128)S(1)} custom-call(f32[3]{0:T(128)S(1)} %copy-done.8, f32[5]{0:T(128)S(1)} %copy-done.9, f32[16,8,128]{2,1,0:T(8,128)S(1)} %copy-done.7, f32[5,4,32,128]{3,2,1,0:T(8,128)S(1)} %get-tuple-element.54.refs_5_.refs_0_, f32[5,4,32,128]{3,2,1,0:T(8,128)S(1)} %get-tuple-element.55.refs_6_.refs_1_, ...), custom_call_target="tpu_custom_call" | custom-call | bytes 15000000 | tf_op jit(solution)/shard_map/second_step_0/pallas_call | solution.py:481
  69.9 2.4 %collective-permute-done.13.refs_2_ = f32[5,4,32,128]{3,2,1,0:T(8,128)S(1)} collective-permute-done((f32[5,4,32,128]{3,2,1,0:T(8,128)S(1)}, f32[5,4,32,128]{3,2,1,0:T(8,128)S(1)}, u32[]{:S(2)}, u32[]{:S(2)}) %collective-permute-start.13) | collective-permute-done | bytes 327712 | tf_op jit(solution)/shard_map/ppermute | solution.py:474
  72.4 5.1 %second_step_1.1 = (f32[2,5,4,8,128]{4,3,2,1,0:T(8,128)S(1)}, f32[2,5,4,8,128]{4,3,2,1,0:T(8,128)S(1)}, f32[2,5,4,8,128]{4,3,2,1,0:T(8,128)S(1)}, f32[2,5,4,8,12...) custom-call(f32[3]{0:T(128)S(1)} %copy-done.8, ...), custom_call_target="tpu_custom_call" | custom-call | bytes 15000000 | tf_op jit(solution)/shard_map/second_step_1/pallas_call | solution.py:481
  77.5 1.7 %collective-permute-start.16 = (f32[2,5,4,8,128]{4,3,2,1,0:T(8,128)S(1)}, f32[2,5,4,8,128]{4,3,2,1,0:T(8,128)S(1)}, u32[]{:S(2)}, u32[]{:S(2)}) collective-permute-start(f32[2,5,4,8,128]{4,3,2,1,0:T(8,128)S(1)} %get-tuple-element.62), channel_id=1, source_target_pairs={{0,4},{1,5},{2,6},{3,7},{4,0},{5,1},{6,2},{7,3},{8,12},{9,13},{10,... | collective-permute-start | bytes 491528 | tf_op jit(solution)/shard_map/ppermute | solution.py:478
  79.2 1.5 %collective-permute-start.17 = (f32[2,5,4,8,128]{4,3,2,1,0:T(8,128)}, f32[2,5,4,8,128]{4,3,2,1,0:T(8,128)S(1)}, u32[]{:S(2)}, u32[]{:S(2)}) collective-permute-start(f32[2,5,4,8,128]{4,3,2,1,0:T(8,128)} %get-tuple-element.63), channel_id=1, source_target_pairs={{0,2},{1,3},{2,0},{3,1},{4,6},{5,7},{6,4},{7,5},{8,10},{9,11},{10,... | collective-permute-start | bytes 491528 | tf_op jit(solution)/shard_map/ppermute | solution.py:478
  81.3 2.6 %collective-permute-start.20 = (f32[2,5,4,8,128]{4,3,2,1,0:T(8,128)S(1)}, f32[2,5,4,8,128]{4,3,2,1,0:T(8,128)S(1)}, u32[]{:S(2)}, u32[]{:S(2)}) collective-permute-start(f32[2,5,4,8,128]{4,3,2,1,0:T(8,128)S(1)} %get-tuple-element.66), channel_id=1, source_target_pairs={{0,6},{1,7},{2,4},{3,5},{4,2},{5,3},{6,0},{7,1},{8,14},{9,15},{10,... | collective-permute-start | bytes 491528 | tf_op jit(solution)/shard_map/ppermute | solution.py:478
  84.5 1.5 %collective-permute-start.21 = (f32[2,5,4,8,128]{4,3,2,1,0:T(8,128)S(1)}, f32[2,5,4,8,128]{4,3,2,1,0:T(8,128)S(1)}, u32[]{:S(2)}, u32[]{:S(2)}) collective-permute-start(f32[2,5,4,8,128]{4,3,2,1,0:T(8,128)S(1)} %get-tuple-element.67), channel_id=1, source_target_pairs={{0,7},{1,6},{2,5},{3,4},{4,3},{5,2},{6,1},{7,0},{8,15},{9,14},{10,... | collective-permute-start | bytes 491528 | tf_op jit(solution)/shard_map/ppermute | solution.py:478
  87.3 1.7 %collective-permute-done.19.refs_5_ = f32[2,5,4,8,128]{4,3,2,1,0:T(8,128)S(1)} collective-permute-done((f32[2,5,4,8,128]{4,3,2,1,0:T(8,128)S(1)}, f32[2,5,4,8,128]{4,3,2,1,0:T(8,128)S(1)}, u32[]{:S(2)}, u32[]{:S(2)}) %collective-permute-start.19) | collective-permute-done | bytes 163872 | tf_op jit(solution)/shard_map/ppermute | solution.py:478
  88.9 4.3 %collective-permute-done.20.refs_6_ = f32[2,5,4,8,128]{4,3,2,1,0:T(8,128)S(1)} collective-permute-done((f32[2,5,4,8,128]{4,3,2,1,0:T(8,128)S(1)}, f32[2,5,4,8,128]{4,3,2,1,0:T(8,128)S(1)}, u32[]{:S(2)}, u32[]{:S(2)}) %collective-permute-start.20) | collective-permute-done | bytes 163872 | tf_op jit(solution)/shard_map/ppermute | solution.py:478
  93.2 2.1 %collective-permute-done.21.refs_7_ = f32[2,5,4,8,128]{4,3,2,1,0:T(8,128)S(1)} collective-permute-done((f32[2,5,4,8,128]{4,3,2,1,0:T(8,128)S(1)}, f32[2,5,4,8,128]{4,3,2,1,0:T(8,128)S(1)}, u32[]{:S(2)}, u32[]{:S(2)}) %collective-permute-start.21) | collective-permute-done | bytes 163872 | tf_op jit(solution)/shard_map/ppermute | solution.py:478
  95.3 3.8 %gram.1 = (f32[5,16,4,8,128]{4,3,2,1,0:T(8,128)}, f32[32,8,128]{2,1,0:T(8,128)S(1)}) custom-call(bf16[40,48,512]{2,1,0:T(8,128)(2,1)S(1)} %split.1.first_parts, f32[2,5,4,8,128]{4,3,2,1,0:T(8,128)S(1)} %get-tuple-element.60.refs_0_, f32[2,5,4,8,128]{4,3,2,1,0:T(8,128)S(1)} %collective-permute-done.15.refs_1_, ...), custom_call_target="tpu_custom_call" | custom-call | tf_op jit(solution)/shard_map/gram/pallas_call | solution.py:571
  99.1 15.3 %all_to_all.15.parts_ref = f32[32,8,128]{2,1,0:T(8,128)S(1)} all-to-all(f32[32,8,128]{2,1,0:T(8,128)S(1)} %get-tuple-element.69), channel_id=1, replica_groups=mesh['gx'=8,'gy'=4] {'gx','gy'}, dimensions={0} | all-to-all | bytes 262144 | tf_op jit(solution)/shard_map/all_to_all | solution.py:583
  114.4 3.3 %factor.1 = f32[32,32]{1,0:T(8,128)} custom-call(f32[32,8,128]{2,1,0:T(8,128)S(1)} %all_to_all.15.parts_ref), custom_call_target="tpu_custom_call" | custom-call | tf_op jit(solution)/shard_map/factor/pallas_call | solution.py:584
  (47 shorter events, 8.4 us)
Async XLA Ops:
  3.1 37.0 %copy-start.8 = (f32[3]{0:T(128)S(1)}, f32[3]{0:T(128)}, u32[]{:S(2)}) copy-start(f32[3]{0:T(128)} %vel_ref.7) | copy-start | bytes 40
  3.1 37.0 %copy-start.9 = (f32[5]{0:T(128)S(1)}, f32[5]{0:T(128)}, u32[]{:S(2)}) copy-start(f32[5]{0:T(128)} %vec_ref.7) | copy-start | bytes 64
  3.1 4.9 %collective-permute-start = (f32[44,8,128]{2,1,0:T(8,128)S(1)}, f32[44,8,128]{2,1,0:T(8,128)S(1)}, u32[]{:S(2)}, u32[]{:S(2)}) collective-permute-start(f32[44,8,128]{2,1,0:T(8,128)S(1)} %get-tuple-element.37), channel_id=1, source_target_pairs={{0,1},{1,0},{2,3},{3,2},{4,5},{5,4},{6,7},{7,6},{8,9},{9,8},{10,11... | collective-permute-start | bytes 540680 | tf_op jit(solution)/shard_map/ppermute | solution.py:478
  3.6 8.0 %collective-permute-start.1 = (f32[44,8,128]{2,1,0:T(8,128)S(1)}, f32[44,8,128]{2,1,0:T(8,128)S(1)}, u32[]{:S(2)}, u32[]{:S(2)}) collective-permute-start(f32[44,8,128]{2,1,0:T(8,128)S(1)} %get-tuple-element.42), channel_id=1, source_target_pairs={{0,4},{1,5},{2,6},{3,7},{4,0},{5,1},{6,2},{7,3},{8,12},{9,13},{10,... | collective-permute-start | bytes 540680 | tf_op jit(solution)/shard_map/ppermute | solution.py:478
  6.2 12.0 %collective-permute-start.2 = (f32[44,8,128]{2,1,0:T(8,128)S(1)}, f32[44,8,128]{2,1,0:T(8,128)S(1)}, u32[]{:S(2)}, u32[]{:S(2)}) collective-permute-start(f32[44,8,128]{2,1,0:T(8,128)S(1)} %get-tuple-element.43), channel_id=1, source_target_pairs={{0,2},{1,3},{2,0},{3,1},{4,6},{5,7},{6,4},{7,5},{8,10},{9,11},{10,... | collective-permute-start | bytes 540680 | tf_op jit(solution)/shard_map/ppermute | solution.py:478
  7.7 10.5 %collective-permute-start.3 = (f32[44,8,128]{2,1,0:T(8,128)S(1)}, f32[44,8,128]{2,1,0:T(8,128)S(1)}, u32[]{:S(2)}, u32[]{:S(2)}) collective-permute-start(f32[44,8,128]{2,1,0:T(8,128)S(1)} %get-tuple-element.44), channel_id=1, source_target_pairs={{0,5},{1,4},{2,7},{3,6},{4,1},{5,0},{6,3},{7,2},{8,13},{9,12},{10,... | collective-permute-start | bytes 540680 | tf_op jit(solution)/shard_map/ppermute | solution.py:478
  7.7 10.5 %collective-permute-start.4 = (f32[44,8,128]{2,1,0:T(8,128)S(1)}, f32[44,8,128]{2,1,0:T(8,128)S(1)}, u32[]{:S(2)}, u32[]{:S(2)}) collective-permute-start(f32[44,8,128]{2,1,0:T(8,128)S(1)} %get-tuple-element.45), channel_id=1, source_target_pairs={{0,3},{1,2},{2,1},{3,0},{4,7},{5,6},{6,5},{7,4},{8,11},{9,10},{10,... | collective-permute-start | bytes 540680 | tf_op jit(solution)/shard_map/ppermute | solution.py:478
  8.0 12.8 %collective-permute-start.5 = (f32[44,8,128]{2,1,0:T(8,128)S(1)}, f32[44,8,128]{2,1,0:T(8,128)S(1)}, u32[]{:S(2)}, u32[]{:S(2)}) collective-permute-start(f32[44,8,128]{2,1,0:T(8,128)S(1)} %get-tuple-element.46), channel_id=1, source_target_pairs={{0,6},{1,7},{2,4},{3,5},{4,2},{5,3},{6,0},{7,1},{8,14},{9,15},{10,... | collective-permute-start | bytes 540680 | tf_op jit(solution)/shard_map/ppermute | solution.py:478
  11.6 14.1 %collective-permute-start.6 = (f32[44,8,128]{2,1,0:T(8,128)S(1)}, f32[44,8,128]{2,1,0:T(8,128)S(1)}, u32[]{:S(2)}, u32[]{:S(2)}) collective-permute-start(f32[44,8,128]{2,1,0:T(8,128)S(1)} %get-tuple-element.47), channel_id=1, source_target_pairs={{0,7},{1,6},{2,5},{3,4},{4,3},{5,2},{6,1},{7,0},{8,15},{9,14},{10,... | collective-permute-start | bytes 540680 | tf_op jit(solution)/shard_map/ppermute | solution.py:478
  13.3 21.6 %all-to-all-start = ((f32[32,2,8,128]{3,2,1,0:T(8,128)}), f32[32,2,8,128]{3,2,1,0:T(8,128)S(1)}, u32[]{:S(2)}, u32[]{:S(2)}) async-start(f32[32,2,8,128]{3,2,1,0:T(8,128)} %get-tuple-element.38), calls=%async_computation | async-start | bytes 524288 | tf_op jit(solution)/shard_map/all_to_all | solution.py:498
  26.7 13.3 %collective-permute-start.9 = (f32[4,24,8,128]{3,2,1,0:T(8,128)S(1)}, f32[4,24,8,128]{3,2,1,0:T(8,128)S(1)}, u32[]{:S(2)}, u32[]{:S(2)}) collective-permute-start(f32[4,24,8,128]{3,2,1,0:T(8,128)S(1)} %get-tuple-element.51.refs_0_), channel_id=1, source_target_pairs={{0,8},{1,9},{2,10},{3,11},{4,12},{5,13},{6,14},{7,15},{8,0},{9,1},... | collective-permute-start | bytes 1179656 | tf_op jit(solution)/shard_map/ppermute | solution.py:474
  28.4 11.6 %collective-permute-start.10 = (f32[4,24,8,128]{3,2,1,0:T(8,128)S(1)}, f32[4,24,8,128]{3,2,1,0:T(8,128)S(1)}, u32[]{:S(2)}, u32[]{:S(2)}) collective-permute-start(f32[4,24,8,128]{3,2,1,0:T(8,128)S(1)} %get-tuple-element.52.refs_1_), channel_id=1, source_target_pairs={{8,16},{9,17},{10,18},{11,19},{12,20},{13,21},{14,22},{15,23},{16,... | collective-permute-start | bytes 1179656 | tf_op jit(solution)/shard_map/ppermute | solution.py:474
  29.1 19.5 %collective-permute-start.7 = (f32[4,20,8,128]{3,2,1,0:T(8,128)S(1)}, f32[4,20,8,128]{3,2,1,0:T(8,128)}, u32[]{:S(2)}, u32[]{:S(2)}) collective-permute-start(f32[4,20,8,128]{3,2,1,0:T(8,128)S(1)} %get-tuple-element.48.refs_0_), channel_id=1, source_target_pairs={{0,8},{1,9},{2,10},{3,11},{4,12},{5,13},{6,14},{7,15},{8,0},{9,1},... | collective-permute-start | bytes 983048 | tf_op jit(solution)/shard_map/ppermute | solution.py:474
  33.5 15.1 %collective-permute-start.8 = (f32[4,20,8,128]{3,2,1,0:T(8,128)}, f32[4,20,8,128]{3,2,1,0:T(8,128)}, u32[]{:S(2)}, u32[]{:S(2)}) collective-permute-start(f32[4,20,8,128]{3,2,1,0:T(8,128)} %get-tuple-element.49.refs_1_), channel_id=1, source_target_pairs={{8,16},{9,17},{10,18},{11,19},{12,20},{13,21},{14,22},{15,23},{16,... | collective-permute-start | bytes 983048 | tf_op jit(solution)/shard_map/ppermute | solution.py:474
  40.0 14.9 %copy-start.4 = (f32[16,8,128]{2,1,0:T(8,128)}, f32[16,8,128]{2,1,0:T(8,128)S(1)}, u32[]{:S(2)}) copy-start(f32[16,8,128]{2,1,0:T(8,128)S(1)} %get-tuple-element.39.wall_ref) | copy-start | bytes 196612
  40.0 14.9 %copy-start.6 = (f32[16,8,128]{2,1,0:T(8,128)}, f32[16,8,128]{2,1,0:T(8,128)S(1)}, u32[]{:S(2)}) copy-start(f32[16,8,128]{2,1,0:T(8,128)S(1)} %get-tuple-element.50.wall_ref) | copy-start | bytes 196612
  44.5 11.4 %collective-permute-start.11 = (f32[5,4,32,128]{3,2,1,0:T(8,128)S(1)}, f32[5,4,32,128]{3,2,1,0:T(8,128)S(1)}, u32[]{:S(2)}, u32[]{:S(2)}) collective-permute-start(f32[5,4,32,128]{3,2,1,0:T(8,128)S(1)} %get-tuple-element.54.refs_5_.refs_0_), channel_id=1, source_target_pairs={{0,8},{1,9},{2,10},{3,11},{4,12},{5,13},{6,14},{7,15},{8,0},{9,1},... | collective-permute-start | bytes 983048 | tf_op jit(solution)/shard_map/ppermute | solution.py:474
  47.9 8.7 %collective-permute-start.12 = (f32[5,4,32,128]{3,2,1,0:T(8,128)S(1)}, f32[5,4,32,128]{3,2,1,0:T(8,128)S(1)}, u32[]{:S(2)}, u32[]{:S(2)}) collective-permute-start(f32[5,4,32,128]{3,2,1,0:T(8,128)S(1)} %get-tuple-element.55.refs_6_.refs_1_), channel_id=1, source_target_pairs={{8,16},{9,17},{10,18},{11,19},{12,20},{13,21},{14,22},{15,23},{16,... | collective-permute-start | bytes 983048 | tf_op jit(solution)/shard_map/ppermute | solution.py:474
  57.4 7.4 %copy-start.1 = (f32[5,4,32,128]{3,2,1,0:T(8,128)S(1)}, f32[5,4,32,128]{3,2,1,0:T(8,128)}, u32[]{:S(2)}) copy-start(f32[5,4,32,128]{3,2,1,0:T(8,128)} %copy-done) | copy-start | bytes 983044
  57.4 7.4 %copy-start.3 = (f32[5,4,32,128]{3,2,1,0:T(8,128)S(1)}, f32[5,4,32,128]{3,2,1,0:T(8,128)}, u32[]{:S(2)}) copy-start(f32[5,4,32,128]{3,2,1,0:T(8,128)} %copy-done.2) | copy-start | bytes 983044
  57.4 28.7 %all-to-all-start.1 = ((f32[8,2,5,4,8,128]{5,4,3,2,1,0:T(8,128)}), f32[8,2,5,4,8,128]{5,4,3,2,1,0:T(8,128)S(1)}, u32[]{:S(2)}, u32[]{:S(2)}) async-start(f32[8,2,5,4,8,128]{5,4,3,2,1,0:T(8,128)} %get-tuple-element.57), calls=%async_computation.1 | async-start | bytes 2621440 | tf_op jit(solution)/shard_map/all_to_all | solution.py:540
  61.1 11.3 %copy-start.5 = (f32[16,8,128]{2,1,0:T(8,128)S(1)}, f32[16,8,128]{2,1,0:T(8,128)}, u32[]{:S(2)}) copy-start(f32[16,8,128]{2,1,0:T(8,128)} %copy-done.4) | copy-start | bytes 196612
  61.1 11.3 %collective-permute-start.13 = (f32[5,4,32,128]{3,2,1,0:T(8,128)S(1)}, f32[5,4,32,128]{3,2,1,0:T(8,128)S(1)}, u32[]{:S(2)}, u32[]{:S(2)}) collective-permute-start(f32[5,4,32,128]{3,2,1,0:T(8,128)S(1)} %get-tuple-element.58.refs_0_), channel_id=1, source_target_pairs={{0,8},{1,9},{2,10},{3,11},{4,12},{5,13},{6,14},{7,15},{8,0},{9,1},... | collective-permute-start | bytes 983048 | tf_op jit(solution)/shard_map/ppermute | solution.py:474
  64.1 8.3 %collective-permute-start.14 = (f32[5,4,32,128]{3,2,1,0:T(8,128)S(1)}, f32[5,4,32,128]{3,2,1,0:T(8,128)S(1)}, u32[]{:S(2)}, u32[]{:S(2)}) collective-permute-start(f32[5,4,32,128]{3,2,1,0:T(8,128)S(1)} %get-tuple-element.59.refs_1_), channel_id=1, source_target_pairs={{8,16},{9,17},{10,18},{11,19},{12,20},{13,21},{14,22},{15,23},{16,... | collective-permute-start | bytes 983048 | tf_op jit(solution)/shard_map/ppermute | solution.py:474
  64.8 0.8 copy-start.7
  77.5 3.8 %collective-permute-start.15 = (f32[2,5,4,8,128]{4,3,2,1,0:T(8,128)S(1)}, f32[2,5,4,8,128]{4,3,2,1,0:T(8,128)S(1)}, u32[]{:S(2)}, u32[]{:S(2)}) collective-permute-start(f32[2,5,4,8,128]{4,3,2,1,0:T(8,128)S(1)} %get-tuple-element.61), channel_id=1, source_target_pairs={{0,1},{1,0},{2,3},{3,2},{4,5},{5,4},{6,7},{7,6},{8,9},{9,8},{10,11... | collective-permute-start | bytes 491528 | tf_op jit(solution)/shard_map/ppermute | solution.py:478
  77.5 7.0 %collective-permute-start.16 = (f32[2,5,4,8,128]{4,3,2,1,0:T(8,128)S(1)}, f32[2,5,4,8,128]{4,3,2,1,0:T(8,128)S(1)}, u32[]{:S(2)}, u32[]{:S(2)}) collective-permute-start(f32[2,5,4,8,128]{4,3,2,1,0:T(8,128)S(1)} %get-tuple-element.62), channel_id=1, source_target_pairs={{0,4},{1,5},{2,6},{3,7},{4,0},{5,1},{6,2},{7,3},{8,12},{9,13},{10,... | collective-permute-start | bytes 491528 | tf_op jit(solution)/shard_map/ppermute | solution.py:478
  79.2 7.7 %collective-permute-start.17 = (f32[2,5,4,8,128]{4,3,2,1,0:T(8,128)}, f32[2,5,4,8,128]{4,3,2,1,0:T(8,128)S(1)}, u32[]{:S(2)}, u32[]{:S(2)}) collective-permute-start(f32[2,5,4,8,128]{4,3,2,1,0:T(8,128)} %get-tuple-element.63), channel_id=1, source_target_pairs={{0,2},{1,3},{2,0},{3,1},{4,6},{5,7},{6,4},{7,5},{8,10},{9,11},{10,... | collective-permute-start | bytes 491528 | tf_op jit(solution)/shard_map/ppermute | solution.py:478
  80.7 6.6 %collective-permute-start.18 = (f32[2,5,4,8,128]{4,3,2,1,0:T(8,128)S(1)}, f32[2,5,4,8,128]{4,3,2,1,0:T(8,128)S(1)}, u32[]{:S(2)}, u32[]{:S(2)}) collective-permute-start(f32[2,5,4,8,128]{4,3,2,1,0:T(8,128)S(1)} %get-tuple-element.64), channel_id=1, source_target_pairs={{0,5},{1,4},{2,7},{3,6},{4,1},{5,0},{6,3},{7,2},{8,13},{9,12},{10,... | collective-permute-start | bytes 491528 | tf_op jit(solution)/shard_map/ppermute | solution.py:478
  80.8 8.2 %collective-permute-start.19 = (f32[2,5,4,8,128]{4,3,2,1,0:T(8,128)S(1)}, f32[2,5,4,8,128]{4,3,2,1,0:T(8,128)S(1)}, u32[]{:S(2)}, u32[]{:S(2)}) collective-permute-start(f32[2,5,4,8,128]{4,3,2,1,0:T(8,128)S(1)} %get-tuple-element.65), channel_id=1, source_target_pairs={{0,3},{1,2},{2,1},{3,0},{4,7},{5,6},{6,5},{7,4},{8,11},{9,10},{10,... | collective-permute-start | bytes 491528 | tf_op jit(solution)/shard_map/ppermute | solution.py:478
  81.3 12.0 %collective-permute-start.20 = (f32[2,5,4,8,128]{4,3,2,1,0:T(8,128)S(1)}, f32[2,5,4,8,128]{4,3,2,1,0:T(8,128)S(1)}, u32[]{:S(2)}, u32[]{:S(2)}) collective-permute-start(f32[2,5,4,8,128]{4,3,2,1,0:T(8,128)S(1)} %get-tuple-element.66), channel_id=1, source_target_pairs={{0,6},{1,7},{2,4},{3,5},{4,2},{5,3},{6,0},{7,1},{8,14},{9,15},{10,... | collective-permute-start | bytes 491528 | tf_op jit(solution)/shard_map/ppermute | solution.py:478
  84.5 10.8 %collective-permute-start.21 = (f32[2,5,4,8,128]{4,3,2,1,0:T(8,128)S(1)}, f32[2,5,4,8,128]{4,3,2,1,0:T(8,128)S(1)}, u32[]{:S(2)}, u32[]{:S(2)}) collective-permute-start(f32[2,5,4,8,128]{4,3,2,1,0:T(8,128)S(1)} %get-tuple-element.67), channel_id=1, source_target_pairs={{0,7},{1,6},{2,5},{3,4},{4,3},{5,2},{6,1},{7,0},{8,15},{9,14},{10,... | collective-permute-start | bytes 491528 | tf_op jit(solution)/shard_map/ppermute | solution.py:478
  (2 other events, 1.5 us)

commit v5 on v4

--- a/solution.py
+++ b/solution.py
@@ -245,13 +245,25 @@
         src = dst
 
 
-def write_pieces(sources, pieces):
-    for m in range(MEMBERS):
-        row = ROWS * (m % 4)
-        for j, (ref, starts) in enumerate(sources):
-            for f in range(FIELDS):
-                for x in range(DEEP):
-                    pieces[m, j, f, x] = ref[f, starts[m // 4] + x, row : row + ROWS, :]
+def write_pieces(sources, near, far, member):
+    for flip, pieces in enumerate((near, far)):
+        for e in range(MEMBERS // 2):
+            to = member ^ (2 * e + flip)
+            row = pl.multiple_of((to % 4) * ROWS, ROWS)
+            start = DEEP + DEEP * (to // 4)
+            for j, source in enumerate(sources):
+                for f in range(FIELDS):
+                    for x in range(DEEP):
+                        pieces[e, j, f, x] = source[f, start + x, pl.ds(row, ROWS), :]
+
+
+def merge_kernel(near, far, *targets):
+    for e, target in enumerate(targets):
+        for b, source in enumerate((near, far)):
+            for j in range(2):
+                for f in range(FIELDS):
+                    for x in range(DEEP):
+                        target[b, j, f, x] = source[e + 1, j, f, x]
 
 
 def block_starts(group):
@@ -312,8 +324,7 @@
     if mode == 0:
         a_ref, b_ref, sponge_ref, base, va, vb = refs
     else:
-        sponge_ref, a_other, b_other, a_ref, b_ref = refs[:5]
-        pieces, base, va, vb = refs[5:]
+        sponge_ref, a_other, b_other, a_ref, b_ref, near, far, base, va, vb = refs
     group, member = position()
     starts = block_starts(group)
     for source, start in zip(blocks, starts):
@@ -337,7 +348,7 @@
             for x in range(DEEP):
                 va[f, starts[0] + x] = a_other[f, x]
                 va[f, starts[1] + x] = b_other[f, x]
-        write_pieces([(va, (DEEP, 2 * DEEP)), (vb, (DEEP, 2 * DEEP))], pieces)
+        write_pieces((va, vb), near, far, member)
 
 
 def second_kernel(groups, mode, vel_ref, vec_ref, wall_ref, *refs):
@@ -385,9 +396,21 @@
     return jnp.concatenate(rows, axis=1)
 
 
-def split_kernel(first, parts_ref):
+def split_kernel(near, far, one, two, three, parts_ref, columns):
+    _, member = position()
+    tiles = FIELDS * DEEP
+    for e, got in enumerate((None, one, two, three)):
+        for b in range(2):
+            other = member ^ (2 * e + b)
+            for j in range(2):
+                for f in range(FIELDS):
+                    for x in range(DEEP):
+                        at = ((2 * other + j) * tiles + f * DEEP + x) * ROWS
+                        value = got[b, j, f, x] if e else (near, far)[b][0, j, f, x]
+                        columns[pl.ds(pl.multiple_of(at, ROWS), ROWS), :] = value
+
     def body(r, carry):
-        parts_ref[r] = three_parts(chunk_of(first, r))
+        parts_ref[r] = three_parts(chunk_of(columns, r))
         return carry
 
     lax.fori_loop(0, parts_ref.shape[0], body, 0, unroll=4)
@@ -473,9 +496,9 @@
     def exchange(a, b):
         return a, b, lax.ppermute(a, AXES, swap(True)), lax.ppermute(b, AXES, swap(False))
 
-    def spread(pieces):
-        sent = zip(pieces[1:], TURNS[1:])
-        return [pieces[0]] + [lax.ppermute(piece, AXES, inside(d)) for piece, d in sent]
+    def spread(pieces, at=0):
+        turns = TURNS[at : at + len(pieces)]
+        return [lax.ppermute(p, AXES, inside(d)) if d else p for p, d in zip(pieces, turns)]
 
     def call(kernel, name, micros, out_shape, inputs, scratch=(), scalars=0):
         return pl.pallas_call(
@@ -514,6 +537,7 @@
     field = [pltpu.VMEM((FIELDS, 4 * DEEP, 4 * ROWS, LANES), F32)] * 3
     border = shape(FIELDS, DEEP, 4 * ROWS, LANES)
     piece = shape(2, FIELDS, DEEP, ROWS, LANES)
+    quarter = shape(MEMBERS // 2, 2, FIELDS, DEEP, ROWS, LANES)
     constants = (mean_velocity, wall_vector)
     a0, b0, sponge_ext = call(
         functools.partial(first_kernel, groups, 0),
@@ -525,19 +549,26 @@
         2,
     )
     next_blocks = [exchange(a0, b0)]
-    a1, b1, first = call(
+    a1, b1, near, far = call(
         functools.partial(first_kernel, groups, 1),
         "first_step_1",
         5.0,
-        [border, border, shape(MEMBERS, 2, FIELDS, DEEP, ROWS, LANES)],
+        [border, border, quarter, quarter],
         (*constants, walls[1], *blocks[1], sponge_ext, a0, b0),
         field,
         2,
     )
     next_blocks.append(exchange(a1, b1))
-    members = [[g * MEMBERS + m for m in range(MEMBERS)] for g in range(groups)]
-    first, _ = lax.optimization_barrier((first, next_blocks[0]))
-    first = lax.all_to_all(first, AXES, 0, 0, axis_index_groups=members)
+    far, _ = lax.optimization_barrier((far, next_blocks[0]))
+    far = lax.ppermute(far, AXES, inside(1))
+    merged = call(
+        merge_kernel,
+        "merge",
+        1,
+        [shape(2, 2, FIELDS, DEEP, ROWS, LANES)] * 3,
+        [near, far],
+    )
+    first = [lax.ppermute(m, AXES, inside(2 * e + 2)) for e, m in enumerate(merged)]
     (second_0,) = call(
         functools.partial(second_kernel, groups, 0),
         "second_step_0",
@@ -556,7 +587,9 @@
         field,
         2,
     )
-    second = spread(second)
+    second = spread(second[:4]) + list(second[4:])
+    second[4:], first = lax.optimization_barrier((second[4:], first))
+    second[4:] = spread(second[4:], 4)
 
     row_count = FIELDS * DEEP * ROWS
     (parts,) = call(
@@ -564,7 +597,8 @@
         "split",
         2,
         [jax.ShapeDtypeStruct((row_count // CHUNK, 6 * MEMBERS, CHUNK * LANES), jnp.bfloat16)],
-        [first.reshape(2 * MEMBERS * row_count, LANES)],
+        [near, far, *first],
+        [pltpu.VMEM((2 * MEMBERS * row_count, LANES), F32)],
     )
     rows_total = float(FIELDS * cells_x * gx_size * cells_y * gy_size * cells_z)
     snap_count = STEPS * 2 * MEMBERS

time: 118 us -> 112 us (0.949)
  blocking collectives: 15.3 us -> 12.3 us
  Pallas kernels: 36.6 us -> 33.9 us
  local copies, waits for them, and re-layouts: 2.35 us -> 0.01 us
  waiting for transfers between devices: 20.8 us -> 23.1 us
    all_to_all x1 -> x0, starting transfers between devices: 3.73 us -> none  [local(): first = lax.all_to_all(first, AXES, 0, 0, axis_index_groups=members)]
    ppermute x14 -> x18, waiting for transfers between devices: 17.3 us -> 20.6 us  [the longest x14 17.4 us: spread(): lax.ppermute(p, AXES, inside(d))]
    all_to_all x1, blocking collectives: 15.3 us -> 12.3 us  [local(): grams = lax.all_to_all(grams, AXES, 0, 0)]
    ppermute x14 -> x18, starting transfers between devices: 17.4 us -> 20.3 us  [the longest x14 16.7 us: spread(): lax.ppermute(p, AXES, inside(d))]
    pallas_call x7 -> x8, Pallas kernels: 27 us -> 24.3 us  [call(): pl.pallas_call(kernel, out_shape=out_shape, in_specs=[SMEM] * scalars + [...]
    unnamed x20 -> x4, local copies, waits for them, and re-layouts: 2.35 us -> 0.01 us
    ppermute x4, starting transfers between devices: 12.5 us -> 14 us  [exchange(): lax.ppermute(a, AXES, swap(True))]
  transfers between devices with their start and end apart: 24 -> 27, of which waited for: 10 -> 9; matrix products, arithmetic and copies ran while one was open for 0% -> 0% of each run, Pallas kernels for 23% -> 22%
where the time goes in v5:
time: 112 us
  starting transfers between devices  41.8 us (37%)
  Pallas kernels  33.9 us (30%)
  waiting for transfers between devices  23.1 us (21%)
  blocking collectives  12.3 us (11%)
    pallas_call x8, Pallas kernels, call(): pl.pallas_call(kernel, out_shape=out_shape, in_specs=[SMEM] * scalars + [...  24.3 us
    ppermute x14, waiting for transfers between devices, spread(): lax.ppermute(p, AXES, inside(d))  17.4 us
    ppermute x14, starting transfers between devices, spread(): lax.ppermute(p, AXES, inside(d))  16.7 us
    ppermute x4, starting transfers between devices, exchange(): lax.ppermute(a, AXES, swap(True))  14 us
    all_to_all x1, blocking collectives, local(): grams = lax.all_to_all(grams, AXES, 0, 0)  12.3 us
    all_to_all x1, starting transfers between devices, local(): wall = lax.all_to_all(wall, AXES, 0, 0)  4.87 us
    pallas_call x1, Pallas kernels, local(): pl.pallas_call(gram_kernel, out_shape=[jax.ShapeDtypeStruct(state_in.shap...  3.79 us
    ppermute x3, starting transfers between devices, local(): lax.ppermute(m, AXES, inside(2 * e + 2))  3.55 us
  transfers between devices with their start and end apart: 27, of which 9 were waited for; matrix products, arithmetic and copies ran while one was open for 0% of the time, Pallas kernels for 22%

profile of v5, /device:TPU:0, one launch (start us, length us, event | category | flops | bytes accessed | tf_op | source)
XLA Modules:
  0.0 112.0 jit_solution(16240425792859514220)
XLA Ops:
  0.6 2.4 %pack.1 = (f32[44,8,128]{2,1,0:T(8,128)S(1)}, f32[44,8,128]{2,1,0:T(8,128)S(1)}, f32[44,8,128]{2,1,0:T(8,128)S(1)}, f32[44,8,128]{2,1,0:T(8,128)S(1)}, f32[44,8,...) custom-call(f32[5,64,8,128]{3,2,1,0:T(8,128)} %bitcast.1, ...), custom_call_target="tpu_custom_call" | custom-call | bytes 6000000 | tf_op jit(solution)/shard_map/pack/pallas_call | solution.py:110
  3.6 2.6 %collective-permute-start.1 = (f32[44,8,128]{2,1,0:T(8,128)S(1)}, f32[44,8,128]{2,1,0:T(8,128)S(1)}, u32[]{:S(2)}, u32[]{:S(2)}) collective-permute-start(f32[44,8,128]{2,1,0:T(8,128)S(1)} %get-tuple-element.53), channel_id=1, source_target_pairs={{0,4},{1,5},{2,6},{3,7},{4,0},{5,1},{6,2},{7,3},{8,12},{9,13},{10,... | collective-permute-start | bytes 540680 | tf_op jit(solution)/shard_map/ppermute | solution.py:501
  6.2 1.5 %collective-permute-start.2 = (f32[44,8,128]{2,1,0:T(8,128)S(1)}, f32[44,8,128]{2,1,0:T(8,128)S(1)}, u32[]{:S(2)}, u32[]{:S(2)}) collective-permute-start(f32[44,8,128]{2,1,0:T(8,128)S(1)} %get-tuple-element.54), channel_id=1, source_target_pairs={{0,2},{1,3},{2,0},{3,1},{4,6},{5,7},{6,4},{7,5},{8,10},{9,11},{10,... | collective-permute-start | bytes 540680 | tf_op jit(solution)/shard_map/ppermute | solution.py:501
  8.0 2.9 %collective-permute-start.5 = (f32[44,8,128]{2,1,0:T(8,128)S(1)}, f32[44,8,128]{2,1,0:T(8,128)S(1)}, u32[]{:S(2)}, u32[]{:S(2)}) collective-permute-start(f32[44,8,128]{2,1,0:T(8,128)S(1)} %get-tuple-element.57), channel_id=1, source_target_pairs={{0,6},{1,7},{2,4},{3,5},{4,2},{5,3},{6,0},{7,1},{8,14},{9,15},{10,... | collective-permute-start | bytes 540680 | tf_op jit(solution)/shard_map/ppermute | solution.py:501
  11.6 1.7 %collective-permute-start.6 = (f32[44,8,128]{2,1,0:T(8,128)S(1)}, f32[44,8,128]{2,1,0:T(8,128)S(1)}, u32[]{:S(2)}, u32[]{:S(2)}) collective-permute-start(f32[44,8,128]{2,1,0:T(8,128)S(1)} %get-tuple-element.58), channel_id=1, source_target_pairs={{0,7},{1,6},{2,5},{3,4},{4,3},{5,2},{6,1},{7,0},{8,15},{9,14},{10,... | collective-permute-start | bytes 540680 | tf_op jit(solution)/shard_map/ppermute | solution.py:501
  13.3 4.9 %all-to-all-start = ((f32[32,2,8,128]{3,2,1,0:T(8,128)}), f32[32,2,8,128]{3,2,1,0:T(8,128)S(1)}, u32[]{:S(2)}, u32[]{:S(2)}) async-start(f32[32,2,8,128]{3,2,1,0:T(8,128)} %get-tuple-element.49), calls=%async_computation | async-start | bytes 524288 | tf_op jit(solution)/shard_map/all_to_all | solution.py:521
  18.2 2.6 %collective-permute-done.5.refs_6_ = f32[44,8,128]{2,1,0:T(8,128)S(1)} collective-permute-done((f32[44,8,128]{2,1,0:T(8,128)S(1)}, f32[44,8,128]{2,1,0:T(8,128)S(1)}, u32[]{:S(2)}, u32[]{:S(2)}) %collective-permute-start.5) | collective-permute-done | bytes 180256 | tf_op jit(solution)/shard_map/ppermute | solution.py:501
  20.8 4.9 %collective-permute-done.6.refs_7_ = f32[44,8,128]{2,1,0:T(8,128)S(1)} collective-permute-done((f32[44,8,128]{2,1,0:T(8,128)S(1)}, f32[44,8,128]{2,1,0:T(8,128)S(1)}, u32[]{:S(2)}, u32[]{:S(2)}) %collective-permute-start.6) | collective-permute-done | bytes 180256 | tf_op jit(solution)/shard_map/ppermute | solution.py:501
  25.9 1.8 %collective-permute-start.9 = (f32[4,24,8,128]{3,2,1,0:T(8,128)S(1)}, f32[4,24,8,128]{3,2,1,0:T(8,128)S(1)}, u32[]{:S(2)}, u32[]{:S(2)}) collective-permute-start(f32[4,24,8,128]{3,2,1,0:T(8,128)S(1)} %get-tuple-element.62.refs_0_), channel_id=1, source_target_pairs={{0,8},{1,9},{2,10},{3,11},{4,12},{5,13},{6,14},{7,15},{8,0},{9,1},... | collective-permute-start | bytes 1179656 | tf_op jit(solution)/shard_map/ppermute | solution.py:497
  28.4 4.4 %collective-permute-start.7 = (f32[4,20,8,128]{3,2,1,0:T(8,128)S(1)}, f32[4,20,8,128]{3,2,1,0:T(8,128)S(1)}, u32[]{:S(2)}, u32[]{:S(2)}) collective-permute-start(f32[4,20,8,128]{3,2,1,0:T(8,128)S(1)} %get-tuple-element.59.refs_0_), channel_id=1, source_target_pairs={{0,8},{1,9},{2,10},{3,11},{4,12},{5,13},{6,14},{7,15},{8,0},{9,1},... | collective-permute-start | bytes 983048 | tf_op jit(solution)/shard_map/ppermute | solution.py:497
  33.5 5.1 %forcing.1 = (f32[16,8,128]{2,1,0:T(8,128)S(1)}, f32[16,8,128]{2,1,0:T(8,128)S(1)}) custom-call(f32[32,2,8,128]{3,2,1,0:T(8,128)S(1)} %all-to-all-done.parts), custom_call_target="tpu_custom_call" | custom-call | bytes 15000000 | tf_op jit(solution)/shard_map/forcing/pallas_call | solution.py:504
  38.7 4.5 %first_step_0.1 = (f32[5,4,32,128]{3,2,1,0:T(8,128)S(1)}, f32[5,4,32,128]{3,2,1,0:T(8,128)S(1)}, f32[16,32,128]{2,1,0:T(8,128)S(1)}) custom-call(f32[3]{0:T(128)S(1)} %copy-done, f32[5]{0:T(128)S(1)} %copy-done.1, f32[16,8,128]{2,1,0:T(8,128)S(1)} %get-tuple-element.61.wall_ref, f32[4,24,8,128]{3,2,1,0:T(8,128)S(1)} %get-tuple-element.62.refs_0_, ...), custom_call_target="tpu_custom_call" | custom-call | bytes 15000000 | tf_op jit(solution)/shard_map/first_step_0/pallas_call | solution.py:504
  43.1 4.1 %collective-permute-start.11 = (f32[5,4,32,128]{3,2,1,0:T(8,128)S(1)}, f32[5,4,32,128]{3,2,1,0:T(8,128)S(1)}, u32[]{:S(2)}, u32[]{:S(2)}) collective-permute-start(f32[5,4,32,128]{3,2,1,0:T(8,128)S(1)} %get-tuple-element.65.refs_5_.refs_0_), channel_id=1, source_target_pairs={{0,8},{1,9},{2,10},{3,11},{4,12},{5,13},{6,14},{7,15},{8,0},{9,1},... | collective-permute-start | bytes 983048 | tf_op jit(solution)/shard_map/ppermute | solution.py:497
  47.9 4.7 %first_step_1.1 = (f32[5,4,32,128]{3,2,1,0:T(8,128)S(1)}, f32[5,4,32,128]{3,2,1,0:T(8,128)S(1)}, f32[4,2,5,4,8,128]{5,4,3,2,1,0:T(8,128)S(1)}, f32[4,2,5,4,8,128]{5,4,3,2,1,0:T(8,128)S(1)}) custom-call(f32[3]{0:T(128)S(1)} %copy-done, f32[5]{0:T(128)S(1)} %copy-done.1, f32[16,8,128]{2,1,0:T(8,128)S(1)} %get-tuple-element.50.wall_ref, ...), custom_call_target="tpu_custom_call" | custom-call | bytes 15000000 | tf_op jit(solution)/shard_map/first_step_1/pallas_call | solution.py:504
  52.6 2.5 %collective-permute-done.11.refs_2_ = f32[5,4,32,128]{3,2,1,0:T(8,128)S(1)} collective-permute-done((f32[5,4,32,128]{3,2,1,0:T(8,128)S(1)}, f32[5,4,32,128]{3,2,1,0:T(8,128)S(1)}, u32[]{:S(2)}, u32[]{:S(2)}) %collective-permute-start.11) | collective-permute-done | bytes 327712 | tf_op jit(solution)/shard_map/ppermute | solution.py:497
  55.1 3.6 %collective-permute-start.14 = (f32[5,4,32,128]{3,2,1,0:T(8,128)S(1)}, f32[5,4,32,128]{3,2,1,0:T(8,128)S(1)}, u32[]{:S(2)}, u32[]{:S(2)}) collective-permute-start(f32[5,4,32,128]{3,2,1,0:T(8,128)S(1)} %get-tuple-element.70.refs_0_), channel_id=1, source_target_pairs={{0,8},{1,9},{2,10},{3,11},{4,12},{5,13},{6,14},{7,15},{8,0},{9,1},... | collective-permute-start | bytes 983048 | tf_op jit(solution)/shard_map/ppermute | solution.py:497
  59.5 1.6 %collective-permute-start.16 = (f32[2,2,5,4,8,128]{5,4,3,2,1,0:T(8,128)S(1)}, f32[2,2,5,4,8,128]{5,4,3,2,1,0:T(8,128)S(1)}, u32[]{:S(2)}, u32[]{:S(2)}) collective-permute-start(f32[2,2,5,4,8,128]{5,4,3,2,1,0:T(8,128)S(1)} %get-tuple-element.76), channel_id=1, source_target_pairs={{0,2},{1,3},{2,0},{3,1},{4,6},{5,7},{6,4},{7,5},{8,10},{9,11},{10,... | collective-permute-start | bytes 983048 | tf_op jit(solution)/shard_map/ppermute | solution.py:571
  61.1 1.4 %collective-permute-start.17 = (f32[2,2,5,4,8,128]{5,4,3,2,1,0:T(8,128)S(1)}, f32[2,2,5,4,8,128]{5,4,3,2,1,0:T(8,128)S(1)}, u32[]{:S(2)}, u32[]{:S(2)}) collective-permute-start(f32[2,2,5,4,8,128]{5,4,3,2,1,0:T(8,128)S(1)} %get-tuple-element.77), channel_id=1, source_target_pairs={{0,4},{1,5},{2,6},{3,7},{4,0},{5,1},{6,2},{7,3},{8,12},{9,13},{10,... | collective-permute-start | bytes 983048 | tf_op jit(solution)/shard_map/ppermute | solution.py:571
  63.1 4.4 %second_step_0.1.refs_5_ = f32[5,8,32,128]{3,2,1,0:T(8,128)S(1)} custom-call(f32[3]{0:T(128)S(1)} %copy-done, f32[5]{0:T(128)S(1)} %copy-done.1, f32[16,8,128]{2,1,0:T(8,128)S(1)} %get-tuple-element.61.wall_ref, f32[5,4,32,128]{3,2,1,0:T(8,128)S(1)} %get-tuple-element.65.refs_5_.refs_0_, f32[5,4,32,128]{3,2,1,0:T(8,128)S(1)} %get-tuple-element.66.refs_6_.refs_1_, ...), custom_call_target="tpu_custom_call" | custom-call | bytes 15000000 | tf_op jit(solution)/shard_map/second_step_0/pallas_call | solution.py:504
  67.5 4.5 %second_step_1.1 = (f32[2,5,4,8,128]{4,3,2,1,0:T(8,128)S(1)}, f32[2,5,4,8,128]{4,3,2,1,0:T(8,128)S(1)}, f32[2,5,4,8,128]{4,3,2,1,0:T(8,128)S(1)}, f32[2,5,4,8,12...) custom-call(f32[3]{0:T(128)S(1)} %copy-done, ...), custom_call_target="tpu_custom_call" | custom-call | bytes 15000000 | tf_op jit(solution)/shard_map/second_step_1/pallas_call | solution.py:504
  72.1 1.7 %collective-permute-start.20 = (f32[2,5,4,8,128]{4,3,2,1,0:T(8,128)S(1)}, f32[2,5,4,8,128]{4,3,2,1,0:T(8,128)S(1)}, u32[]{:S(2)}, u32[]{:S(2)}) collective-permute-start(f32[2,5,4,8,128]{4,3,2,1,0:T(8,128)S(1)} %get-tuple-element.84), channel_id=1, source_target_pairs={{0,4},{1,5},{2,6},{3,7},{4,0},{5,1},{6,2},{7,3},{8,12},{9,13},{10,... | collective-permute-start | bytes 491528 | tf_op jit(solution)/shard_map/ppermute | solution.py:501
  73.8 1.3 %collective-permute-start.21 = (f32[2,5,4,8,128]{4,3,2,1,0:T(8,128)S(1)}, f32[2,5,4,8,128]{4,3,2,1,0:T(8,128)S(1)}, u32[]{:S(2)}, u32[]{:S(2)}) collective-permute-start(f32[2,5,4,8,128]{4,3,2,1,0:T(8,128)S(1)} %get-tuple-element.85), channel_id=1, source_target_pairs={{0,2},{1,3},{2,0},{3,1},{4,6},{5,7},{6,4},{7,5},{8,10},{9,11},{10,... | collective-permute-start | bytes 491528 | tf_op jit(solution)/shard_map/ppermute | solution.py:501
  75.0 2.6 %collective-permute-done.17.two = f32[2,2,5,4,8,128]{5,4,3,2,1,0:T(8,128)S(1)} collective-permute-done((f32[2,2,5,4,8,128]{5,4,3,2,1,0:T(8,128)S(1)}, f32[2,2,5,4,8,128]{5,4,3,2,1,0:T(8,128)S(1)}, u32[]{:S(2)}, u32[]{:S(2)}) %collective-permute-start.17) | collective-permute-done | bytes 327712 | tf_op jit(solution)/shard_map/ppermute | solution.py:571
  78.3 1.5 %collective-permute-start.23 = (f32[2,5,4,8,128]{4,3,2,1,0:T(8,128)S(1)}, f32[2,5,4,8,128]{4,3,2,1,0:T(8,128)S(1)}, u32[]{:S(2)}, u32[]{:S(2)}) collective-permute-start(f32[2,5,4,8,128]{4,3,2,1,0:T(8,128)S(1)} %get-tuple-element.87), channel_id=1, source_target_pairs={{0,3},{1,2},{2,1},{3,0},{4,7},{5,6},{6,5},{7,4},{8,11},{9,10},{10,... | collective-permute-start | bytes 491528 | tf_op jit(solution)/shard_map/ppermute | solution.py:501
  79.8 1.7 %collective-permute-start.24 = (f32[2,5,4,8,128]{4,3,2,1,0:T(8,128)S(1)}, f32[2,5,4,8,128]{4,3,2,1,0:T(8,128)S(1)}, u32[]{:S(2)}, u32[]{:S(2)}) collective-permute-start(f32[2,5,4,8,128]{4,3,2,1,0:T(8,128)S(1)} %get-tuple-element.88), channel_id=1, source_target_pairs={{0,6},{1,7},{2,4},{3,5},{4,2},{5,3},{6,0},{7,1},{8,14},{9,15},{10,... | collective-permute-start | bytes 491528 | tf_op jit(solution)/shard_map/ppermute | solution.py:501
  81.5 1.0 collective-permute-start.25
  83.5 1.0 collective-permute-done.22.refs_4_
  84.5 5.5 %collective-permute-done.24.refs_6_ = f32[2,5,4,8,128]{4,3,2,1,0:T(8,128)S(1)} collective-permute-done((f32[2,5,4,8,128]{4,3,2,1,0:T(8,128)S(1)}, f32[2,5,4,8,128]{4,3,2,1,0:T(8,128)S(1)}, u32[]{:S(2)}, u32[]{:S(2)}) %collective-permute-start.24) | collective-permute-done | bytes 163872 | tf_op jit(solution)/shard_map/ppermute | solution.py:501
  90.0 2.7 %collective-permute-done.25.refs_7_ = f32[2,5,4,8,128]{4,3,2,1,0:T(8,128)S(1)} collective-permute-done((f32[2,5,4,8,128]{4,3,2,1,0:T(8,128)S(1)}, f32[2,5,4,8,128]{4,3,2,1,0:T(8,128)S(1)}, u32[]{:S(2)}, u32[]{:S(2)}) %collective-permute-start.25) | collective-permute-done | bytes 163872 | tf_op jit(solution)/shard_map/ppermute | solution.py:501
  92.6 3.8 %gram.1 = (f32[5,16,4,8,128]{4,3,2,1,0:T(8,128)}, f32[32,8,128]{2,1,0:T(8,128)S(1)}) custom-call(bf16[40,48,512]{2,1,0:T(8,128)(2,1)S(1)} %split.1.first_parts, f32[2,5,4,8,128]{4,3,2,1,0:T(8,128)S(1)} %get-tuple-element.82.refs_0_, f32[2,5,4,8,128]{4,3,2,1,0:T(8,128)S(1)} %collective-permute-done.19.refs_1_, ...), custom_call_target="tpu_custom_call" | custom-call | tf_op jit(solution)/shard_map/gram/pallas_call | solution.py:605
  96.4 12.3 %all_to_all.10.parts_ref = f32[32,8,128]{2,1,0:T(8,128)S(1)} all-to-all(f32[32,8,128]{2,1,0:T(8,128)S(1)} %get-tuple-element.91), channel_id=1, replica_groups=mesh['gx'=8,'gy'=4] {'gx','gy'}, dimensions={0} | all-to-all | bytes 262144 | tf_op jit(solution)/shard_map/all_to_all | solution.py:617
  108.7 3.3 %factor.1 = f32[32,32]{1,0:T(8,128)} custom-call(f32[32,8,128]{2,1,0:T(8,128)S(1)} %all_to_all.10.parts_ref), custom_call_target="tpu_custom_call" | custom-call | tf_op jit(solution)/shard_map/factor/pallas_call | solution.py:618
  (38 shorter events, 6.9 us)
Async XLA Ops:
  3.1 35.6 %copy-start = (f32[3]{0:T(128)S(1)}, f32[3]{0:T(128)}, u32[]{:S(2)}) copy-start(f32[3]{0:T(128)} %vel_ref.7) | copy-start | bytes 40
  3.1 35.6 %copy-start.1 = (f32[5]{0:T(128)S(1)}, f32[5]{0:T(128)}, u32[]{:S(2)}) copy-start(f32[5]{0:T(128)} %vec_ref.7) | copy-start | bytes 64
  3.1 4.9 %collective-permute-start = (f32[44,8,128]{2,1,0:T(8,128)S(1)}, f32[44,8,128]{2,1,0:T(8,128)S(1)}, u32[]{:S(2)}, u32[]{:S(2)}) collective-permute-start(f32[44,8,128]{2,1,0:T(8,128)S(1)} %get-tuple-element.48), channel_id=1, source_target_pairs={{0,1},{1,0},{2,3},{3,2},{4,5},{5,4},{6,7},{7,6},{8,9},{9,8},{10,11... | collective-permute-start | bytes 540680 | tf_op jit(solution)/shard_map/ppermute | solution.py:501
  3.6 8.0 %collective-permute-start.1 = (f32[44,8,128]{2,1,0:T(8,128)S(1)}, f32[44,8,128]{2,1,0:T(8,128)S(1)}, u32[]{:S(2)}, u32[]{:S(2)}) collective-permute-start(f32[44,8,128]{2,1,0:T(8,128)S(1)} %get-tuple-element.53), channel_id=1, source_target_pairs={{0,4},{1,5},{2,6},{3,7},{4,0},{5,1},{6,2},{7,3},{8,12},{9,13},{10,... | collective-permute-start | bytes 540680 | tf_op jit(solution)/shard_map/ppermute | solution.py:501
  6.2 12.0 %collective-permute-start.2 = (f32[44,8,128]{2,1,0:T(8,128)S(1)}, f32[44,8,128]{2,1,0:T(8,128)S(1)}, u32[]{:S(2)}, u32[]{:S(2)}) collective-permute-start(f32[44,8,128]{2,1,0:T(8,128)S(1)} %get-tuple-element.54), channel_id=1, source_target_pairs={{0,2},{1,3},{2,0},{3,1},{4,6},{5,7},{6,4},{7,5},{8,10},{9,11},{10,... | collective-permute-start | bytes 540680 | tf_op jit(solution)/shard_map/ppermute | solution.py:501
  7.7 10.5 %collective-permute-start.3 = (f32[44,8,128]{2,1,0:T(8,128)S(1)}, f32[44,8,128]{2,1,0:T(8,128)S(1)}, u32[]{:S(2)}, u32[]{:S(2)}) collective-permute-start(f32[44,8,128]{2,1,0:T(8,128)S(1)} %get-tuple-element.55), channel_id=1, source_target_pairs={{0,5},{1,4},{2,7},{3,6},{4,1},{5,0},{6,3},{7,2},{8,13},{9,12},{10,... | collective-permute-start | bytes 540680 | tf_op jit(solution)/shard_map/ppermute | solution.py:501
  7.7 10.5 %collective-permute-start.4 = (f32[44,8,128]{2,1,0:T(8,128)S(1)}, f32[44,8,128]{2,1,0:T(8,128)S(1)}, u32[]{:S(2)}, u32[]{:S(2)}) collective-permute-start(f32[44,8,128]{2,1,0:T(8,128)S(1)} %get-tuple-element.56), channel_id=1, source_target_pairs={{0,3},{1,2},{2,1},{3,0},{4,7},{5,6},{6,5},{7,4},{8,11},{9,10},{10,... | collective-permute-start | bytes 540680 | tf_op jit(solution)/shard_map/ppermute | solution.py:501
  8.0 12.8 %collective-permute-start.5 = (f32[44,8,128]{2,1,0:T(8,128)S(1)}, f32[44,8,128]{2,1,0:T(8,128)S(1)}, u32[]{:S(2)}, u32[]{:S(2)}) collective-permute-start(f32[44,8,128]{2,1,0:T(8,128)S(1)} %get-tuple-element.57), channel_id=1, source_target_pairs={{0,6},{1,7},{2,4},{3,5},{4,2},{5,3},{6,0},{7,1},{8,14},{9,15},{10,... | collective-permute-start | bytes 540680 | tf_op jit(solution)/shard_map/ppermute | solution.py:501
  11.6 14.1 %collective-permute-start.6 = (f32[44,8,128]{2,1,0:T(8,128)S(1)}, f32[44,8,128]{2,1,0:T(8,128)S(1)}, u32[]{:S(2)}, u32[]{:S(2)}) collective-permute-start(f32[44,8,128]{2,1,0:T(8,128)S(1)} %get-tuple-element.58), channel_id=1, source_target_pairs={{0,7},{1,6},{2,5},{3,4},{4,3},{5,2},{6,1},{7,0},{8,15},{9,14},{10,... | collective-permute-start | bytes 540680 | tf_op jit(solution)/shard_map/ppermute | solution.py:501
  13.3 20.2 %all-to-all-start = ((f32[32,2,8,128]{3,2,1,0:T(8,128)}), f32[32,2,8,128]{3,2,1,0:T(8,128)S(1)}, u32[]{:S(2)}, u32[]{:S(2)}) async-start(f32[32,2,8,128]{3,2,1,0:T(8,128)} %get-tuple-element.49), calls=%async_computation | async-start | bytes 524288 | tf_op jit(solution)/shard_map/all_to_all | solution.py:521
  25.9 12.7 %collective-permute-start.9 = (f32[4,24,8,128]{3,2,1,0:T(8,128)S(1)}, f32[4,24,8,128]{3,2,1,0:T(8,128)S(1)}, u32[]{:S(2)}, u32[]{:S(2)}) collective-permute-start(f32[4,24,8,128]{3,2,1,0:T(8,128)S(1)} %get-tuple-element.62.refs_0_), channel_id=1, source_target_pairs={{0,8},{1,9},{2,10},{3,11},{4,12},{5,13},{6,14},{7,15},{8,0},{9,1},... | collective-permute-start | bytes 1179656 | tf_op jit(solution)/shard_map/ppermute | solution.py:497
  27.8 10.9 %collective-permute-start.10 = (f32[4,24,8,128]{3,2,1,0:T(8,128)S(1)}, f32[4,24,8,128]{3,2,1,0:T(8,128)S(1)}, u32[]{:S(2)}, u32[]{:S(2)}) collective-permute-start(f32[4,24,8,128]{3,2,1,0:T(8,128)S(1)} %get-tuple-element.63.refs_1_), channel_id=1, source_target_pairs={{8,16},{9,17},{10,18},{11,19},{12,20},{13,21},{14,22},{15,23},{16,... | collective-permute-start | bytes 1179656 | tf_op jit(solution)/shard_map/ppermute | solution.py:497
  28.4 19.5 %collective-permute-start.7 = (f32[4,20,8,128]{3,2,1,0:T(8,128)S(1)}, f32[4,20,8,128]{3,2,1,0:T(8,128)S(1)}, u32[]{:S(2)}, u32[]{:S(2)}) collective-permute-start(f32[4,20,8,128]{3,2,1,0:T(8,128)S(1)} %get-tuple-element.59.refs_0_), channel_id=1, source_target_pairs={{0,8},{1,9},{2,10},{3,11},{4,12},{5,13},{6,14},{7,15},{8,0},{9,1},... | collective-permute-start | bytes 983048 | tf_op jit(solution)/shard_map/ppermute | solution.py:497
  32.8 15.1 %collective-permute-start.8 = (f32[4,20,8,128]{3,2,1,0:T(8,128)S(1)}, f32[4,20,8,128]{3,2,1,0:T(8,128)S(1)}, u32[]{:S(2)}, u32[]{:S(2)}) collective-permute-start(f32[4,20,8,128]{3,2,1,0:T(8,128)S(1)} %get-tuple-element.60.refs_1_), channel_id=1, source_target_pairs={{8,16},{9,17},{10,18},{11,19},{12,20},{13,21},{14,22},{15,23},{16,... | collective-permute-start | bytes 983048 | tf_op jit(solution)/shard_map/ppermute | solution.py:497
  43.1 12.0 %collective-permute-start.11 = (f32[5,4,32,128]{3,2,1,0:T(8,128)S(1)}, f32[5,4,32,128]{3,2,1,0:T(8,128)S(1)}, u32[]{:S(2)}, u32[]{:S(2)}) collective-permute-start(f32[5,4,32,128]{3,2,1,0:T(8,128)S(1)} %get-tuple-element.65.refs_5_.refs_0_), channel_id=1, source_target_pairs={{0,8},{1,9},{2,10},{3,11},{4,12},{5,13},{6,14},{7,15},{8,0},{9,1},... | collective-permute-start | bytes 983048 | tf_op jit(solution)/shard_map/ppermute | solution.py:497
  47.3 7.9 %collective-permute-start.12 = (f32[5,4,32,128]{3,2,1,0:T(8,128)S(1)}, f32[5,4,32,128]{3,2,1,0:T(8,128)S(1)}, u32[]{:S(2)}, u32[]{:S(2)}) collective-permute-start(f32[5,4,32,128]{3,2,1,0:T(8,128)S(1)} %get-tuple-element.66.refs_6_.refs_1_), channel_id=1, source_target_pairs={{8,16},{9,17},{10,18},{11,19},{12,20},{13,21},{14,22},{15,23},{16,... | collective-permute-start | bytes 983048 | tf_op jit(solution)/shard_map/ppermute | solution.py:497
  55.1 4.3 %collective-permute-start.13 = (f32[4,2,5,4,8,128]{5,4,3,2,1,0:T(8,128)S(1)}, f32[4,2,5,4,8,128]{5,4,3,2,1,0:T(8,128)S(1)}, u32[]{:S(2)}, u32[]{:S(2)}) collective-permute-start(f32[4,2,5,4,8,128]{5,4,3,2,1,0:T(8,128)S(1)} %get-tuple-element.69), channel_id=1, source_target_pairs={{0,1},{1,0},{2,3},{3,2},{4,5},{5,4},{6,7},{7,6},{8,9},{9,8},{10,11... | collective-permute-start | bytes 1966088 | tf_op jit(solution)/shard_map/ppermute | solution.py:563
  55.1 12.3 %collective-permute-start.14 = (f32[5,4,32,128]{3,2,1,0:T(8,128)S(1)}, f32[5,4,32,128]{3,2,1,0:T(8,128)S(1)}, u32[]{:S(2)}, u32[]{:S(2)}) collective-permute-start(f32[5,4,32,128]{3,2,1,0:T(8,128)S(1)} %get-tuple-element.70.refs_0_), channel_id=1, source_target_pairs={{0,8},{1,9},{2,10},{3,11},{4,12},{5,13},{6,14},{7,15},{8,0},{9,1},... | collective-permute-start | bytes 983048 | tf_op jit(solution)/shard_map/ppermute | solution.py:497
  58.8 8.7 %collective-permute-start.15 = (f32[5,4,32,128]{3,2,1,0:T(8,128)S(1)}, f32[5,4,32,128]{3,2,1,0:T(8,128)S(1)}, u32[]{:S(2)}, u32[]{:S(2)}) collective-permute-start(f32[5,4,32,128]{3,2,1,0:T(8,128)S(1)} %get-tuple-element.71.refs_1_), channel_id=1, source_target_pairs={{8,16},{9,17},{10,18},{11,19},{12,20},{13,21},{14,22},{15,23},{16,... | collective-permute-start | bytes 983048 | tf_op jit(solution)/shard_map/ppermute | solution.py:497
  59.5 14.3 %collective-permute-start.16 = (f32[2,2,5,4,8,128]{5,4,3,2,1,0:T(8,128)S(1)}, f32[2,2,5,4,8,128]{5,4,3,2,1,0:T(8,128)S(1)}, u32[]{:S(2)}, u32[]{:S(2)}) collective-permute-start(f32[2,2,5,4,8,128]{5,4,3,2,1,0:T(8,128)S(1)} %get-tuple-element.76), channel_id=1, source_target_pairs={{0,2},{1,3},{2,0},{3,1},{4,6},{5,7},{6,4},{7,5},{8,10},{9,11},{10,... | collective-permute-start | bytes 983048 | tf_op jit(solution)/shard_map/ppermute | solution.py:571
  61.1 16.5 %collective-permute-start.17 = (f32[2,2,5,4,8,128]{5,4,3,2,1,0:T(8,128)S(1)}, f32[2,2,5,4,8,128]{5,4,3,2,1,0:T(8,128)S(1)}, u32[]{:S(2)}, u32[]{:S(2)}) collective-permute-start(f32[2,2,5,4,8,128]{5,4,3,2,1,0:T(8,128)S(1)} %get-tuple-element.77), channel_id=1, source_target_pairs={{0,4},{1,5},{2,6},{3,7},{4,0},{5,1},{6,2},{7,3},{8,12},{9,13},{10,... | collective-permute-start | bytes 983048 | tf_op jit(solution)/shard_map/ppermute | solution.py:571
  62.5 15.8 %collective-permute-start.18 = (f32[2,2,5,4,8,128]{5,4,3,2,1,0:T(8,128)S(1)}, f32[2,2,5,4,8,128]{5,4,3,2,1,0:T(8,128)S(1)}, u32[]{:S(2)}, u32[]{:S(2)}) collective-permute-start(f32[2,2,5,4,8,128]{5,4,3,2,1,0:T(8,128)S(1)} %get-tuple-element.78), channel_id=1, source_target_pairs={{0,6},{1,7},{2,4},{3,5},{4,2},{5,3},{6,0},{7,1},{8,14},{9,15},{10,... | collective-permute-start | bytes 983048 | tf_op jit(solution)/shard_map/ppermute | solution.py:571
  72.0 7.8 %collective-permute-start.19 = (f32[2,5,4,8,128]{4,3,2,1,0:T(8,128)S(1)}, f32[2,5,4,8,128]{4,3,2,1,0:T(8,128)S(1)}, u32[]{:S(2)}, u32[]{:S(2)}) collective-permute-start(f32[2,5,4,8,128]{4,3,2,1,0:T(8,128)S(1)} %get-tuple-element.83), channel_id=1, source_target_pairs={{0,1},{1,0},{2,3},{3,2},{4,5},{5,4},{6,7},{7,6},{8,9},{9,8},{10,11... | collective-permute-start | bytes 491528 | tf_op jit(solution)/shard_map/ppermute | solution.py:501
  72.1 9.4 %collective-permute-start.20 = (f32[2,5,4,8,128]{4,3,2,1,0:T(8,128)S(1)}, f32[2,5,4,8,128]{4,3,2,1,0:T(8,128)S(1)}, u32[]{:S(2)}, u32[]{:S(2)}) collective-permute-start(f32[2,5,4,8,128]{4,3,2,1,0:T(8,128)S(1)} %get-tuple-element.84), channel_id=1, source_target_pairs={{0,4},{1,5},{2,6},{3,7},{4,0},{5,1},{6,2},{7,3},{8,12},{9,13},{10,... | collective-permute-start | bytes 491528 | tf_op jit(solution)/shard_map/ppermute | solution.py:501
  73.8 9.7 %collective-permute-start.21 = (f32[2,5,4,8,128]{4,3,2,1,0:T(8,128)S(1)}, f32[2,5,4,8,128]{4,3,2,1,0:T(8,128)S(1)}, u32[]{:S(2)}, u32[]{:S(2)}) collective-permute-start(f32[2,5,4,8,128]{4,3,2,1,0:T(8,128)S(1)} %get-tuple-element.85), channel_id=1, source_target_pairs={{0,2},{1,3},{2,0},{3,1},{4,6},{5,7},{6,4},{7,5},{8,10},{9,11},{10,... | collective-permute-start | bytes 491528 | tf_op jit(solution)/shard_map/ppermute | solution.py:501
  78.3 6.2 %collective-permute-start.22 = (f32[2,5,4,8,128]{4,3,2,1,0:T(8,128)S(1)}, f32[2,5,4,8,128]{4,3,2,1,0:T(8,128)S(1)}, u32[]{:S(2)}, u32[]{:S(2)}) collective-permute-start(f32[2,5,4,8,128]{4,3,2,1,0:T(8,128)S(1)} %get-tuple-element.86), channel_id=1, source_target_pairs={{0,5},{1,4},{2,7},{3,6},{4,1},{5,0},{6,3},{7,2},{8,13},{9,12},{10,... | collective-permute-start | bytes 491528 | tf_op jit(solution)/shard_map/ppermute | solution.py:501
  78.3 6.2 %collective-permute-start.23 = (f32[2,5,4,8,128]{4,3,2,1,0:T(8,128)S(1)}, f32[2,5,4,8,128]{4,3,2,1,0:T(8,128)S(1)}, u32[]{:S(2)}, u32[]{:S(2)}) collective-permute-start(f32[2,5,4,8,128]{4,3,2,1,0:T(8,128)S(1)} %get-tuple-element.87), channel_id=1, source_target_pairs={{0,3},{1,2},{2,1},{3,0},{4,7},{5,6},{6,5},{7,4},{8,11},{9,10},{10,... | collective-permute-start | bytes 491528 | tf_op jit(solution)/shard_map/ppermute | solution.py:501
  79.8 10.2 %collective-permute-start.24 = (f32[2,5,4,8,128]{4,3,2,1,0:T(8,128)S(1)}, f32[2,5,4,8,128]{4,3,2,1,0:T(8,128)S(1)}, u32[]{:S(2)}, u32[]{:S(2)}) collective-permute-start(f32[2,5,4,8,128]{4,3,2,1,0:T(8,128)S(1)} %get-tuple-element.88), channel_id=1, source_target_pairs={{0,6},{1,7},{2,4},{3,5},{4,2},{5,3},{6,0},{7,1},{8,14},{9,15},{10,... | collective-permute-start | bytes 491528 | tf_op jit(solution)/shard_map/ppermute | solution.py:501
  81.5 11.1 %collective-permute-start.25 = (f32[2,5,4,8,128]{4,3,2,1,0:T(8,128)S(1)}, f32[2,5,4,8,128]{4,3,2,1,0:T(8,128)S(1)}, u32[]{:S(2)}, u32[]{:S(2)}) collective-permute-start(f32[2,5,4,8,128]{4,3,2,1,0:T(8,128)S(1)} %get-tuple-element.89), channel_id=1, source_target_pairs={{0,7},{1,6},{2,5},{3,4},{4,3},{5,2},{6,1},{7,0},{8,15},{9,14},{10,... | collective-permute-start | bytes 491528 | tf_op jit(solution)/shard_map/ppermute | solution.py:501

commit v6 on v5

--- a/solution.py
+++ b/solution.py
@@ -219,11 +219,14 @@
                 dst[f, i, pl.ds(ROWS * t, ROWS), :] = new[f][t]
         return carry
 
-    def two_planes(n, carry):
-        plane(low + 2 * n, carry)
-        return plane(low + 2 * n + 1, carry)
-
-    lax.fori_loop(0, (high - low) // 2, two_planes, 0)
+    count = (high - low) // 2
+
+    def half(n, carry):
+        for k in range(count):
+            plane(low + count * n + k, carry)
+        return carry
+
+    lax.fori_loop(0, 2, half, 0)
 
 
 def run_step(step, base, va, vb, sponge_ref, wall_ref, vel, wall_vec, has_low, has_high):

time: 112 us -> 112 us (level)
  Pallas kernels: 33.9 us -> 31.1 us
  waiting for transfers between devices: 23.1 us -> 25.2 us
    pallas_call x8, Pallas kernels: 24.3 us -> 21.6 us  [call(): pl.pallas_call(kernel, out_shape=out_shape, in_specs=[SMEM] * scalars + [...]
  transfers between devices with their start and end apart: 27 -> 27, of which waited for: 9 -> 10; matrix products, arithmetic and copies ran while one was open for 0% -> 0% of each run, Pallas kernels for 22% -> 19%
where the time goes in v6:
time: 112 us; the launch traced here: 111 us
  starting transfers between devices  41.8 us (37%)
  Pallas kernels  31.1 us (28%)
  waiting for transfers between devices  25.2 us (22%)
  blocking collectives  12.3 us (11%)
    pallas_call x8, Pallas kernels, call(): pl.pallas_call(kernel, out_shape=out_shape, in_specs=[SMEM] * scalars + [...  21.6 us
    ppermute x14, waiting for transfers between devices, spread(): lax.ppermute(p, AXES, inside(d))  17.4 us
    ppermute x14, starting transfers between devices, spread(): lax.ppermute(p, AXES, inside(d))  16.7 us
    ppermute x4, starting transfers between devices, exchange(): lax.ppermute(a, AXES, swap(True))  14 us
    all_to_all x1, blocking collectives, local(): grams = lax.all_to_all(grams, AXES, 0, 0)  12.3 us
    all_to_all x1, starting transfers between devices, local(): wall = lax.all_to_all(wall, AXES, 0, 0)  4.87 us
    ppermute x3, waiting for transfers between devices, local(): lax.ppermute(m, AXES, inside(2 * e + 2))  4.26 us
    pallas_call x1, Pallas kernels, local(): pl.pallas_call(gram_kernel, out_shape=[jax.ShapeDtypeStruct(state_in.shap...  3.78 us
  transfers between devices with their start and end apart: 27, of which 10 were waited for; matrix products, arithmetic and copies ran while one was open for 0% of the time, Pallas kernels for 19%

profile of v6, /device:TPU:0, one launch (start us, length us, event | category | flops | bytes accessed | tf_op | source)
XLA Modules:
  0.0 111.4 jit_solution(13838729267954627112)
XLA Ops:
  0.6 2.4 %pack.1 = (f32[44,8,128]{2,1,0:T(8,128)S(1)}, f32[44,8,128]{2,1,0:T(8,128)S(1)}, f32[44,8,128]{2,1,0:T(8,128)S(1)}, f32[44,8,128]{2,1,0:T(8,128)S(1)}, f32[44,8,...) custom-call(f32[5,64,8,128]{3,2,1,0:T(8,128)} %bitcast.1, ...), custom_call_target="tpu_custom_call" | custom-call | bytes 6000000 | tf_op jit(solution)/shard_map/pack/pallas_call | solution.py:110
  3.6 2.6 %collective-permute-start.1 = (f32[44,8,128]{2,1,0:T(8,128)S(1)}, f32[44,8,128]{2,1,0:T(8,128)S(1)}, u32[]{:S(2)}, u32[]{:S(2)}) collective-permute-start(f32[44,8,128]{2,1,0:T(8,128)S(1)} %get-tuple-element.53), channel_id=1, source_target_pairs={{0,4},{1,5},{2,6},{3,7},{4,0},{5,1},{6,2},{7,3},{8,12},{9,13},{10,... | collective-permute-start | bytes 540680 | tf_op jit(solution)/shard_map/ppermute | solution.py:504
  6.2 1.5 %collective-permute-start.2 = (f32[44,8,128]{2,1,0:T(8,128)S(1)}, f32[44,8,128]{2,1,0:T(8,128)S(1)}, u32[]{:S(2)}, u32[]{:S(2)}) collective-permute-start(f32[44,8,128]{2,1,0:T(8,128)S(1)} %get-tuple-element.54), channel_id=1, source_target_pairs={{0,2},{1,3},{2,0},{3,1},{4,6},{5,7},{6,4},{7,5},{8,10},{9,11},{10,... | collective-permute-start | bytes 540680 | tf_op jit(solution)/shard_map/ppermute | solution.py:504
  8.0 2.9 %collective-permute-start.5 = (f32[44,8,128]{2,1,0:T(8,128)S(1)}, f32[44,8,128]{2,1,0:T(8,128)S(1)}, u32[]{:S(2)}, u32[]{:S(2)}) collective-permute-start(f32[44,8,128]{2,1,0:T(8,128)S(1)} %get-tuple-element.57), channel_id=1, source_target_pairs={{0,6},{1,7},{2,4},{3,5},{4,2},{5,3},{6,0},{7,1},{8,14},{9,15},{10,... | collective-permute-start | bytes 540680 | tf_op jit(solution)/shard_map/ppermute | solution.py:504
  11.6 1.7 %collective-permute-start.6 = (f32[44,8,128]{2,1,0:T(8,128)S(1)}, f32[44,8,128]{2,1,0:T(8,128)S(1)}, u32[]{:S(2)}, u32[]{:S(2)}) collective-permute-start(f32[44,8,128]{2,1,0:T(8,128)S(1)} %get-tuple-element.58), channel_id=1, source_target_pairs={{0,7},{1,6},{2,5},{3,4},{4,3},{5,2},{6,1},{7,0},{8,15},{9,14},{10,... | collective-permute-start | bytes 540680 | tf_op jit(solution)/shard_map/ppermute | solution.py:504
  13.3 4.9 %all-to-all-start = ((f32[32,2,8,128]{3,2,1,0:T(8,128)}), f32[32,2,8,128]{3,2,1,0:T(8,128)S(1)}, u32[]{:S(2)}, u32[]{:S(2)}) async-start(f32[32,2,8,128]{3,2,1,0:T(8,128)} %get-tuple-element.49), calls=%async_computation | async-start | bytes 524288 | tf_op jit(solution)/shard_map/all_to_all | solution.py:524
  18.2 2.6 %collective-permute-done.5.refs_6_ = f32[44,8,128]{2,1,0:T(8,128)S(1)} collective-permute-done((f32[44,8,128]{2,1,0:T(8,128)S(1)}, f32[44,8,128]{2,1,0:T(8,128)S(1)}, u32[]{:S(2)}, u32[]{:S(2)}) %collective-permute-start.5) | collective-permute-done | bytes 180256 | tf_op jit(solution)/shard_map/ppermute | solution.py:504
  20.8 4.9 %collective-permute-done.6.refs_7_ = f32[44,8,128]{2,1,0:T(8,128)S(1)} collective-permute-done((f32[44,8,128]{2,1,0:T(8,128)S(1)}, f32[44,8,128]{2,1,0:T(8,128)S(1)}, u32[]{:S(2)}, u32[]{:S(2)}) %collective-permute-start.6) | collective-permute-done | bytes 180256 | tf_op jit(solution)/shard_map/ppermute | solution.py:504
  25.9 1.8 %collective-permute-start.9 = (f32[4,24,8,128]{3,2,1,0:T(8,128)S(1)}, f32[4,24,8,128]{3,2,1,0:T(8,128)S(1)}, u32[]{:S(2)}, u32[]{:S(2)}) collective-permute-start(f32[4,24,8,128]{3,2,1,0:T(8,128)S(1)} %get-tuple-element.62.refs_0_), channel_id=1, source_target_pairs={{0,8},{1,9},{2,10},{3,11},{4,12},{5,13},{6,14},{7,15},{8,0},{9,1},... | collective-permute-start | bytes 1179656 | tf_op jit(solution)/shard_map/ppermute | solution.py:500
  28.4 4.4 %collective-permute-start.7 = (f32[4,20,8,128]{3,2,1,0:T(8,128)S(1)}, f32[4,20,8,128]{3,2,1,0:T(8,128)S(1)}, u32[]{:S(2)}, u32[]{:S(2)}) collective-permute-start(f32[4,20,8,128]{3,2,1,0:T(8,128)S(1)} %get-tuple-element.59.refs_0_), channel_id=1, source_target_pairs={{0,8},{1,9},{2,10},{3,11},{4,12},{5,13},{6,14},{7,15},{8,0},{9,1},... | collective-permute-start | bytes 983048 | tf_op jit(solution)/shard_map/ppermute | solution.py:500
  33.5 5.1 %forcing.1 = (f32[16,8,128]{2,1,0:T(8,128)S(1)}, f32[16,8,128]{2,1,0:T(8,128)S(1)}) custom-call(f32[32,2,8,128]{3,2,1,0:T(8,128)S(1)} %all-to-all-done.parts), custom_call_target="tpu_custom_call" | custom-call | bytes 15000000 | tf_op jit(solution)/shard_map/forcing/pallas_call | solution.py:507
  38.7 3.8 %first_step_0.1 = (f32[5,4,32,128]{3,2,1,0:T(8,128)S(1)}, f32[5,4,32,128]{3,2,1,0:T(8,128)S(1)}, f32[16,32,128]{2,1,0:T(8,128)S(1)}) custom-call(f32[3]{0:T(128)S(1)} %copy-done, f32[5]{0:T(128)S(1)} %copy-done.1, f32[16,8,128]{2,1,0:T(8,128)S(1)} %get-tuple-element.61.wall_ref, f32[4,24,8,128]{3,2,1,0:T(8,128)S(1)} %get-tuple-element.62.refs_0_, ...), custom_call_target="tpu_custom_call" | custom-call | bytes 15000000 | tf_op jit(solution)/shard_map/first_step_0/pallas_call | solution.py:507
  42.4 4.1 %collective-permute-start.11 = (f32[5,4,32,128]{3,2,1,0:T(8,128)S(1)}, f32[5,4,32,128]{3,2,1,0:T(8,128)S(1)}, u32[]{:S(2)}, u32[]{:S(2)}) collective-permute-start(f32[5,4,32,128]{3,2,1,0:T(8,128)S(1)} %get-tuple-element.65.refs_5_.refs_0_), channel_id=1, source_target_pairs={{0,8},{1,9},{2,10},{3,11},{4,12},{5,13},{6,14},{7,15},{8,0},{9,1},... | collective-permute-start | bytes 983048 | tf_op jit(solution)/shard_map/ppermute | solution.py:500
  47.3 4.0 %first_step_1.1 = (f32[5,4,32,128]{3,2,1,0:T(8,128)S(1)}, f32[5,4,32,128]{3,2,1,0:T(8,128)S(1)}, f32[4,2,5,4,8,128]{5,4,3,2,1,0:T(8,128)S(1)}, f32[4,2,5,4,8,128]{5,4,3,2,1,0:T(8,128)S(1)}) custom-call(f32[3]{0:T(128)S(1)} %copy-done, f32[5]{0:T(128)S(1)} %copy-done.1, f32[16,8,128]{2,1,0:T(8,128)S(1)} %get-tuple-element.50.wall_ref, ...), custom_call_target="tpu_custom_call" | custom-call | bytes 15000000 | tf_op jit(solution)/shard_map/first_step_1/pallas_call | solution.py:507
  51.2 3.2 %collective-permute-done.11.refs_2_ = f32[5,4,32,128]{3,2,1,0:T(8,128)S(1)} collective-permute-done((f32[5,4,32,128]{3,2,1,0:T(8,128)S(1)}, f32[5,4,32,128]{3,2,1,0:T(8,128)S(1)}, u32[]{:S(2)}, u32[]{:S(2)}) %collective-permute-start.11) | collective-permute-done | bytes 327712 | tf_op jit(solution)/shard_map/ppermute | solution.py:500
  54.4 3.6 %collective-permute-start.14 = (f32[5,4,32,128]{3,2,1,0:T(8,128)S(1)}, f32[5,4,32,128]{3,2,1,0:T(8,128)S(1)}, u32[]{:S(2)}, u32[]{:S(2)}) collective-permute-start(f32[5,4,32,128]{3,2,1,0:T(8,128)S(1)} %get-tuple-element.70.refs_0_), channel_id=1, source_target_pairs={{0,8},{1,9},{2,10},{3,11},{4,12},{5,13},{6,14},{7,15},{8,0},{9,1},... | collective-permute-start | bytes 983048 | tf_op jit(solution)/shard_map/ppermute | solution.py:500
  58.8 1.6 %collective-permute-start.16 = (f32[2,2,5,4,8,128]{5,4,3,2,1,0:T(8,128)S(1)}, f32[2,2,5,4,8,128]{5,4,3,2,1,0:T(8,128)S(1)}, u32[]{:S(2)}, u32[]{:S(2)}) collective-permute-start(f32[2,2,5,4,8,128]{5,4,3,2,1,0:T(8,128)S(1)} %get-tuple-element.76), channel_id=1, source_target_pairs={{0,2},{1,3},{2,0},{3,1},{4,6},{5,7},{6,4},{7,5},{8,10},{9,11},{10,... | collective-permute-start | bytes 983048 | tf_op jit(solution)/shard_map/ppermute | solution.py:574
  60.4 1.4 %collective-permute-start.17 = (f32[2,2,5,4,8,128]{5,4,3,2,1,0:T(8,128)S(1)}, f32[2,2,5,4,8,128]{5,4,3,2,1,0:T(8,128)S(1)}, u32[]{:S(2)}, u32[]{:S(2)}) collective-permute-start(f32[2,2,5,4,8,128]{5,4,3,2,1,0:T(8,128)S(1)} %get-tuple-element.77), channel_id=1, source_target_pairs={{0,4},{1,5},{2,6},{3,7},{4,0},{5,1},{6,2},{7,3},{8,12},{9,13},{10,... | collective-permute-start | bytes 983048 | tf_op jit(solution)/shard_map/ppermute | solution.py:574
  62.4 3.7 %second_step_0.1.refs_5_ = f32[5,8,32,128]{3,2,1,0:T(8,128)S(1)} custom-call(f32[3]{0:T(128)S(1)} %copy-done, f32[5]{0:T(128)S(1)} %copy-done.1, f32[16,8,128]{2,1,0:T(8,128)S(1)} %get-tuple-element.61.wall_ref, f32[5,4,32,128]{3,2,1,0:T(8,128)S(1)} %get-tuple-element.65.refs_5_.refs_0_, f32[5,4,32,128]{3,2,1,0:T(8,128)S(1)} %get-tuple-element.66.refs_6_.refs_1_, ...), custom_call_target="tpu_custom_call" | custom-call | bytes 15000000 | tf_op jit(solution)/shard_map/second_step_0/pallas_call | solution.py:507
  66.5 3.8 %second_step_1.1 = (f32[2,5,4,8,128]{4,3,2,1,0:T(8,128)S(1)}, f32[2,5,4,8,128]{4,3,2,1,0:T(8,128)S(1)}, f32[2,5,4,8,128]{4,3,2,1,0:T(8,128)S(1)}, f32[2,5,4,8,12...) custom-call(f32[3]{0:T(128)S(1)} %copy-done, ...), custom_call_target="tpu_custom_call" | custom-call | bytes 15000000 | tf_op jit(solution)/shard_map/second_step_1/pallas_call | solution.py:507
  70.4 1.7 %collective-permute-start.20 = (f32[2,5,4,8,128]{4,3,2,1,0:T(8,128)S(1)}, f32[2,5,4,8,128]{4,3,2,1,0:T(8,128)S(1)}, u32[]{:S(2)}, u32[]{:S(2)}) collective-permute-start(f32[2,5,4,8,128]{4,3,2,1,0:T(8,128)S(1)} %get-tuple-element.84), channel_id=1, source_target_pairs={{0,4},{1,5},{2,6},{3,7},{4,0},{5,1},{6,2},{7,3},{8,12},{9,13},{10,... | collective-permute-start | bytes 491528 | tf_op jit(solution)/shard_map/ppermute | solution.py:504
  72.1 1.3 %collective-permute-start.21 = (f32[2,5,4,8,128]{4,3,2,1,0:T(8,128)S(1)}, f32[2,5,4,8,128]{4,3,2,1,0:T(8,128)S(1)}, u32[]{:S(2)}, u32[]{:S(2)}) collective-permute-start(f32[2,5,4,8,128]{4,3,2,1,0:T(8,128)S(1)} %get-tuple-element.85), channel_id=1, source_target_pairs={{0,2},{1,3},{2,0},{3,1},{4,6},{5,7},{6,4},{7,5},{8,10},{9,11},{10,... | collective-permute-start | bytes 491528 | tf_op jit(solution)/shard_map/ppermute | solution.py:504
  73.3 3.6 %collective-permute-done.17.two = f32[2,2,5,4,8,128]{5,4,3,2,1,0:T(8,128)S(1)} collective-permute-done((f32[2,2,5,4,8,128]{5,4,3,2,1,0:T(8,128)S(1)}, f32[2,2,5,4,8,128]{5,4,3,2,1,0:T(8,128)S(1)}, u32[]{:S(2)}, u32[]{:S(2)}) %collective-permute-start.17) | collective-permute-done | bytes 327712 | tf_op jit(solution)/shard_map/ppermute | solution.py:574
  77.6 1.6 %collective-permute-start.23 = (f32[2,5,4,8,128]{4,3,2,1,0:T(8,128)S(1)}, f32[2,5,4,8,128]{4,3,2,1,0:T(8,128)S(1)}, u32[]{:S(2)}, u32[]{:S(2)}) collective-permute-start(f32[2,5,4,8,128]{4,3,2,1,0:T(8,128)S(1)} %get-tuple-element.87), channel_id=1, source_target_pairs={{0,3},{1,2},{2,1},{3,0},{4,7},{5,6},{6,5},{7,4},{8,11},{9,10},{10,... | collective-permute-start | bytes 491528 | tf_op jit(solution)/shard_map/ppermute | solution.py:504
  79.2 1.6 %collective-permute-start.24 = (f32[2,5,4,8,128]{4,3,2,1,0:T(8,128)S(1)}, f32[2,5,4,8,128]{4,3,2,1,0:T(8,128)S(1)}, u32[]{:S(2)}, u32[]{:S(2)}) collective-permute-start(f32[2,5,4,8,128]{4,3,2,1,0:T(8,128)S(1)} %get-tuple-element.88), channel_id=1, source_target_pairs={{0,6},{1,7},{2,4},{3,5},{4,2},{5,3},{6,0},{7,1},{8,14},{9,15},{10,... | collective-permute-start | bytes 491528 | tf_op jit(solution)/shard_map/ppermute | solution.py:504
  80.8 1.0 collective-permute-start.25
  82.8 1.0 collective-permute-done.22.refs_4_
  83.8 5.5 %collective-permute-done.24.refs_6_ = f32[2,5,4,8,128]{4,3,2,1,0:T(8,128)S(1)} collective-permute-done((f32[2,5,4,8,128]{4,3,2,1,0:T(8,128)S(1)}, f32[2,5,4,8,128]{4,3,2,1,0:T(8,128)S(1)}, u32[]{:S(2)}, u32[]{:S(2)}) %collective-permute-start.24) | collective-permute-done | bytes 163872 | tf_op jit(solution)/shard_map/ppermute | solution.py:504
  89.3 2.7 %collective-permute-done.25.refs_7_ = f32[2,5,4,8,128]{4,3,2,1,0:T(8,128)S(1)} collective-permute-done((f32[2,5,4,8,128]{4,3,2,1,0:T(8,128)S(1)}, f32[2,5,4,8,128]{4,3,2,1,0:T(8,128)S(1)}, u32[]{:S(2)}, u32[]{:S(2)}) %collective-permute-start.25) | collective-permute-done | bytes 163872 | tf_op jit(solution)/shard_map/ppermute | solution.py:504
  91.9 3.8 %gram.1 = (f32[5,16,4,8,128]{4,3,2,1,0:T(8,128)}, f32[32,8,128]{2,1,0:T(8,128)S(1)}) custom-call(bf16[40,48,512]{2,1,0:T(8,128)(2,1)S(1)} %split.1.first_parts, f32[2,5,4,8,128]{4,3,2,1,0:T(8,128)S(1)} %get-tuple-element.82.refs_0_, f32[2,5,4,8,128]{4,3,2,1,0:T(8,128)S(1)} %collective-permute-done.19.refs_1_, ...), custom_call_target="tpu_custom_call" | custom-call | tf_op jit(solution)/shard_map/gram/pallas_call | solution.py:608
  95.7 12.3 %all_to_all.10.parts_ref = f32[32,8,128]{2,1,0:T(8,128)S(1)} all-to-all(f32[32,8,128]{2,1,0:T(8,128)S(1)} %get-tuple-element.91), channel_id=1, replica_groups=mesh['gx'=8,'gy'=4] {'gx','gy'}, dimensions={0} | all-to-all | bytes 262144 | tf_op jit(solution)/shard_map/all_to_all | solution.py:620
  108.0 3.3 %factor.1 = f32[32,32]{1,0:T(8,128)} custom-call(f32[32,8,128]{2,1,0:T(8,128)S(1)} %all_to_all.10.parts_ref), custom_call_target="tpu_custom_call" | custom-call | tf_op jit(solution)/shard_map/factor/pallas_call | solution.py:621
  (38 shorter events, 7.2 us)
Async XLA Ops:
  3.1 35.6 %copy-start = (f32[3]{0:T(128)S(1)}, f32[3]{0:T(128)}, u32[]{:S(2)}) copy-start(f32[3]{0:T(128)} %vel_ref.7) | copy-start | bytes 40
  3.1 35.6 %copy-start.1 = (f32[5]{0:T(128)S(1)}, f32[5]{0:T(128)}, u32[]{:S(2)}) copy-start(f32[5]{0:T(128)} %vec_ref.7) | copy-start | bytes 64
  3.1 4.9 %collective-permute-start = (f32[44,8,128]{2,1,0:T(8,128)S(1)}, f32[44,8,128]{2,1,0:T(8,128)S(1)}, u32[]{:S(2)}, u32[]{:S(2)}) collective-permute-start(f32[44,8,128]{2,1,0:T(8,128)S(1)} %get-tuple-element.48), channel_id=1, source_target_pairs={{0,1},{1,0},{2,3},{3,2},{4,5},{5,4},{6,7},{7,6},{8,9},{9,8},{10,11... | collective-permute-start | bytes 540680 | tf_op jit(solution)/shard_map/ppermute | solution.py:504
  3.6 8.0 %collective-permute-start.1 = (f32[44,8,128]{2,1,0:T(8,128)S(1)}, f32[44,8,128]{2,1,0:T(8,128)S(1)}, u32[]{:S(2)}, u32[]{:S(2)}) collective-permute-start(f32[44,8,128]{2,1,0:T(8,128)S(1)} %get-tuple-element.53), channel_id=1, source_target_pairs={{0,4},{1,5},{2,6},{3,7},{4,0},{5,1},{6,2},{7,3},{8,12},{9,13},{10,... | collective-permute-start | bytes 540680 | tf_op jit(solution)/shard_map/ppermute | solution.py:504
  6.2 12.0 %collective-permute-start.2 = (f32[44,8,128]{2,1,0:T(8,128)S(1)}, f32[44,8,128]{2,1,0:T(8,128)S(1)}, u32[]{:S(2)}, u32[]{:S(2)}) collective-permute-start(f32[44,8,128]{2,1,0:T(8,128)S(1)} %get-tuple-element.54), channel_id=1, source_target_pairs={{0,2},{1,3},{2,0},{3,1},{4,6},{5,7},{6,4},{7,5},{8,10},{9,11},{10,... | collective-permute-start | bytes 540680 | tf_op jit(solution)/shard_map/ppermute | solution.py:504
  7.7 10.5 %collective-permute-start.3 = (f32[44,8,128]{2,1,0:T(8,128)S(1)}, f32[44,8,128]{2,1,0:T(8,128)S(1)}, u32[]{:S(2)}, u32[]{:S(2)}) collective-permute-start(f32[44,8,128]{2,1,0:T(8,128)S(1)} %get-tuple-element.55), channel_id=1, source_target_pairs={{0,5},{1,4},{2,7},{3,6},{4,1},{5,0},{6,3},{7,2},{8,13},{9,12},{10,... | collective-permute-start | bytes 540680 | tf_op jit(solution)/shard_map/ppermute | solution.py:504
  7.7 10.5 %collective-permute-start.4 = (f32[44,8,128]{2,1,0:T(8,128)S(1)}, f32[44,8,128]{2,1,0:T(8,128)S(1)}, u32[]{:S(2)}, u32[]{:S(2)}) collective-permute-start(f32[44,8,128]{2,1,0:T(8,128)S(1)} %get-tuple-element.56), channel_id=1, source_target_pairs={{0,3},{1,2},{2,1},{3,0},{4,7},{5,6},{6,5},{7,4},{8,11},{9,10},{10,... | collective-permute-start | bytes 540680 | tf_op jit(solution)/shard_map/ppermute | solution.py:504
  8.0 12.8 %collective-permute-start.5 = (f32[44,8,128]{2,1,0:T(8,128)S(1)}, f32[44,8,128]{2,1,0:T(8,128)S(1)}, u32[]{:S(2)}, u32[]{:S(2)}) collective-permute-start(f32[44,8,128]{2,1,0:T(8,128)S(1)} %get-tuple-element.57), channel_id=1, source_target_pairs={{0,6},{1,7},{2,4},{3,5},{4,2},{5,3},{6,0},{7,1},{8,14},{9,15},{10,... | collective-permute-start | bytes 540680 | tf_op jit(solution)/shard_map/ppermute | solution.py:504
  11.6 14.1 %collective-permute-start.6 = (f32[44,8,128]{2,1,0:T(8,128)S(1)}, f32[44,8,128]{2,1,0:T(8,128)S(1)}, u32[]{:S(2)}, u32[]{:S(2)}) collective-permute-start(f32[44,8,128]{2,1,0:T(8,128)S(1)} %get-tuple-element.58), channel_id=1, source_target_pairs={{0,7},{1,6},{2,5},{3,4},{4,3},{5,2},{6,1},{7,0},{8,15},{9,14},{10,... | collective-permute-start | bytes 540680 | tf_op jit(solution)/shard_map/ppermute | solution.py:504
  13.3 20.2 %all-to-all-start = ((f32[32,2,8,128]{3,2,1,0:T(8,128)}), f32[32,2,8,128]{3,2,1,0:T(8,128)S(1)}, u32[]{:S(2)}, u32[]{:S(2)}) async-start(f32[32,2,8,128]{3,2,1,0:T(8,128)} %get-tuple-element.49), calls=%async_computation | async-start | bytes 524288 | tf_op jit(solution)/shard_map/all_to_all | solution.py:524
  25.9 12.7 %collective-permute-start.9 = (f32[4,24,8,128]{3,2,1,0:T(8,128)S(1)}, f32[4,24,8,128]{3,2,1,0:T(8,128)S(1)}, u32[]{:S(2)}, u32[]{:S(2)}) collective-permute-start(f32[4,24,8,128]{3,2,1,0:T(8,128)S(1)} %get-tuple-element.62.refs_0_), channel_id=1, source_target_pairs={{0,8},{1,9},{2,10},{3,11},{4,12},{5,13},{6,14},{7,15},{8,0},{9,1},... | collective-permute-start | bytes 1179656 | tf_op jit(solution)/shard_map/ppermute | solution.py:500
  27.8 10.9 %collective-permute-start.10 = (f32[4,24,8,128]{3,2,1,0:T(8,128)S(1)}, f32[4,24,8,128]{3,2,1,0:T(8,128)S(1)}, u32[]{:S(2)}, u32[]{:S(2)}) collective-permute-start(f32[4,24,8,128]{3,2,1,0:T(8,128)S(1)} %get-tuple-element.63.refs_1_), channel_id=1, source_target_pairs={{8,16},{9,17},{10,18},{11,19},{12,20},{13,21},{14,22},{15,23},{16,... | collective-permute-start | bytes 1179656 | tf_op jit(solution)/shard_map/ppermute | solution.py:500
  28.4 18.8 %collective-permute-start.7 = (f32[4,20,8,128]{3,2,1,0:T(8,128)S(1)}, f32[4,20,8,128]{3,2,1,0:T(8,128)S(1)}, u32[]{:S(2)}, u32[]{:S(2)}) collective-permute-start(f32[4,20,8,128]{3,2,1,0:T(8,128)S(1)} %get-tuple-element.59.refs_0_), channel_id=1, source_target_pairs={{0,8},{1,9},{2,10},{3,11},{4,12},{5,13},{6,14},{7,15},{8,0},{9,1},... | collective-permute-start | bytes 983048 | tf_op jit(solution)/shard_map/ppermute | solution.py:500
  32.8 14.4 %collective-permute-start.8 = (f32[4,20,8,128]{3,2,1,0:T(8,128)S(1)}, f32[4,20,8,128]{3,2,1,0:T(8,128)S(1)}, u32[]{:S(2)}, u32[]{:S(2)}) collective-permute-start(f32[4,20,8,128]{3,2,1,0:T(8,128)S(1)} %get-tuple-element.60.refs_1_), channel_id=1, source_target_pairs={{8,16},{9,17},{10,18},{11,19},{12,20},{13,21},{14,22},{15,23},{16,... | collective-permute-start | bytes 983048 | tf_op jit(solution)/shard_map/ppermute | solution.py:500
  42.4 12.0 %collective-permute-start.11 = (f32[5,4,32,128]{3,2,1,0:T(8,128)S(1)}, f32[5,4,32,128]{3,2,1,0:T(8,128)S(1)}, u32[]{:S(2)}, u32[]{:S(2)}) collective-permute-start(f32[5,4,32,128]{3,2,1,0:T(8,128)S(1)} %get-tuple-element.65.refs_5_.refs_0_), channel_id=1, source_target_pairs={{0,8},{1,9},{2,10},{3,11},{4,12},{5,13},{6,14},{7,15},{8,0},{9,1},... | collective-permute-start | bytes 983048 | tf_op jit(solution)/shard_map/ppermute | solution.py:500
  46.6 7.9 %collective-permute-start.12 = (f32[5,4,32,128]{3,2,1,0:T(8,128)S(1)}, f32[5,4,32,128]{3,2,1,0:T(8,128)S(1)}, u32[]{:S(2)}, u32[]{:S(2)}) collective-permute-start(f32[5,4,32,128]{3,2,1,0:T(8,128)S(1)} %get-tuple-element.66.refs_6_.refs_1_), channel_id=1, source_target_pairs={{8,16},{9,17},{10,18},{11,19},{12,20},{13,21},{14,22},{15,23},{16,... | collective-permute-start | bytes 983048 | tf_op jit(solution)/shard_map/ppermute | solution.py:500
  54.4 4.3 %collective-permute-start.13 = (f32[4,2,5,4,8,128]{5,4,3,2,1,0:T(8,128)S(1)}, f32[4,2,5,4,8,128]{5,4,3,2,1,0:T(8,128)S(1)}, u32[]{:S(2)}, u32[]{:S(2)}) collective-permute-start(f32[4,2,5,4,8,128]{5,4,3,2,1,0:T(8,128)S(1)} %get-tuple-element.69), channel_id=1, source_target_pairs={{0,1},{1,0},{2,3},{3,2},{4,5},{5,4},{6,7},{7,6},{8,9},{9,8},{10,11... | collective-permute-start | bytes 1966088 | tf_op jit(solution)/shard_map/ppermute | solution.py:566
  54.4 12.0 %collective-permute-start.14 = (f32[5,4,32,128]{3,2,1,0:T(8,128)S(1)}, f32[5,4,32,128]{3,2,1,0:T(8,128)S(1)}, u32[]{:S(2)}, u32[]{:S(2)}) collective-permute-start(f32[5,4,32,128]{3,2,1,0:T(8,128)S(1)} %get-tuple-element.70.refs_0_), channel_id=1, source_target_pairs={{0,8},{1,9},{2,10},{3,11},{4,12},{5,13},{6,14},{7,15},{8,0},{9,1},... | collective-permute-start | bytes 983048 | tf_op jit(solution)/shard_map/ppermute | solution.py:500
  58.1 8.4 %collective-permute-start.15 = (f32[5,4,32,128]{3,2,1,0:T(8,128)S(1)}, f32[5,4,32,128]{3,2,1,0:T(8,128)S(1)}, u32[]{:S(2)}, u32[]{:S(2)}) collective-permute-start(f32[5,4,32,128]{3,2,1,0:T(8,128)S(1)} %get-tuple-element.71.refs_1_), channel_id=1, source_target_pairs={{8,16},{9,17},{10,18},{11,19},{12,20},{13,21},{14,22},{15,23},{16,... | collective-permute-start | bytes 983048 | tf_op jit(solution)/shard_map/ppermute | solution.py:500
  58.8 13.2 %collective-permute-start.16 = (f32[2,2,5,4,8,128]{5,4,3,2,1,0:T(8,128)S(1)}, f32[2,2,5,4,8,128]{5,4,3,2,1,0:T(8,128)S(1)}, u32[]{:S(2)}, u32[]{:S(2)}) collective-permute-start(f32[2,2,5,4,8,128]{5,4,3,2,1,0:T(8,128)S(1)} %get-tuple-element.76), channel_id=1, source_target_pairs={{0,2},{1,3},{2,0},{3,1},{4,6},{5,7},{6,4},{7,5},{8,10},{9,11},{10,... | collective-permute-start | bytes 983048 | tf_op jit(solution)/shard_map/ppermute | solution.py:574
  60.4 16.5 %collective-permute-start.17 = (f32[2,2,5,4,8,128]{5,4,3,2,1,0:T(8,128)S(1)}, f32[2,2,5,4,8,128]{5,4,3,2,1,0:T(8,128)S(1)}, u32[]{:S(2)}, u32[]{:S(2)}) collective-permute-start(f32[2,2,5,4,8,128]{5,4,3,2,1,0:T(8,128)S(1)} %get-tuple-element.77), channel_id=1, source_target_pairs={{0,4},{1,5},{2,6},{3,7},{4,0},{5,1},{6,2},{7,3},{8,12},{9,13},{10,... | collective-permute-start | bytes 983048 | tf_op jit(solution)/shard_map/ppermute | solution.py:574
  61.8 15.8 %collective-permute-start.18 = (f32[2,2,5,4,8,128]{5,4,3,2,1,0:T(8,128)S(1)}, f32[2,2,5,4,8,128]{5,4,3,2,1,0:T(8,128)S(1)}, u32[]{:S(2)}, u32[]{:S(2)}) collective-permute-start(f32[2,2,5,4,8,128]{5,4,3,2,1,0:T(8,128)S(1)} %get-tuple-element.78), channel_id=1, source_target_pairs={{0,6},{1,7},{2,4},{3,5},{4,2},{5,3},{6,0},{7,1},{8,14},{9,15},{10,... | collective-permute-start | bytes 983048 | tf_op jit(solution)/shard_map/ppermute | solution.py:574
  70.3 8.9 %collective-permute-start.19 = (f32[2,5,4,8,128]{4,3,2,1,0:T(8,128)S(1)}, f32[2,5,4,8,128]{4,3,2,1,0:T(8,128)S(1)}, u32[]{:S(2)}, u32[]{:S(2)}) collective-permute-start(f32[2,5,4,8,128]{4,3,2,1,0:T(8,128)S(1)} %get-tuple-element.83), channel_id=1, source_target_pairs={{0,1},{1,0},{2,3},{3,2},{4,5},{5,4},{6,7},{7,6},{8,9},{9,8},{10,11... | collective-permute-start | bytes 491528 | tf_op jit(solution)/shard_map/ppermute | solution.py:504
  70.4 10.4 %collective-permute-start.20 = (f32[2,5,4,8,128]{4,3,2,1,0:T(8,128)S(1)}, f32[2,5,4,8,128]{4,3,2,1,0:T(8,128)S(1)}, u32[]{:S(2)}, u32[]{:S(2)}) collective-permute-start(f32[2,5,4,8,128]{4,3,2,1,0:T(8,128)S(1)} %get-tuple-element.84), channel_id=1, source_target_pairs={{0,4},{1,5},{2,6},{3,7},{4,0},{5,1},{6,2},{7,3},{8,12},{9,13},{10,... | collective-permute-start | bytes 491528 | tf_op jit(solution)/shard_map/ppermute | solution.py:504
  72.1 10.7 %collective-permute-start.21 = (f32[2,5,4,8,128]{4,3,2,1,0:T(8,128)S(1)}, f32[2,5,4,8,128]{4,3,2,1,0:T(8,128)S(1)}, u32[]{:S(2)}, u32[]{:S(2)}) collective-permute-start(f32[2,5,4,8,128]{4,3,2,1,0:T(8,128)S(1)} %get-tuple-element.85), channel_id=1, source_target_pairs={{0,2},{1,3},{2,0},{3,1},{4,6},{5,7},{6,4},{7,5},{8,10},{9,11},{10,... | collective-permute-start | bytes 491528 | tf_op jit(solution)/shard_map/ppermute | solution.py:504
  77.6 6.2 %collective-permute-start.22 = (f32[2,5,4,8,128]{4,3,2,1,0:T(8,128)S(1)}, f32[2,5,4,8,128]{4,3,2,1,0:T(8,128)S(1)}, u32[]{:S(2)}, u32[]{:S(2)}) collective-permute-start(f32[2,5,4,8,128]{4,3,2,1,0:T(8,128)S(1)} %get-tuple-element.86), channel_id=1, source_target_pairs={{0,5},{1,4},{2,7},{3,6},{4,1},{5,0},{6,3},{7,2},{8,13},{9,12},{10,... | collective-permute-start | bytes 491528 | tf_op jit(solution)/shard_map/ppermute | solution.py:504
  77.6 6.2 %collective-permute-start.23 = (f32[2,5,4,8,128]{4,3,2,1,0:T(8,128)S(1)}, f32[2,5,4,8,128]{4,3,2,1,0:T(8,128)S(1)}, u32[]{:S(2)}, u32[]{:S(2)}) collective-permute-start(f32[2,5,4,8,128]{4,3,2,1,0:T(8,128)S(1)} %get-tuple-element.87), channel_id=1, source_target_pairs={{0,3},{1,2},{2,1},{3,0},{4,7},{5,6},{6,5},{7,4},{8,11},{9,10},{10,... | collective-permute-start | bytes 491528 | tf_op jit(solution)/shard_map/ppermute | solution.py:504
  79.2 10.0 %collective-permute-start.24 = (f32[2,5,4,8,128]{4,3,2,1,0:T(8,128)S(1)}, f32[2,5,4,8,128]{4,3,2,1,0:T(8,128)S(1)}, u32[]{:S(2)}, u32[]{:S(2)}) collective-permute-start(f32[2,5,4,8,128]{4,3,2,1,0:T(8,128)S(1)} %get-tuple-element.88), channel_id=1, source_target_pairs={{0,6},{1,7},{2,4},{3,5},{4,2},{5,3},{6,0},{7,1},{8,14},{9,15},{10,... | collective-permute-start | bytes 491528 | tf_op jit(solution)/shard_map/ppermute | solution.py:504
  80.8 11.1 %collective-permute-start.25 = (f32[2,5,4,8,128]{4,3,2,1,0:T(8,128)S(1)}, f32[2,5,4,8,128]{4,3,2,1,0:T(8,128)S(1)}, u32[]{:S(2)}, u32[]{:S(2)}) collective-permute-start(f32[2,5,4,8,128]{4,3,2,1,0:T(8,128)S(1)} %get-tuple-element.89), channel_id=1, source_target_pairs={{0,7},{1,6},{2,5},{3,4},{4,3},{5,2},{6,1},{7,0},{8,15},{9,14},{10,... | collective-permute-start | bytes 491528 | tf_op jit(solution)/shard_map/ppermute | solution.py:504

commit v7 on v5

--- a/solution.py
+++ b/solution.py
@@ -176,7 +176,7 @@
     flux_low = jnp.where(not_low, flux, 0.0)
     tiles = range(4)
 
-    def plane(i, carry):
+    def plane(i):
         def load(ref, f, at):
             return [ref[f, at, pl.ds(ROWS * t, ROWS), :] for t in tiles]
 
@@ -217,13 +217,9 @@
         for f in range(FIELDS):
             for t in tiles:
                 dst[f, i, pl.ds(ROWS * t, ROWS), :] = new[f][t]
-        return carry
-
-    def two_planes(n, carry):
-        plane(low + 2 * n, carry)
-        return plane(low + 2 * n + 1, carry)
-
-    lax.fori_loop(0, (high - low) // 2, two_planes, 0)
+
+    for i in range(low, high):
+        plane(i)
 
 
 def run_step(step, base, va, vb, sponge_ref, wall_ref, vel, wall_vec, has_low, has_high):
@@ -587,9 +583,9 @@
         field,
         2,
     )
-    second = spread(second[:4]) + list(second[4:])
-    second[4:], first = lax.optimization_barrier((second[4:], first))
-    second[4:] = spread(second[4:], 4)
+    second = spread(second[:5]) + list(second[5:])
+    second[5:], first = lax.optimization_barrier((second[5:], first))
+    second[5:] = spread(second[5:], 5)
 
     row_count = FIELDS * DEEP * ROWS
     (parts,) = call(

time: 112 us -> 112 us (level)
  Pallas kernels: 33.9 us -> 31.3 us
  waiting for transfers between devices: 23.1 us -> 25.7 us
    pallas_call x8, Pallas kernels: 24.3 us -> 21.7 us  [call(): pl.pallas_call(kernel, out_shape=out_shape, in_specs=[SMEM] * scalars + [...]
  transfers between devices with their start and end apart: 27 -> 27, of which waited for: 9 -> 11; matrix products, arithmetic and copies ran while one was open for 0% -> 0% of each run, Pallas kernels for 22% -> 20%
where the time goes in v7:
time: 112 us; the launch traced here: 111 us
  starting transfers between devices  41.5 us (37%)
  Pallas kernels  31.3 us (28%)
  waiting for transfers between devices  25.7 us (23%)
  blocking collectives  12.1 us (11%)
    pallas_call x8, Pallas kernels, call(): pl.pallas_call(kernel, out_shape=out_shape, in_specs=[SMEM] * scalars + [...  21.7 us
    ppermute x14, waiting for transfers between devices, spread(): lax.ppermute(p, AXES, inside(d))  18 us
    ppermute x14, starting transfers between devices, spread(): lax.ppermute(p, AXES, inside(d))  16.4 us
    ppermute x4, starting transfers between devices, exchange(): lax.ppermute(a, AXES, swap(True))  14 us
    all_to_all x1, blocking collectives, local(): grams = lax.all_to_all(grams, AXES, 0, 0)  12.1 us
    all_to_all x1, starting transfers between devices, local(): wall = lax.all_to_all(wall, AXES, 0, 0)  4.87 us
    ppermute x3, waiting for transfers between devices, local(): lax.ppermute(m, AXES, inside(2 * e + 2))  4.27 us
    pallas_call x1, Pallas kernels, local(): pl.pallas_call(gram_kernel, out_shape=[jax.ShapeDtypeStruct(state_in.shap...  3.79 us
  transfers between devices with their start and end apart: 27, of which 11 were waited for; matrix products, arithmetic and copies ran while one was open for 0% of the time, Pallas kernels for 20%

profile of v7, /device:TPU:0, one launch (start us, length us, event | category | flops | bytes accessed | tf_op | source)
XLA Modules:
  0.0 111.4 jit_solution(14379426775633243806)
XLA Ops:
  0.6 2.4 %pack.1 = (f32[44,8,128]{2,1,0:T(8,128)S(1)}, f32[44,8,128]{2,1,0:T(8,128)S(1)}, f32[44,8,128]{2,1,0:T(8,128)S(1)}, f32[44,8,128]{2,1,0:T(8,128)S(1)}, f32[44,8,...) custom-call(f32[5,64,8,128]{3,2,1,0:T(8,128)} %bitcast.1, ...), custom_call_target="tpu_custom_call" | custom-call | bytes 6000000 | tf_op jit(solution)/shard_map/pack/pallas_call | solution.py:110
  3.6 2.6 %collective-permute-start.1 = (f32[44,8,128]{2,1,0:T(8,128)S(1)}, f32[44,8,128]{2,1,0:T(8,128)S(1)}, u32[]{:S(2)}, u32[]{:S(2)}) collective-permute-start(f32[44,8,128]{2,1,0:T(8,128)S(1)} %get-tuple-element.52), channel_id=1, source_target_pairs={{0,4},{1,5},{2,6},{3,7},{4,0},{5,1},{6,2},{7,3},{8,12},{9,13},{10,... | collective-permute-start | bytes 540680 | tf_op jit(solution)/shard_map/ppermute | solution.py:497
  6.2 1.5 %collective-permute-start.2 = (f32[44,8,128]{2,1,0:T(8,128)S(1)}, f32[44,8,128]{2,1,0:T(8,128)S(1)}, u32[]{:S(2)}, u32[]{:S(2)}) collective-permute-start(f32[44,8,128]{2,1,0:T(8,128)S(1)} %get-tuple-element.53), channel_id=1, source_target_pairs={{0,2},{1,3},{2,0},{3,1},{4,6},{5,7},{6,4},{7,5},{8,10},{9,11},{10,... | collective-permute-start | bytes 540680 | tf_op jit(solution)/shard_map/ppermute | solution.py:497
  8.0 2.9 %collective-permute-start.5 = (f32[44,8,128]{2,1,0:T(8,128)S(1)}, f32[44,8,128]{2,1,0:T(8,128)S(1)}, u32[]{:S(2)}, u32[]{:S(2)}) collective-permute-start(f32[44,8,128]{2,1,0:T(8,128)S(1)} %get-tuple-element.56), channel_id=1, source_target_pairs={{0,6},{1,7},{2,4},{3,5},{4,2},{5,3},{6,0},{7,1},{8,14},{9,15},{10,... | collective-permute-start | bytes 540680 | tf_op jit(solution)/shard_map/ppermute | solution.py:497
  11.6 1.7 %collective-permute-start.6 = (f32[44,8,128]{2,1,0:T(8,128)S(1)}, f32[44,8,128]{2,1,0:T(8,128)S(1)}, u32[]{:S(2)}, u32[]{:S(2)}) collective-permute-start(f32[44,8,128]{2,1,0:T(8,128)S(1)} %get-tuple-element.57), channel_id=1, source_target_pairs={{0,7},{1,6},{2,5},{3,4},{4,3},{5,2},{6,1},{7,0},{8,15},{9,14},{10,... | collective-permute-start | bytes 540680 | tf_op jit(solution)/shard_map/ppermute | solution.py:497
  13.3 4.9 %all-to-all-start = ((f32[32,2,8,128]{3,2,1,0:T(8,128)}), f32[32,2,8,128]{3,2,1,0:T(8,128)S(1)}, u32[]{:S(2)}, u32[]{:S(2)}) async-start(f32[32,2,8,128]{3,2,1,0:T(8,128)} %get-tuple-element.48), calls=%async_computation | async-start | bytes 524288 | tf_op jit(solution)/shard_map/all_to_all | solution.py:517
  18.2 2.6 %collective-permute-done.5.refs_6_ = f32[44,8,128]{2,1,0:T(8,128)S(1)} collective-permute-done((f32[44,8,128]{2,1,0:T(8,128)S(1)}, f32[44,8,128]{2,1,0:T(8,128)S(1)}, u32[]{:S(2)}, u32[]{:S(2)}) %collective-permute-start.5) | collective-permute-done | bytes 180256 | tf_op jit(solution)/shard_map/ppermute | solution.py:497
  20.8 4.9 %collective-permute-done.6.refs_7_ = f32[44,8,128]{2,1,0:T(8,128)S(1)} collective-permute-done((f32[44,8,128]{2,1,0:T(8,128)S(1)}, f32[44,8,128]{2,1,0:T(8,128)S(1)}, u32[]{:S(2)}, u32[]{:S(2)}) %collective-permute-start.6) | collective-permute-done | bytes 180256 | tf_op jit(solution)/shard_map/ppermute | solution.py:497
  25.9 1.8 %collective-permute-start.9 = (f32[4,24,8,128]{3,2,1,0:T(8,128)S(1)}, f32[4,24,8,128]{3,2,1,0:T(8,128)S(1)}, u32[]{:S(2)}, u32[]{:S(2)}) collective-permute-start(f32[4,24,8,128]{3,2,1,0:T(8,128)S(1)} %get-tuple-element.61.refs_0_), channel_id=1, source_target_pairs={{0,8},{1,9},{2,10},{3,11},{4,12},{5,13},{6,14},{7,15},{8,0},{9,1},... | collective-permute-start | bytes 1179656 | tf_op jit(solution)/shard_map/ppermute | solution.py:493
  28.4 4.4 %collective-permute-start.7 = (f32[4,20,8,128]{3,2,1,0:T(8,128)S(1)}, f32[4,20,8,128]{3,2,1,0:T(8,128)S(1)}, u32[]{:S(2)}, u32[]{:S(2)}) collective-permute-start(f32[4,20,8,128]{3,2,1,0:T(8,128)S(1)} %get-tuple-element.58.refs_0_), channel_id=1, source_target_pairs={{0,8},{1,9},{2,10},{3,11},{4,12},{5,13},{6,14},{7,15},{8,0},{9,1},... | collective-permute-start | bytes 983048 | tf_op jit(solution)/shard_map/ppermute | solution.py:493
  33.5 5.1 %forcing.1 = (f32[16,8,128]{2,1,0:T(8,128)S(1)}, f32[16,8,128]{2,1,0:T(8,128)S(1)}) custom-call(f32[32,2,8,128]{3,2,1,0:T(8,128)S(1)} %all-to-all-done.parts), custom_call_target="tpu_custom_call" | custom-call | bytes 15000000 | tf_op jit(solution)/shard_map/forcing/pallas_call | solution.py:500
  38.7 3.8 %first_step_0.1 = (f32[5,4,32,128]{3,2,1,0:T(8,128)S(1)}, f32[5,4,32,128]{3,2,1,0:T(8,128)S(1)}, f32[16,32,128]{2,1,0:T(8,128)S(1)}) custom-call(f32[3]{0:T(128)S(1)} %copy-done, f32[5]{0:T(128)S(1)} %copy-done.1, f32[16,8,128]{2,1,0:T(8,128)S(1)} %get-tuple-element.60.wall_ref, f32[4,24,8,128]{3,2,1,0:T(8,128)S(1)} %get-tuple-element.61.refs_0_, ...), custom_call_target="tpu_custom_call" | custom-call | bytes 15000000 | tf_op jit(solution)/shard_map/first_step_0/pallas_call | solution.py:500
  42.4 4.1 %collective-permute-start.11 = (f32[5,4,32,128]{3,2,1,0:T(8,128)S(1)}, f32[5,4,32,128]{3,2,1,0:T(8,128)S(1)}, u32[]{:S(2)}, u32[]{:S(2)}) collective-permute-start(f32[5,4,32,128]{3,2,1,0:T(8,128)S(1)} %get-tuple-element.64.refs_5_.refs_0_), channel_id=1, source_target_pairs={{0,8},{1,9},{2,10},{3,11},{4,12},{5,13},{6,14},{7,15},{8,0},{9,1},... | collective-permute-start | bytes 983048 | tf_op jit(solution)/shard_map/ppermute | solution.py:493
  47.3 4.0 %first_step_1.1 = (f32[5,4,32,128]{3,2,1,0:T(8,128)S(1)}, f32[5,4,32,128]{3,2,1,0:T(8,128)S(1)}, f32[4,2,5,4,8,128]{5,4,3,2,1,0:T(8,128)S(1)}, f32[4,2,5,4,8,128]{5,4,3,2,1,0:T(8,128)S(1)}) custom-call(f32[3]{0:T(128)S(1)} %copy-done, f32[5]{0:T(128)S(1)} %copy-done.1, f32[16,8,128]{2,1,0:T(8,128)S(1)} %get-tuple-element.49.wall_ref, ...), custom_call_target="tpu_custom_call" | custom-call | bytes 15000000 | tf_op jit(solution)/shard_map/first_step_1/pallas_call | solution.py:500
  51.3 3.2 %collective-permute-done.11.refs_2_ = f32[5,4,32,128]{3,2,1,0:T(8,128)S(1)} collective-permute-done((f32[5,4,32,128]{3,2,1,0:T(8,128)S(1)}, f32[5,4,32,128]{3,2,1,0:T(8,128)S(1)}, u32[]{:S(2)}, u32[]{:S(2)}) %collective-permute-start.11) | collective-permute-done | bytes 327712 | tf_op jit(solution)/shard_map/ppermute | solution.py:493
  54.4 3.6 %collective-permute-start.14 = (f32[5,4,32,128]{3,2,1,0:T(8,128)S(1)}, f32[5,4,32,128]{3,2,1,0:T(8,128)S(1)}, u32[]{:S(2)}, u32[]{:S(2)}) collective-permute-start(f32[5,4,32,128]{3,2,1,0:T(8,128)S(1)} %get-tuple-element.69.refs_0_), channel_id=1, source_target_pairs={{0,8},{1,9},{2,10},{3,11},{4,12},{5,13},{6,14},{7,15},{8,0},{9,1},... | collective-permute-start | bytes 983048 | tf_op jit(solution)/shard_map/ppermute | solution.py:493
  58.8 1.6 %collective-permute-start.16 = (f32[2,2,5,4,8,128]{5,4,3,2,1,0:T(8,128)S(1)}, f32[2,2,5,4,8,128]{5,4,3,2,1,0:T(8,128)S(1)}, u32[]{:S(2)}, u32[]{:S(2)}) collective-permute-start(f32[2,2,5,4,8,128]{5,4,3,2,1,0:T(8,128)S(1)} %get-tuple-element.74), channel_id=1, source_target_pairs={{0,2},{1,3},{2,0},{3,1},{4,6},{5,7},{6,4},{7,5},{8,10},{9,11},{10,... | collective-permute-start | bytes 983048 | tf_op jit(solution)/shard_map/ppermute | solution.py:567
  60.4 1.4 %collective-permute-start.17 = (f32[2,2,5,4,8,128]{5,4,3,2,1,0:T(8,128)S(1)}, f32[2,2,5,4,8,128]{5,4,3,2,1,0:T(8,128)S(1)}, u32[]{:S(2)}, u32[]{:S(2)}) collective-permute-start(f32[2,2,5,4,8,128]{5,4,3,2,1,0:T(8,128)S(1)} %get-tuple-element.75), channel_id=1, source_target_pairs={{0,4},{1,5},{2,6},{3,7},{4,0},{5,1},{6,2},{7,3},{8,12},{9,13},{10,... | collective-permute-start | bytes 983048 | tf_op jit(solution)/shard_map/ppermute | solution.py:567
  62.4 3.8 %second_step_0.1.refs_5_ = f32[5,8,32,128]{3,2,1,0:T(8,128)S(1)} custom-call(f32[3]{0:T(128)S(1)} %copy-done, f32[5]{0:T(128)S(1)} %copy-done.1, f32[16,8,128]{2,1,0:T(8,128)S(1)} %get-tuple-element.60.wall_ref, f32[5,4,32,128]{3,2,1,0:T(8,128)S(1)} %get-tuple-element.64.refs_5_.refs_0_, f32[5,4,32,128]{3,2,1,0:T(8,128)S(1)} %get-tuple-element.65.refs_6_.refs_1_, ...), custom_call_target="tpu_custom_call" | custom-call | bytes 15000000 | tf_op jit(solution)/shard_map/second_step_0/pallas_call | solution.py:500
  66.4 3.8 %second_step_1.1 = (f32[2,5,4,8,128]{4,3,2,1,0:T(8,128)S(1)}, f32[2,5,4,8,128]{4,3,2,1,0:T(8,128)S(1)}, f32[2,5,4,8,128]{4,3,2,1,0:T(8,128)S(1)}, f32[2,5,4,8,12...) custom-call(f32[3]{0:T(128)S(1)} %copy-done, ...), custom_call_target="tpu_custom_call" | custom-call | bytes 15000000 | tf_op jit(solution)/shard_map/second_step_1/pallas_call | solution.py:500
  70.3 1.7 %collective-permute-start.20 = (f32[2,5,4,8,128]{4,3,2,1,0:T(8,128)S(1)}, f32[2,5,4,8,128]{4,3,2,1,0:T(8,128)S(1)}, u32[]{:S(2)}, u32[]{:S(2)}) collective-permute-start(f32[2,5,4,8,128]{4,3,2,1,0:T(8,128)S(1)} %get-tuple-element.82), channel_id=1, source_target_pairs={{0,4},{1,5},{2,6},{3,7},{4,0},{5,1},{6,2},{7,3},{8,12},{9,13},{10,... | collective-permute-start | bytes 491528 | tf_op jit(solution)/shard_map/ppermute | solution.py:497
  72.0 1.3 %collective-permute-start.21 = (f32[2,5,4,8,128]{4,3,2,1,0:T(8,128)S(1)}, f32[2,5,4,8,128]{4,3,2,1,0:T(8,128)S(1)}, u32[]{:S(2)}, u32[]{:S(2)}) collective-permute-start(f32[2,5,4,8,128]{4,3,2,1,0:T(8,128)S(1)} %get-tuple-element.83), channel_id=1, source_target_pairs={{0,2},{1,3},{2,0},{3,1},{4,6},{5,7},{6,4},{7,5},{8,10},{9,11},{10,... | collective-permute-start | bytes 491528 | tf_op jit(solution)/shard_map/ppermute | solution.py:497
  73.3 3.6 %collective-permute-done.17.two = f32[2,2,5,4,8,128]{5,4,3,2,1,0:T(8,128)S(1)} collective-permute-done((f32[2,2,5,4,8,128]{5,4,3,2,1,0:T(8,128)S(1)}, f32[2,2,5,4,8,128]{5,4,3,2,1,0:T(8,128)S(1)}, u32[]{:S(2)}, u32[]{:S(2)}) %collective-permute-start.17) | collective-permute-done | bytes 327712 | tf_op jit(solution)/shard_map/ppermute | solution.py:567
  77.6 1.3 %collective-permute-start.23 = (f32[2,5,4,8,128]{4,3,2,1,0:T(8,128)S(1)}, f32[2,5,4,8,128]{4,3,2,1,0:T(8,128)S(1)}, u32[]{:S(2)}, u32[]{:S(2)}) collective-permute-start(f32[2,5,4,8,128]{4,3,2,1,0:T(8,128)S(1)} %get-tuple-element.85), channel_id=1, source_target_pairs={{0,3},{1,2},{2,1},{3,0},{4,7},{5,6},{6,5},{7,4},{8,11},{9,10},{10,... | collective-permute-start | bytes 491528 | tf_op jit(solution)/shard_map/ppermute | solution.py:497
  78.9 1.2 %collective-permute-start.24 = (f32[2,5,4,8,128]{4,3,2,1,0:T(8,128)S(1)}, f32[2,5,4,8,128]{4,3,2,1,0:T(8,128)S(1)}, u32[]{:S(2)}, u32[]{:S(2)}) collective-permute-start(f32[2,5,4,8,128]{4,3,2,1,0:T(8,128)S(1)} %get-tuple-element.86), channel_id=1, source_target_pairs={{0,6},{1,7},{2,4},{3,5},{4,2},{5,3},{6,0},{7,1},{8,14},{9,15},{10,... | collective-permute-start | bytes 491528 | tf_op jit(solution)/shard_map/ppermute | solution.py:497
  80.5 1.3 %collective-permute-start.25 = (f32[2,5,4,8,128]{4,3,2,1,0:T(8,128)S(1)}, f32[2,5,4,8,128]{4,3,2,1,0:T(8,128)S(1)}, u32[]{:S(2)}, u32[]{:S(2)}) collective-permute-start(f32[2,5,4,8,128]{4,3,2,1,0:T(8,128)S(1)} %get-tuple-element.87), channel_id=1, source_target_pairs={{0,7},{1,6},{2,5},{3,4},{4,3},{5,2},{6,1},{7,0},{8,15},{9,14},{10,... | collective-permute-start | bytes 491528 | tf_op jit(solution)/shard_map/ppermute | solution.py:497
  81.8 1.0 split.1.first_parts
  83.5 5.0 %collective-permute-done.24.refs_6_ = f32[2,5,4,8,128]{4,3,2,1,0:T(8,128)S(1)} collective-permute-done((f32[2,5,4,8,128]{4,3,2,1,0:T(8,128)S(1)}, f32[2,5,4,8,128]{4,3,2,1,0:T(8,128)S(1)}, u32[]{:S(2)}, u32[]{:S(2)}) %collective-permute-start.24) | collective-permute-done | bytes 163872 | tf_op jit(solution)/shard_map/ppermute | solution.py:497
  88.5 3.7 %collective-permute-done.25.refs_7_ = f32[2,5,4,8,128]{4,3,2,1,0:T(8,128)S(1)} collective-permute-done((f32[2,5,4,8,128]{4,3,2,1,0:T(8,128)S(1)}, f32[2,5,4,8,128]{4,3,2,1,0:T(8,128)S(1)}, u32[]{:S(2)}, u32[]{:S(2)}) %collective-permute-start.25) | collective-permute-done | bytes 163872 | tf_op jit(solution)/shard_map/ppermute | solution.py:497
  92.2 3.8 %gram.1 = (f32[5,16,4,8,128]{4,3,2,1,0:T(8,128)}, f32[32,8,128]{2,1,0:T(8,128)S(1)}) custom-call(bf16[40,48,512]{2,1,0:T(8,128)(2,1)S(1)} %split.1.first_parts, f32[2,5,4,8,128]{4,3,2,1,0:T(8,128)S(1)} %get-tuple-element.80.refs_0_, f32[2,5,4,8,128]{4,3,2,1,0:T(8,128)S(1)} %collective-permute-done.19.refs_1_, ...), custom_call_target="tpu_custom_call" | custom-call | tf_op jit(solution)/shard_map/gram/pallas_call | solution.py:601
  96.0 12.1 %all_to_all.10.parts_ref = f32[32,8,128]{2,1,0:T(8,128)S(1)} all-to-all(f32[32,8,128]{2,1,0:T(8,128)S(1)} %get-tuple-element.89), channel_id=1, replica_groups=mesh['gx'=8,'gy'=4] {'gx','gy'}, dimensions={0} | all-to-all | bytes 262144 | tf_op jit(solution)/shard_map/all_to_all | solution.py:613
  108.0 3.3 %factor.1 = f32[32,32]{1,0:T(8,128)} custom-call(f32[32,8,128]{2,1,0:T(8,128)S(1)} %all_to_all.10.parts_ref), custom_call_target="tpu_custom_call" | custom-call | tf_op jit(solution)/shard_map/factor/pallas_call | solution.py:614
  (38 shorter events, 7.2 us)
Async XLA Ops:
  3.1 35.6 %copy-start = (f32[3]{0:T(128)S(1)}, f32[3]{0:T(128)}, u32[]{:S(2)}) copy-start(f32[3]{0:T(128)} %vel_ref.7) | copy-start | bytes 40
  3.1 35.6 %copy-start.1 = (f32[5]{0:T(128)S(1)}, f32[5]{0:T(128)}, u32[]{:S(2)}) copy-start(f32[5]{0:T(128)} %vec_ref.7) | copy-start | bytes 64
  3.1 4.9 %collective-permute-start = (f32[44,8,128]{2,1,0:T(8,128)S(1)}, f32[44,8,128]{2,1,0:T(8,128)S(1)}, u32[]{:S(2)}, u32[]{:S(2)}) collective-permute-start(f32[44,8,128]{2,1,0:T(8,128)S(1)} %get-tuple-element.47), channel_id=1, source_target_pairs={{0,1},{1,0},{2,3},{3,2},{4,5},{5,4},{6,7},{7,6},{8,9},{9,8},{10,11... | collective-permute-start | bytes 540680 | tf_op jit(solution)/shard_map/ppermute | solution.py:497
  3.6 8.0 %collective-permute-start.1 = (f32[44,8,128]{2,1,0:T(8,128)S(1)}, f32[44,8,128]{2,1,0:T(8,128)S(1)}, u32[]{:S(2)}, u32[]{:S(2)}) collective-permute-start(f32[44,8,128]{2,1,0:T(8,128)S(1)} %get-tuple-element.52), channel_id=1, source_target_pairs={{0,4},{1,5},{2,6},{3,7},{4,0},{5,1},{6,2},{7,3},{8,12},{9,13},{10,... | collective-permute-start | bytes 540680 | tf_op jit(solution)/shard_map/ppermute | solution.py:497
  6.2 12.0 %collective-permute-start.2 = (f32[44,8,128]{2,1,0:T(8,128)S(1)}, f32[44,8,128]{2,1,0:T(8,128)S(1)}, u32[]{:S(2)}, u32[]{:S(2)}) collective-permute-start(f32[44,8,128]{2,1,0:T(8,128)S(1)} %get-tuple-element.53), channel_id=1, source_target_pairs={{0,2},{1,3},{2,0},{3,1},{4,6},{5,7},{6,4},{7,5},{8,10},{9,11},{10,... | collective-permute-start | bytes 540680 | tf_op jit(solution)/shard_map/ppermute | solution.py:497
  7.7 10.5 %collective-permute-start.3 = (f32[44,8,128]{2,1,0:T(8,128)S(1)}, f32[44,8,128]{2,1,0:T(8,128)S(1)}, u32[]{:S(2)}, u32[]{:S(2)}) collective-permute-start(f32[44,8,128]{2,1,0:T(8,128)S(1)} %get-tuple-element.54), channel_id=1, source_target_pairs={{0,5},{1,4},{2,7},{3,6},{4,1},{5,0},{6,3},{7,2},{8,13},{9,12},{10,... | collective-permute-start | bytes 540680 | tf_op jit(solution)/shard_map/ppermute | solution.py:497
  7.7 10.5 %collective-permute-start.4 = (f32[44,8,128]{2,1,0:T(8,128)S(1)}, f32[44,8,128]{2,1,0:T(8,128)S(1)}, u32[]{:S(2)}, u32[]{:S(2)}) collective-permute-start(f32[44,8,128]{2,1,0:T(8,128)S(1)} %get-tuple-element.55), channel_id=1, source_target_pairs={{0,3},{1,2},{2,1},{3,0},{4,7},{5,6},{6,5},{7,4},{8,11},{9,10},{10,... | collective-permute-start | bytes 540680 | tf_op jit(solution)/shard_map/ppermute | solution.py:497
  8.0 12.8 %collective-permute-start.5 = (f32[44,8,128]{2,1,0:T(8,128)S(1)}, f32[44,8,128]{2,1,0:T(8,128)S(1)}, u32[]{:S(2)}, u32[]{:S(2)}) collective-permute-start(f32[44,8,128]{2,1,0:T(8,128)S(1)} %get-tuple-element.56), channel_id=1, source_target_pairs={{0,6},{1,7},{2,4},{3,5},{4,2},{5,3},{6,0},{7,1},{8,14},{9,15},{10,... | collective-permute-start | bytes 540680 | tf_op jit(solution)/shard_map/ppermute | solution.py:497
  11.6 14.1 %collective-permute-start.6 = (f32[44,8,128]{2,1,0:T(8,128)S(1)}, f32[44,8,128]{2,1,0:T(8,128)S(1)}, u32[]{:S(2)}, u32[]{:S(2)}) collective-permute-start(f32[44,8,128]{2,1,0:T(8,128)S(1)} %get-tuple-element.57), channel_id=1, source_target_pairs={{0,7},{1,6},{2,5},{3,4},{4,3},{5,2},{6,1},{7,0},{8,15},{9,14},{10,... | collective-permute-start | bytes 540680 | tf_op jit(solution)/shard_map/ppermute | solution.py:497
  13.3 20.2 %all-to-all-start = ((f32[32,2,8,128]{3,2,1,0:T(8,128)}), f32[32,2,8,128]{3,2,1,0:T(8,128)S(1)}, u32[]{:S(2)}, u32[]{:S(2)}) async-start(f32[32,2,8,128]{3,2,1,0:T(8,128)} %get-tuple-element.48), calls=%async_computation | async-start | bytes 524288 | tf_op jit(solution)/shard_map/all_to_all | solution.py:517
  25.9 12.7 %collective-permute-start.9 = (f32[4,24,8,128]{3,2,1,0:T(8,128)S(1)}, f32[4,24,8,128]{3,2,1,0:T(8,128)S(1)}, u32[]{:S(2)}, u32[]{:S(2)}) collective-permute-start(f32[4,24,8,128]{3,2,1,0:T(8,128)S(1)} %get-tuple-element.61.refs_0_), channel_id=1, source_target_pairs={{0,8},{1,9},{2,10},{3,11},{4,12},{5,13},{6,14},{7,15},{8,0},{9,1},... | collective-permute-start | bytes 1179656 | tf_op jit(solution)/shard_map/ppermute | solution.py:493
  27.8 10.9 %collective-permute-start.10 = (f32[4,24,8,128]{3,2,1,0:T(8,128)S(1)}, f32[4,24,8,128]{3,2,1,0:T(8,128)S(1)}, u32[]{:S(2)}, u32[]{:S(2)}) collective-permute-start(f32[4,24,8,128]{3,2,1,0:T(8,128)S(1)} %get-tuple-element.62.refs_1_), channel_id=1, source_target_pairs={{8,16},{9,17},{10,18},{11,19},{12,20},{13,21},{14,22},{15,23},{16,... | collective-permute-start | bytes 1179656 | tf_op jit(solution)/shard_map/ppermute | solution.py:493
  28.4 18.8 %collective-permute-start.7 = (f32[4,20,8,128]{3,2,1,0:T(8,128)S(1)}, f32[4,20,8,128]{3,2,1,0:T(8,128)S(1)}, u32[]{:S(2)}, u32[]{:S(2)}) collective-permute-start(f32[4,20,8,128]{3,2,1,0:T(8,128)S(1)} %get-tuple-element.58.refs_0_), channel_id=1, source_target_pairs={{0,8},{1,9},{2,10},{3,11},{4,12},{5,13},{6,14},{7,15},{8,0},{9,1},... | collective-permute-start | bytes 983048 | tf_op jit(solution)/shard_map/ppermute | solution.py:493
  32.8 14.4 %collective-permute-start.8 = (f32[4,20,8,128]{3,2,1,0:T(8,128)S(1)}, f32[4,20,8,128]{3,2,1,0:T(8,128)S(1)}, u32[]{:S(2)}, u32[]{:S(2)}) collective-permute-start(f32[4,20,8,128]{3,2,1,0:T(8,128)S(1)} %get-tuple-element.59.refs_1_), channel_id=1, source_target_pairs={{8,16},{9,17},{10,18},{11,19},{12,20},{13,21},{14,22},{15,23},{16,... | collective-permute-start | bytes 983048 | tf_op jit(solution)/shard_map/ppermute | solution.py:493
  42.4 12.0 %collective-permute-start.11 = (f32[5,4,32,128]{3,2,1,0:T(8,128)S(1)}, f32[5,4,32,128]{3,2,1,0:T(8,128)S(1)}, u32[]{:S(2)}, u32[]{:S(2)}) collective-permute-start(f32[5,4,32,128]{3,2,1,0:T(8,128)S(1)} %get-tuple-element.64.refs_5_.refs_0_), channel_id=1, source_target_pairs={{0,8},{1,9},{2,10},{3,11},{4,12},{5,13},{6,14},{7,15},{8,0},{9,1},... | collective-permute-start | bytes 983048 | tf_op jit(solution)/shard_map/ppermute | solution.py:493
  46.6 7.9 %collective-permute-start.12 = (f32[5,4,32,128]{3,2,1,0:T(8,128)S(1)}, f32[5,4,32,128]{3,2,1,0:T(8,128)S(1)}, u32[]{:S(2)}, u32[]{:S(2)}) collective-permute-start(f32[5,4,32,128]{3,2,1,0:T(8,128)S(1)} %get-tuple-element.65.refs_6_.refs_1_), channel_id=1, source_target_pairs={{8,16},{9,17},{10,18},{11,19},{12,20},{13,21},{14,22},{15,23},{16,... | collective-permute-start | bytes 983048 | tf_op jit(solution)/shard_map/ppermute | solution.py:493
  54.4 4.3 %collective-permute-start.13 = (f32[4,2,5,4,8,128]{5,4,3,2,1,0:T(8,128)S(1)}, f32[4,2,5,4,8,128]{5,4,3,2,1,0:T(8,128)S(1)}, u32[]{:S(2)}, u32[]{:S(2)}) collective-permute-start(f32[4,2,5,4,8,128]{5,4,3,2,1,0:T(8,128)S(1)} %get-tuple-element.68), channel_id=1, source_target_pairs={{0,1},{1,0},{2,3},{3,2},{4,5},{5,4},{6,7},{7,6},{8,9},{9,8},{10,11... | collective-permute-start | bytes 1966088 | tf_op jit(solution)/shard_map/ppermute | solution.py:559
  54.4 12.0 %collective-permute-start.14 = (f32[5,4,32,128]{3,2,1,0:T(8,128)S(1)}, f32[5,4,32,128]{3,2,1,0:T(8,128)S(1)}, u32[]{:S(2)}, u32[]{:S(2)}) collective-permute-start(f32[5,4,32,128]{3,2,1,0:T(8,128)S(1)} %get-tuple-element.69.refs_0_), channel_id=1, source_target_pairs={{0,8},{1,9},{2,10},{3,11},{4,12},{5,13},{6,14},{7,15},{8,0},{9,1},... | collective-permute-start | bytes 983048 | tf_op jit(solution)/shard_map/ppermute | solution.py:493
  58.1 8.4 %collective-permute-start.15 = (f32[5,4,32,128]{3,2,1,0:T(8,128)S(1)}, f32[5,4,32,128]{3,2,1,0:T(8,128)S(1)}, u32[]{:S(2)}, u32[]{:S(2)}) collective-permute-start(f32[5,4,32,128]{3,2,1,0:T(8,128)S(1)} %get-tuple-element.70.refs_1_), channel_id=1, source_target_pairs={{8,16},{9,17},{10,18},{11,19},{12,20},{13,21},{14,22},{15,23},{16,... | collective-permute-start | bytes 983048 | tf_op jit(solution)/shard_map/ppermute | solution.py:493
  58.8 13.2 %collective-permute-start.16 = (f32[2,2,5,4,8,128]{5,4,3,2,1,0:T(8,128)S(1)}, f32[2,2,5,4,8,128]{5,4,3,2,1,0:T(8,128)S(1)}, u32[]{:S(2)}, u32[]{:S(2)}) collective-permute-start(f32[2,2,5,4,8,128]{5,4,3,2,1,0:T(8,128)S(1)} %get-tuple-element.74), channel_id=1, source_target_pairs={{0,2},{1,3},{2,0},{3,1},{4,6},{5,7},{6,4},{7,5},{8,10},{9,11},{10,... | collective-permute-start | bytes 983048 | tf_op jit(solution)/shard_map/ppermute | solution.py:567
  60.4 16.5 %collective-permute-start.17 = (f32[2,2,5,4,8,128]{5,4,3,2,1,0:T(8,128)S(1)}, f32[2,2,5,4,8,128]{5,4,3,2,1,0:T(8,128)S(1)}, u32[]{:S(2)}, u32[]{:S(2)}) collective-permute-start(f32[2,2,5,4,8,128]{5,4,3,2,1,0:T(8,128)S(1)} %get-tuple-element.75), channel_id=1, source_target_pairs={{0,4},{1,5},{2,6},{3,7},{4,0},{5,1},{6,2},{7,3},{8,12},{9,13},{10,... | collective-permute-start | bytes 983048 | tf_op jit(solution)/shard_map/ppermute | solution.py:567
  61.8 15.8 %collective-permute-start.18 = (f32[2,2,5,4,8,128]{5,4,3,2,1,0:T(8,128)S(1)}, f32[2,2,5,4,8,128]{5,4,3,2,1,0:T(8,128)S(1)}, u32[]{:S(2)}, u32[]{:S(2)}) collective-permute-start(f32[2,2,5,4,8,128]{5,4,3,2,1,0:T(8,128)S(1)} %get-tuple-element.76), channel_id=1, source_target_pairs={{0,6},{1,7},{2,4},{3,5},{4,2},{5,3},{6,0},{7,1},{8,14},{9,15},{10,... | collective-permute-start | bytes 983048 | tf_op jit(solution)/shard_map/ppermute | solution.py:567
  70.3 8.6 %collective-permute-start.19 = (f32[2,5,4,8,128]{4,3,2,1,0:T(8,128)S(1)}, f32[2,5,4,8,128]{4,3,2,1,0:T(8,128)S(1)}, u32[]{:S(2)}, u32[]{:S(2)}) collective-permute-start(f32[2,5,4,8,128]{4,3,2,1,0:T(8,128)S(1)} %get-tuple-element.81), channel_id=1, source_target_pairs={{0,1},{1,0},{2,3},{3,2},{4,5},{5,4},{6,7},{7,6},{8,9},{9,8},{10,11... | collective-permute-start | bytes 491528 | tf_op jit(solution)/shard_map/ppermute | solution.py:497
  70.3 10.2 %collective-permute-start.20 = (f32[2,5,4,8,128]{4,3,2,1,0:T(8,128)S(1)}, f32[2,5,4,8,128]{4,3,2,1,0:T(8,128)S(1)}, u32[]{:S(2)}, u32[]{:S(2)}) collective-permute-start(f32[2,5,4,8,128]{4,3,2,1,0:T(8,128)S(1)} %get-tuple-element.82), channel_id=1, source_target_pairs={{0,4},{1,5},{2,6},{3,7},{4,0},{5,1},{6,2},{7,3},{8,12},{9,13},{10,... | collective-permute-start | bytes 491528 | tf_op jit(solution)/shard_map/ppermute | solution.py:497
  72.0 10.8 %collective-permute-start.21 = (f32[2,5,4,8,128]{4,3,2,1,0:T(8,128)S(1)}, f32[2,5,4,8,128]{4,3,2,1,0:T(8,128)S(1)}, u32[]{:S(2)}, u32[]{:S(2)}) collective-permute-start(f32[2,5,4,8,128]{4,3,2,1,0:T(8,128)S(1)} %get-tuple-element.83), channel_id=1, source_target_pairs={{0,2},{1,3},{2,0},{3,1},{4,6},{5,7},{6,4},{7,5},{8,10},{9,11},{10,... | collective-permute-start | bytes 491528 | tf_op jit(solution)/shard_map/ppermute | solution.py:497
  76.9 6.6 %collective-permute-start.22 = (f32[2,5,4,8,128]{4,3,2,1,0:T(8,128)S(1)}, f32[2,5,4,8,128]{4,3,2,1,0:T(8,128)S(1)}, u32[]{:S(2)}, u32[]{:S(2)}) collective-permute-start(f32[2,5,4,8,128]{4,3,2,1,0:T(8,128)S(1)} %get-tuple-element.84), channel_id=1, source_target_pairs={{0,5},{1,4},{2,7},{3,6},{4,1},{5,0},{6,3},{7,2},{8,13},{9,12},{10,... | collective-permute-start | bytes 491528 | tf_op jit(solution)/shard_map/ppermute | solution.py:497
  77.6 6.0 %collective-permute-start.23 = (f32[2,5,4,8,128]{4,3,2,1,0:T(8,128)S(1)}, f32[2,5,4,8,128]{4,3,2,1,0:T(8,128)S(1)}, u32[]{:S(2)}, u32[]{:S(2)}) collective-permute-start(f32[2,5,4,8,128]{4,3,2,1,0:T(8,128)S(1)} %get-tuple-element.85), channel_id=1, source_target_pairs={{0,3},{1,2},{2,1},{3,0},{4,7},{5,6},{6,5},{7,4},{8,11},{9,10},{10,... | collective-permute-start | bytes 491528 | tf_op jit(solution)/shard_map/ppermute | solution.py:497
  78.9 9.6 %collective-permute-start.24 = (f32[2,5,4,8,128]{4,3,2,1,0:T(8,128)S(1)}, f32[2,5,4,8,128]{4,3,2,1,0:T(8,128)S(1)}, u32[]{:S(2)}, u32[]{:S(2)}) collective-permute-start(f32[2,5,4,8,128]{4,3,2,1,0:T(8,128)S(1)} %get-tuple-element.86), channel_id=1, source_target_pairs={{0,6},{1,7},{2,4},{3,5},{4,2},{5,3},{6,0},{7,1},{8,14},{9,15},{10,... | collective-permute-start | bytes 491528 | tf_op jit(solution)/shard_map/ppermute | solution.py:497
  80.5 11.7 %collective-permute-start.25 = (f32[2,5,4,8,128]{4,3,2,1,0:T(8,128)S(1)}, f32[2,5,4,8,128]{4,3,2,1,0:T(8,128)S(1)}, u32[]{:S(2)}, u32[]{:S(2)}) collective-permute-start(f32[2,5,4,8,128]{4,3,2,1,0:T(8,128)S(1)} %get-tuple-element.87), channel_id=1, source_target_pairs={{0,7},{1,6},{2,5},{3,4},{4,3},{5,2},{6,1},{7,0},{8,15},{9,14},{10,... | collective-permute-start | bytes 491528 | tf_op jit(solution)/shard_map/ppermute | solution.py:497

commit v8 on v6

--- a/solution.py
+++ b/solution.py
@@ -266,7 +266,7 @@
             for j in range(2):
                 for f in range(FIELDS):
                     for x in range(DEEP):
-                        target[b, j, f, x] = source[e + 1, j, f, x]
+                        target[b, j, f, x] = source[MEMBERS // 2 - 1 - e, j, f, x]
 
 
 def block_starts(group):
@@ -402,7 +402,7 @@
 def split_kernel(near, far, one, two, three, parts_ref, columns):
     _, member = position()
     tiles = FIELDS * DEEP
-    for e, got in enumerate((None, one, two, three)):
+    for e, got in ((0, None), (3, one), (2, two), (1, three)):
         for b in range(2):
             other = member ^ (2 * e + b)
             for j in range(2):
@@ -571,7 +571,7 @@
         [shape(2, 2, FIELDS, DEEP, ROWS, LANES)] * 3,
         [near, far],
     )
-    first = [lax.ppermute(m, AXES, inside(2 * e + 2)) for e, m in enumerate(merged)]
+    first = [lax.ppermute(m, AXES, inside(2 * (MEMBERS // 2 - 1 - e))) for e, m in enumerate(merged)]
     (second_0,) = call(
         functools.partial(second_kernel, groups, 0),
         "second_step_0",
@@ -590,9 +590,9 @@
         field,
         2,
     )
-    second = spread(second[:4]) + list(second[4:])
-    second[4:], first = lax.optimization_barrier((second[4:], first))
-    second[4:] = spread(second[4:], 4)
+    second = spread(second[:5]) + list(second[5:])
+    second[5:], first = lax.optimization_barrier((second[5:], first))
+    second[5:] = spread(second[5:], 5)
 
     row_count = FIELDS * DEEP * ROWS
     (parts,) = call(

time: 112 us -> 111 us (level)
  waiting for transfers between devices: 25.2 us -> 24 us
  transfers between devices with their start and end apart: 27 -> 27, of which waited for: 10 -> 11; matrix products, arithmetic and copies ran while one was open for 0% -> 0% of each run, Pallas kernels for 19% -> 20%
where the time goes in v8:
time: 111 us; the launch traced here: 110 us
  starting transfers between devices  41.8 us (38%)
  Pallas kernels  31.1 us (28%)
  waiting for transfers between devices  24 us (22%)
  blocking collectives  12.6 us (11%)
    pallas_call x8, Pallas kernels, call(): pl.pallas_call(kernel, out_shape=out_shape, in_specs=[SMEM] * scalars + [...  21.6 us
    ppermute x14, waiting for transfers between devices, spread(): lax.ppermute(p, AXES, inside(d))  17 us
    ppermute x14, starting transfers between devices, spread(): lax.ppermute(p, AXES, inside(d))  16.7 us
    ppermute x4, starting transfers between devices, exchange(): lax.ppermute(a, AXES, swap(True))  14 us
    all_to_all x1, blocking collectives, local(): grams = lax.all_to_all(grams, AXES, 0, 0)  12.6 us
    all_to_all x1, starting transfers between devices, local(): wall = lax.all_to_all(wall, AXES, 0, 0)  4.87 us
    pallas_call x1, Pallas kernels, local(): pl.pallas_call(gram_kernel, out_shape=[jax.ShapeDtypeStruct(state_in.shap...  3.79 us
    ppermute x4, waiting for transfers between devices, exchange(): lax.ppermute(a, AXES, swap(True))  3.55 us
  transfers between devices with their start and end apart: 27, of which 11 were waited for; matrix products, arithmetic and copies ran while one was open for 0% of the time, Pallas kernels for 20%

profile of v8, /device:TPU:0, one launch (start us, length us, event | category | flops | bytes accessed | tf_op | source)
XLA Modules:
  0.0 110.4 jit_solution(8011304655741370542)
XLA Ops:
  0.6 2.4 %pack.1 = (f32[44,8,128]{2,1,0:T(8,128)S(1)}, f32[44,8,128]{2,1,0:T(8,128)S(1)}, f32[44,8,128]{2,1,0:T(8,128)S(1)}, f32[44,8,128]{2,1,0:T(8,128)S(1)}, f32[44,8,...) custom-call(f32[5,64,8,128]{3,2,1,0:T(8,128)} %bitcast.1, ...), custom_call_target="tpu_custom_call" | custom-call | bytes 6000000 | tf_op jit(solution)/shard_map/pack/pallas_call | solution.py:110
  3.6 2.6 %collective-permute-start.1 = (f32[44,8,128]{2,1,0:T(8,128)S(1)}, f32[44,8,128]{2,1,0:T(8,128)S(1)}, u32[]{:S(2)}, u32[]{:S(2)}) collective-permute-start(f32[44,8,128]{2,1,0:T(8,128)S(1)} %get-tuple-element.52), channel_id=1, source_target_pairs={{0,4},{1,5},{2,6},{3,7},{4,0},{5,1},{6,2},{7,3},{8,12},{9,13},{10,... | collective-permute-start | bytes 540680 | tf_op jit(solution)/shard_map/ppermute | solution.py:504
  6.2 1.5 %collective-permute-start.2 = (f32[44,8,128]{2,1,0:T(8,128)S(1)}, f32[44,8,128]{2,1,0:T(8,128)S(1)}, u32[]{:S(2)}, u32[]{:S(2)}) collective-permute-start(f32[44,8,128]{2,1,0:T(8,128)S(1)} %get-tuple-element.53), channel_id=1, source_target_pairs={{0,2},{1,3},{2,0},{3,1},{4,6},{5,7},{6,4},{7,5},{8,10},{9,11},{10,... | collective-permute-start | bytes 540680 | tf_op jit(solution)/shard_map/ppermute | solution.py:504
  8.0 2.9 %collective-permute-start.5 = (f32[44,8,128]{2,1,0:T(8,128)S(1)}, f32[44,8,128]{2,1,0:T(8,128)S(1)}, u32[]{:S(2)}, u32[]{:S(2)}) collective-permute-start(f32[44,8,128]{2,1,0:T(8,128)S(1)} %get-tuple-element.56), channel_id=1, source_target_pairs={{0,6},{1,7},{2,4},{3,5},{4,2},{5,3},{6,0},{7,1},{8,14},{9,15},{10,... | collective-permute-start | bytes 540680 | tf_op jit(solution)/shard_map/ppermute | solution.py:504
  11.6 1.7 %collective-permute-start.6 = (f32[44,8,128]{2,1,0:T(8,128)S(1)}, f32[44,8,128]{2,1,0:T(8,128)S(1)}, u32[]{:S(2)}, u32[]{:S(2)}) collective-permute-start(f32[44,8,128]{2,1,0:T(8,128)S(1)} %get-tuple-element.57), channel_id=1, source_target_pairs={{0,7},{1,6},{2,5},{3,4},{4,3},{5,2},{6,1},{7,0},{8,15},{9,14},{10,... | collective-permute-start | bytes 540680 | tf_op jit(solution)/shard_map/ppermute | solution.py:504
  13.3 4.9 %all-to-all-start = ((f32[32,2,8,128]{3,2,1,0:T(8,128)}), f32[32,2,8,128]{3,2,1,0:T(8,128)S(1)}, u32[]{:S(2)}, u32[]{:S(2)}) async-start(f32[32,2,8,128]{3,2,1,0:T(8,128)} %get-tuple-element.48), calls=%async_computation | async-start | bytes 524288 | tf_op jit(solution)/shard_map/all_to_all | solution.py:524
  18.2 2.6 %collective-permute-done.5.refs_6_ = f32[44,8,128]{2,1,0:T(8,128)S(1)} collective-permute-done((f32[44,8,128]{2,1,0:T(8,128)S(1)}, f32[44,8,128]{2,1,0:T(8,128)S(1)}, u32[]{:S(2)}, u32[]{:S(2)}) %collective-permute-start.5) | collective-permute-done | bytes 180256 | tf_op jit(solution)/shard_map/ppermute | solution.py:504
  20.8 4.9 %collective-permute-done.6.refs_7_ = f32[44,8,128]{2,1,0:T(8,128)S(1)} collective-permute-done((f32[44,8,128]{2,1,0:T(8,128)S(1)}, f32[44,8,128]{2,1,0:T(8,128)S(1)}, u32[]{:S(2)}, u32[]{:S(2)}) %collective-permute-start.6) | collective-permute-done | bytes 180256 | tf_op jit(solution)/shard_map/ppermute | solution.py:504
  25.9 1.8 %collective-permute-start.9 = (f32[4,24,8,128]{3,2,1,0:T(8,128)S(1)}, f32[4,24,8,128]{3,2,1,0:T(8,128)S(1)}, u32[]{:S(2)}, u32[]{:S(2)}) collective-permute-start(f32[4,24,8,128]{3,2,1,0:T(8,128)S(1)} %get-tuple-element.61.refs_0_), channel_id=1, source_target_pairs={{0,8},{1,9},{2,10},{3,11},{4,12},{5,13},{6,14},{7,15},{8,0},{9,1},... | collective-permute-start | bytes 1179656 | tf_op jit(solution)/shard_map/ppermute | solution.py:500
  28.4 4.4 %collective-permute-start.7 = (f32[4,20,8,128]{3,2,1,0:T(8,128)S(1)}, f32[4,20,8,128]{3,2,1,0:T(8,128)S(1)}, u32[]{:S(2)}, u32[]{:S(2)}) collective-permute-start(f32[4,20,8,128]{3,2,1,0:T(8,128)S(1)} %get-tuple-element.58.refs_0_), channel_id=1, source_target_pairs={{0,8},{1,9},{2,10},{3,11},{4,12},{5,13},{6,14},{7,15},{8,0},{9,1},... | collective-permute-start | bytes 983048 | tf_op jit(solution)/shard_map/ppermute | solution.py:500
  33.5 5.1 %forcing.1 = (f32[16,8,128]{2,1,0:T(8,128)S(1)}, f32[16,8,128]{2,1,0:T(8,128)S(1)}) custom-call(f32[32,2,8,128]{3,2,1,0:T(8,128)S(1)} %all-to-all-done.parts), custom_call_target="tpu_custom_call" | custom-call | bytes 15000000 | tf_op jit(solution)/shard_map/forcing/pallas_call | solution.py:507
  38.7 3.8 %first_step_0.1 = (f32[5,4,32,128]{3,2,1,0:T(8,128)S(1)}, f32[5,4,32,128]{3,2,1,0:T(8,128)S(1)}, f32[16,32,128]{2,1,0:T(8,128)S(1)}) custom-call(f32[3]{0:T(128)S(1)} %copy-done, f32[5]{0:T(128)S(1)} %copy-done.1, f32[16,8,128]{2,1,0:T(8,128)S(1)} %get-tuple-element.60.wall_ref, f32[4,24,8,128]{3,2,1,0:T(8,128)S(1)} %get-tuple-element.61.refs_0_, ...), custom_call_target="tpu_custom_call" | custom-call | bytes 15000000 | tf_op jit(solution)/shard_map/first_step_0/pallas_call | solution.py:507
  42.4 4.1 %collective-permute-start.11 = (f32[5,4,32,128]{3,2,1,0:T(8,128)S(1)}, f32[5,4,32,128]{3,2,1,0:T(8,128)S(1)}, u32[]{:S(2)}, u32[]{:S(2)}) collective-permute-start(f32[5,4,32,128]{3,2,1,0:T(8,128)S(1)} %get-tuple-element.64.refs_5_.refs_0_), channel_id=1, source_target_pairs={{0,8},{1,9},{2,10},{3,11},{4,12},{5,13},{6,14},{7,15},{8,0},{9,1},... | collective-permute-start | bytes 983048 | tf_op jit(solution)/shard_map/ppermute | solution.py:500
  47.3 4.0 %first_step_1.1 = (f32[5,4,32,128]{3,2,1,0:T(8,128)S(1)}, f32[5,4,32,128]{3,2,1,0:T(8,128)S(1)}, f32[4,2,5,4,8,128]{5,4,3,2,1,0:T(8,128)S(1)}, f32[4,2,5,4,8,128]{5,4,3,2,1,0:T(8,128)S(1)}) custom-call(f32[3]{0:T(128)S(1)} %copy-done, f32[5]{0:T(128)S(1)} %copy-done.1, f32[16,8,128]{2,1,0:T(8,128)S(1)} %get-tuple-element.49.wall_ref, ...), custom_call_target="tpu_custom_call" | custom-call | bytes 15000000 | tf_op jit(solution)/shard_map/first_step_1/pallas_call | solution.py:507
  51.2 3.2 %collective-permute-done.11.refs_2_ = f32[5,4,32,128]{3,2,1,0:T(8,128)S(1)} collective-permute-done((f32[5,4,32,128]{3,2,1,0:T(8,128)S(1)}, f32[5,4,32,128]{3,2,1,0:T(8,128)S(1)}, u32[]{:S(2)}, u32[]{:S(2)}) %collective-permute-start.11) | collective-permute-done | bytes 327712 | tf_op jit(solution)/shard_map/ppermute | solution.py:500
  54.4 3.6 %collective-permute-start.14 = (f32[5,4,32,128]{3,2,1,0:T(8,128)S(1)}, f32[5,4,32,128]{3,2,1,0:T(8,128)S(1)}, u32[]{:S(2)}, u32[]{:S(2)}) collective-permute-start(f32[5,4,32,128]{3,2,1,0:T(8,128)S(1)} %get-tuple-element.69.refs_0_), channel_id=1, source_target_pairs={{0,8},{1,9},{2,10},{3,11},{4,12},{5,13},{6,14},{7,15},{8,0},{9,1},... | collective-permute-start | bytes 983048 | tf_op jit(solution)/shard_map/ppermute | solution.py:500
  58.8 2.4 %collective-permute-start.16 = (f32[2,2,5,4,8,128]{5,4,3,2,1,0:T(8,128)S(1)}, f32[2,2,5,4,8,128]{5,4,3,2,1,0:T(8,128)S(1)}, u32[]{:S(2)}, u32[]{:S(2)}) collective-permute-start(f32[2,2,5,4,8,128]{5,4,3,2,1,0:T(8,128)S(1)} %get-tuple-element.74), channel_id=1, source_target_pairs={{0,6},{1,7},{2,4},{3,5},{4,2},{5,3},{6,0},{7,1},{8,14},{9,15},{10,... | collective-permute-start | bytes 983048 | tf_op jit(solution)/shard_map/ppermute | solution.py:574
  62.4 3.7 %second_step_0.1.refs_5_ = f32[5,8,32,128]{3,2,1,0:T(8,128)S(1)} custom-call(f32[3]{0:T(128)S(1)} %copy-done, f32[5]{0:T(128)S(1)} %copy-done.1, f32[16,8,128]{2,1,0:T(8,128)S(1)} %get-tuple-element.60.wall_ref, f32[5,4,32,128]{3,2,1,0:T(8,128)S(1)} %get-tuple-element.64.refs_5_.refs_0_, f32[5,4,32,128]{3,2,1,0:T(8,128)S(1)} %get-tuple-element.65.refs_6_.refs_1_, ...), custom_call_target="tpu_custom_call" | custom-call | bytes 15000000 | tf_op jit(solution)/shard_map/second_step_0/pallas_call | solution.py:507
  66.5 3.8 %second_step_1.1 = (f32[2,5,4,8,128]{4,3,2,1,0:T(8,128)S(1)}, f32[2,5,4,8,128]{4,3,2,1,0:T(8,128)S(1)}, f32[2,5,4,8,128]{4,3,2,1,0:T(8,128)S(1)}, f32[2,5,4,8,12...) custom-call(f32[3]{0:T(128)S(1)} %copy-done, ...), custom_call_target="tpu_custom_call" | custom-call | bytes 15000000 | tf_op jit(solution)/shard_map/second_step_1/pallas_call | solution.py:507
  70.4 1.7 %collective-permute-start.20 = (f32[2,5,4,8,128]{4,3,2,1,0:T(8,128)S(1)}, f32[2,5,4,8,128]{4,3,2,1,0:T(8,128)S(1)}, u32[]{:S(2)}, u32[]{:S(2)}) collective-permute-start(f32[2,5,4,8,128]{4,3,2,1,0:T(8,128)S(1)} %get-tuple-element.82), channel_id=1, source_target_pairs={{0,4},{1,5},{2,6},{3,7},{4,0},{5,1},{6,2},{7,3},{8,12},{9,13},{10,... | collective-permute-start | bytes 491528 | tf_op jit(solution)/shard_map/ppermute | solution.py:504
  72.1 1.3 %collective-permute-start.21 = (f32[2,5,4,8,128]{4,3,2,1,0:T(8,128)S(1)}, f32[2,5,4,8,128]{4,3,2,1,0:T(8,128)S(1)}, u32[]{:S(2)}, u32[]{:S(2)}) collective-permute-start(f32[2,5,4,8,128]{4,3,2,1,0:T(8,128)S(1)} %get-tuple-element.83), channel_id=1, source_target_pairs={{0,2},{1,3},{2,0},{3,1},{4,6},{5,7},{6,4},{7,5},{8,10},{9,11},{10,... | collective-permute-start | bytes 491528 | tf_op jit(solution)/shard_map/ppermute | solution.py:504
  73.3 3.4 %collective-permute-done.17.two = f32[2,2,5,4,8,128]{5,4,3,2,1,0:T(8,128)S(1)} collective-permute-done((f32[2,2,5,4,8,128]{5,4,3,2,1,0:T(8,128)S(1)}, f32[2,2,5,4,8,128]{5,4,3,2,1,0:T(8,128)S(1)}, u32[]{:S(2)}, u32[]{:S(2)}) %collective-permute-start.17) | collective-permute-done | bytes 327712 | tf_op jit(solution)/shard_map/ppermute | solution.py:574
  76.8 1.1 %collective-permute-start.22 = (f32[2,5,4,8,128]{4,3,2,1,0:T(8,128)S(1)}, f32[2,5,4,8,128]{4,3,2,1,0:T(8,128)S(1)}, u32[]{:S(2)}, u32[]{:S(2)}) collective-permute-start(f32[2,5,4,8,128]{4,3,2,1,0:T(8,128)S(1)} %get-tuple-element.84), channel_id=1, source_target_pairs={{0,5},{1,4},{2,7},{3,6},{4,1},{5,0},{6,3},{7,2},{8,13},{9,12},{10,... | collective-permute-start | bytes 491528 | tf_op jit(solution)/shard_map/ppermute | solution.py:504
  77.9 1.5 %collective-permute-start.23 = (f32[2,5,4,8,128]{4,3,2,1,0:T(8,128)S(1)}, f32[2,5,4,8,128]{4,3,2,1,0:T(8,128)S(1)}, u32[]{:S(2)}, u32[]{:S(2)}) collective-permute-start(f32[2,5,4,8,128]{4,3,2,1,0:T(8,128)S(1)} %get-tuple-element.85), channel_id=1, source_target_pairs={{0,3},{1,2},{2,1},{3,0},{4,7},{5,6},{6,5},{7,4},{8,11},{9,10},{10,... | collective-permute-start | bytes 491528 | tf_op jit(solution)/shard_map/ppermute | solution.py:504
  80.3 0.9 collective-permute-start.25
  81.2 1.0 split.1.first_parts
  82.2 1.4 %collective-permute-done.22.refs_4_ = f32[2,5,4,8,128]{4,3,2,1,0:T(8,128)S(1)} collective-permute-done((f32[2,5,4,8,128]{4,3,2,1,0:T(8,128)S(1)}, f32[2,5,4,8,128]{4,3,2,1,0:T(8,128)S(1)}, u32[]{:S(2)}, u32[]{:S(2)}) %collective-permute-start.22) | collective-permute-done | bytes 163872 | tf_op jit(solution)/shard_map/ppermute | solution.py:504
  84.0 4.5 %collective-permute-done.24.refs_6_ = f32[2,5,4,8,128]{4,3,2,1,0:T(8,128)S(1)} collective-permute-done((f32[2,5,4,8,128]{4,3,2,1,0:T(8,128)S(1)}, f32[2,5,4,8,128]{4,3,2,1,0:T(8,128)S(1)}, u32[]{:S(2)}, u32[]{:S(2)}) %collective-permute-start.24) | collective-permute-done | bytes 163872 | tf_op jit(solution)/shard_map/ppermute | solution.py:504
  88.5 2.2 %collective-permute-done.25.refs_7_ = f32[2,5,4,8,128]{4,3,2,1,0:T(8,128)S(1)} collective-permute-done((f32[2,5,4,8,128]{4,3,2,1,0:T(8,128)S(1)}, f32[2,5,4,8,128]{4,3,2,1,0:T(8,128)S(1)}, u32[]{:S(2)}, u32[]{:S(2)}) %collective-permute-start.25) | collective-permute-done | bytes 163872 | tf_op jit(solution)/shard_map/ppermute | solution.py:504
  90.7 3.8 %gram.1 = (f32[5,16,4,8,128]{4,3,2,1,0:T(8,128)}, f32[32,8,128]{2,1,0:T(8,128)S(1)}) custom-call(bf16[40,48,512]{2,1,0:T(8,128)(2,1)S(1)} %split.1.first_parts, f32[2,5,4,8,128]{4,3,2,1,0:T(8,128)S(1)} %get-tuple-element.80.refs_0_, f32[2,5,4,8,128]{4,3,2,1,0:T(8,128)S(1)} %collective-permute-done.19.refs_1_, ...), custom_call_target="tpu_custom_call" | custom-call | tf_op jit(solution)/shard_map/gram/pallas_call | solution.py:608
  94.5 12.6 %all_to_all.10.parts_ref = f32[32,8,128]{2,1,0:T(8,128)S(1)} all-to-all(f32[32,8,128]{2,1,0:T(8,128)S(1)} %get-tuple-element.89), channel_id=1, replica_groups=mesh['gx'=8,'gy'=4] {'gx','gy'}, dimensions={0} | all-to-all | bytes 262144 | tf_op jit(solution)/shard_map/all_to_all | solution.py:620
  107.1 3.3 %factor.1 = f32[32,32]{1,0:T(8,128)} custom-call(f32[32,8,128]{2,1,0:T(8,128)S(1)} %all_to_all.10.parts_ref), custom_call_target="tpu_custom_call" | custom-call | tf_op jit(solution)/shard_map/factor/pallas_call | solution.py:621
  (38 shorter events, 7.4 us)
Async XLA Ops:
  3.1 35.6 %copy-start = (f32[3]{0:T(128)S(1)}, f32[3]{0:T(128)}, u32[]{:S(2)}) copy-start(f32[3]{0:T(128)} %vel_ref.7) | copy-start | bytes 40
  3.1 35.6 %copy-start.1 = (f32[5]{0:T(128)S(1)}, f32[5]{0:T(128)}, u32[]{:S(2)}) copy-start(f32[5]{0:T(128)} %vec_ref.7) | copy-start | bytes 64
  3.1 4.9 %collective-permute-start = (f32[44,8,128]{2,1,0:T(8,128)S(1)}, f32[44,8,128]{2,1,0:T(8,128)S(1)}, u32[]{:S(2)}, u32[]{:S(2)}) collective-permute-start(f32[44,8,128]{2,1,0:T(8,128)S(1)} %get-tuple-element.47), channel_id=1, source_target_pairs={{0,1},{1,0},{2,3},{3,2},{4,5},{5,4},{6,7},{7,6},{8,9},{9,8},{10,11... | collective-permute-start | bytes 540680 | tf_op jit(solution)/shard_map/ppermute | solution.py:504
  3.6 8.0 %collective-permute-start.1 = (f32[44,8,128]{2,1,0:T(8,128)S(1)}, f32[44,8,128]{2,1,0:T(8,128)S(1)}, u32[]{:S(2)}, u32[]{:S(2)}) collective-permute-start(f32[44,8,128]{2,1,0:T(8,128)S(1)} %get-tuple-element.52), channel_id=1, source_target_pairs={{0,4},{1,5},{2,6},{3,7},{4,0},{5,1},{6,2},{7,3},{8,12},{9,13},{10,... | collective-permute-start | bytes 540680 | tf_op jit(solution)/shard_map/ppermute | solution.py:504
  6.2 12.0 %collective-permute-start.2 = (f32[44,8,128]{2,1,0:T(8,128)S(1)}, f32[44,8,128]{2,1,0:T(8,128)S(1)}, u32[]{:S(2)}, u32[]{:S(2)}) collective-permute-start(f32[44,8,128]{2,1,0:T(8,128)S(1)} %get-tuple-element.53), channel_id=1, source_target_pairs={{0,2},{1,3},{2,0},{3,1},{4,6},{5,7},{6,4},{7,5},{8,10},{9,11},{10,... | collective-permute-start | bytes 540680 | tf_op jit(solution)/shard_map/ppermute | solution.py:504
  7.7 10.5 %collective-permute-start.3 = (f32[44,8,128]{2,1,0:T(8,128)S(1)}, f32[44,8,128]{2,1,0:T(8,128)S(1)}, u32[]{:S(2)}, u32[]{:S(2)}) collective-permute-start(f32[44,8,128]{2,1,0:T(8,128)S(1)} %get-tuple-element.54), channel_id=1, source_target_pairs={{0,5},{1,4},{2,7},{3,6},{4,1},{5,0},{6,3},{7,2},{8,13},{9,12},{10,... | collective-permute-start | bytes 540680 | tf_op jit(solution)/shard_map/ppermute | solution.py:504
  7.7 10.5 %collective-permute-start.4 = (f32[44,8,128]{2,1,0:T(8,128)S(1)}, f32[44,8,128]{2,1,0:T(8,128)S(1)}, u32[]{:S(2)}, u32[]{:S(2)}) collective-permute-start(f32[44,8,128]{2,1,0:T(8,128)S(1)} %get-tuple-element.55), channel_id=1, source_target_pairs={{0,3},{1,2},{2,1},{3,0},{4,7},{5,6},{6,5},{7,4},{8,11},{9,10},{10,... | collective-permute-start | bytes 540680 | tf_op jit(solution)/shard_map/ppermute | solution.py:504
  8.0 12.8 %collective-permute-start.5 = (f32[44,8,128]{2,1,0:T(8,128)S(1)}, f32[44,8,128]{2,1,0:T(8,128)S(1)}, u32[]{:S(2)}, u32[]{:S(2)}) collective-permute-start(f32[44,8,128]{2,1,0:T(8,128)S(1)} %get-tuple-element.56), channel_id=1, source_target_pairs={{0,6},{1,7},{2,4},{3,5},{4,2},{5,3},{6,0},{7,1},{8,14},{9,15},{10,... | collective-permute-start | bytes 540680 | tf_op jit(solution)/shard_map/ppermute | solution.py:504
  11.6 14.1 %collective-permute-start.6 = (f32[44,8,128]{2,1,0:T(8,128)S(1)}, f32[44,8,128]{2,1,0:T(8,128)S(1)}, u32[]{:S(2)}, u32[]{:S(2)}) collective-permute-start(f32[44,8,128]{2,1,0:T(8,128)S(1)} %get-tuple-element.57), channel_id=1, source_target_pairs={{0,7},{1,6},{2,5},{3,4},{4,3},{5,2},{6,1},{7,0},{8,15},{9,14},{10,... | collective-permute-start | bytes 540680 | tf_op jit(solution)/shard_map/ppermute | solution.py:504
  13.3 20.2 %all-to-all-start = ((f32[32,2,8,128]{3,2,1,0:T(8,128)}), f32[32,2,8,128]{3,2,1,0:T(8,128)S(1)}, u32[]{:S(2)}, u32[]{:S(2)}) async-start(f32[32,2,8,128]{3,2,1,0:T(8,128)} %get-tuple-element.48), calls=%async_computation | async-start | bytes 524288 | tf_op jit(solution)/shard_map/all_to_all | solution.py:524
  25.9 12.7 %collective-permute-start.9 = (f32[4,24,8,128]{3,2,1,0:T(8,128)S(1)}, f32[4,24,8,128]{3,2,1,0:T(8,128)S(1)}, u32[]{:S(2)}, u32[]{:S(2)}) collective-permute-start(f32[4,24,8,128]{3,2,1,0:T(8,128)S(1)} %get-tuple-element.61.refs_0_), channel_id=1, source_target_pairs={{0,8},{1,9},{2,10},{3,11},{4,12},{5,13},{6,14},{7,15},{8,0},{9,1},... | collective-permute-start | bytes 1179656 | tf_op jit(solution)/shard_map/ppermute | solution.py:500
  27.8 10.9 %collective-permute-start.10 = (f32[4,24,8,128]{3,2,1,0:T(8,128)S(1)}, f32[4,24,8,128]{3,2,1,0:T(8,128)S(1)}, u32[]{:S(2)}, u32[]{:S(2)}) collective-permute-start(f32[4,24,8,128]{3,2,1,0:T(8,128)S(1)} %get-tuple-element.62.refs_1_), channel_id=1, source_target_pairs={{8,16},{9,17},{10,18},{11,19},{12,20},{13,21},{14,22},{15,23},{16,... | collective-permute-start | bytes 1179656 | tf_op jit(solution)/shard_map/ppermute | solution.py:500
  28.4 18.8 %collective-permute-start.7 = (f32[4,20,8,128]{3,2,1,0:T(8,128)S(1)}, f32[4,20,8,128]{3,2,1,0:T(8,128)S(1)}, u32[]{:S(2)}, u32[]{:S(2)}) collective-permute-start(f32[4,20,8,128]{3,2,1,0:T(8,128)S(1)} %get-tuple-element.58.refs_0_), channel_id=1, source_target_pairs={{0,8},{1,9},{2,10},{3,11},{4,12},{5,13},{6,14},{7,15},{8,0},{9,1},... | collective-permute-start | bytes 983048 | tf_op jit(solution)/shard_map/ppermute | solution.py:500
  32.8 14.4 %collective-permute-start.8 = (f32[4,20,8,128]{3,2,1,0:T(8,128)S(1)}, f32[4,20,8,128]{3,2,1,0:T(8,128)S(1)}, u32[]{:S(2)}, u32[]{:S(2)}) collective-permute-start(f32[4,20,8,128]{3,2,1,0:T(8,128)S(1)} %get-tuple-element.59.refs_1_), channel_id=1, source_target_pairs={{8,16},{9,17},{10,18},{11,19},{12,20},{13,21},{14,22},{15,23},{16,... | collective-permute-start | bytes 983048 | tf_op jit(solution)/shard_map/ppermute | solution.py:500
  42.4 12.0 %collective-permute-start.11 = (f32[5,4,32,128]{3,2,1,0:T(8,128)S(1)}, f32[5,4,32,128]{3,2,1,0:T(8,128)S(1)}, u32[]{:S(2)}, u32[]{:S(2)}) collective-permute-start(f32[5,4,32,128]{3,2,1,0:T(8,128)S(1)} %get-tuple-element.64.refs_5_.refs_0_), channel_id=1, source_target_pairs={{0,8},{1,9},{2,10},{3,11},{4,12},{5,13},{6,14},{7,15},{8,0},{9,1},... | collective-permute-start | bytes 983048 | tf_op jit(solution)/shard_map/ppermute | solution.py:500
  46.6 7.9 %collective-permute-start.12 = (f32[5,4,32,128]{3,2,1,0:T(8,128)S(1)}, f32[5,4,32,128]{3,2,1,0:T(8,128)S(1)}, u32[]{:S(2)}, u32[]{:S(2)}) collective-permute-start(f32[5,4,32,128]{3,2,1,0:T(8,128)S(1)} %get-tuple-element.65.refs_6_.refs_1_), channel_id=1, source_target_pairs={{8,16},{9,17},{10,18},{11,19},{12,20},{13,21},{14,22},{15,23},{16,... | collective-permute-start | bytes 983048 | tf_op jit(solution)/shard_map/ppermute | solution.py:500
  54.4 4.3 %collective-permute-start.13 = (f32[4,2,5,4,8,128]{5,4,3,2,1,0:T(8,128)S(1)}, f32[4,2,5,4,8,128]{5,4,3,2,1,0:T(8,128)S(1)}, u32[]{:S(2)}, u32[]{:S(2)}) collective-permute-start(f32[4,2,5,4,8,128]{5,4,3,2,1,0:T(8,128)S(1)} %get-tuple-element.68), channel_id=1, source_target_pairs={{0,1},{1,0},{2,3},{3,2},{4,5},{5,4},{6,7},{7,6},{8,9},{9,8},{10,11... | collective-permute-start | bytes 1966088 | tf_op jit(solution)/shard_map/ppermute | solution.py:566
  54.4 12.0 %collective-permute-start.14 = (f32[5,4,32,128]{3,2,1,0:T(8,128)S(1)}, f32[5,4,32,128]{3,2,1,0:T(8,128)S(1)}, u32[]{:S(2)}, u32[]{:S(2)}) collective-permute-start(f32[5,4,32,128]{3,2,1,0:T(8,128)S(1)} %get-tuple-element.69.refs_0_), channel_id=1, source_target_pairs={{0,8},{1,9},{2,10},{3,11},{4,12},{5,13},{6,14},{7,15},{8,0},{9,1},... | collective-permute-start | bytes 983048 | tf_op jit(solution)/shard_map/ppermute | solution.py:500
  58.1 8.4 %collective-permute-start.15 = (f32[5,4,32,128]{3,2,1,0:T(8,128)S(1)}, f32[5,4,32,128]{3,2,1,0:T(8,128)S(1)}, u32[]{:S(2)}, u32[]{:S(2)}) collective-permute-start(f32[5,4,32,128]{3,2,1,0:T(8,128)S(1)} %get-tuple-element.70.refs_1_), channel_id=1, source_target_pairs={{8,16},{9,17},{10,18},{11,19},{12,20},{13,21},{14,22},{15,23},{16,... | collective-permute-start | bytes 983048 | tf_op jit(solution)/shard_map/ppermute | solution.py:500
  58.8 13.2 %collective-permute-start.16 = (f32[2,2,5,4,8,128]{5,4,3,2,1,0:T(8,128)S(1)}, f32[2,2,5,4,8,128]{5,4,3,2,1,0:T(8,128)S(1)}, u32[]{:S(2)}, u32[]{:S(2)}) collective-permute-start(f32[2,2,5,4,8,128]{5,4,3,2,1,0:T(8,128)S(1)} %get-tuple-element.74), channel_id=1, source_target_pairs={{0,6},{1,7},{2,4},{3,5},{4,2},{5,3},{6,0},{7,1},{8,14},{9,15},{10,... | collective-permute-start | bytes 983048 | tf_op jit(solution)/shard_map/ppermute | solution.py:574
  61.2 15.5 %collective-permute-start.17 = (f32[2,2,5,4,8,128]{5,4,3,2,1,0:T(8,128)S(1)}, f32[2,2,5,4,8,128]{5,4,3,2,1,0:T(8,128)S(1)}, u32[]{:S(2)}, u32[]{:S(2)}) collective-permute-start(f32[2,2,5,4,8,128]{5,4,3,2,1,0:T(8,128)S(1)} %get-tuple-element.75), channel_id=1, source_target_pairs={{0,4},{1,5},{2,6},{3,7},{4,0},{5,1},{6,2},{7,3},{8,12},{9,13},{10,... | collective-permute-start | bytes 983048 | tf_op jit(solution)/shard_map/ppermute | solution.py:574
  61.9 16.0 %collective-permute-start.18 = (f32[2,2,5,4,8,128]{5,4,3,2,1,0:T(8,128)S(1)}, f32[2,2,5,4,8,128]{5,4,3,2,1,0:T(8,128)S(1)}, u32[]{:S(2)}, u32[]{:S(2)}) collective-permute-start(f32[2,2,5,4,8,128]{5,4,3,2,1,0:T(8,128)S(1)} %get-tuple-element.76), channel_id=1, source_target_pairs={{0,2},{1,3},{2,0},{3,1},{4,6},{5,7},{6,4},{7,5},{8,10},{9,11},{10,... | collective-permute-start | bytes 983048 | tf_op jit(solution)/shard_map/ppermute | solution.py:574
  70.3 9.1 %collective-permute-start.19 = (f32[2,5,4,8,128]{4,3,2,1,0:T(8,128)S(1)}, f32[2,5,4,8,128]{4,3,2,1,0:T(8,128)S(1)}, u32[]{:S(2)}, u32[]{:S(2)}) collective-permute-start(f32[2,5,4,8,128]{4,3,2,1,0:T(8,128)S(1)} %get-tuple-element.81), channel_id=1, source_target_pairs={{0,1},{1,0},{2,3},{3,2},{4,5},{5,4},{6,7},{7,6},{8,9},{9,8},{10,11... | collective-permute-start | bytes 491528 | tf_op jit(solution)/shard_map/ppermute | solution.py:504
  70.4 9.9 %collective-permute-start.20 = (f32[2,5,4,8,128]{4,3,2,1,0:T(8,128)S(1)}, f32[2,5,4,8,128]{4,3,2,1,0:T(8,128)S(1)}, u32[]{:S(2)}, u32[]{:S(2)}) collective-permute-start(f32[2,5,4,8,128]{4,3,2,1,0:T(8,128)S(1)} %get-tuple-element.82), channel_id=1, source_target_pairs={{0,4},{1,5},{2,6},{3,7},{4,0},{5,1},{6,2},{7,3},{8,12},{9,13},{10,... | collective-permute-start | bytes 491528 | tf_op jit(solution)/shard_map/ppermute | solution.py:504
  72.1 10.1 %collective-permute-start.21 = (f32[2,5,4,8,128]{4,3,2,1,0:T(8,128)S(1)}, f32[2,5,4,8,128]{4,3,2,1,0:T(8,128)S(1)}, u32[]{:S(2)}, u32[]{:S(2)}) collective-permute-start(f32[2,5,4,8,128]{4,3,2,1,0:T(8,128)S(1)} %get-tuple-element.83), channel_id=1, source_target_pairs={{0,2},{1,3},{2,0},{3,1},{4,6},{5,7},{6,4},{7,5},{8,10},{9,11},{10,... | collective-permute-start | bytes 491528 | tf_op jit(solution)/shard_map/ppermute | solution.py:504
  76.8 6.8 %collective-permute-start.22 = (f32[2,5,4,8,128]{4,3,2,1,0:T(8,128)S(1)}, f32[2,5,4,8,128]{4,3,2,1,0:T(8,128)S(1)}, u32[]{:S(2)}, u32[]{:S(2)}) collective-permute-start(f32[2,5,4,8,128]{4,3,2,1,0:T(8,128)S(1)} %get-tuple-element.84), channel_id=1, source_target_pairs={{0,5},{1,4},{2,7},{3,6},{4,1},{5,0},{6,3},{7,2},{8,13},{9,12},{10,... | collective-permute-start | bytes 491528 | tf_op jit(solution)/shard_map/ppermute | solution.py:504
  77.9 6.1 %collective-permute-start.23 = (f32[2,5,4,8,128]{4,3,2,1,0:T(8,128)S(1)}, f32[2,5,4,8,128]{4,3,2,1,0:T(8,128)S(1)}, u32[]{:S(2)}, u32[]{:S(2)}) collective-permute-start(f32[2,5,4,8,128]{4,3,2,1,0:T(8,128)S(1)} %get-tuple-element.85), channel_id=1, source_target_pairs={{0,3},{1,2},{2,1},{3,0},{4,7},{5,6},{6,5},{7,4},{8,11},{9,10},{10,... | collective-permute-start | bytes 491528 | tf_op jit(solution)/shard_map/ppermute | solution.py:504
  79.4 9.1 %collective-permute-start.24 = (f32[2,5,4,8,128]{4,3,2,1,0:T(8,128)S(1)}, f32[2,5,4,8,128]{4,3,2,1,0:T(8,128)S(1)}, u32[]{:S(2)}, u32[]{:S(2)}) collective-permute-start(f32[2,5,4,8,128]{4,3,2,1,0:T(8,128)S(1)} %get-tuple-element.86), channel_id=1, source_target_pairs={{0,6},{1,7},{2,4},{3,5},{4,2},{5,3},{6,0},{7,1},{8,14},{9,15},{10,... | collective-permute-start | bytes 491528 | tf_op jit(solution)/shard_map/ppermute | solution.py:504
  80.3 10.4 %collective-permute-start.25 = (f32[2,5,4,8,128]{4,3,2,1,0:T(8,128)S(1)}, f32[2,5,4,8,128]{4,3,2,1,0:T(8,128)S(1)}, u32[]{:S(2)}, u32[]{:S(2)}) collective-permute-start(f32[2,5,4,8,128]{4,3,2,1,0:T(8,128)S(1)} %get-tuple-element.87), channel_id=1, source_target_pairs={{0,7},{1,6},{2,5},{3,4},{4,3},{5,2},{6,1},{7,0},{8,15},{9,14},{10,... | collective-permute-start | bytes 491528 | tf_op jit(solution)/shard_map/ppermute | solution.py:504
